TPU v7x, 32 devices: a whole 2x2x4 slice. The times are simulated.
32 devices in a mesh: rel: 2 (over x), ent: 16 (over z, y, core).
Axes of the slice: x: 2, y: 2, z: 4, core: 2. Of those that a mesh axis runs over, the one named last changes fastest.
Arguments:
- state: bfloat16 [4096, 1024], P('ent', 'rel'), may hold values from -4 to 4
- rel_weight: bfloat16 [24, 1024, 1024], P('rel', 'ent'), may hold values from -0.0390625 to 0.0390625
- gate_weight: bfloat16 [1024, 1024], P(None, 'rel'), may hold values from -0.1875 to 0.1875
- gate_bias: float32 [1024], P('rel'), may hold values from -4 to 4
- update_bias: float32 [1024], P('rel'), may hold values from -3 to 3
- tile_values: bfloat16 [2, 256, 128, 128], P('rel', 'ent'), may hold values from 0 to 0.119628906
- tile_index: int32 [2, 3, 256], P('rel', None, 'ent'), may hold values from 0 to 31, as said below
- tile_count: int32 [2, 16], P('rel', 'ent'), may hold values from 1 to 16, as said below
Outputs:
- new_state: bfloat16 [4096, 1024], P('ent', 'rel')
Inputs may be any that keep to these rules, and one draw needn't show every extreme that they name: `tile_index`: row 0 names a source tile of the whole graph, row 1 a destination tile of the partition that owns the slot (below 2), row 2 a relation within the group (below 12). `tile_count`: slots of a partition at or past its count are padding; in every group some partition fills all 16 slots.
All inputs are finite; a program needn't handle non-finite values.
Results may differ from a plain program's by a relative error of at most 0.0065.
Values may be sent and summed in bfloat16 or wider, within the bound.
No kernel may reach another device: no remote copies, remote signals or barrier semaphores. Data moves between devices by JAX's collectives and lax.ppermute only.
A program may use at most 128 MiB of HBM per device.

v0:
```python
import jax
import jax.numpy as jnp
from jax import lax
from jax.sharding import PartitionSpec as P


def collect(gathered, tile_values, tile_index, tile_count, rel_dev, per_tile):
    tile_rows = tile_values.shape[-1]
    features = gathered.shape[1]
    stacked = gathered.reshape(-1, tile_rows, features)
    listing = tile_index[0]
    values = tile_values[0]
    live_total = tile_count[0, 0]
    classes = per_tile * rel_dev
    slab_rows = min(8, values.shape[0])
    class_ids = jnp.arange(classes, dtype=jnp.int32)

    def accumulate(turn_num, summed):
        first_slot = turn_num * slab_rows
        slab_values = lax.dynamic_slice_in_dim(values, first_slot, slab_rows, 0)
        picked = lax.dynamic_slice_in_dim(listing, first_slot, slab_rows, 1)
        sources = stacked[picked[0]]
        product = jnp.einsum(
            "sij,sjh->sih", slab_values, sources, preferred_element_type=jnp.float32
        )
        slot_ids = first_slot + jnp.arange(slab_rows, dtype=jnp.int32)
        live_mask = (slot_ids < live_total).astype(jnp.float32)
        target = picked[1] * rel_dev + picked[2]
        select = (target[:, None] == class_ids[None, :]).astype(jnp.float32) * live_mask[:, None]
        return summed + jnp.einsum("sk,sih->kih", select, product, precision=lax.Precision.HIGHEST)

    initial = jnp.zeros((classes, tile_rows, features), jnp.float32)
    turn_total = (live_total + slab_rows - 1) // slab_rows
    return lax.fori_loop(0, turn_total, accumulate, initial)


def shards(
    state, rel_weight, gate_weight, gate_bias, update_bias, tile_values, tile_index, tile_count
):
    rel_dev = rel_weight.shape[0]
    ent_dev = state.shape[0]
    tile_rows = tile_values.shape[-1]
    per_tile = ent_dev // tile_rows
    features = rel_weight.shape[2]
    relation_full = lax.all_gather(rel_weight, "ent", axis=1, tiled=True)
    columns = state
    own_rows = lax.all_gather(columns, "rel", axis=1, tiled=True)
    gathered = lax.all_gather(own_rows, "ent", axis=0, tiled=True)
    summed = collect(gathered, tile_values, tile_index, tile_count, rel_dev, per_tile)
    aggregate = summed.astype(jnp.bfloat16).reshape(per_tile, rel_dev, tile_rows, features)
    group_terms = jnp.einsum(
        "drih,rhk->dik", aggregate, relation_full, preferred_element_type=jnp.float32
    )
    message = lax.psum_scatter(
        group_terms.reshape(ent_dev, features).astype(jnp.bfloat16),
        "rel",
        scatter_dimension=1,
        tiled=True,
    ).astype(jnp.float32)
    gate_open = jax.nn.sigmoid(
        jnp.dot(own_rows, gate_weight, preferred_element_type=jnp.float32) + gate_bias
    )
    update = jnp.tanh(message + update_bias)
    columns = ((1.0 - gate_open) * columns.astype(jnp.float32) + gate_open * update).astype(
        jnp.bfloat16
    )
    return columns


def solution(mesh):
    in_specs = (
        P("ent", "rel"),
        P("rel", "ent", None),
        P(None, "rel"),
        P("rel"),
        P("rel"),
        P("rel", "ent", None, None),
        P("rel", None, "ent"),
        P("rel", "ent"),
    )
    out_specs = P("ent", "rel")
    return jax.shard_map(shards, mesh=mesh, in_specs=in_specs, out_specs=out_specs, check_vma=False)
```

profile of v0, /device:TPU:0, one launch (start us, length us, event | category | flops | bytes accessed | tf_op | source)
XLA Modules:
  0.0 259.8 jit_solution(18171304255130396383)
XLA Ops:
  6.5 0.0 copy-start
  6.5 0.0 all-gather.3.cloned.1.call-start
  6.5 12.1 %all_gather.9 = bf16[256,1024]{1,0:T(8,128)(2,1)} all-gather(bf16[256,512]{1,0:T(8,128)(2,1)} %param.10), channel_id=1, replica_groups=mesh['rel'=2,'ent'=16] {'rel'}, dimensions={1}, use_global_device_ids=true | all-gather | bytes 786432 | tf_op jit(solution)/shard_map/all_gather | solution.py:47
  18.6 0.0 all-gather.3.cloned.1.call-update
  18.6 0.0 all-gather.5.cloned.1.call-start
  18.7 0.7 all-gather.5.cloned.1.call-update
  19.4 0.0 reduce-scatter.2.cloned.1.call-start
  20.1 0.7 copy.20
  20.8 72.6 %all-gather.3.cloned.1.call-done = bf16[4096,1024]{1,0:T(8,128)(2,1)} async-done(((bf16[256,1024]{1,0:T(8,128)(2,1)}), bf16[4096,1024]{1,0:T(8,128)(2,1)}) %all-gather.3.cloned.1.call-update) | async-done | bytes 8388624 | tf_op jit(solution)/shard_map/all_gather | solution.py:48
  93.4 6.2 %broadcast_in_dim.2 = f32[24,128,1024]{2,0,1:T(8,128)} broadcast(f32[]{:T(128)} %constant.34.clone.1), dimensions={} | broadcast | bytes 12582916 | tf_op jit(solution)/shard_map/broadcast_in_dim | solution.py:32
  99.6 45.0 %while.11 = (s32[]{:T(128)}, f32[24,128,1024]{2,0,1:T(8,128)}, s32[]{:T(128)}, s32[3,16]{1,0:T(4,128)S(1)}, s32[]{:T(128)}, /*index=5*/bf16[16,128,128]{2,1,0:T(...) while((s32[]{:T(128)}, f32[24,128,1024]{2,0,1:T(8,128)}, ...), condition=%wide.region_1.2_spmd.clone, body=%wide.region_0.1_spmd.clone.sunk | while | flops 573572544 | bytes 40112808 | solution.py:34
  99.6 0.1 constant_dynamic-slice_fusion.2
  99.7 4.6 %gather_fusion = bf16[8,128,1024]{2,1,0:T(8,128)(2,1)S(1)} fusion(bf16[32,128,1024]{2,1,0:T(8,128)(2,1)} %get-tuple-element.152, s32[1024]{0:T(1024)S(1)} %pad_clamp_fusion.2), kind=kCustom, calls=%fused_computation.clone.clone.1 | custom fusion | bytes 4194336 | tf_op jit(solution)/shard_map/while/body/gather | solution.py:22
  104.3 1.6 fusion.34
  106.0 0.7 compare_convert_fusion.2
  106.7 15.7 %convolution_add_fusion.3 = f32[24,128,1024]{2,0,1:T(8,128)} fusion(f32[24,128,1024]{2,0,1:T(8,128)} %get-tuple-element.136, f32[8,128,1024]{2,1,0:T(8,128)S(1)} %fusion.34, f32[8]{0:T(128)S(1)} %compare_convert_fusion.2, s32[8]{0:T(128)S(1)} %add_bitcast_fusion.2), kind=kOutput, calls=%fused_computation.2.clone.1 | convolution fusion | flops 305136000 | bytes 29360192 | tf_op jit(solution)/shard_map/while/body/sk,sih->kih/dot_general | solution.py:30
  122.3 0.1 constant_dynamic-slice_fusion.2
  122.4 4.3 %gather_fusion = bf16[8,128,1024]{2,1,0:T(8,128)(2,1)S(1)} fusion(bf16[32,128,1024]{2,1,0:T(8,128)(2,1)} %get-tuple-element.152, s32[1024]{0:T(1024)S(1)} %pad_clamp_fusion.2), kind=kCustom, calls=%fused_computation.clone.clone.1 | custom fusion | bytes 4194336 | tf_op jit(solution)/shard_map/while/body/gather | solution.py:22
  126.7 1.6 fusion.34
  128.4 0.7 compare_convert_fusion.2
  129.0 15.5 %convolution_add_fusion.3 = f32[24,128,1024]{2,0,1:T(8,128)} fusion(f32[24,128,1024]{2,0,1:T(8,128)} %get-tuple-element.136, f32[8,128,1024]{2,1,0:T(8,128)S(1)} %fusion.34, f32[8]{0:T(128)S(1)} %compare_convert_fusion.2, s32[8]{0:T(128)S(1)} %add_bitcast_fusion.2), kind=kOutput, calls=%fused_computation.2.clone.1 | convolution fusion | flops 305136000 | bytes 29360192 | tf_op jit(solution)/shard_map/while/body/sk,sih->kih/dot_general | solution.py:30
  144.6 14.2 %copy.19 = bf16[24,128,1024]{2,1,0:T(8,128)(2,1)} copy(f32[24,128,1024]{2,0,1:T(8,128)} %get-tuple-element.48) | data formatting | bytes 18874368 | tf_op jit(solution)/shard_map/while | solution.py:34
  158.7 6.6 %copy.13 = bf16[2,128,1024,12]{2,1,0,3:T(8,128)(2,1)} copy(bf16[2,128,1024,12]{2,1,3,0:T(8,128)(2,1)} %bitcast.39) | data formatting | bytes 12582912 | tf_op jit(solution)/shard_map/drih,rhk->dik/dot_general | solution.py:51
  165.3 56.8 %all-gather.5.cloned.1.call-done = bf16[12,1024,1024]{2,1,0:T(8,128)(2,1)} async-done(((bf16[12,64,1024]{2,1,0:T(8,128)(2,1)}), bf16[12,1024,1024]{2,1,0:T(8,128)(2,1)}) %all-gather.5.cloned.1.call-update) | async-done | bytes 25165840 | tf_op jit(solution)/shard_map/all_gather | solution.py:45
  222.1 0.0 copy-start.1
  222.1 0.0 copy-start.2
  222.1 0.0 copy-start.3
  222.1 0.0 copy-start.4
  222.1 14.1 %fusion.13 = bf16[256,1024]{1,0:T(8,128)(2,1)} fusion(bf16[256,1024,12]{1,0,2:T(8,128)(2,1)} %bitcast.41, bf16[12,1024,1024]{2,1,0:T(8,128)(2,1)} %all-gather.5.cloned.1.call-done), kind=kOutput, calls=%fused_computation.22 | convolution fusion | flops 6442713088 | bytes 31981568 | tf_op jit(solution)/shard_map/drih,rhk->dik/dot_general | solution.py:51
  236.2 0.0 reduce-scatter.2.cloned.1.call-update
  236.3 14.8 %reduce-scatter.2.cloned.1.call-done = bf16[256,512]{1,0:T(8,128)(2,1)} async-done(((bf16[256,1024]{1,0:T(8,128)(2,1)}), bf16[256,512]{1,0:T(8,128)(2,1)}) %reduce-scatter.2.cloned.1.call-update) | async-done | bytes 262160 | tf_op jit(solution)/shard_map/reduce_scatter | solution.py:54
  251.0 0.0 copy-done
  251.0 0.0 copy-done.1
  251.0 0.0 copy-done.2
  251.0 0.0 copy-done.3
  251.0 0.0 copy-done.4
  251.1 2.3 add_convert_fusion
  (6 shorter events, 0.0 us)
Async XLA Ops:
  6.5 244.5 %copy-start = (bf16[1024,512]{1,0:T(8,128)(2,1)S(1)}, bf16[1024,512]{1,0:T(8,128)(2,1)}, u32[]{:S(2)}) copy-start(bf16[1024,512]{1,0:T(8,128)(2,1)} %param.12) | copy-start | bytes 3145732
  6.5 86.9 %all-gather.3.cloned.1.call-start = ((), (), s32[]{:S(2)}) async-start(), calls=%async_computation.1 | async-start | bytes 8912896 | tf_op jit(solution)/shard_map/all_gather | solution.py:48
  18.6 203.5 %all-gather.5.cloned.1.call-start = ((), (), s32[]{:S(2)}) async-start(), calls=%async_computation.2 | async-start | bytes 26738688 | tf_op jit(solution)/shard_map/all_gather | solution.py:45
  19.4 231.7 %reduce-scatter.2.cloned.1.call-start = ((), (), s32[]{:S(2)}) async-start(), calls=%async_computation.3 | async-start | bytes 786432 | tf_op jit(solution)/shard_map/reduce_scatter | solution.py:54
  222.1 29.0 %copy-start.1 = (bf16[256,1024]{1,0:T(8,128)(2,1)S(1)}, bf16[256,1024]{1,0:T(8,128)(2,1)}, u32[]{:S(2)}) copy-start(bf16[256,1024]{1,0:T(8,128)(2,1)} %all_gather.9) | copy-start | bytes 1572868
  222.1 29.0 %copy-start.2 = (bf16[256,512]{1,0:T(8,128)(2,1)S(1)}, bf16[256,512]{1,0:T(8,128)(2,1)}, u32[]{:S(2)}) copy-start(bf16[256,512]{1,0:T(8,128)(2,1)} %param.10) | copy-start | bytes 786436
  222.1 29.0 %copy-start.3 = (f32[512]{0:T(512)S(1)}, f32[512]{0:T(512)}, u32[]{:S(2)}) copy-start(f32[512]{0:T(512)} %param.14) | copy-start | bytes 6148
  222.1 29.0 %copy-start.4 = (f32[512]{0:T(512)S(1)}, f32[512]{0:T(512)}, u32[]{:S(2)}) copy-start(f32[512]{0:T(512)} %param.13) | copy-start | bytes 6148
Sparse Core Ops, SparseCore 0:
  18.7 74.6 all-gather.2
  94.9 127.0 all-gather.4
  236.4 14.6 reduce-scatter.1
where the time goes:
time: 260 us
  waiting for transfers between devices  145 us (56%)
  matrix products  50.9 us (20%)
  local copies, waits for them, and re-layouts  36.7 us (14%)
  between operations  13.8 us (5%)
  blocking collectives  12.1 us (5%)
    all_gather x1, waiting for transfers between devices, shards(): gathered = lax.all_gather(own_rows, 'ent', axis=0, tiled=True)  72.6 us
    all_gather x1, waiting for transfers between devices, shards(): relation_full = lax.all_gather(rel_weight, 'ent', axis=1, tiled=True)  56.8 us
    dot_general x2, matrix products, accumulate(): jnp.einsum('sk,sih->kih', select, product, precision=lax.Precision.HIGHEST)  31.2 us
    reduce_scatter x1, waiting for transfers between devices, shards(): lax.psum_scatter(group_terms.reshape(ent_dev, features).astype(jnp.bfloat...  14.8 us
    while x1, local copies, waits for them, and re-layouts, collect(): return lax.fori_loop(0, turn_total, accumulate, initial)  14.2 us
    dot_general x1, matrix products, shards(): jnp.einsum('drih,rhk->dik', aggregate, relation_full, preferred_element_t...  14.1 us
    all_gather x1, blocking collectives, shards(): own_rows = lax.all_gather(columns, 'rel', axis=1, tiled=True)  12.1 us
    gather x2, local copies, waits for them, and re-layouts, accumulate(): sources = stacked[picked[0]]  8.9 us
  transfers between devices with their start and end apart: 3, of which 3 were waited for; matrix products, arithmetic and copies ran while one was open for 28% of the time, Pallas kernels for 0%

commit v1 on v0

v1 whole, which is shorter than its diff:
```python
import functools

import jax
import jax.numpy as jnp
from jax import lax
from jax.experimental import pallas as pl
from jax.experimental.pallas import tpu as pltpu
from jax.sharding import PartitionSpec as P


F32 = jnp.float32
BF16 = jnp.bfloat16
ANY = pl.BlockSpec(memory_space=pl.ANY)
SMEM = pl.BlockSpec(memory_space=pltpu.SMEM)
VMEM = pl.BlockSpec(memory_space=pltpu.VMEM)
GROUP = 4
NOTE_ROWS = 16


def swap(value, axis, size, bit):
    return lax.ppermute(value, axis, [(i, i ^ bit) for i in range(size)])


def pack_kernel(n_rel, where, note, *refs):
    halves, outs = refs[:n_rel], refs[n_rel:]
    rows, width = halves[0].shape[0], outs[0].shape[1]
    for j, out in enumerate(outs):
        start = pl.multiple_of(where[1, j], width)
        for r, half in enumerate(halves):

            @pl.when(where[0, j] == r)
            def _(half=half, out=out, start=start):
                out[:rows] = half[:, pl.ds(start, width)]

        if out.shape[0] > rows:
            out[rows:] = note[...]


def gate_kernel(n_rel, rel, weight, bias, *refs):
    halves, out = refs[:n_rel], refs[n_rel]
    depth = halves[0].shape[1]
    total = jnp.zeros(out.shape, F32) + bias[...]
    for r, half in enumerate(halves):
        start = pl.multiple_of(lax.bitwise_xor(rel[0], r) * depth, depth)
        total += jnp.dot(half[...], weight[pl.ds(start, depth), :], preferred_element_type=F32)
    out[...] = jax.nn.sigmoid(total)


def messages_kernel(plan, table, counts, home, *refs):
    js, members, tile_ways, n_weights, n_rel, tile_rows = plan
    states, refs = refs[:members], refs[members:]
    n_tiles = sum(len(ways) for ways in tile_ways)
    tiles, refs = refs[:n_tiles], refs[n_tiles:]
    weights, refs = refs[:n_weights], refs[n_weights:]
    outs, refs = refs[:len(js) * n_rel], refs[len(js) * n_rel:]
    rows_held, lists, made, held, acc, state_sem, tile_sem, weight_sem = refs
    slots = lists.shape[1]
    per_tile = acc.shape[0] - 1
    features = acc.shape[-1]
    own = features // n_rel
    block = weights[0].shape[1]
    per_member = states[0].shape[0]

    loads = []
    for i, ref in enumerate(states):
        loads.append(
            pltpu.make_async_copy(ref, rows_held.at[pl.ds(i * per_member, per_member)], state_sem.at[i])
        )
        loads[-1].start()
    first = 0
    tile_loads = []
    for g, ways in enumerate(tile_ways):
        options = [
            pltpu.make_async_copy(tiles[first + w], lists.at[g], tile_sem.at[g]) for w in range(len(ways))
        ]
        for w, option in enumerate(options):
            if len(options) == 1:
                option.start()
            else:
                pl.when(home[2] == w)(option.start)
        tile_loads.append(options[0])
        first += len(ways)
    weight_loads = []
    done = {}
    for n, ref in enumerate(weights):
        i = n_member(n, n_weights, members)
        start = pl.multiple_of(lax.bitwise_xor(home[0], i) * block, block)
        low = done.get(i, 0)
        done[i] = low + ref.shape[0]
        weight_loads.append(
            pltpu.make_async_copy(
                ref, held.at[pl.ds(low, ref.shape[0]), pl.ds(start, block), :], weight_sem.at[n]
            )
        )
        weight_loads[-1].start()
    for load in loads:
        load.wait()
    for g, j in enumerate(js):
        tile_loads[g].wait()

        def step(n, _, g=g, j=j):
            for u in range(GROUP):
                s = n * GROUP + u
                rows = rows_held[table[0, j * slots + s]]
                made[g, s] = jnp.dot(lists[g, s], rows, preferred_element_type=F32).astype(BF16)
            return 0

        lax.fori_loop(0, counts[j], step, 0)
    for load in weight_loads:
        load.wait()
    for g, j in enumerate(js):
        acc[:per_tile] = jnp.zeros((per_tile,) + acc.shape[1:], F32)

        def step(n, _, g=g, j=j):
            for u in range(GROUP):
                s = n * GROUP + u
                target = table[1, j * slots + s]
                acc[target] += jnp.dot(
                    made[g, s], held[table[2, j * slots + s]], preferred_element_type=F32
                )
            return 0

        lax.fori_loop(0, counts[j], step, 0)
        for r in range(n_rel):
            start = pl.multiple_of(lax.bitwise_xor(home[1], r) * own, own)
            out = outs[g * n_rel + r]
            for t in range(per_tile):
                out[t * tile_rows:(t + 1) * tile_rows] = acc[t, :, pl.ds(start, own)].astype(out.dtype)


def n_member(n, n_weights, members):
    whole = 2 * members - n_weights
    return n if n < whole else whole + (n - whole) // 2


def finish_kernel(state, gate_open, bias, *refs):
    terms, out = refs[:-1], refs[-1]
    message = sum(term[...].astype(F32) for term in terms)
    update = jnp.tanh(message + bias[...])
    opened = gate_open[...]
    out[...] = ((1.0 - opened) * state[...].astype(F32) + opened * update).astype(BF16)


def shards(
    n_rel, n_ent, chunks, state, rel_weight, gate_weight, gate_bias, update_bias,
    tile_values, tile_index, tile_count
):
    members = n_ent // chunks
    rel_dev, _, features = rel_weight.shape
    ent_dev, own_features = state.shape
    tile_rows = tile_values.shape[-1]
    slots = tile_values.shape[1]
    per_tile = ent_dev // tile_rows
    width = features // chunks
    rel = lax.axis_index("rel")
    ent = lax.axis_index("ent")
    part, member = ent // members, ent % members
    line = chunks == 4 and members == 4 and n_rel == 2

    def along(value, pairs):
        perm = [(a * members + m, b * members + m) for a, b in pairs for m in range(members)]
        return lax.ppermute(value, "ent", perm)

    def partner(value, j):
        return along(value, [(q, q ^ j) for q in range(chunks)])

    halves = [state] + [swap(state, "rel", n_rel, r) for r in range(1, n_rel)]

    values = tile_values[0]
    if line:
        near = along(values, [(0, 1), (1, 0), (2, 3), (3, 2)])
        middle = along(values, [(1, 2), (2, 1)])
        inward = along(values, [(0, 2), (3, 1)])
        edge_two = along(middle, [(2, 3), (1, 0)])
        edge_three = along(inward, [(2, 3), (1, 0)])
        tiles = [[values], [near], [inward, edge_two], [middle, edge_three]]
    else:
        tiles = [[values]] + [[partner(values, j)] for j in range(1, chunks)]

    note = jnp.zeros((NOTE_ROWS, width), BF16)
    note = note.at[:3, :slots].set(tile_index[0].astype(BF16))
    note = note.at[3, :1].set(tile_count[0].astype(BF16))
    asked = lax.bitwise_xor(part, jnp.arange(chunks, dtype=jnp.int32))
    per_half = chunks // n_rel
    where = jnp.stack([lax.bitwise_xor(asked // per_half, rel), (asked % per_half) * width])
    pieces = pl.pallas_call(
        functools.partial(pack_kernel, n_rel),
        out_shape=[
            jax.ShapeDtypeStruct((ent_dev + (NOTE_ROWS if j else 0), width), BF16)
            for j in range(chunks)
        ],
        in_specs=[SMEM] + [VMEM] * (n_rel + 1),
        out_specs=[VMEM] * chunks,
        compiler_params=pltpu.CompilerParams(vmem_limit_bytes=8 << 20),
        name="pack",
    )(where, note, *halves)
    moved = [partner(pieces[j], j) for j in range(1, chunks)]
    own = jnp.stack([pieces[0]] + [m[:ent_dev] for m in moved])
    notes = jnp.stack([note] + [m[ent_dev:] for m in moved])
    notes = notes[:, :4, :slots].astype(jnp.int32)
    counts = notes[:, 3, 0]
    source, target, relation = notes[:, 0], notes[:, 1], notes[:, 2]
    live = jnp.arange(slots, dtype=jnp.int32)[None] < counts[:, None]
    owner = source // per_tile
    place = lax.bitwise_xor(owner % members, member) * chunks
    place = (place + lax.bitwise_xor(part, owner // members)) * per_tile + source % per_tile
    table = jnp.stack([
        jnp.where(live, place, 0).reshape(-1),
        jnp.where(live, target, per_tile).reshape(-1),
        jnp.where(live, relation, 0).reshape(-1),
    ])
    turns = (counts + GROUP - 1) // GROUP

    own = own.reshape(chunks * per_tile, tile_rows, width)
    cut = max(1, rel_dev - max(1, rel_dev // 4))
    parts = (rel_weight[:cut], rel_weight[cut:])
    states, weights = [own], [(rel_weight,)]
    high = True
    bits = [1 << b for b in reversed(range(members.bit_length() - 1))]
    order = [0]
    for bit in bits:
        states = states + [swap(v, "ent", n_ent, bit) for v in states]
        more = []
        for i, held in enumerate(weights):
            if i == 0 and high:
                more.append(tuple(swap(v, "ent", n_ent, bit) for v in parts))
            elif i == 0:
                more.append((swap(rel_weight, "ent", n_ent, bit),))
            else:
                more.append(tuple(swap(v, "ent", n_ent, bit) for v in held))
        weights = weights + more
        order = order + [o | bit for o in order]
        high = False
    states = [states[order.index(i)] for i in range(members)]
    weights = [weights[order.index(i)] for i in range(members)]
    whole = [w for w in weights if len(w) == 1]
    assert all(len(w) == 1 for w in weights[:len(whole)])
    weights = [v for held in weights for v in held]
    edge = jnp.logical_or(part == 0, part == chunks - 1).astype(jnp.int32)
    home = jnp.stack([member, rel, edge])

    gate_open = pl.pallas_call(
        functools.partial(gate_kernel, n_rel),
        out_shape=jax.ShapeDtypeStruct((ent_dev, own_features), F32),
        in_specs=[SMEM] + [VMEM] * (n_rel + 2),
        out_specs=VMEM,
        compiler_params=pltpu.CompilerParams(vmem_limit_bytes=12 << 20),
        name="gate",
    )(rel.reshape(1), gate_weight, gate_bias[None], *halves)

    def partial_messages(js):
        ways = [tiles[j] for j in js]
        flat = [t for way in ways for t in way]
        plan = (js, members, tuple((0,) * len(way) for way in ways), len(weights), n_rel, tile_rows)
        n = len(js)
        shapes = []
        for _ in js:
            shapes.append(jax.ShapeDtypeStruct((ent_dev, own_features), F32))
            shapes += [jax.ShapeDtypeStruct((ent_dev, own_features), BF16)] * (n_rel - 1)
        return pl.pallas_call(
            functools.partial(messages_kernel, plan),
            out_shape=shapes,
            in_specs=[SMEM] * 3 + [ANY] * (members + len(flat) + len(weights)),
            out_specs=[VMEM] * len(shapes),
            scratch_shapes=[
                pltpu.VMEM((members * chunks * per_tile, tile_rows, width), BF16),
                pltpu.VMEM((n, slots, tile_rows, tile_rows), BF16),
                pltpu.VMEM((n, slots, tile_rows, width), BF16),
                pltpu.VMEM((rel_dev, width, features), BF16),
                pltpu.VMEM((per_tile + 1, tile_rows, features), F32),
                pltpu.SemaphoreType.DMA((members,)),
                pltpu.SemaphoreType.DMA((n,)),
                pltpu.SemaphoreType.DMA((len(weights),)),
            ],
            cost_estimate=pl.CostEstimate(
                flops=2 * n * slots * tile_rows * width * (features + tile_rows),
                bytes_accessed=2 * rel_dev * width * features,
                transcendentals=0,
            ),
            compiler_params=pltpu.CompilerParams(vmem_limit_bytes=24 << 20),
        )(table, turns, home, *states, *flat, *weights)

    half = chunks // 2
    far = tuple(reversed(range(half, chunks)))
    close = tuple(reversed(range(half)))
    terms = []
    made = list(partial_messages(far)) + list(partial_messages(close))
    for g, j in enumerate(far + close):
        term = made[g * n_rel]
        for r in range(1, n_rel):
            term = term + swap(made[g * n_rel + r], "rel", n_rel, r).astype(F32)
        if j:
            term = partner(term.astype(BF16), j)
        terms.append(term)
    return pl.pallas_call(
        finish_kernel,
        out_shape=jax.ShapeDtypeStruct((ent_dev, own_features), BF16),
        in_specs=[VMEM] * (3 + len(terms)),
        out_specs=VMEM,
        compiler_params=pltpu.CompilerParams(vmem_limit_bytes=12 << 20),
        name="finish",
    )(state, gate_open, update_bias[None], *terms)


def solution(mesh):
    n_rel, n_ent = mesh.shape["rel"], mesh.shape["ent"]
    chunks = max(4, n_rel)
    in_specs = (
        P("ent", "rel"),
        P("rel", "ent", None),
        P(None, "rel"),
        P("rel"),
        P("rel"),
        P("rel", "ent", None, None),
        P("rel", None, "ent"),
        P("rel", "ent"),
    )
    return jax.shard_map(
        functools.partial(shards, n_rel, n_ent, chunks),
        mesh=mesh, in_specs=in_specs, out_specs=P("ent", "rel"), check_vma=False,
    )
```

time: 260 us -> 137 us (0.53)
  waiting for transfers between devices: 145 us -> 69.3 us
  matrix products: 50.9 us -> 0 us
  starting transfers between devices: 0.08 us -> 40.3 us
  local copies, waits for them, and re-layouts: 36.7 us -> 8.75 us
  between operations: 13.8 us -> 0.97 us
  Pallas kernels: 0 us -> 12.6 us
  blocking collectives: 12.1 us -> 0 us
  other arithmetic: 1.36 us -> 4.32 us
    all_gather x2 -> x0, waiting for transfers between devices: 129 us -> none  [the longest x1 72.6 us: shards(): gathered = lax.all_gather(own_rows, 'ent', axis=0, tiled=True)]
    ppermute x0 -> x24, waiting for transfers between devices: none -> 69.3 us  [the longest x11 41.1 us: along(): return lax.ppermute(value, 'ent', perm)]
    dot_general x6 -> x0, matrix products: 50.9 us -> none  [the longest x2 31.2 us: accumulate(): jnp.einsum('sk,sih->kih', select, product, precision=lax.Precision.HIGHEST)]
    ppermute x0 -> x24, starting transfers between devices: none -> 40.3 us  [the longest x11 26.4 us: along(): return lax.ppermute(value, 'ent', perm)]
    reduce_scatter x1 -> x0, waiting for transfers between devices: 14.8 us -> none  [shards(): lax.psum_scatter(group_terms.reshape(ent_dev, features).astype(jnp.bfloat...]
    while x1 -> x0, local copies, waits for them, and re-layouts: 14.2 us -> none  [collect(): return lax.fori_loop(0, turn_total, accumulate, initial)]
    pallas_call x0 -> x5, Pallas kernels: none -> 12.6 us  [the longest x2 9.94 us: partial_messages(): pl.pallas_call(functools.partial(messages_kernel, plan), out_shape=shapes...]
    all_gather x1 -> x0, blocking collectives: 12.1 us -> none  [shards(): own_rows = lax.all_gather(columns, 'rel', axis=1, tiled=True)]
  transfers between devices with their start and end apart: 3 -> 24, of which waited for: 3 -> 10; matrix products, arithmetic and copies ran while one was open for 28% -> 7% of each run, Pallas kernels for 0% -> 8%
where the time goes in v1:
time: 137 us; the launch traced here: 136 us
  waiting for transfers between devices  69.3 us (51%)
  starting transfers between devices  40.3 us (29%)
  Pallas kernels  12.6 us (9%)
  local copies, waits for them, and re-layouts  8.75 us (6%)
  other arithmetic  4.32 us (3%)
    ppermute x11, waiting for transfers between devices, along(): return lax.ppermute(value, 'ent', perm)  41.1 us
    ppermute x13, waiting for transfers between devices, swap(): return lax.ppermute(value, axis, [(i, i ^ bit) for i in range(size)])  28.2 us
    ppermute x11, starting transfers between devices, along(): return lax.ppermute(value, 'ent', perm)  26.4 us
    ppermute x13, starting transfers between devices, swap(): return lax.ppermute(value, axis, [(i, i ^ bit) for i in range(size)])  13.9 us
    pallas_call x2, Pallas kernels, partial_messages(): pl.pallas_call(functools.partial(messages_kernel, plan), out_shape=shapes...  9.94 us
    unnamed x31, local copies, waits for them, and re-layouts  3.79 us
  transfers between devices with their start and end apart: 24, of which 10 were waited for; matrix products, arithmetic and copies ran while one was open for 7% of the time, Pallas kernels for 8%

profile of v1, /device:TPU:0, one launch (start us, length us, event | category | flops | bytes accessed | tf_op | source)
XLA Modules:
  0.0 136.3 jit_solution(17678101486173171484)
XLA Ops:
  0.0 3.0 %collective-permute-start = (bf16[256,512]{1,0:T(8,128)(2,1)}, bf16[256,512]{1,0:T(8,128)(2,1)S(1)}, u32[]{:S(2)}, u32[]{:S(2)}) collective-permute-start(bf16[256,512]{1,0:T(8,128)(2,1)} %state.1), channel_id=1, source_target_pairs={{0,16},{16,0},{1,17},{17,1},{2,18},{18,2},{3,19},{19,3},{4,20},{20... | collective-permute-start | bytes 786440 | tf_op jit(solution)/shard_map/ppermute | solution.py:21
  3.0 0.7 convert_element_type.35
  4.4 5.0 %collective-permute-done.refs_1_ = bf16[256,512]{1,0:T(8,128)(2,1)S(1)} collective-permute-done((bf16[256,512]{1,0:T(8,128)(2,1)}, bf16[256,512]{1,0:T(8,128)(2,1)S(1)}, u32[]{:S(2)}, u32[]{:S(2)}) %collective-permute-start) | collective-permute-done | bytes 262176 | tf_op jit(solution)/shard_map/ppermute | solution.py:21
  9.5 0.9 copy-done.1
  10.4 1.3 pack.1
  11.7 0.6 copy-done.10
  12.4 3.9 %collective-permute-start.3 = (bf16[272,256]{1,0:T(8,128)(2,1)S(1)}, bf16[272,256]{1,0:T(8,128)(2,1)S(1)}, u32[]{:S(2)}, u32[]{:S(2)}) collective-permute-start(bf16[272,256]{1,0:T(8,128)(2,1)S(1)} %get-tuple-element.43), channel_id=1, source_target_pairs={{0,12},{1,13},{2,14},{3,15},{4,8},{5,9},{6,10},{7,11},{8,4},{9,5},... | collective-permute-start | bytes 417800 | tf_op jit(solution)/shard_map/ppermute | solution.py:162
  16.2 1.6 %collective-permute-start.7 = (bf16[16,128,128]{2,1,0:T(8,128)(2,1)}, bf16[16,128,128]{2,1,0:T(8,128)(2,1)}, u32[]{:S(2)}, u32[]{:S(2)}) collective-permute-start(bf16[16,128,128]{2,1,0:T(8,128)(2,1)} %bitcast.24), channel_id=1, source_target_pairs={{4,8},{5,9},{6,10},{7,11},{8,4},{9,5},{10,6},{11,7},{20,24},{21,25... | collective-permute-start | bytes 1572872 | tf_op jit(solution)/shard_map/ppermute | solution.py:162
  17.8 4.2 %collective-permute-start.8 = (bf16[16,128,128]{2,1,0:T(8,128)(2,1)}, bf16[16,128,128]{2,1,0:T(8,128)(2,1)}, u32[]{:S(2)}, u32[]{:S(2)}) collective-permute-start(bf16[16,128,128]{2,1,0:T(8,128)(2,1)} %bitcast.25), channel_id=1, source_target_pairs={{0,8},{1,9},{2,10},{3,11},{12,4},{13,5},{14,6},{15,7},{16,24},{17,... | collective-permute-start | bytes 1572872 | tf_op jit(solution)/shard_map/ppermute | solution.py:162
  22.0 2.4 %slice.89 = bf16[9,64,1024]{2,1,0:T(8,128)(2,1)} slice(bf16[12,64,1024]{2,1,0:T(8,128)(2,1)} %refs_6_.1), slice={[0:9], [0:64], [0:1024]} | slice | bytes 2359296 | tf_op jit(solution)/shard_map/slice | solution.py:216
  24.4 1.5 %collective-permute-start.12 = (bf16[9,64,1024]{2,1,0:T(8,128)(2,1)}, bf16[9,64,1024]{2,1,0:T(8,128)(2,1)}, u32[]{:S(2)}, u32[]{:S(2)}) collective-permute-start(bf16[9,64,1024]{2,1,0:T(8,128)(2,1)} %slice.89), channel_id=1, source_target_pairs={{0,2},{1,3},{2,0},{3,1},{4,6},{5,7},{6,4},{7,5},{8,10},{9,11},{10,... | collective-permute-start | bytes 3538952 | tf_op jit(solution)/shard_map/ppermute | solution.py:21
  26.0 0.6 collective-permute-start.13
  26.6 10.8 %collective-permute-start.2 = (bf16[272,256]{1,0:T(8,128)(2,1)S(1)}, bf16[272,256]{1,0:T(8,128)(2,1)S(1)}, u32[]{:S(2)}, u32[]{:S(2)}) collective-permute-start(bf16[272,256]{1,0:T(8,128)(2,1)S(1)} %get-tuple-element.42), channel_id=1, source_target_pairs={{0,8},{1,9},{2,10},{3,11},{4,12},{5,13},{6,14},{7,15},{8,0},{9,1},... | collective-permute-start | bytes 417800 | tf_op jit(solution)/shard_map/ppermute | solution.py:162
  37.4 12.2 %collective-permute-done.2 = bf16[272,256]{1,0:T(8,128)(2,1)S(1)} collective-permute-done((bf16[272,256]{1,0:T(8,128)(2,1)S(1)}, bf16[272,256]{1,0:T(8,128)(2,1)S(1)}, u32[]{:S(2)}, u32[]{:S(2)}) %collective-permute-start.2) | collective-permute-done | bytes 139296 | tf_op jit(solution)/shard_map/ppermute | solution.py:162
  49.7 9.3 %collective-permute-done.13.refs_11_.refs_9_ = bf16[3,64,1024]{2,1,0:T(8,128)(2,1)S(1)} collective-permute-done((bf16[3,64,1024]{2,1,0:T(8,128)(2,1)S(1)}, bf16[3,64,1024]{2,1,0:T(8,128)(2,1)S(1)}, u32[]{:S(2)}, u32[]{:S(2)}) %collective-permute-start.13) | collective-permute-done | bytes 393248 | tf_op jit(solution)/shard_map/ppermute | solution.py:21
  59.1 0.5 collective-permute-start.15
  59.7 1.8 %pad_maximum_fusion = bf16[4,256,256]{2,1,0:T(8,128)(2,1)} fusion(bf16[1,256,256]{2,1,0:T(8,128)(2,1)S(1)} %slice_bitcast_fusion, bf16[1,256,256]{2,1,0:T(8,128)(2,1)S(1)} %slice_bitcast_fusion.1, bf16[1,256,256]{2,1,0:T(8,128)(2,1)S(1)} %slice_bitcast_fusion.2, bf16[1,256,256]{2,1,0:T(8,128)(2,1)} %bitcast.28), kind=kLoop, calls=%fused_computation | loop fusion | flops 786432 | bytes 1048576 | tf_op jit(solution)/shard_map/stack | solution.py:198
  61.5 0.5 collective-permute-start.4
  62.0 1.5 %collective-permute-start.5 = (bf16[8,128,256]{2,1,0:T(8,128)(2,1)}, bf16[8,128,256]{2,1,0:T(8,128)(2,1)}, u32[]{:S(2)}, u32[]{:S(2)}) collective-permute-start(bf16[8,128,256]{2,1,0:T(8,128)(2,1)} %bitcast.13.refs_0_), channel_id=1, source_target_pairs={{0,2},{1,3},{2,0},{3,1},{4,6},{5,7},{6,4},{7,5},{8,10},{9,11},{10,... | collective-permute-start | bytes 1572872 | tf_op jit(solution)/shard_map/ppermute | solution.py:21
  63.5 0.2 slice_reduce_fusion.3
  63.7 0.4 copy-done.13
  64.1 0.7 copy-done.3
  64.8 1.3 collective-permute-start.9
  66.2 0.7 lt.60
  66.9 0.8 slice_reduce_fusion.2
  67.7 0.6 squeeze.15
  68.3 0.1 squeeze.17
  68.4 0.1 squeeze.16
  68.5 1.3 collective-permute-start.10
  69.8 6.4 %collective-permute-done.5.refs_2_ = bf16[8,128,256]{2,1,0:T(8,128)(2,1)} collective-permute-done((bf16[8,128,256]{2,1,0:T(8,128)(2,1)}, bf16[8,128,256]{2,1,0:T(8,128)(2,1)}, u32[]{:S(2)}, u32[]{:S(2)}) %collective-permute-start.5) | collective-permute-done | bytes 524320 | tf_op jit(solution)/shard_map/ppermute | solution.py:21
  76.2 0.7 fusion.2
  76.9 4.9 %collective-permute-done.9.refs_5_ = bf16[16,128,128]{2,1,0:T(8,128)(2,1)} collective-permute-done((bf16[16,128,128]{2,1,0:T(8,128)(2,1)}, bf16[16,128,128]{2,1,0:T(8,128)(2,1)}, u32[]{:S(2)}, u32[]{:S(2)}) %collective-permute-start.9) | collective-permute-done | bytes 524320 | tf_op jit(solution)/shard_map/ppermute | solution.py:162
  81.8 0.7 and_select_fusion.counts
  82.5 10.4 %collective-permute-done.10.refs_7_ = bf16[16,128,128]{2,1,0:T(8,128)(2,1)S(1)} collective-permute-done((bf16[16,128,128]{2,1,0:T(8,128)(2,1)}, bf16[16,128,128]{2,1,0:T(8,128)(2,1)S(1)}, u32[]{:S(2)}, u32[]{:S(2)}) %collective-permute-start.10) | collective-permute-done | bytes 524320 | tf_op jit(solution)/shard_map/ppermute | solution.py:162
  93.0 1.0 copy-done.4
  94.0 4.2 %shard_map.82 = (f32[256,512]{1,0:T(8,128)S(1)}, bf16[256,512]{1,0:T(8,128)(2,1)S(1)}, f32[256,512]{1,0:T(8,128)S(1)}, bf16[256,512]{1,0:T(8,128)(2,1)S(1)}) custom-call(s32[3,64]{1,0:T(4,128)S(1)} %pad_add_fusion.table, s32[4]{0:T(128)S(1)} %and_select_fusion.counts, s32[3]{0:T(128)S(1)} %pad_add_fusion.2.home, bf16[8,128,256]{2,1,0:T(8,128)(2,1)} %bitcast.13.refs_0_, ...), custom_call_target="tpu_custom_call" | custom-call | flops 2415919104 | bytes 6291456 | tf_op jit(solution)/shard_map/pallas_call | solution.py:260
  98.2 3.2 %collective-permute-start.16 = (bf16[256,512]{1,0:T(8,128)(2,1)S(1)}, bf16[256,512]{1,0:T(8,128)(2,1)S(1)}, u32[]{:S(2)}, u32[]{:S(2)}) collective-permute-start(bf16[256,512]{1,0:T(8,128)(2,1)S(1)} %get-tuple-element.46), channel_id=1, source_target_pairs={{0,16},{16,0},{1,17},{17,1},{2,18},{18,2},{3,19},{19,3},{4,20},{20... | collective-permute-start | bytes 786440 | tf_op jit(solution)/shard_map/ppermute | solution.py:21
  101.5 1.5 %collective-permute-done.20.refs_4_ = bf16[16,128,128]{2,1,0:T(8,128)(2,1)S(1)} collective-permute-done((bf16[16,128,128]{2,1,0:T(8,128)(2,1)}, bf16[16,128,128]{2,1,0:T(8,128)(2,1)S(1)}, u32[]{:S(2)}, u32[]{:S(2)}) %collective-permute-start.20) | collective-permute-done | bytes 524320 | tf_op jit(solution)/shard_map/ppermute | solution.py:162
  103.0 5.7 %shard_map.83 = (f32[256,512]{1,0:T(8,128)S(1)}, bf16[256,512]{1,0:T(8,128)(2,1)S(1)}, f32[256,512]{1,0:T(8,128)S(1)}, bf16[256,512]{1,0:T(8,128)(2,1)S(1)}) custom-call(s32[3,64]{1,0:T(4,128)S(1)} %pad_add_fusion.table, s32[4]{0:T(128)S(1)} %and_select_fusion.counts, s32[3]{0:T(128)S(1)} %pad_add_fusion.2.home, bf16[8,128,256]{2,1,0:T(8,128)(2,1)} %bitcast.13.refs_0_, ...), custom_call_target="tpu_custom_call" | custom-call | flops 2415919104 | bytes 6291456 | tf_op jit(solution)/shard_map/pallas_call | solution.py:260
  108.7 2.9 %collective-permute-start.21 = (bf16[256,512]{1,0:T(8,128)(2,1)S(1)}, bf16[256,512]{1,0:T(8,128)(2,1)S(1)}, u32[]{:S(2)}, u32[]{:S(2)}) collective-permute-start(bf16[256,512]{1,0:T(8,128)(2,1)S(1)} %get-tuple-element.50), channel_id=1, source_target_pairs={{0,16},{16,0},{1,17},{17,1},{2,18},{18,2},{3,19},{19,3},{4,20},{20... | collective-permute-start | bytes 786440 | tf_op jit(solution)/shard_map/ppermute | solution.py:21
  111.8 0.4 collective-permute-start.17
  112.3 2.9 %collective-permute-start.19 = (bf16[256,512]{1,0:T(8,128)(2,1)S(1)}, bf16[256,512]{1,0:T(8,128)(2,1)S(1)}, u32[]{:S(2)}, u32[]{:S(2)}) collective-permute-start(bf16[256,512]{1,0:T(8,128)(2,1)S(1)} %add_convert_fusion.1), channel_id=1, source_target_pairs={{0,8},{1,9},{2,10},{3,11},{4,12},{5,13},{6,14},{7,15},{8,0},{9,1},... | collective-permute-start | bytes 786440 | tf_op jit(solution)/shard_map/ppermute | solution.py:162
  115.2 3.6 %collective-permute-done.21 = bf16[256,512]{1,0:T(8,128)(2,1)S(1)} collective-permute-done((bf16[256,512]{1,0:T(8,128)(2,1)S(1)}, bf16[256,512]{1,0:T(8,128)(2,1)S(1)}, u32[]{:S(2)}, u32[]{:S(2)}) %collective-permute-start.21) | collective-permute-done | bytes 262176 | tf_op jit(solution)/shard_map/ppermute | solution.py:21
  118.8 0.1 add_convert_fusion
  119.0 0.5 gate.1.gate_open
  119.5 3.9 %collective-permute-done.23 = bf16[256,512]{1,0:T(8,128)(2,1)S(1)} collective-permute-done((bf16[256,512]{1,0:T(8,128)(2,1)S(1)}, bf16[256,512]{1,0:T(8,128)(2,1)S(1)}, u32[]{:S(2)}, u32[]{:S(2)}) %collective-permute-start.23) | collective-permute-done | bytes 262176 | tf_op jit(solution)/shard_map/ppermute | solution.py:21
  123.4 12.0 %collective-permute-done.19.refs_1_ = bf16[256,512]{1,0:T(8,128)(2,1)S(1)} collective-permute-done((bf16[256,512]{1,0:T(8,128)(2,1)S(1)}, bf16[256,512]{1,0:T(8,128)(2,1)S(1)}, u32[]{:S(2)}, u32[]{:S(2)}) %collective-permute-start.19) | collective-permute-done | bytes 262176 | tf_op jit(solution)/shard_map/ppermute | solution.py:162
  135.4 0.9 finish.1
  (66 shorter events, 1.0 us)
Async XLA Ops:
  0.0 9.5 %collective-permute-start = (bf16[256,512]{1,0:T(8,128)(2,1)}, bf16[256,512]{1,0:T(8,128)(2,1)S(1)}, u32[]{:S(2)}, u32[]{:S(2)}) collective-permute-start(bf16[256,512]{1,0:T(8,128)(2,1)} %state.1), channel_id=1, source_target_pairs={{0,16},{16,0},{1,17},{17,1},{2,18},{18,2},{3,19},{19,3},{4,20},{20... | collective-permute-start | bytes 786440 | tf_op jit(solution)/shard_map/ppermute | solution.py:21
  9.5 1.0 copy-start.1
  10.4 5.8 %copy-start.7 = (bf16[256,512]{1,0:T(8,128)(2,1)}, bf16[256,512]{1,0:T(8,128)(2,1)S(1)}, u32[]{:S(2)}) copy-start(bf16[256,512]{1,0:T(8,128)(2,1)S(1)} %collective-permute-done.refs_1_) | copy-start | bytes 786436
  11.7 0.6 copy-start.10
  12.4 14.2 %collective-permute-start.3 = (bf16[272,256]{1,0:T(8,128)(2,1)S(1)}, bf16[272,256]{1,0:T(8,128)(2,1)S(1)}, u32[]{:S(2)}, u32[]{:S(2)}) collective-permute-start(bf16[272,256]{1,0:T(8,128)(2,1)S(1)} %get-tuple-element.43), channel_id=1, source_target_pairs={{0,12},{1,13},{2,14},{3,15},{4,8},{5,9},{6,10},{7,11},{8,4},{9,5},... | collective-permute-start | bytes 417800 | tf_op jit(solution)/shard_map/ppermute | solution.py:162
  16.2 9.7 %copy-start = (bf16[12,64,1024]{2,1,0:T(8,128)(2,1)S(1)}, bf16[12,64,1024]{2,1,0:T(8,128)(2,1)}, u32[]{:S(2)}) copy-start(bf16[12,64,1024]{2,1,0:T(8,128)(2,1)} %refs_6_.1) | copy-start | bytes 4718596
  16.2 45.2 %collective-permute-start.7 = (bf16[16,128,128]{2,1,0:T(8,128)(2,1)}, bf16[16,128,128]{2,1,0:T(8,128)(2,1)}, u32[]{:S(2)}, u32[]{:S(2)}) collective-permute-start(bf16[16,128,128]{2,1,0:T(8,128)(2,1)} %bitcast.24), channel_id=1, source_target_pairs={{4,8},{5,9},{6,10},{7,11},{8,4},{9,5},{10,6},{11,7},{20,24},{21,25... | collective-permute-start | bytes 1572872 | tf_op jit(solution)/shard_map/ppermute | solution.py:162
  17.8 44.1 %collective-permute-start.8 = (bf16[16,128,128]{2,1,0:T(8,128)(2,1)}, bf16[16,128,128]{2,1,0:T(8,128)(2,1)}, u32[]{:S(2)}, u32[]{:S(2)}) collective-permute-start(bf16[16,128,128]{2,1,0:T(8,128)(2,1)} %bitcast.25), channel_id=1, source_target_pairs={{0,8},{1,9},{2,10},{3,11},{12,4},{13,5},{14,6},{15,7},{16,24},{17,... | collective-permute-start | bytes 1572872 | tf_op jit(solution)/shard_map/ppermute | solution.py:162
  24.4 35.2 %collective-permute-start.12 = (bf16[9,64,1024]{2,1,0:T(8,128)(2,1)}, bf16[9,64,1024]{2,1,0:T(8,128)(2,1)}, u32[]{:S(2)}, u32[]{:S(2)}) collective-permute-start(bf16[9,64,1024]{2,1,0:T(8,128)(2,1)} %slice.89), channel_id=1, source_target_pairs={{0,2},{1,3},{2,0},{3,1},{4,6},{5,7},{6,4},{7,5},{8,10},{9,11},{10,... | collective-permute-start | bytes 3538952 | tf_op jit(solution)/shard_map/ppermute | solution.py:21
  26.0 33.1 %collective-permute-start.13 = (bf16[3,64,1024]{2,1,0:T(8,128)(2,1)S(1)}, bf16[3,64,1024]{2,1,0:T(8,128)(2,1)S(1)}, u32[]{:S(2)}, u32[]{:S(2)}) collective-permute-start(bf16[3,64,1024]{2,1,0:T(8,128)(2,1)S(1)} %slice.90), channel_id=1, source_target_pairs={{0,2},{1,3},{2,0},{3,1},{4,6},{5,7},{6,4},{7,5},{8,10},{9,11},{10,... | collective-permute-start | bytes 1179656 | tf_op jit(solution)/shard_map/ppermute | solution.py:21
  26.6 23.0 %collective-permute-start.2 = (bf16[272,256]{1,0:T(8,128)(2,1)S(1)}, bf16[272,256]{1,0:T(8,128)(2,1)S(1)}, u32[]{:S(2)}, u32[]{:S(2)}) collective-permute-start(bf16[272,256]{1,0:T(8,128)(2,1)S(1)} %get-tuple-element.42), channel_id=1, source_target_pairs={{0,8},{1,9},{2,10},{3,11},{4,12},{5,13},{6,14},{7,15},{8,0},{9,1},... | collective-permute-start | bytes 417800 | tf_op jit(solution)/shard_map/ppermute | solution.py:162
  49.6 9.4 %collective-permute-start.1 = (bf16[272,256]{1,0:T(8,128)(2,1)}, bf16[272,256]{1,0:T(8,128)(2,1)S(1)}, u32[]{:S(2)}, u32[]{:S(2)}) collective-permute-start(bf16[272,256]{1,0:T(8,128)(2,1)} %get-tuple-element.41), channel_id=1, source_target_pairs={{0,4},{1,5},{2,6},{3,7},{4,0},{5,1},{6,2},{7,3},{8,12},{9,13},{10,... | collective-permute-start | bytes 417800 | tf_op jit(solution)/shard_map/ppermute | solution.py:162
  59.0 33.9 %collective-permute-start.11 = (bf16[12,64,1024]{2,1,0:T(8,128)(2,1)S(1)}, bf16[12,64,1024]{2,1,0:T(8,128)(2,1)S(1)}, u32[]{:S(2)}, u32[]{:S(2)}) collective-permute-start(bf16[12,64,1024]{2,1,0:T(8,128)(2,1)S(1)} %copy-done), channel_id=1, source_target_pairs={{0,1},{1,0},{2,3},{3,2},{4,5},{5,4},{6,7},{7,6},{8,9},{9,8},{10,11... | collective-permute-start | bytes 4718600 | tf_op jit(solution)/shard_map/ppermute | solution.py:21
  59.1 4.6 %collective-permute-start.15 = (bf16[3,64,1024]{2,1,0:T(8,128)(2,1)S(1)}, bf16[3,64,1024]{2,1,0:T(8,128)(2,1)S(1)}, u32[]{:S(2)}, u32[]{:S(2)}) collective-permute-start(bf16[3,64,1024]{2,1,0:T(8,128)(2,1)S(1)} %collective-permute-done.13.refs_11_.refs_9_), channel_id=1, source_target_pairs={{0,1},{1,0},{2,3},{3,2},{4,5},{5,4},{6,7},{7,6},{8,9},{9,8},{10,11... | collective-permute-start | bytes 1179656 | tf_op jit(solution)/shard_map/ppermute | solution.py:21
  59.6 33.4 %collective-permute-start.14 = (bf16[9,64,1024]{2,1,0:T(8,128)(2,1)}, bf16[9,64,1024]{2,1,0:T(8,128)(2,1)}, u32[]{:S(2)}, u32[]{:S(2)}) collective-permute-start(bf16[9,64,1024]{2,1,0:T(8,128)(2,1)} %collective-permute-done.12.refs_10_.refs_8_), channel_id=1, source_target_pairs={{0,1},{1,0},{2,3},{3,2},{4,5},{5,4},{6,7},{7,6},{8,9},{9,8},{10,11... | collective-permute-start | bytes 3538952 | tf_op jit(solution)/shard_map/ppermute | solution.py:21
  61.5 7.0 %collective-permute-start.4 = (bf16[8,128,256]{2,1,0:T(8,128)(2,1)}, bf16[8,128,256]{2,1,0:T(8,128)(2,1)}, u32[]{:S(2)}, u32[]{:S(2)}) collective-permute-start(bf16[8,128,256]{2,1,0:T(8,128)(2,1)} %bitcast.13.refs_0_), channel_id=1, source_target_pairs={{0,1},{1,0},{2,3},{3,2},{4,5},{5,4},{6,7},{7,6},{8,9},{9,8},{10,11... | collective-permute-start | bytes 1572872 | tf_op jit(solution)/shard_map/ppermute | solution.py:21
  62.0 14.2 %collective-permute-start.5 = (bf16[8,128,256]{2,1,0:T(8,128)(2,1)}, bf16[8,128,256]{2,1,0:T(8,128)(2,1)}, u32[]{:S(2)}, u32[]{:S(2)}) collective-permute-start(bf16[8,128,256]{2,1,0:T(8,128)(2,1)} %bitcast.13.refs_0_), channel_id=1, source_target_pairs={{0,2},{1,3},{2,0},{3,1},{4,6},{5,7},{6,4},{7,5},{8,10},{9,11},{10,... | collective-permute-start | bytes 1572872 | tf_op jit(solution)/shard_map/ppermute | solution.py:21
  63.5 0.6 copy-start.13
  63.7 2.5 %copy-start.14 = (s32[4]{0:T(128)}, s32[4]{0:T(128)S(1)}, u32[]{:S(2)}) copy-start(s32[4]{0:T(128)S(1)} %slice_reduce_fusion.3) | copy-start | bytes 52
  64.1 0.7 copy-start.3
  64.8 17.0 %collective-permute-start.9 = (bf16[16,128,128]{2,1,0:T(8,128)(2,1)}, bf16[16,128,128]{2,1,0:T(8,128)(2,1)}, u32[]{:S(2)}, u32[]{:S(2)}) collective-permute-start(bf16[16,128,128]{2,1,0:T(8,128)(2,1)} %collective-permute-done.8.refs_6_), channel_id=1, source_target_pairs={{8,12},{9,13},{10,14},{11,15},{4,0},{5,1},{6,2},{7,3},{24,28},{25,... | collective-permute-start | bytes 1572872 | tf_op jit(solution)/shard_map/ppermute | solution.py:162
  68.5 24.5 %collective-permute-start.10 = (bf16[16,128,128]{2,1,0:T(8,128)(2,1)}, bf16[16,128,128]{2,1,0:T(8,128)(2,1)S(1)}, u32[]{:S(2)}, u32[]{:S(2)}) collective-permute-start(bf16[16,128,128]{2,1,0:T(8,128)(2,1)} %collective-permute-done.7.refs_4_), channel_id=1, source_target_pairs={{8,12},{9,13},{10,14},{11,15},{4,0},{5,1},{6,2},{7,3},{24,28},{25,... | collective-permute-start | bytes 1572872 | tf_op jit(solution)/shard_map/ppermute | solution.py:162
  76.2 16.8 %collective-permute-start.6 = (bf16[8,128,256]{2,1,0:T(8,128)(2,1)}, bf16[8,128,256]{2,1,0:T(8,128)(2,1)S(1)}, u32[]{:S(2)}, u32[]{:S(2)}) collective-permute-start(bf16[8,128,256]{2,1,0:T(8,128)(2,1)} %collective-permute-done.5.refs_2_), channel_id=1, source_target_pairs={{0,1},{1,0},{2,3},{3,2},{4,5},{5,4},{6,7},{7,6},{8,9},{9,8},{10,11... | collective-permute-start | bytes 1572872 | tf_op jit(solution)/shard_map/ppermute | solution.py:21
  81.8 21.2 %collective-permute-start.20 = (bf16[16,128,128]{2,1,0:T(8,128)(2,1)}, bf16[16,128,128]{2,1,0:T(8,128)(2,1)S(1)}, u32[]{:S(2)}, u32[]{:S(2)}) collective-permute-start(bf16[16,128,128]{2,1,0:T(8,128)(2,1)} %bitcast.26), channel_id=1, source_target_pairs={{0,4},{1,5},{2,6},{3,7},{4,0},{5,1},{6,2},{7,3},{8,12},{9,13},{10,... | collective-permute-start | bytes 1572872 | tf_op jit(solution)/shard_map/ppermute | solution.py:162
  93.0 1.0 copy-start.4
  94.0 9.0 %copy-start.5 = (bf16[3,64,1024]{2,1,0:T(8,128)(2,1)S(1)}, bf16[3,64,1024]{2,1,0:T(8,128)(2,1)}, u32[]{:S(2)}) copy-start(bf16[3,64,1024]{2,1,0:T(8,128)(2,1)} %copy-done.3) | copy-start | bytes 1179652
  94.0 9.0 %copy-start.9 = (bf16[1,16,128,128]{3,2,1,0:T(8,128)(2,1)S(1)}, bf16[1,16,128,128]{3,2,1,0:T(8,128)(2,1)}, u32[]{:S(2)}) copy-start(bf16[1,16,128,128]{3,2,1,0:T(8,128)(2,1)} %param.17) | copy-start | bytes 1572868
  98.2 13.5 %collective-permute-start.16 = (bf16[256,512]{1,0:T(8,128)(2,1)S(1)}, bf16[256,512]{1,0:T(8,128)(2,1)S(1)}, u32[]{:S(2)}, u32[]{:S(2)}) collective-permute-start(bf16[256,512]{1,0:T(8,128)(2,1)S(1)} %get-tuple-element.46), channel_id=1, source_target_pairs={{0,16},{16,0},{1,17},{17,1},{2,18},{18,2},{3,19},{19,3},{4,20},{20... | collective-permute-start | bytes 786440 | tf_op jit(solution)/shard_map/ppermute | solution.py:21
  101.4 10.8 %collective-permute-start.18 = (bf16[256,512]{1,0:T(8,128)(2,1)S(1)}, bf16[256,512]{1,0:T(8,128)(2,1)S(1)}, u32[]{:S(2)}, u32[]{:S(2)}) collective-permute-start(bf16[256,512]{1,0:T(8,128)(2,1)S(1)} %get-tuple-element.48), channel_id=1, source_target_pairs={{0,16},{16,0},{1,17},{17,1},{2,18},{18,2},{3,19},{19,3},{4,20},{20... | collective-permute-start | bytes 786440 | tf_op jit(solution)/shard_map/ppermute | solution.py:21
  108.7 10.1 %collective-permute-start.21 = (bf16[256,512]{1,0:T(8,128)(2,1)S(1)}, bf16[256,512]{1,0:T(8,128)(2,1)S(1)}, u32[]{:S(2)}, u32[]{:S(2)}) collective-permute-start(bf16[256,512]{1,0:T(8,128)(2,1)S(1)} %get-tuple-element.50), channel_id=1, source_target_pairs={{0,16},{16,0},{1,17},{17,1},{2,18},{18,2},{3,19},{19,3},{4,20},{20... | collective-permute-start | bytes 786440 | tf_op jit(solution)/shard_map/ppermute | solution.py:21
  111.6 11.7 %collective-permute-start.23 = (bf16[256,512]{1,0:T(8,128)(2,1)S(1)}, bf16[256,512]{1,0:T(8,128)(2,1)S(1)}, u32[]{:S(2)}, u32[]{:S(2)}) collective-permute-start(bf16[256,512]{1,0:T(8,128)(2,1)S(1)} %get-tuple-element.52), channel_id=1, source_target_pairs={{0,16},{16,0},{1,17},{17,1},{2,18},{18,2},{3,19},{19,3},{4,20},{20... | collective-permute-start | bytes 786440 | tf_op jit(solution)/shard_map/ppermute | solution.py:21
  111.8 7.2 %copy-start.2 = (bf16[256,512]{1,0:T(8,128)(2,1)S(1)}, bf16[256,512]{1,0:T(8,128)(2,1)}, u32[]{:S(2)}) copy-start(bf16[256,512]{1,0:T(8,128)(2,1)} %state.1) | copy-start | bytes 786436
  111.8 7.2 %copy-start.6 = (bf16[1024,512]{1,0:T(8,128)(2,1)S(1)}, bf16[1024,512]{1,0:T(8,128)(2,1)}, u32[]{:S(2)}) copy-start(bf16[1024,512]{1,0:T(8,128)(2,1)} %weight.1) | copy-start | bytes 3145732
  111.8 7.2 %copy-start.8 = (bf16[256,512]{1,0:T(8,128)(2,1)S(1)}, bf16[256,512]{1,0:T(8,128)(2,1)}, u32[]{:S(2)}) copy-start(bf16[256,512]{1,0:T(8,128)(2,1)} %copy-done.7) | copy-start | bytes 786436
  111.8 7.2 %copy-start.11 = (f32[512]{0:T(512)S(1)}, f32[512]{0:T(512)}, u32[]{:S(2)}) copy-start(f32[512]{0:T(512)} %param.15) | copy-start | bytes 6148
  111.8 11.6 %collective-permute-start.17 = (bf16[256,512]{1,0:T(8,128)(2,1)S(1)}, bf16[256,512]{1,0:T(8,128)(2,1)S(1)}, u32[]{:S(2)}, u32[]{:S(2)}) collective-permute-start(bf16[256,512]{1,0:T(8,128)(2,1)S(1)} %add_convert_fusion.2), channel_id=1, source_target_pairs={{0,12},{1,13},{2,14},{3,15},{4,8},{5,9},{6,10},{7,11},{8,4},{9,5},... | collective-permute-start | bytes 786440 | tf_op jit(solution)/shard_map/ppermute | solution.py:162
  112.3 23.1 %collective-permute-start.19 = (bf16[256,512]{1,0:T(8,128)(2,1)S(1)}, bf16[256,512]{1,0:T(8,128)(2,1)S(1)}, u32[]{:S(2)}, u32[]{:S(2)}) collective-permute-start(bf16[256,512]{1,0:T(8,128)(2,1)S(1)} %add_convert_fusion.1), channel_id=1, source_target_pairs={{0,8},{1,9},{2,10},{3,11},{4,12},{5,13},{6,14},{7,15},{8,0},{9,1},... | collective-permute-start | bytes 786440 | tf_op jit(solution)/shard_map/ppermute | solution.py:162
  118.9 16.5 %collective-permute-start.22 = (bf16[256,512]{1,0:T(8,128)(2,1)S(1)}, bf16[256,512]{1,0:T(8,128)(2,1)S(1)}, u32[]{:S(2)}, u32[]{:S(2)}) collective-permute-start(bf16[256,512]{1,0:T(8,128)(2,1)S(1)} %add_convert_fusion), channel_id=1, source_target_pairs={{0,4},{1,5},{2,6},{3,7},{4,0},{5,1},{6,2},{7,3},{8,12},{9,13},{10,... | collective-permute-start | bytes 786440 | tf_op jit(solution)/shard_map/ppermute | solution.py:162
  119.5 15.9 %copy-start.12 = (f32[512]{0:T(512)S(1)}, f32[512]{0:T(512)}, u32[]{:S(2)}) copy-start(f32[512]{0:T(512)} %param.16) | copy-start | bytes 6148

commit v2 on v1

v2 whole, which is shorter than its diff:
```python
import functools

import jax
import jax.numpy as jnp
from jax import lax
from jax.experimental import pallas as pl
from jax.experimental.pallas import tpu as pltpu
from jax.sharding import PartitionSpec as P


F32 = jnp.float32
BF16 = jnp.bfloat16
ANY = pl.BlockSpec(memory_space=pl.ANY)
SMEM = pl.BlockSpec(memory_space=pltpu.SMEM)
VMEM = pl.BlockSpec(memory_space=pltpu.VMEM)
GROUP = 4
NOTE_ROWS = 16


def swap(value, axis, size, bit):
    return lax.ppermute(value, axis, [(i, i ^ bit) for i in range(size)])


def pack_kernel(n_rel, where, note, *refs):
    halves, outs = refs[:n_rel], refs[n_rel:]
    rows, width = halves[0].shape[0], outs[0].shape[1]
    for j, out in enumerate(outs):
        start = pl.multiple_of(where[1, j], width)
        for r, half in enumerate(halves):

            @pl.when(where[0, j] == r)
            def _(half=half, out=out, start=start):
                out[:rows] = half[:, pl.ds(start, width)]

        out[rows:] = note[...]


def gate_kernel(n_rel, rel, weight, bias, *refs):
    halves, out = refs[:n_rel], refs[n_rel]
    depth = halves[0].shape[1]
    total = jnp.zeros(out.shape, F32) + bias[...]
    for r, half in enumerate(halves):
        start = pl.multiple_of(lax.bitwise_xor(rel[0], r) * depth, depth)
        total += jnp.dot(half[...], weight[pl.ds(start, depth), :], preferred_element_type=F32)
    out[...] = jax.nn.sigmoid(total)


def stack_kernel(count, *refs):
    pieces, (out, notes) = refs[:count], refs[count:]
    rows = out.shape[1]
    for j, piece in enumerate(pieces):
        out[j] = piece[:rows]
        notes[j] = piece[rows:]


def take(refs, *counts):
    out = []
    for count in counts:
        out.append(refs[:count])
        refs = refs[count:]
    return out + [refs]


def start_tiles(way_counts, way, tiles, lists, sems):
    loads = []
    for g, count in enumerate(way_counts):
        options = [pltpu.make_async_copy(tiles[w], lists.at[g], sems.at[g]) for w in range(count)]
        tiles = tiles[count:]
        for w, option in enumerate(options):
            if count == 1:
                option.start()
            else:
                pl.when(way == w)(option.start)
        loads.append(options[0])
    return loads


def start_weights(members, member, weights, held, sems):
    half = members // 2
    per_block = len(weights) // half
    loads = []
    for n, ref in enumerate(weights):
        i, p = n // per_block, n % per_block
        block = ref.shape[1]
        low = sum(weights[i * per_block + q].shape[0] for q in range(p))
        start = pl.multiple_of(lax.bitwise_xor(i, member % half) * block, block)
        loads.append(
            pltpu.make_async_copy(
                ref, held.at[pl.ds(low, ref.shape[0]), pl.ds(start, block), :], sems.at[n]
            )
        )
        loads[-1].start()
    return loads


def multiply_tiles(turns, table, base, swapped, lists, rows_held, made):
    def step(n, _):
        for u in range(GROUP):
            s = n * GROUP + u
            product = jnp.dot(lists[s], rows_held[table[0, base + s]], preferred_element_type=F32)
            turned = pltpu.roll(product, product.shape[1] // 2, 1)
            made[s] = jnp.where(swapped, turned, product).astype(BF16)
        return 0

    lax.fori_loop(0, turns, step, 0)


def add_messages(turns, table, base, made, own, other, acc):
    acc[:-1] = jnp.zeros((acc.shape[0] - 1,) + acc.shape[1:], F32)

    def step(n, _):
        for u in range(GROUP):
            s = n * GROUP + u
            relation = table[2, base + s]
            weight = jnp.concatenate([own[relation], other[relation]], axis=0)
            acc[table[1, base + s]] += jnp.dot(made[s], weight, preferred_element_type=F32)
        return 0

    lax.fori_loop(0, turns, step, 0)


def put_messages(n_rel, rel, acc, outs):
    per_tile, tile_rows, features = acc.shape[0] - 1, acc.shape[1], acc.shape[2]
    own = features // n_rel
    for r in range(n_rel):
        start = pl.multiple_of(lax.bitwise_xor(rel, r) * own, own)
        for t in range(per_tile):
            outs[r][t * tile_rows:(t + 1) * tile_rows] = acc[t, :, pl.ds(start, own)].astype(outs[r].dtype)


def early_kernel(members, way_counts, n_weights, table, turns, home, *refs):
    states, tiles, weights, rest = take(refs, members, sum(way_counts), n_weights)
    made, held, rows_held, lists, state_sem, tile_sem, weight_sem = rest
    slots = lists.shape[1]
    per_member = states[0].shape[0]
    loads = [
        pltpu.make_async_copy(ref, rows_held.at[pl.ds(i * per_member, per_member)], state_sem.at[i])
        for i, ref in enumerate(states)
    ]
    for load in loads:
        load.start()
    tile_loads = start_tiles(way_counts, home[2], tiles, lists, tile_sem)
    weight_loads = start_weights(members, home[0], weights, held, weight_sem)
    for load in loads:
        load.wait()
    swapped = home[0] >= members // 2
    for j, load in enumerate(tile_loads):
        load.wait()
        multiply_tiles(turns[j], table, j * slots, swapped, lists.at[j], rows_held, made.at[j])
    for load in weight_loads:
        load.wait()


def first_kernel(members, j, n_rel, n_weights, table, turns, home, made, own, *refs):
    weights, outs, rest = take(refs, n_weights, n_rel)
    other, acc, weight_sem = rest
    slots = made.shape[1]
    for load in start_weights(members, home[0], weights, other, weight_sem):
        load.wait()
    add_messages(turns[j], table, j * slots, made.at[j], own, other, acc)
    put_messages(n_rel, home[1], acc, outs)


def late_kernel(members, way_counts, js, n_rel, table, turns, home, rows_held, own, other, *refs):
    tiles, outs, rest = take(refs, sum(way_counts), len(js) * n_rel)
    lists, made, acc, tile_sem = rest
    slots = lists.shape[1]
    loads = start_tiles(way_counts, home[2], tiles, lists, tile_sem)
    for g, j in enumerate(js):
        loads[g].wait()
        multiply_tiles(
            turns[j], table, j * slots, home[0] >= members // 2, lists.at[g], rows_held, made.at[g]
        )
        add_messages(turns[j], table, j * slots, made.at[g], own, other, acc)
        put_messages(n_rel, home[1], acc, outs[g * n_rel:(g + 1) * n_rel])


def near_kernel(js, n_rel, table, turns, home, made, own, other, *refs):
    outs, acc = refs[:-1], refs[-1]
    slots = made.shape[1]
    for g, j in enumerate(js):
        add_messages(turns[j], table, j * slots, made.at[j], own, other, acc)
        put_messages(n_rel, home[1], acc, outs[g * n_rel:(g + 1) * n_rel])


def finish_kernel(used, state, gate_open, bias, *refs):
    terms, out = refs[:-1], refs[-1]
    message = sum(term[...].astype(F32) for term in terms[:-1])
    message = jnp.where(used[0] == 1, message + terms[-1][...].astype(F32), message)
    update = jnp.tanh(message + bias[...])
    opened = gate_open[...]
    out[...] = ((1.0 - opened) * state[...].astype(F32) + opened * update).astype(BF16)


def shards(
    n_rel, n_ent, chunks, state, rel_weight, gate_weight, gate_bias, update_bias,
    tile_values, tile_index, tile_count
):
    members = n_ent // chunks
    rel_dev, _, features = rel_weight.shape
    ent_dev, own_features = state.shape
    tile_rows = tile_values.shape[-1]
    slots = tile_values.shape[1]
    per_tile = ent_dev // tile_rows
    width = features // chunks
    rel = lax.axis_index("rel")
    ent = lax.axis_index("ent")
    part, member = ent // members, ent % members
    line = chunks == 4 and members == 4 and n_rel == 2

    def along(value, pairs):
        perm = [(a * members + m, b * members + m) for a, b in pairs for m in range(members)]
        return lax.ppermute(value, "ent", perm)

    def partner(value, j):
        return along(value, [(q, q ^ j) for q in range(chunks)])

    halves = [state] + [swap(state, "rel", n_rel, r) for r in range(1, n_rel)]

    values = tile_values[0]
    if line:
        near = along(values, [(0, 1), (1, 0), (2, 3), (3, 2)])
        middle = along(values, [(1, 2), (2, 1)])
        inward = along(values, [(0, 2), (3, 1)])
        edge_two = along(middle, [(2, 3), (1, 0)])
        edge_three = along(inward, [(2, 3), (1, 0)])
        tiles = [[values], [near], [inward, edge_two], [middle, edge_three]]
    else:
        tiles = [[values]] + [[partner(values, j)] for j in range(1, chunks)]

    note = jnp.zeros((NOTE_ROWS, width), BF16)
    note = note.at[:3, :slots].set(tile_index[0].astype(BF16))
    note = note.at[3, :1].set(tile_count[0].astype(BF16))
    asked = lax.bitwise_xor(part, jnp.arange(chunks, dtype=jnp.int32))
    per_half = chunks // n_rel
    where = jnp.stack([lax.bitwise_xor(asked // per_half, rel), (asked % per_half) * width])
    pieces = pl.pallas_call(
        functools.partial(pack_kernel, n_rel),
        out_shape=[jax.ShapeDtypeStruct((ent_dev + NOTE_ROWS, width), BF16) for _ in range(chunks)],
        in_specs=[SMEM] + [VMEM] * (n_rel + 1),
        out_specs=[VMEM] * chunks,
        compiler_params=pltpu.CompilerParams(vmem_limit_bytes=8 << 20),
        name="pack",
    )(where, note, *halves)
    moved = [partner(pieces[j], j) for j in range(1, chunks)]
    own, notes = pl.pallas_call(
        functools.partial(stack_kernel, chunks),
        out_shape=[
            jax.ShapeDtypeStruct((chunks, ent_dev, width), BF16),
            jax.ShapeDtypeStruct((chunks, NOTE_ROWS, width), BF16),
        ],
        in_specs=[VMEM] * chunks,
        out_specs=[VMEM] * 2,
        compiler_params=pltpu.CompilerParams(vmem_limit_bytes=8 << 20),
        name="stk",
    )(pieces[0], *moved)
    notes = notes[:, :4, :slots].astype(jnp.int32)
    counts = notes[:, 3, 0]
    source, target, relation = notes[:, 0], notes[:, 1], notes[:, 2]
    live = jnp.arange(slots, dtype=jnp.int32)[None] < counts[:, None]
    owner = source // per_tile
    place = lax.bitwise_xor(owner % members, member) * chunks
    place = (place + lax.bitwise_xor(part, owner // members)) * per_tile + source % per_tile
    table = jnp.stack([
        jnp.where(live, place, 0).reshape(-1),
        jnp.where(live, target, per_tile).reshape(-1),
        jnp.where(live, relation, 0).reshape(-1),
    ])
    turns = (counts + GROUP - 1) // GROUP

    own = own.reshape(chunks * per_tile, tile_rows, width)
    cut = max(1, rel_dev - max(1, rel_dev // 4))
    parts = (rel_weight[:cut], rel_weight[cut:])
    states, weights = [own], [(rel_weight,)]
    high = True
    bits = [1 << b for b in reversed(range(members.bit_length() - 1))]
    order = [0]
    for bit in bits:
        states = states + [swap(v, "ent", n_ent, bit) for v in states]
        more = []
        for i, held in enumerate(weights):
            if i == 0 and high:
                more.append(tuple(swap(v, "ent", n_ent, bit) for v in parts))
            elif i == 0:
                more.append((swap(rel_weight, "ent", n_ent, bit),))
            else:
                more.append(tuple(swap(v, "ent", n_ent, bit) for v in held))
        weights = weights + more
        order = order + [o | bit for o in order]
        high = False
    states = [states[order.index(i)] for i in range(members)]
    weights = [weights[order.index(i)] for i in range(members)]
    own_weights = [v for held in weights[:members // 2] for v in held]
    other_weights = [v for held in weights[members // 2:] for v in held]
    edge = jnp.logical_or(part == 0, part == chunks - 1).astype(jnp.int32)
    home = jnp.stack([member, rel, edge])

    gate_open = pl.pallas_call(
        functools.partial(gate_kernel, n_rel),
        out_shape=jax.ShapeDtypeStruct((ent_dev, own_features), F32),
        in_specs=[SMEM] + [VMEM] * (n_rel + 2),
        out_specs=VMEM,
        compiler_params=pltpu.CompilerParams(vmem_limit_bytes=12 << 20),
        name="gate",
    )(rel.reshape(1), gate_weight, gate_bias[None], *halves)

    early, late = tuple(range(3)), tuple(range(3, chunks))
    early_ways = [len(tiles[j]) for j in early]
    late_ways = [len(tiles[j]) for j in late]
    half_shape = (rel_dev, width // 2, features)
    products = jax.ShapeDtypeStruct((len(early), slots, tile_rows, width), BF16)
    acc_scratch = pltpu.VMEM((per_tile + 1, tile_rows, features), F32)

    def call(body, operands, in_specs, out_shape, scratch, flops):
        return pl.pallas_call(
            body,
            out_shape=out_shape,
            in_specs=[SMEM] * 3 + in_specs,
            out_specs=[VMEM] * len(out_shape),
            scratch_shapes=scratch,
            cost_estimate=pl.CostEstimate(
                flops=flops, bytes_accessed=rel_dev * width * features, transcendentals=0
            ),
            compiler_params=pltpu.CompilerParams(vmem_limit_bytes=16 << 20),
        )(table, turns, home, *operands)

    def message_shapes(count):
        shape = (ent_dev, own_features)
        one = [jax.ShapeDtypeStruct(shape, F32)] + [jax.ShapeDtypeStruct(shape, BF16)] * (n_rel - 1)
        return one * count

    slot_flops = 2 * slots * tile_rows * width
    flat = [t for j in early for t in tiles[j]]
    made, own_half, rows_held = call(
        functools.partial(early_kernel, members, early_ways, len(own_weights)),
        [*states, *flat, *own_weights],
        [ANY] * (members + len(flat) + len(own_weights)),
        [
            products,
            jax.ShapeDtypeStruct(half_shape, BF16),
            jax.ShapeDtypeStruct((members * chunks * per_tile, tile_rows, width), BF16),
        ],
        [
            pltpu.VMEM((len(early), slots, tile_rows, tile_rows), BF16),
            pltpu.SemaphoreType.DMA((members,)),
            pltpu.SemaphoreType.DMA((len(early),)),
            pltpu.SemaphoreType.DMA((len(own_weights),)),
        ],
        len(early) * slot_flops * tile_rows,
    )
    *two, other_half = call(
        functools.partial(first_kernel, members, 2, n_rel, len(other_weights)),
        [made, own_half, *other_weights],
        [VMEM] * 2 + [ANY] * len(other_weights),
        message_shapes(1) + [jax.ShapeDtypeStruct(half_shape, BF16)],
        [acc_scratch, pltpu.SemaphoreType.DMA((len(other_weights),))],
        slot_flops * features,
    )
    flat = [t for j in late for t in tiles[j]]
    rest = call(
        functools.partial(late_kernel, members, late_ways, late, n_rel),
        [rows_held, own_half, other_half, *flat],
        [VMEM] * 3 + [ANY] * len(flat),
        message_shapes(len(late)),
        [
            pltpu.VMEM((len(late), slots, tile_rows, tile_rows), BF16),
            pltpu.VMEM((len(late), slots, tile_rows, width), BF16),
            acc_scratch,
            pltpu.SemaphoreType.DMA((len(late),)),
        ],
        len(late) * slot_flops * (features + tile_rows),
    )
    results = {2: two}
    for j in (1, 0):
        results[j] = call(
            functools.partial(near_kernel, (j,), n_rel),
            [made, own_half, other_half],
            [VMEM] * 3,
            message_shapes(1),
            [acc_scratch],
            slot_flops * features,
        )
    for g, j in enumerate(late):
        results[j] = rest[g * n_rel:(g + 1) * n_rel]

    def summed(j):
        term = results[j][0]
        for r in range(1, n_rel):
            term = term + swap(results[j][r], "rel", n_rel, r).astype(F32)
        return term

    if line:
        passed = along(summed(2).astype(BF16), [(0, 1), (1, 3), (3, 2), (2, 0)])
        three = summed(3)
        across = along(three.astype(BF16), [(0, 3), (3, 0)])
        total = (three + passed.astype(F32)).astype(BF16)
        total = along(total, [(1, 2), (2, 1)])
        terms = [summed(0), partner(summed(1).astype(BF16), 1), across, total, passed]
        used = edge
    else:
        terms = [summed(0)]
        terms += [partner(summed(j).astype(BF16), j) for j in range(1, chunks)]
        used = jnp.ones((), jnp.int32)
    return pl.pallas_call(
        finish_kernel,
        out_shape=jax.ShapeDtypeStruct((ent_dev, own_features), BF16),
        in_specs=[SMEM] + [VMEM] * (3 + len(terms)),
        out_specs=VMEM,
        compiler_params=pltpu.CompilerParams(vmem_limit_bytes=12 << 20),
        name="finish",
    )(used.reshape(1), state, gate_open, update_bias[None], *terms)


def solution(mesh):
    n_rel, n_ent = mesh.shape["rel"], mesh.shape["ent"]
    chunks = max(4, n_rel)
    in_specs = (
        P("ent", "rel"),
        P("rel", "ent", None),
        P(None, "rel"),
        P("rel"),
        P("rel"),
        P("rel", "ent", None, None),
        P("rel", None, "ent"),
        P("rel", "ent"),
    )
    return jax.shard_map(
        functools.partial(shards, n_rel, n_ent, chunks),
        mesh=mesh, in_specs=in_specs, out_specs=P("ent", "rel"), check_vma=False,
    )
```

time: 137 us -> 140 us (1.022)
  waiting for transfers between devices: 69.3 us -> 78.6 us
  other arithmetic: 4.32 us -> 0.55 us
  starting transfers between devices: 40.3 us -> 36.7 us
  Pallas kernels: 12.6 us -> 14.5 us
    ppermute x13, waiting for transfers between devices: 28.2 us -> 43.1 us  [swap(): return lax.ppermute(value, axis, [(i, i ^ bit) for i in range(size)])]
    ppermute x11 -> x12, waiting for transfers between devices: 41.1 us -> 35.5 us  [along(): return lax.ppermute(value, 'ent', perm)]
    ppermute x11 -> x12, starting transfers between devices: 26.4 us -> 21 us  [along(): return lax.ppermute(value, 'ent', perm)]
    pallas_call x2 -> x6, Pallas kernels: 9.94 us -> 12.4 us  [the longest x5 11.5 us: call(): pl.pallas_call(body, out_shape=out_shape, in_specs=[SMEM] * 3 + in_specs,...]
    ppermute x13, starting transfers between devices: 13.9 us -> 15.8 us  [swap(): return lax.ppermute(value, axis, [(i, i ^ bit) for i in range(size)])]
    another operation x1 -> x0, other arithmetic: 1.78 us -> none  [shards(): own = jnp.stack([pieces[0]] + [m[:ent_dev] for m in moved])]
    unnamed x31 -> x33, local copies, waits for them, and re-layouts: 3.79 us -> 4.75 us
  transfers between devices with their start and end apart: 24 -> 25, of which waited for: 10 -> 10; matrix products, arithmetic and copies ran while one was open for 7% -> 1% of each run, Pallas kernels for 8% -> 10%
where the time goes in v2:
time: 140 us
  waiting for transfers between devices  78.6 us (56%)
  starting transfers between devices  36.7 us (26%)
  Pallas kernels  14.5 us (10%)
  local copies, waits for them, and re-layouts  8.61 us (6%)
    ppermute x13, waiting for transfers between devices, swap(): return lax.ppermute(value, axis, [(i, i ^ bit) for i in range(size)])  43.1 us
    ppermute x12, waiting for transfers between devices, along(): return lax.ppermute(value, 'ent', perm)  35.5 us
    ppermute x12, starting transfers between devices, along(): return lax.ppermute(value, 'ent', perm)  21 us
    ppermute x13, starting transfers between devices, swap(): return lax.ppermute(value, axis, [(i, i ^ bit) for i in range(size)])  15.8 us
    pallas_call x5, Pallas kernels, call(): pl.pallas_call(body, out_shape=out_shape, in_specs=[SMEM] * 3 + in_specs,...  11.5 us
    unnamed x33, local copies, waits for them, and re-layouts  4.75 us
    slice x2, local copies, waits for them, and re-layouts, shards(): parts = (rel_weight[:cut], rel_weight[cut:])  3.28 us
  transfers between devices with their start and end apart: 25, of which 10 were waited for; matrix products, arithmetic and copies ran while one was open for 1% of the time, Pallas kernels for 10%

profile of v2, /device:TPU:0, one launch (start us, length us, event | category | flops | bytes accessed | tf_op | source)
XLA Modules:
  0.0 139.9 jit_solution(17151712508304591874)
XLA Ops:
  0.0 2.5 %slice.65 = bf16[9,64,1024]{2,1,0:T(8,128)(2,1)} slice(bf16[12,64,1024]{2,1,0:T(8,128)(2,1)} %refs_8_.1), slice={[0:9], [0:64], [0:1024]} | slice | bytes 2359296 | tf_op jit(solution)/shard_map/slice | solution.py:273
  2.5 3.0 %collective-permute-start.12 = (bf16[9,64,1024]{2,1,0:T(8,128)(2,1)}, bf16[9,64,1024]{2,1,0:T(8,128)(2,1)}, u32[]{:S(2)}, u32[]{:S(2)}) collective-permute-start(bf16[9,64,1024]{2,1,0:T(8,128)(2,1)} %slice.65), channel_id=1, source_target_pairs={{0,2},{1,3},{2,0},{3,1},{4,6},{5,7},{6,4},{7,5},{8,10},{9,11},{10,... | collective-permute-start | bytes 3538952 | tf_op jit(solution)/shard_map/ppermute | solution.py:21
  5.5 1.5 %collective-permute-start = (bf16[256,512]{1,0:T(8,128)(2,1)S(1)}, bf16[256,512]{1,0:T(8,128)(2,1)S(1)}, u32[]{:S(2)}, u32[]{:S(2)}) collective-permute-start(bf16[256,512]{1,0:T(8,128)(2,1)S(1)} %copy-done.1), channel_id=1, source_target_pairs={{0,16},{16,0},{1,17},{17,1},{2,18},{18,2},{3,19},{19,3},{4,20},{20... | collective-permute-start | bytes 786440 | tf_op jit(solution)/shard_map/ppermute | solution.py:21
  7.0 0.8 slice.66
  7.8 0.5 collective-permute-start.13
  9.1 4.2 %collective-permute-done.refs_1_ = bf16[256,512]{1,0:T(8,128)(2,1)S(1)} collective-permute-done((bf16[256,512]{1,0:T(8,128)(2,1)S(1)}, bf16[256,512]{1,0:T(8,128)(2,1)S(1)}, u32[]{:S(2)}, u32[]{:S(2)}) %collective-permute-start) | collective-permute-done | bytes 262176 | tf_op jit(solution)/shard_map/ppermute | solution.py:21
  13.3 0.6 pack.1
  13.9 1.6 %collective-permute-start.1 = (bf16[272,256]{1,0:T(8,128)(2,1)S(1)}, bf16[272,256]{1,0:T(8,128)(2,1)S(1)}, u32[]{:S(2)}, u32[]{:S(2)}) collective-permute-start(bf16[272,256]{1,0:T(8,128)(2,1)S(1)} %get-tuple-element.48), channel_id=1, source_target_pairs={{0,4},{1,5},{2,6},{3,7},{4,0},{5,1},{6,2},{7,3},{8,12},{9,13},{10,... | collective-permute-start | bytes 417800 | tf_op jit(solution)/shard_map/ppermute | solution.py:213
  15.6 2.6 %collective-permute-start.2 = (bf16[272,256]{1,0:T(8,128)(2,1)S(1)}, bf16[272,256]{1,0:T(8,128)(2,1)S(1)}, u32[]{:S(2)}, u32[]{:S(2)}) collective-permute-start(bf16[272,256]{1,0:T(8,128)(2,1)S(1)} %get-tuple-element.49), channel_id=1, source_target_pairs={{0,8},{1,9},{2,10},{3,11},{4,12},{5,13},{6,14},{7,15},{8,0},{9,1},... | collective-permute-start | bytes 417800 | tf_op jit(solution)/shard_map/ppermute | solution.py:213
  18.2 1.5 %collective-permute-start.9 = (bf16[16,128,128]{2,1,0:T(8,128)(2,1)}, bf16[16,128,128]{2,1,0:T(8,128)(2,1)}, u32[]{:S(2)}, u32[]{:S(2)}) collective-permute-start(bf16[16,128,128]{2,1,0:T(8,128)(2,1)} %bitcast.6.refs_4_), channel_id=1, source_target_pairs={{4,8},{5,9},{6,10},{7,11},{8,4},{9,5},{10,6},{11,7},{20,24},{21,25... | collective-permute-start | bytes 1572872 | tf_op jit(solution)/shard_map/ppermute | solution.py:213
  19.6 20.5 %collective-permute-done.13.refs_1_ = bf16[3,64,1024]{2,1,0:T(8,128)(2,1)S(1)} collective-permute-done((bf16[3,64,1024]{2,1,0:T(8,128)(2,1)}, bf16[3,64,1024]{2,1,0:T(8,128)(2,1)S(1)}, u32[]{:S(2)}, u32[]{:S(2)}) %collective-permute-start.13) | collective-permute-done | bytes 393248 | tf_op jit(solution)/shard_map/ppermute | solution.py:21
  40.1 5.5 %collective-permute-start.8 = (bf16[16,128,128]{2,1,0:T(8,128)(2,1)}, bf16[16,128,128]{2,1,0:T(8,128)(2,1)}, u32[]{:S(2)}, u32[]{:S(2)}) collective-permute-start(bf16[16,128,128]{2,1,0:T(8,128)(2,1)} %bitcast.6.refs_4_), channel_id=1, source_target_pairs={{0,8},{1,9},{2,10},{3,11},{12,4},{13,5},{14,6},{15,7},{16,24},{17,... | collective-permute-start | bytes 1572872 | tf_op jit(solution)/shard_map/ppermute | solution.py:213
  45.6 0.7 copy-done.7
  46.3 0.7 copy-done.9
  47.0 1.3 collective-permute-start.3
  48.3 23.1 %collective-permute-done.3.refs_3_ = bf16[272,256]{1,0:T(8,128)(2,1)S(1)} collective-permute-done((bf16[272,256]{1,0:T(8,128)(2,1)S(1)}, bf16[272,256]{1,0:T(8,128)(2,1)S(1)}, u32[]{:S(2)}, u32[]{:S(2)}) %collective-permute-start.3) | collective-permute-done | bytes 139296 | tf_op jit(solution)/shard_map/ppermute | solution.py:213
  71.4 0.7 copy-done.11
  72.2 0.9 copy-done.8
  73.1 0.9 copy-done.10
  74.0 0.9 copy-done.12
  74.9 0.8 stk.1
  75.7 1.5 %collective-permute-start.5 = (bf16[8,128,256]{2,1,0:T(8,128)(2,1)}, bf16[8,128,256]{2,1,0:T(8,128)(2,1)}, u32[]{:S(2)}, u32[]{:S(2)}) collective-permute-start(bf16[8,128,256]{2,1,0:T(8,128)(2,1)} %bitcast.5.refs_0_), channel_id=1, source_target_pairs={{0,2},{1,3},{2,0},{3,1},{4,6},{5,7},{6,4},{7,5},{8,10},{9,11},{10,... | collective-permute-start | bytes 1572872 | tf_op jit(solution)/shard_map/ppermute | solution.py:21
  77.3 0.2 collective-permute-start.4
  77.5 1.3 collective-permute-start.10
  78.8 0.3 collective-permute-start.14
  79.4 0.2 slice_reduce_fusion.3
  79.8 10.6 %collective-permute-done.5.refs_2_ = bf16[8,128,256]{2,1,0:T(8,128)(2,1)} collective-permute-done((bf16[8,128,256]{2,1,0:T(8,128)(2,1)}, bf16[8,128,256]{2,1,0:T(8,128)(2,1)}, u32[]{:S(2)}, u32[]{:S(2)}) %collective-permute-start.5) | collective-permute-done | bytes 524320 | tf_op jit(solution)/shard_map/ppermute | solution.py:21
  90.4 1.3 collective-permute-start.19
  91.7 2.1 %collective-permute-done.10.refs_7_ = bf16[16,128,128]{2,1,0:T(8,128)(2,1)} collective-permute-done((bf16[16,128,128]{2,1,0:T(8,128)(2,1)}, bf16[16,128,128]{2,1,0:T(8,128)(2,1)}, u32[]{:S(2)}, u32[]{:S(2)}) %collective-permute-start.10) | collective-permute-done | bytes 524320 | tf_op jit(solution)/shard_map/ppermute | solution.py:213
  93.9 2.1 %collective-permute-done.6.refs_3_ = bf16[8,128,256]{2,1,0:T(8,128)(2,1)S(1)} collective-permute-done((bf16[8,128,256]{2,1,0:T(8,128)(2,1)}, bf16[8,128,256]{2,1,0:T(8,128)(2,1)S(1)}, u32[]{:S(2)}, u32[]{:S(2)}) %collective-permute-start.6) | collective-permute-done | bytes 524320 | tf_op jit(solution)/shard_map/ppermute | solution.py:21
  95.9 3.5 %shard_map.82 = (bf16[3,16,128,256]{3,2,1,0:T(8,128)(2,1)S(1)}, bf16[12,128,1024]{2,1,0:T(8,128)(2,1)S(1)}, bf16[32,128,256]{2,1,0:T(8,128)(2,1)S(1)}) custom-call(s32[3,64]{1,0:T(4,128)S(1)} %pad_add_fusion.table, s32[4]{0:T(128)S(1)} %and_select_fusion.turns, s32[3]{0:T(128)S(1)} %pad_add_fusion.2.home, bf16[8,128,256]{2,1,0:T(8,128)(2,1)} %bitcast.5.refs_0_, ...), custom_call_target="tpu_custom_call" | custom-call | flops 402653184 | bytes 3145728 | tf_op jit(solution)/shard_map/pallas_call | solution.py:315
  99.5 2.9 %shard_map.83 = (f32[256,512]{1,0:T(8,128)S(1)}, bf16[256,512]{1,0:T(8,128)(2,1)S(1)}, bf16[12,128,1024]{2,1,0:T(8,128)(2,1)S(1)}) custom-call(s32[3,64]{1,0:T(4,128)S(1)} %pad_add_fusion.table, s32[4]{0:T(128)S(1)} %and_select_fusion.turns, s32[3]{0:T(128)S(1)} %pad_add_fusion.2.home, bf16[3,16,128,256]{3,2,1,0:T(8,128)(2,1)S(1)} %get-tuple-element.53.made, ...), custom_call_target="tpu_custom_call" | custom-call | flops 1073741824 | bytes 3145728 | tf_op jit(solution)/shard_map/pallas_call | solution.py:315
  102.3 2.0 %collective-permute-start.22 = (bf16[256,512]{1,0:T(8,128)(2,1)S(1)}, bf16[256,512]{1,0:T(8,128)(2,1)S(1)}, u32[]{:S(2)}, u32[]{:S(2)}) collective-permute-start(bf16[256,512]{1,0:T(8,128)(2,1)S(1)} %get-tuple-element.64), channel_id=1, source_target_pairs={{0,16},{16,0},{1,17},{17,1},{2,18},{18,2},{3,19},{19,3},{4,20},{20... | collective-permute-start | bytes 786440 | tf_op jit(solution)/shard_map/ppermute | solution.py:21
  104.3 2.5 %collective-permute-done.19.refs_1_ = bf16[16,128,128]{2,1,0:T(8,128)(2,1)S(1)} collective-permute-done((bf16[16,128,128]{2,1,0:T(8,128)(2,1)}, bf16[16,128,128]{2,1,0:T(8,128)(2,1)S(1)}, u32[]{:S(2)}, u32[]{:S(2)}) %collective-permute-start.19) | collective-permute-done | bytes 524320 | tf_op jit(solution)/shard_map/ppermute | solution.py:213
  106.8 1.4 %shard_map.86 = (f32[256,512]{1,0:T(8,128)S(1)}, bf16[256,512]{1,0:T(8,128)(2,1)S(1)}) custom-call(s32[3,64]{1,0:T(4,128)S(1)} %pad_add_fusion.table, s32[4]{0:T(128)S(1)} %and_select_fusion.turns, s32[3]{0:T(128)S(1)} %pad_add_fusion.2.home, bf16[32,128,256]{2,1,0:T(8,128)(2,1)S(1)} %get-tuple-element.60.rows_held, ...), custom_call_target="tpu_custom_call" | custom-call | flops 1207959552 | bytes 3145728 | tf_op jit(solution)/shard_map/pallas_call | solution.py:315
  108.3 3.6 %collective-permute-start.20 = (bf16[256,512]{1,0:T(8,128)(2,1)S(1)}, bf16[256,512]{1,0:T(8,128)(2,1)S(1)}, u32[]{:S(2)}, u32[]{:S(2)}) collective-permute-start(bf16[256,512]{1,0:T(8,128)(2,1)S(1)} %get-tuple-element.62), channel_id=1, source_target_pairs={{0,16},{16,0},{1,17},{17,1},{2,18},{18,2},{3,19},{19,3},{4,20},{20... | collective-permute-start | bytes 786440 | tf_op jit(solution)/shard_map/ppermute | solution.py:21
  111.9 1.2 shard_map.85
  113.0 1.0 collective-permute-start.17
  114.3 2.5 %shard_map.84 = (f32[256,512]{1,0:T(8,128)S(1)}, bf16[256,512]{1,0:T(8,128)(2,1)S(1)}) custom-call(s32[3,64]{1,0:T(4,128)S(1)} %pad_add_fusion.table, s32[4]{0:T(128)S(1)} %and_select_fusion.turns, s32[3]{0:T(128)S(1)} %pad_add_fusion.2.home, bf16[3,16,128,256]{3,2,1,0:T(8,128)(2,1)S(1)} %get-tuple-element.53.made, ...), custom_call_target="tpu_custom_call" | custom-call | flops 1073741824 | bytes 3145728 | tf_op jit(solution)/shard_map/pallas_call | solution.py:315
  116.9 2.1 %collective-permute-start.16 = (bf16[256,512]{1,0:T(8,128)(2,1)S(1)}, bf16[256,512]{1,0:T(8,128)(2,1)S(1)}, u32[]{:S(2)}, u32[]{:S(2)}) collective-permute-start(bf16[256,512]{1,0:T(8,128)(2,1)S(1)} %get-tuple-element.57), channel_id=1, source_target_pairs={{0,16},{16,0},{1,17},{17,1},{2,18},{18,2},{3,19},{19,3},{4,20},{20... | collective-permute-start | bytes 786440 | tf_op jit(solution)/shard_map/ppermute | solution.py:21
  119.0 5.7 %collective-permute-done.17 = bf16[256,512]{1,0:T(8,128)(2,1)S(1)} collective-permute-done((bf16[256,512]{1,0:T(8,128)(2,1)S(1)}, bf16[256,512]{1,0:T(8,128)(2,1)S(1)}, u32[]{:S(2)}, u32[]{:S(2)}) %collective-permute-start.17) | collective-permute-done | bytes 262176 | tf_op jit(solution)/shard_map/ppermute | solution.py:21
  124.7 0.4 collective-permute-start.18
  125.2 4.6 %collective-permute-start.21 = (bf16[256,512]{1,0:T(8,128)(2,1)S(1)}, bf16[256,512]{1,0:T(8,128)(2,1)S(1)}, u32[]{:S(2)}, u32[]{:S(2)}) collective-permute-start(bf16[256,512]{1,0:T(8,128)(2,1)S(1)} %get-tuple-element.69), channel_id=1, source_target_pairs={{0,12},{1,13},{2,14},{3,15},{12,0},{13,1},{14,2},{15,3},{16,28},{1... | collective-permute-start | bytes 786440 | tf_op jit(solution)/shard_map/ppermute | solution.py:213
  129.8 0.7 collective-permute-start.24
  130.6 0.5 gate.1.gate_open
  131.1 0.4 collective-permute-done.18.refs_1_
  131.5 7.4 %collective-permute-done.21.refs_2_ = bf16[256,512]{1,0:T(8,128)(2,1)S(1)} collective-permute-done((bf16[256,512]{1,0:T(8,128)(2,1)S(1)}, bf16[256,512]{1,0:T(8,128)(2,1)S(1)}, u32[]{:S(2)}, u32[]{:S(2)}) %collective-permute-start.21) | collective-permute-done | bytes 262176 | tf_op jit(solution)/shard_map/ppermute | solution.py:213
  138.9 1.0 finish.1
  (67 shorter events, 1.2 us)
Async XLA Ops:
  0.0 7.0 %copy-start = (bf16[12,64,1024]{2,1,0:T(8,128)(2,1)S(1)}, bf16[12,64,1024]{2,1,0:T(8,128)(2,1)}, u32[]{:S(2)}) copy-start(bf16[12,64,1024]{2,1,0:T(8,128)(2,1)} %refs_8_.1) | copy-start | bytes 4718596
  0.0 5.5 %copy-start.1 = (bf16[256,512]{1,0:T(8,128)(2,1)S(1)}, bf16[256,512]{1,0:T(8,128)(2,1)}, u32[]{:S(2)}) copy-start(bf16[256,512]{1,0:T(8,128)(2,1)} %state.1) | copy-start | bytes 786436
  0.0 8.3 %copy-start.15 = (s32[1,3,16]{2,0,1:T(1,128)S(1)}, s32[1,3,16]{2,0,1:T(1,128)}, u32[]{:S(2)}) copy-start(s32[1,3,16]{2,0,1:T(1,128)} %param.18) | copy-start | bytes 580
  2.5 76.3 %collective-permute-start.12 = (bf16[9,64,1024]{2,1,0:T(8,128)(2,1)}, bf16[9,64,1024]{2,1,0:T(8,128)(2,1)}, u32[]{:S(2)}, u32[]{:S(2)}) collective-permute-start(bf16[9,64,1024]{2,1,0:T(8,128)(2,1)} %slice.65), channel_id=1, source_target_pairs={{0,2},{1,3},{2,0},{3,1},{4,6},{5,7},{6,4},{7,5},{8,10},{9,11},{10,... | collective-permute-start | bytes 3538952 | tf_op jit(solution)/shard_map/ppermute | solution.py:21
  5.5 7.8 %collective-permute-start = (bf16[256,512]{1,0:T(8,128)(2,1)S(1)}, bf16[256,512]{1,0:T(8,128)(2,1)S(1)}, u32[]{:S(2)}, u32[]{:S(2)}) collective-permute-start(bf16[256,512]{1,0:T(8,128)(2,1)S(1)} %copy-done.1), channel_id=1, source_target_pairs={{0,16},{16,0},{1,17},{17,1},{2,18},{18,2},{3,19},{19,3},{4,20},{20... | collective-permute-start | bytes 786440 | tf_op jit(solution)/shard_map/ppermute | solution.py:21
  7.8 32.3 %collective-permute-start.13 = (bf16[3,64,1024]{2,1,0:T(8,128)(2,1)}, bf16[3,64,1024]{2,1,0:T(8,128)(2,1)S(1)}, u32[]{:S(2)}, u32[]{:S(2)}) collective-permute-start(bf16[3,64,1024]{2,1,0:T(8,128)(2,1)} %slice.66), channel_id=1, source_target_pairs={{0,2},{1,3},{2,0},{3,1},{4,6},{5,7},{6,4},{7,5},{8,10},{9,11},{10,... | collective-permute-start | bytes 1179656 | tf_op jit(solution)/shard_map/ppermute | solution.py:21
  13.3 35.0 %copy-start.3 = (bf16[256,512]{1,0:T(8,128)(2,1)}, bf16[256,512]{1,0:T(8,128)(2,1)S(1)}, u32[]{:S(2)}) copy-start(bf16[256,512]{1,0:T(8,128)(2,1)S(1)} %collective-permute-done.refs_1_) | copy-start | bytes 786436
  13.9 31.7 %collective-permute-start.1 = (bf16[272,256]{1,0:T(8,128)(2,1)S(1)}, bf16[272,256]{1,0:T(8,128)(2,1)S(1)}, u32[]{:S(2)}, u32[]{:S(2)}) collective-permute-start(bf16[272,256]{1,0:T(8,128)(2,1)S(1)} %get-tuple-element.48), channel_id=1, source_target_pairs={{0,4},{1,5},{2,6},{3,7},{4,0},{5,1},{6,2},{7,3},{8,12},{9,13},{10,... | collective-permute-start | bytes 417800 | tf_op jit(solution)/shard_map/ppermute | solution.py:213
  15.6 30.7 %collective-permute-start.2 = (bf16[272,256]{1,0:T(8,128)(2,1)S(1)}, bf16[272,256]{1,0:T(8,128)(2,1)S(1)}, u32[]{:S(2)}, u32[]{:S(2)}) collective-permute-start(bf16[272,256]{1,0:T(8,128)(2,1)S(1)} %get-tuple-element.49), channel_id=1, source_target_pairs={{0,8},{1,9},{2,10},{3,11},{4,12},{5,13},{6,14},{7,15},{8,0},{9,1},... | collective-permute-start | bytes 417800 | tf_op jit(solution)/shard_map/ppermute | solution.py:213
  18.2 57.6 %collective-permute-start.9 = (bf16[16,128,128]{2,1,0:T(8,128)(2,1)}, bf16[16,128,128]{2,1,0:T(8,128)(2,1)}, u32[]{:S(2)}, u32[]{:S(2)}) collective-permute-start(bf16[16,128,128]{2,1,0:T(8,128)(2,1)} %bitcast.6.refs_4_), channel_id=1, source_target_pairs={{4,8},{5,9},{6,10},{7,11},{8,4},{9,5},{10,6},{11,7},{20,24},{21,25... | collective-permute-start | bytes 1572872 | tf_op jit(solution)/shard_map/ppermute | solution.py:213
  40.1 8.2 %copy-start.5 = (bf16[3,64,1024]{2,1,0:T(8,128)(2,1)}, bf16[3,64,1024]{2,1,0:T(8,128)(2,1)S(1)}, u32[]{:S(2)}) copy-start(bf16[3,64,1024]{2,1,0:T(8,128)(2,1)S(1)} %collective-permute-done.13.refs_1_) | copy-start | bytes 1179652
  40.1 37.1 %collective-permute-start.8 = (bf16[16,128,128]{2,1,0:T(8,128)(2,1)}, bf16[16,128,128]{2,1,0:T(8,128)(2,1)}, u32[]{:S(2)}, u32[]{:S(2)}) collective-permute-start(bf16[16,128,128]{2,1,0:T(8,128)(2,1)} %bitcast.6.refs_4_), channel_id=1, source_target_pairs={{0,8},{1,9},{2,10},{3,11},{12,4},{13,5},{14,6},{15,7},{16,24},{17,... | collective-permute-start | bytes 1572872 | tf_op jit(solution)/shard_map/ppermute | solution.py:213
  45.6 0.7 copy-start.7
  46.3 31.2 %collective-permute-start.7 = (bf16[16,128,128]{2,1,0:T(8,128)(2,1)}, bf16[16,128,128]{2,1,0:T(8,128)(2,1)}, u32[]{:S(2)}, u32[]{:S(2)}) collective-permute-start(bf16[16,128,128]{2,1,0:T(8,128)(2,1)} %bitcast.6.refs_4_), channel_id=1, source_target_pairs={{0,4},{1,5},{2,6},{3,7},{4,0},{5,1},{6,2},{7,3},{8,12},{9,13},{10,... | collective-permute-start | bytes 1572872 | tf_op jit(solution)/shard_map/ppermute | solution.py:213
  46.3 0.7 copy-start.9
  47.0 24.5 %collective-permute-start.3 = (bf16[272,256]{1,0:T(8,128)(2,1)S(1)}, bf16[272,256]{1,0:T(8,128)(2,1)S(1)}, u32[]{:S(2)}, u32[]{:S(2)}) collective-permute-start(bf16[272,256]{1,0:T(8,128)(2,1)S(1)} %get-tuple-element.50), channel_id=1, source_target_pairs={{0,12},{1,13},{2,14},{3,15},{4,8},{5,9},{6,10},{7,11},{8,4},{9,5},... | collective-permute-start | bytes 417800 | tf_op jit(solution)/shard_map/ppermute | solution.py:213
  71.4 0.7 copy-start.11
  72.1 23.8 %collective-permute-start.11 = (bf16[12,64,1024]{2,1,0:T(8,128)(2,1)S(1)}, bf16[12,64,1024]{2,1,0:T(8,128)(2,1)S(1)}, u32[]{:S(2)}, u32[]{:S(2)}) collective-permute-start(bf16[12,64,1024]{2,1,0:T(8,128)(2,1)S(1)} %copy-done), channel_id=1, source_target_pairs={{0,1},{1,0},{2,3},{3,2},{4,5},{5,4},{6,7},{7,6},{8,9},{9,8},{10,11... | collective-permute-start | bytes 4718600 | tf_op jit(solution)/shard_map/ppermute | solution.py:21
  72.2 0.9 copy-start.8
  73.1 0.9 copy-start.10
  74.0 0.9 copy-start.12
  75.7 14.7 %collective-permute-start.5 = (bf16[8,128,256]{2,1,0:T(8,128)(2,1)}, bf16[8,128,256]{2,1,0:T(8,128)(2,1)}, u32[]{:S(2)}, u32[]{:S(2)}) collective-permute-start(bf16[8,128,256]{2,1,0:T(8,128)(2,1)} %bitcast.5.refs_0_), channel_id=1, source_target_pairs={{0,2},{1,3},{2,0},{3,1},{4,6},{5,7},{6,4},{7,5},{8,10},{9,11},{10,... | collective-permute-start | bytes 1572872 | tf_op jit(solution)/shard_map/ppermute | solution.py:21
  77.3 13.1 %collective-permute-start.4 = (bf16[8,128,256]{2,1,0:T(8,128)(2,1)}, bf16[8,128,256]{2,1,0:T(8,128)(2,1)}, u32[]{:S(2)}, u32[]{:S(2)}) collective-permute-start(bf16[8,128,256]{2,1,0:T(8,128)(2,1)} %bitcast.5.refs_0_), channel_id=1, source_target_pairs={{0,1},{1,0},{2,3},{3,2},{4,5},{5,4},{6,7},{7,6},{8,9},{9,8},{10,11... | collective-permute-start | bytes 1572872 | tf_op jit(solution)/shard_map/ppermute | solution.py:21
  77.5 16.3 %collective-permute-start.10 = (bf16[16,128,128]{2,1,0:T(8,128)(2,1)}, bf16[16,128,128]{2,1,0:T(8,128)(2,1)}, u32[]{:S(2)}, u32[]{:S(2)}) collective-permute-start(bf16[16,128,128]{2,1,0:T(8,128)(2,1)} %collective-permute-done.9.refs_0_), channel_id=1, source_target_pairs={{8,12},{9,13},{10,14},{11,15},{4,0},{5,1},{6,2},{7,3},{24,28},{25,... | collective-permute-start | bytes 1572872 | tf_op jit(solution)/shard_map/ppermute | solution.py:213
  78.8 20.7 %collective-permute-start.14 = (bf16[9,64,1024]{2,1,0:T(8,128)(2,1)}, bf16[9,64,1024]{2,1,0:T(8,128)(2,1)}, u32[]{:S(2)}, u32[]{:S(2)}) collective-permute-start(bf16[9,64,1024]{2,1,0:T(8,128)(2,1)} %collective-permute-done.12.refs_0_), channel_id=1, source_target_pairs={{0,1},{1,0},{2,3},{3,2},{4,5},{5,4},{6,7},{7,6},{8,9},{9,8},{10,11... | collective-permute-start | bytes 3538952 | tf_op jit(solution)/shard_map/ppermute | solution.py:21
  90.4 9.1 %collective-permute-start.15 = (bf16[3,64,1024]{2,1,0:T(8,128)(2,1)}, bf16[3,64,1024]{2,1,0:T(8,128)(2,1)S(1)}, u32[]{:S(2)}, u32[]{:S(2)}) collective-permute-start(bf16[3,64,1024]{2,1,0:T(8,128)(2,1)} %copy-done.5), channel_id=1, source_target_pairs={{0,1},{1,0},{2,3},{3,2},{4,5},{5,4},{6,7},{7,6},{8,9},{9,8},{10,11... | collective-permute-start | bytes 1179656 | tf_op jit(solution)/shard_map/ppermute | solution.py:21
  90.4 16.4 %collective-permute-start.19 = (bf16[16,128,128]{2,1,0:T(8,128)(2,1)}, bf16[16,128,128]{2,1,0:T(8,128)(2,1)S(1)}, u32[]{:S(2)}, u32[]{:S(2)}) collective-permute-start(bf16[16,128,128]{2,1,0:T(8,128)(2,1)} %collective-permute-done.8.refs_6_), channel_id=1, source_target_pairs={{8,12},{9,13},{10,14},{11,15},{4,0},{5,1},{6,2},{7,3},{24,28},{25,... | collective-permute-start | bytes 1572872 | tf_op jit(solution)/shard_map/ppermute | solution.py:213
  93.8 2.1 %collective-permute-start.6 = (bf16[8,128,256]{2,1,0:T(8,128)(2,1)}, bf16[8,128,256]{2,1,0:T(8,128)(2,1)S(1)}, u32[]{:S(2)}, u32[]{:S(2)}) collective-permute-start(bf16[8,128,256]{2,1,0:T(8,128)(2,1)} %collective-permute-done.5.refs_2_), channel_id=1, source_target_pairs={{0,1},{1,0},{2,3},{3,2},{4,5},{5,4},{6,7},{7,6},{8,9},{9,8},{10,11... | collective-permute-start | bytes 1572872 | tf_op jit(solution)/shard_map/ppermute | solution.py:21
  93.9 5.6 %copy-start.6 = (bf16[3,64,1024]{2,1,0:T(8,128)(2,1)S(1)}, bf16[3,64,1024]{2,1,0:T(8,128)(2,1)}, u32[]{:S(2)}) copy-start(bf16[3,64,1024]{2,1,0:T(8,128)(2,1)} %copy-done.5) | copy-start | bytes 1179652
  102.3 11.7 %collective-permute-start.22 = (bf16[256,512]{1,0:T(8,128)(2,1)S(1)}, bf16[256,512]{1,0:T(8,128)(2,1)S(1)}, u32[]{:S(2)}, u32[]{:S(2)}) collective-permute-start(bf16[256,512]{1,0:T(8,128)(2,1)S(1)} %get-tuple-element.64), channel_id=1, source_target_pairs={{0,16},{16,0},{1,17},{17,1},{2,18},{18,2},{3,19},{19,3},{4,20},{20... | collective-permute-start | bytes 786440 | tf_op jit(solution)/shard_map/ppermute | solution.py:21
  108.3 16.8 %collective-permute-start.20 = (bf16[256,512]{1,0:T(8,128)(2,1)S(1)}, bf16[256,512]{1,0:T(8,128)(2,1)S(1)}, u32[]{:S(2)}, u32[]{:S(2)}) collective-permute-start(bf16[256,512]{1,0:T(8,128)(2,1)S(1)} %get-tuple-element.62), channel_id=1, source_target_pairs={{0,16},{16,0},{1,17},{17,1},{2,18},{18,2},{3,19},{19,3},{4,20},{20... | collective-permute-start | bytes 786440 | tf_op jit(solution)/shard_map/ppermute | solution.py:21
  113.0 11.6 %collective-permute-start.17 = (bf16[256,512]{1,0:T(8,128)(2,1)S(1)}, bf16[256,512]{1,0:T(8,128)(2,1)S(1)}, u32[]{:S(2)}, u32[]{:S(2)}) collective-permute-start(bf16[256,512]{1,0:T(8,128)(2,1)S(1)} %get-tuple-element.59), channel_id=1, source_target_pairs={{0,16},{16,0},{1,17},{17,1},{2,18},{18,2},{3,19},{19,3},{4,20},{20... | collective-permute-start | bytes 786440 | tf_op jit(solution)/shard_map/ppermute | solution.py:21
  114.1 11.0 %collective-permute-start.23 = (bf16[256,512]{1,0:T(8,128)(2,1)S(1)}, bf16[256,512]{1,0:T(8,128)(2,1)S(1)}, u32[]{:S(2)}, u32[]{:S(2)}) collective-permute-start(bf16[256,512]{1,0:T(8,128)(2,1)S(1)} %add_convert_fusion.1), channel_id=1, source_target_pairs={{0,4},{1,5},{2,6},{3,7},{4,12},{5,13},{6,14},{7,15},{12,8},{13,9},... | collective-permute-start | bytes 786440 | tf_op jit(solution)/shard_map/ppermute | solution.py:213
  116.8 13.7 %copy-start.2 = (bf16[1024,512]{1,0:T(8,128)(2,1)S(1)}, bf16[1024,512]{1,0:T(8,128)(2,1)}, u32[]{:S(2)}) copy-start(bf16[1024,512]{1,0:T(8,128)(2,1)} %weight.1) | copy-start | bytes 3145732
  116.9 13.7 %copy-start.4 = (bf16[256,512]{1,0:T(8,128)(2,1)S(1)}, bf16[256,512]{1,0:T(8,128)(2,1)}, u32[]{:S(2)}) copy-start(bf16[256,512]{1,0:T(8,128)(2,1)} %copy-done.3) | copy-start | bytes 786436
  116.9 13.7 %copy-start.14 = (f32[512]{0:T(512)S(1)}, f32[512]{0:T(512)}, u32[]{:S(2)}) copy-start(f32[512]{0:T(512)} %param.15) | copy-start | bytes 6148
  116.9 14.2 %collective-permute-start.16 = (bf16[256,512]{1,0:T(8,128)(2,1)S(1)}, bf16[256,512]{1,0:T(8,128)(2,1)S(1)}, u32[]{:S(2)}, u32[]{:S(2)}) collective-permute-start(bf16[256,512]{1,0:T(8,128)(2,1)S(1)} %get-tuple-element.57), channel_id=1, source_target_pairs={{0,16},{16,0},{1,17},{17,1},{2,18},{18,2},{3,19},{19,3},{4,20},{20... | collective-permute-start | bytes 786440 | tf_op jit(solution)/shard_map/ppermute | solution.py:21
  124.7 6.8 %collective-permute-start.18 = (bf16[256,512]{1,0:T(8,128)(2,1)S(1)}, bf16[256,512]{1,0:T(8,128)(2,1)S(1)}, u32[]{:S(2)}, u32[]{:S(2)}) collective-permute-start(bf16[256,512]{1,0:T(8,128)(2,1)S(1)} %add_convert_fusion.2), channel_id=1, source_target_pairs={{0,4},{1,5},{2,6},{3,7},{4,0},{5,1},{6,2},{7,3},{8,12},{9,13},{10,... | collective-permute-start | bytes 786440 | tf_op jit(solution)/shard_map/ppermute | solution.py:213
  125.2 13.7 %collective-permute-start.21 = (bf16[256,512]{1,0:T(8,128)(2,1)S(1)}, bf16[256,512]{1,0:T(8,128)(2,1)S(1)}, u32[]{:S(2)}, u32[]{:S(2)}) collective-permute-start(bf16[256,512]{1,0:T(8,128)(2,1)S(1)} %get-tuple-element.69), channel_id=1, source_target_pairs={{0,12},{1,13},{2,14},{3,15},{12,0},{13,1},{14,2},{15,3},{16,28},{1... | collective-permute-start | bytes 786440 | tf_op jit(solution)/shard_map/ppermute | solution.py:213
  129.8 9.0 %collective-permute-start.24 = (bf16[256,512]{1,0:T(8,128)(2,1)S(1)}, bf16[256,512]{1,0:T(8,128)(2,1)S(1)}, u32[]{:S(2)}, u32[]{:S(2)}) collective-permute-start(bf16[256,512]{1,0:T(8,128)(2,1)S(1)} %get-tuple-element.68), channel_id=1, source_target_pairs={{4,8},{5,9},{6,10},{7,11},{8,4},{9,5},{10,6},{11,7},{20,24},{21,25... | collective-permute-start | bytes 786440 | tf_op jit(solution)/shard_map/ppermute | solution.py:213
  130.6 8.3 %copy-start.13 = (f32[512]{0:T(512)S(1)}, f32[512]{0:T(512)}, u32[]{:S(2)}) copy-start(f32[512]{0:T(512)} %param.16) | copy-start | bytes 6148

commit v3 on v2

--- a/solution.py
+++ b/solution.py
@@ -21,16 +21,20 @@
     return lax.ppermute(value, axis, [(i, i ^ bit) for i in range(size)])
 
 
-def pack_kernel(n_rel, where, note, *refs):
-    halves, outs = refs[:n_rel], refs[n_rel:]
-    rows, width = halves[0].shape[0], outs[0].shape[1]
+def pack_kernel(n_rel, where, note, state, *refs):
+    others, outs = refs[:n_rel - 1], refs[n_rel - 1:]
+    rows, width = outs[0].shape[0] - NOTE_ROWS, outs[0].shape[1]
+    first = pl.multiple_of(where[2, 0], rows)
     for j, out in enumerate(outs):
         start = pl.multiple_of(where[1, j], width)
-        for r, half in enumerate(halves):
+        for r in range(n_rel):
 
             @pl.when(where[0, j] == r)
-            def _(half=half, out=out, start=start):
-                out[:rows] = half[:, pl.ds(start, width)]
+            def _(r=r, out=out, start=start):
+                if r:
+                    out[:rows] = others[r - 1][:, pl.ds(start, width)]
+                else:
+                    out[:rows] = state[pl.ds(first, rows), pl.ds(start, width)]
 
         out[rows:] = note[...]
 
@@ -94,10 +98,14 @@
 
 
 def multiply_tiles(turns, table, base, swapped, lists, rows_held, made):
+    tile_rows = lists.shape[1]
+
     def step(n, _):
         for u in range(GROUP):
             s = n * GROUP + u
-            product = jnp.dot(lists[s], rows_held[table[0, base + s]], preferred_element_type=F32)
+            first = pl.multiple_of(table[3, base + s], tile_rows)
+            rows = rows_held[table[0, base + s], pl.ds(first, tile_rows), :]
+            product = jnp.dot(lists[s], rows, preferred_element_type=F32)
             turned = pltpu.roll(product, product.shape[1] // 2, 1)
             made[s] = jnp.where(swapped, turned, product).astype(BF16)
         return 0
@@ -128,17 +136,17 @@
             outs[r][t * tile_rows:(t + 1) * tile_rows] = acc[t, :, pl.ds(start, own)].astype(outs[r].dtype)
 
 
-def early_kernel(members, way_counts, n_weights, table, turns, home, *refs):
-    states, tiles, weights, rest = take(refs, members, sum(way_counts), n_weights)
+def early_kernel(members, places, way_counts, n_weights, table, turns, home, *refs):
+    states, tiles, weights, rest = take(refs, len(places), sum(way_counts), n_weights)
     made, held, rows_held, lists, state_sem, tile_sem, weight_sem = rest
     slots = lists.shape[1]
-    per_member = states[0].shape[0]
-    loads = [
-        pltpu.make_async_copy(ref, rows_held.at[pl.ds(i * per_member, per_member)], state_sem.at[i])
-        for i, ref in enumerate(states)
-    ]
-    for load in loads:
-        load.start()
+    chunks, rows = states[0].shape[0], states[0].shape[1]
+    loads = []
+    for n, ((i, r), ref) in enumerate(zip(places, states)):
+        first = pl.multiple_of(lax.bitwise_xor(home[1], r) * rows, rows)
+        to = rows_held.at[pl.ds(i * chunks, chunks), pl.ds(first, rows), :]
+        loads.append(pltpu.make_async_copy(ref, to, state_sem.at[n]))
+        loads[-1].start()
     tile_loads = start_tiles(way_counts, home[2], tiles, lists, tile_sem)
     weight_loads = start_weights(members, home[0], weights, held, weight_sem)
     for load in loads:
@@ -215,6 +223,11 @@
     def partner(value, j):
         return along(value, [(q, q ^ j) for q in range(chunks)])
 
+    rows = ent_dev // n_rel
+    others = []
+    for r in range(1, n_rel):
+        asked_rows = lax.dynamic_slice_in_dim(state, lax.bitwise_xor(rel, r) * rows, rows, 0)
+        others.append(swap(asked_rows, "rel", n_rel, r))
     halves = [state] + [swap(state, "rel", n_rel, r) for r in range(1, n_rel)]
 
     values = tile_values[0]
@@ -233,20 +246,24 @@
     note = note.at[3, :1].set(tile_count[0].astype(BF16))
     asked = lax.bitwise_xor(part, jnp.arange(chunks, dtype=jnp.int32))
     per_half = chunks // n_rel
-    where = jnp.stack([lax.bitwise_xor(asked // per_half, rel), (asked % per_half) * width])
+    where = jnp.stack([
+        lax.bitwise_xor(asked // per_half, rel),
+        (asked % per_half) * width,
+        jnp.full((chunks,), rel * rows, jnp.int32),
+    ])
     pieces = pl.pallas_call(
         functools.partial(pack_kernel, n_rel),
-        out_shape=[jax.ShapeDtypeStruct((ent_dev + NOTE_ROWS, width), BF16) for _ in range(chunks)],
+        out_shape=[jax.ShapeDtypeStruct((rows + NOTE_ROWS, width), BF16) for _ in range(chunks)],
         in_specs=[SMEM] + [VMEM] * (n_rel + 1),
         out_specs=[VMEM] * chunks,
         compiler_params=pltpu.CompilerParams(vmem_limit_bytes=8 << 20),
         name="pack",
-    )(where, note, *halves)
+    )(where, note, state, *others)
     moved = [partner(pieces[j], j) for j in range(1, chunks)]
     own, notes = pl.pallas_call(
         functools.partial(stack_kernel, chunks),
         out_shape=[
-            jax.ShapeDtypeStruct((chunks, ent_dev, width), BF16),
+            jax.ShapeDtypeStruct((chunks, rows, width), BF16),
             jax.ShapeDtypeStruct((chunks, NOTE_ROWS, width), BF16),
         ],
         in_specs=[VMEM] * chunks,
@@ -260,26 +277,38 @@
     live = jnp.arange(slots, dtype=jnp.int32)[None] < counts[:, None]
     owner = source // per_tile
     place = lax.bitwise_xor(owner % members, member) * chunks
-    place = (place + lax.bitwise_xor(part, owner // members)) * per_tile + source % per_tile
+    place = place + lax.bitwise_xor(part, owner // members)
     table = jnp.stack([
         jnp.where(live, place, 0).reshape(-1),
         jnp.where(live, target, per_tile).reshape(-1),
         jnp.where(live, relation, 0).reshape(-1),
+        (source % per_tile * tile_rows).reshape(-1),
     ])
     turns = (counts + GROUP - 1) // GROUP
 
-    own = own.reshape(chunks * per_tile, tile_rows, width)
-    cut = max(1, rel_dev - max(1, rel_dev // 4))
+    cut = max(1, rel_dev * 7 // 12)
     parts = (rel_weight[:cut], rel_weight[cut:])
-    states, weights = [own], [(rel_weight,)]
-    high = True
     bits = [1 << b for b in reversed(range(members.bit_length() - 1))]
-    order = [0]
+    rel_bits = [1 << b for b in reversed(range(n_rel.bit_length() - 1))]
+    states, places = [own], [(0, 0)]
+
+    def spread(axis, size, bit):
+        more = [swap(v, axis, size, bit) for v in states]
+        step = (0, bit) if axis == "rel" else (bit, 0)
+        places.extend([(i | step[0], r | step[1]) for i, r in places])
+        states.extend(more)
+
+    for bit in bits[:-1]:
+        spread("ent", n_ent, bit)
+    for bit in rel_bits:
+        spread("rel", n_rel, bit)
+    spread("ent", n_ent, bits[-1])
+
+    weights, order = [(rel_weight,)], [0]
     for bit in bits:
-        states = states + [swap(v, "ent", n_ent, bit) for v in states]
         more = []
         for i, held in enumerate(weights):
-            if i == 0 and high:
+            if i == 0 and bit == bits[0]:
                 more.append(tuple(swap(v, "ent", n_ent, bit) for v in parts))
             elif i == 0:
                 more.append((swap(rel_weight, "ent", n_ent, bit),))
@@ -287,8 +316,6 @@
                 more.append(tuple(swap(v, "ent", n_ent, bit) for v in held))
         weights = weights + more
         order = order + [o | bit for o in order]
-        high = False
-    states = [states[order.index(i)] for i in range(members)]
     weights = [weights[order.index(i)] for i in range(members)]
     own_weights = [v for held in weights[:members // 2] for v in held]
     other_weights = [v for held in weights[members // 2:] for v in held]
@@ -332,17 +359,17 @@
     slot_flops = 2 * slots * tile_rows * width
     flat = [t for j in early for t in tiles[j]]
     made, own_half, rows_held = call(
-        functools.partial(early_kernel, members, early_ways, len(own_weights)),
+        functools.partial(early_kernel, members, tuple(places), early_ways, len(own_weights)),
         [*states, *flat, *own_weights],
-        [ANY] * (members + len(flat) + len(own_weights)),
+        [ANY] * (len(states) + len(flat) + len(own_weights)),
         [
             products,
             jax.ShapeDtypeStruct(half_shape, BF16),
-            jax.ShapeDtypeStruct((members * chunks * per_tile, tile_rows, width), BF16),
+            jax.ShapeDtypeStruct((members * chunks, ent_dev, width), BF16),
         ],
         [
             pltpu.VMEM((len(early), slots, tile_rows, tile_rows), BF16),
-            pltpu.SemaphoreType.DMA((members,)),
+            pltpu.SemaphoreType.DMA((len(states),)),
             pltpu.SemaphoreType.DMA((len(early),)),
             pltpu.SemaphoreType.DMA((len(own_weights),)),
         ],
@@ -383,23 +410,24 @@
     for g, j in enumerate(late):
         results[j] = rest[g * n_rel:(g + 1) * n_rel]
 
-    def summed(j):
+    def summed(j, dtype=BF16):
+        moved = [swap(v, "rel", n_rel, r + 1) for r, v in enumerate(results[j][1:])]
         term = results[j][0]
-        for r in range(1, n_rel):
-            term = term + swap(results[j][r], "rel", n_rel, r).astype(F32)
-        return term
+        for other in moved:
+            term = term + other.astype(F32)
+        return term.astype(dtype)
 
     if line:
-        passed = along(summed(2).astype(BF16), [(0, 1), (1, 3), (3, 2), (2, 0)])
-        three = summed(3)
-        across = along(three.astype(BF16), [(0, 3), (3, 0)])
-        total = (three + passed.astype(F32)).astype(BF16)
+        passed = along(summed(2), [(0, 1), (1, 3), (3, 2), (2, 0)])
+        three = lax.optimization_barrier(summed(3))
+        across = along(three, [(0, 3), (3, 0)])
+        total = (three.astype(F32) + passed.astype(F32)).astype(BF16)
         total = along(total, [(1, 2), (2, 1)])
-        terms = [summed(0), partner(summed(1).astype(BF16), 1), across, total, passed]
+        terms = [summed(0, F32), partner(summed(1), 1), across, total, passed]
         used = edge
     else:
-        terms = [summed(0)]
-        terms += [partner(summed(j).astype(BF16), j) for j in range(1, chunks)]
+        terms = [summed(0, F32)]
+        terms += [partner(summed(j), j) for j in range(1, chunks)]
         used = jnp.ones((), jnp.int32)
     return pl.pallas_call(
         finish_kernel,

time: 140 us -> 125 us (0.89)
  waiting for transfers between devices: 78.6 us -> 57.8 us
  local copies, waits for them, and re-layouts: 8.61 us -> 12 us
  starting transfers between devices: 36.7 us -> 38.5 us
    ppermute x13 -> x18, waiting for transfers between devices: 43.1 us -> 16.2 us  [swap(): return lax.ppermute(value, axis, [(i, i ^ bit) for i in range(size)])]
    ppermute x12, waiting for transfers between devices: 35.5 us -> 41.6 us  [along(): return lax.ppermute(value, 'ent', perm)]
    unnamed x33, local copies, waits for them, and re-layouts: 4.75 us -> 7.16 us
    ppermute x13 -> x18, starting transfers between devices: 15.8 us -> 17.5 us  [swap(): return lax.ppermute(value, axis, [(i, i ^ bit) for i in range(size)])]
  transfers between devices with their start and end apart: 25 -> 30, of which waited for: 10 -> 13; matrix products, arithmetic and copies ran while one was open for 1% -> 4% of each run, Pallas kernels for 10% -> 10%
where the time goes in v3:
time: 125 us
  waiting for transfers between devices  57.8 us (46%)
  starting transfers between devices  38.5 us (31%)
  Pallas kernels  13.9 us (11%)
  local copies, waits for them, and re-layouts  12 us (10%)
  other arithmetic  1.34 us (1%)
    ppermute x12, waiting for transfers between devices, along(): return lax.ppermute(value, 'ent', perm)  41.6 us
    ppermute x12, starting transfers between devices, along(): return lax.ppermute(value, 'ent', perm)  21 us
    ppermute x18, starting transfers between devices, swap(): return lax.ppermute(value, axis, [(i, i ^ bit) for i in range(size)])  17.5 us
    ppermute x18, waiting for transfers between devices, swap(): return lax.ppermute(value, axis, [(i, i ^ bit) for i in range(size)])  16.2 us
    pallas_call x5, Pallas kernels, call(): pl.pallas_call(body, out_shape=out_shape, in_specs=[SMEM] * 3 + in_specs,...  11.8 us
    unnamed x33, local copies, waits for them, and re-layouts  7.16 us
    slice x2, local copies, waits for them, and re-layouts, shards(): parts = (rel_weight[:cut], rel_weight[cut:])  3.12 us
  transfers between devices with their start and end apart: 30, of which 13 were waited for; matrix products, arithmetic and copies ran while one was open for 4% of the time, Pallas kernels for 10%

profile of v3, /device:TPU:0, one launch (start us, length us, event | category | flops | bytes accessed | tf_op | source)
XLA Modules:
  0.0 124.5 jit_solution(5581350368266228901)
XLA Ops:
  0.0 1.0 constant_dynamic-slice_fusion
  1.0 3.0 %collective-permute-start.1 = (bf16[128,512]{1,0:T(8,128)(2,1)S(1)}, bf16[128,512]{1,0:T(8,128)(2,1)S(1)}, u32[]{:S(2)}, u32[]{:S(2)}) collective-permute-start(bf16[128,512]{1,0:T(8,128)(2,1)S(1)} %constant_dynamic-slice_fusion), channel_id=1, source_target_pairs={{0,16},{16,0},{1,17},{17,1},{2,18},{18,2},{3,19},{19,3},{4,20},{20... | collective-permute-start | bytes 393224 | tf_op jit(solution)/shard_map/ppermute | solution.py:21
  4.2 0.7 convert_element_type.44
  5.6 1.9 %collective-permute-done.1.refs_0_ = bf16[128,512]{1,0:T(8,128)(2,1)S(1)} collective-permute-done((bf16[128,512]{1,0:T(8,128)(2,1)S(1)}, bf16[128,512]{1,0:T(8,128)(2,1)S(1)}, u32[]{:S(2)}, u32[]{:S(2)}) %collective-permute-start.1) | collective-permute-done | bytes 131104 | tf_op jit(solution)/shard_map/ppermute | solution.py:21
  7.6 0.9 copy-done.1
  9.2 1.9 %collective-permute-start.2 = (bf16[144,256]{1,0:T(8,128)(2,1)S(1)}, bf16[144,256]{1,0:T(8,128)(2,1)S(1)}, u32[]{:S(2)}, u32[]{:S(2)}) collective-permute-start(bf16[144,256]{1,0:T(8,128)(2,1)S(1)} %get-tuple-element.48), channel_id=1, source_target_pairs={{0,4},{1,5},{2,6},{3,7},{4,0},{5,1},{6,2},{7,3},{8,12},{9,13},{10,... | collective-permute-start | bytes 221192 | tf_op jit(solution)/shard_map/ppermute | solution.py:221
  11.1 2.6 %collective-permute-start.3 = (bf16[144,256]{1,0:T(8,128)(2,1)S(1)}, bf16[144,256]{1,0:T(8,128)(2,1)S(1)}, u32[]{:S(2)}, u32[]{:S(2)}) collective-permute-start(bf16[144,256]{1,0:T(8,128)(2,1)S(1)} %get-tuple-element.49), channel_id=1, source_target_pairs={{0,8},{1,9},{2,10},{3,11},{4,12},{5,13},{6,14},{7,15},{8,0},{9,1},... | collective-permute-start | bytes 221192 | tf_op jit(solution)/shard_map/ppermute | solution.py:221
  13.7 1.4 %collective-permute-start.14 = (bf16[16,128,128]{2,1,0:T(8,128)(2,1)}, bf16[16,128,128]{2,1,0:T(8,128)(2,1)}, u32[]{:S(2)}, u32[]{:S(2)}) collective-permute-start(bf16[16,128,128]{2,1,0:T(8,128)(2,1)} %bitcast.5.refs_8_), channel_id=1, source_target_pairs={{4,8},{5,9},{6,10},{7,11},{8,4},{9,5},{10,6},{11,7},{20,24},{21,25... | collective-permute-start | bytes 1572872 | tf_op jit(solution)/shard_map/ppermute | solution.py:221
  15.1 3.3 %collective-permute-done.3.refs_2_ = bf16[144,256]{1,0:T(8,128)(2,1)S(1)} collective-permute-done((bf16[144,256]{1,0:T(8,128)(2,1)S(1)}, bf16[144,256]{1,0:T(8,128)(2,1)S(1)}, u32[]{:S(2)}, u32[]{:S(2)}) %collective-permute-start.3) | collective-permute-done | bytes 73760 | tf_op jit(solution)/shard_map/ppermute | solution.py:221
  18.4 1.5 %collective-permute-done.4.refs_3_ = bf16[144,256]{1,0:T(8,128)(2,1)S(1)} collective-permute-done((bf16[144,256]{1,0:T(8,128)(2,1)S(1)}, bf16[144,256]{1,0:T(8,128)(2,1)S(1)}, u32[]{:S(2)}, u32[]{:S(2)}) %collective-permute-start.4) | collective-permute-done | bytes 73760 | tf_op jit(solution)/shard_map/ppermute | solution.py:221
  19.9 1.6 %collective-permute-start.5 = (bf16[4,128,256]{2,1,0:T(8,128)(2,1)S(1)}, bf16[4,128,256]{2,1,0:T(8,128)(2,1)S(1)}, u32[]{:S(2)}, u32[]{:S(2)}) collective-permute-start(bf16[4,128,256]{2,1,0:T(8,128)(2,1)S(1)} %get-tuple-element.52.refs_0_), channel_id=1, source_target_pairs={{0,2},{1,3},{2,0},{3,1},{4,6},{5,7},{6,4},{7,5},{8,10},{9,11},{10,... | collective-permute-start | bytes 786440 | tf_op jit(solution)/shard_map/ppermute | solution.py:21
  21.5 1.5 %collective-permute-start.6 = (bf16[4,128,256]{2,1,0:T(8,128)(2,1)S(1)}, bf16[4,128,256]{2,1,0:T(8,128)(2,1)S(1)}, u32[]{:S(2)}, u32[]{:S(2)}) collective-permute-start(bf16[4,128,256]{2,1,0:T(8,128)(2,1)S(1)} %get-tuple-element.52.refs_0_), channel_id=1, source_target_pairs={{0,16},{16,0},{1,17},{17,1},{2,18},{18,2},{3,19},{19,3},{4,20},{20... | collective-permute-start | bytes 786440 | tf_op jit(solution)/shard_map/ppermute | solution.py:21
  23.0 2.2 %slice.65 = bf16[7,64,1024]{2,1,0:T(8,128)(2,1)} slice(bf16[12,64,1024]{2,1,0:T(8,128)(2,1)} %refs_12_.1), slice={[0:7], [0:64], [0:1024]} | slice | bytes 1835008 | tf_op jit(solution)/shard_map/slice | solution.py:290
  26.4 5.4 %collective-permute-start.13 = (bf16[16,128,128]{2,1,0:T(8,128)(2,1)}, bf16[16,128,128]{2,1,0:T(8,128)(2,1)}, u32[]{:S(2)}, u32[]{:S(2)}) collective-permute-start(bf16[16,128,128]{2,1,0:T(8,128)(2,1)} %bitcast.5.refs_8_), channel_id=1, source_target_pairs={{0,8},{1,9},{2,10},{3,11},{12,4},{13,5},{14,6},{15,7},{16,24},{17,... | collective-permute-start | bytes 1572872 | tf_op jit(solution)/shard_map/ppermute | solution.py:221
  31.8 0.9 slice.66
  32.8 0.7 copy-done.10
  33.5 1.5 %collective-permute-start.18 = (bf16[5,64,1024]{2,1,0:T(8,128)(2,1)}, bf16[5,64,1024]{2,1,0:T(8,128)(2,1)}, u32[]{:S(2)}, u32[]{:S(2)}) collective-permute-start(bf16[5,64,1024]{2,1,0:T(8,128)(2,1)} %slice.66), channel_id=1, source_target_pairs={{0,2},{1,3},{2,0},{3,1},{4,6},{5,7},{6,4},{7,5},{8,10},{9,11},{10,... | collective-permute-start | bytes 1966088 | tf_op jit(solution)/shard_map/ppermute | solution.py:21
  35.1 8.5 %collective-permute-done.13.refs_10_ = bf16[16,128,128]{2,1,0:T(8,128)(2,1)} collective-permute-done((bf16[16,128,128]{2,1,0:T(8,128)(2,1)}, bf16[16,128,128]{2,1,0:T(8,128)(2,1)}, u32[]{:S(2)}, u32[]{:S(2)}) %collective-permute-start.13) | collective-permute-done | bytes 524320 | tf_op jit(solution)/shard_map/ppermute | solution.py:221
  43.6 1.5 %collective-permute-start.7 = (bf16[4,128,256]{2,1,0:T(8,128)(2,1)}, bf16[4,128,256]{2,1,0:T(8,128)(2,1)}, u32[]{:S(2)}, u32[]{:S(2)}) collective-permute-start(bf16[4,128,256]{2,1,0:T(8,128)(2,1)} %copy-done.6), channel_id=1, source_target_pairs={{0,16},{16,0},{1,17},{17,1},{2,18},{18,2},{3,19},{19,3},{4,20},{20... | collective-permute-start | bytes 786440 | tf_op jit(solution)/shard_map/ppermute | solution.py:21
  45.1 8.3 %collective-permute-done.12.refs_9_ = bf16[16,128,128]{2,1,0:T(8,128)(2,1)} collective-permute-done((bf16[16,128,128]{2,1,0:T(8,128)(2,1)}, bf16[16,128,128]{2,1,0:T(8,128)(2,1)}, u32[]{:S(2)}, u32[]{:S(2)}) %collective-permute-start.12) | collective-permute-done | bytes 524320 | tf_op jit(solution)/shard_map/ppermute | solution.py:221
  53.6 8.7 %collective-permute-done.18.refs_1_ = bf16[5,64,1024]{2,1,0:T(8,128)(2,1)} collective-permute-done((bf16[5,64,1024]{2,1,0:T(8,128)(2,1)}, bf16[5,64,1024]{2,1,0:T(8,128)(2,1)}, u32[]{:S(2)}, u32[]{:S(2)}) %collective-permute-start.18) | collective-permute-done | bytes 655392 | tf_op jit(solution)/shard_map/ppermute | solution.py:21
  63.0 0.7 copy-done.12
  64.5 1.3 %collective-permute-start.15 = (bf16[16,128,128]{2,1,0:T(8,128)(2,1)}, bf16[16,128,128]{2,1,0:T(8,128)(2,1)S(1)}, u32[]{:S(2)}, u32[]{:S(2)}) collective-permute-start(bf16[16,128,128]{2,1,0:T(8,128)(2,1)} %collective-permute-done.14.refs_0_), channel_id=1, source_target_pairs={{8,12},{9,13},{10,14},{11,15},{4,0},{5,1},{6,2},{7,3},{24,28},{25,... | collective-permute-start | bytes 1572872 | tf_op jit(solution)/shard_map/ppermute | solution.py:221
  65.8 1.3 %collective-permute-start.24 = (bf16[16,128,128]{2,1,0:T(8,128)(2,1)}, bf16[16,128,128]{2,1,0:T(8,128)(2,1)S(1)}, u32[]{:S(2)}, u32[]{:S(2)}) collective-permute-start(bf16[16,128,128]{2,1,0:T(8,128)(2,1)} %collective-permute-done.13.refs_10_), channel_id=1, source_target_pairs={{8,12},{9,13},{10,14},{11,15},{4,0},{5,1},{6,2},{7,3},{24,28},{25,... | collective-permute-start | bytes 1572872 | tf_op jit(solution)/shard_map/ppermute | solution.py:221
  67.2 14.2 %collective-permute-done.15.refs_11_ = bf16[16,128,128]{2,1,0:T(8,128)(2,1)S(1)} collective-permute-done((bf16[16,128,128]{2,1,0:T(8,128)(2,1)}, bf16[16,128,128]{2,1,0:T(8,128)(2,1)S(1)}, u32[]{:S(2)}, u32[]{:S(2)}) %collective-permute-start.15) | collective-permute-done | bytes 524320 | tf_op jit(solution)/shard_map/ppermute | solution.py:221
  82.0 0.9 copy-done.5
  82.9 0.9 copy-done.7
  83.9 0.9 copy-done.9
  84.8 0.9 copy-done.11
  85.8 0.9 copy-done.13
  86.7 3.6 %shard_map.82 = (bf16[3,16,128,256]{3,2,1,0:T(8,128)(2,1)S(1)}, bf16[12,128,1024]{2,1,0:T(8,128)(2,1)S(1)}, bf16[16,256,256]{2,1,0:T(8,128)(2,1)S(1)}) custom-call(s32[4,64]{1,0:T(4,128)S(1)} %pad_add_fusion.table, s32[4]{0:T(128)S(1)} %and_select_fusion.turns, s32[3]{0:T(128)S(1)} %pad_add_fusion.1.home, bf16[4,128,256]{2,1,0:T(8,128)(2,1)S(1)} %copy-done.5, ...), custom_call_target="tpu_custom_call" | custom-call | flops 402653184 | bytes 3145728 | tf_op jit(solution)/shard_map/pallas_call | solution.py:342
  90.3 3.0 %shard_map.83 = (f32[256,512]{1,0:T(8,128)S(1)}, bf16[256,512]{1,0:T(8,128)(2,1)S(1)}, bf16[12,128,1024]{2,1,0:T(8,128)(2,1)S(1)}) custom-call(s32[4,64]{1,0:T(4,128)S(1)} %pad_add_fusion.table, s32[4]{0:T(128)S(1)} %and_select_fusion.turns, s32[3]{0:T(128)S(1)} %pad_add_fusion.1.home, bf16[3,16,128,256]{3,2,1,0:T(8,128)(2,1)S(1)} %get-tuple-element.53.made, ...), custom_call_target="tpu_custom_call" | custom-call | flops 1073741824 | bytes 3145728 | tf_op jit(solution)/shard_map/pallas_call | solution.py:342
  93.4 2.0 %collective-permute-start.27 = (bf16[256,512]{1,0:T(8,128)(2,1)S(1)}, bf16[256,512]{1,0:T(8,128)(2,1)S(1)}, u32[]{:S(2)}, u32[]{:S(2)}) collective-permute-start(bf16[256,512]{1,0:T(8,128)(2,1)S(1)} %get-tuple-element.64), channel_id=1, source_target_pairs={{0,16},{16,0},{1,17},{17,1},{2,18},{18,2},{3,19},{19,3},{4,20},{20... | collective-permute-start | bytes 786440 | tf_op jit(solution)/shard_map/ppermute | solution.py:21
  95.4 1.5 %shard_map.86 = (f32[256,512]{1,0:T(8,128)S(1)}, bf16[256,512]{1,0:T(8,128)(2,1)S(1)}) custom-call(s32[4,64]{1,0:T(4,128)S(1)} %pad_add_fusion.table, s32[4]{0:T(128)S(1)} %and_select_fusion.turns, s32[3]{0:T(128)S(1)} %pad_add_fusion.1.home, bf16[16,256,256]{2,1,0:T(8,128)(2,1)S(1)} %get-tuple-element.60.rows_held, ...), custom_call_target="tpu_custom_call" | custom-call | flops 1207959552 | bytes 3145728 | tf_op jit(solution)/shard_map/pallas_call | solution.py:342
  96.8 2.2 %collective-permute-start.25 = (bf16[256,512]{1,0:T(8,128)(2,1)S(1)}, bf16[256,512]{1,0:T(8,128)(2,1)S(1)}, u32[]{:S(2)}, u32[]{:S(2)}) collective-permute-start(bf16[256,512]{1,0:T(8,128)(2,1)S(1)} %get-tuple-element.62), channel_id=1, source_target_pairs={{0,16},{16,0},{1,17},{17,1},{2,18},{18,2},{3,19},{19,3},{4,20},{20... | collective-permute-start | bytes 786440 | tf_op jit(solution)/shard_map/ppermute | solution.py:21
  99.0 1.2 shard_map.85
  100.2 2.5 %shard_map.84 = (f32[256,512]{1,0:T(8,128)S(1)}, bf16[256,512]{1,0:T(8,128)(2,1)S(1)}) custom-call(s32[4,64]{1,0:T(4,128)S(1)} %pad_add_fusion.table, s32[4]{0:T(128)S(1)} %and_select_fusion.turns, s32[3]{0:T(128)S(1)} %pad_add_fusion.1.home, bf16[3,16,128,256]{3,2,1,0:T(8,128)(2,1)S(1)} %get-tuple-element.53.made, ...), custom_call_target="tpu_custom_call" | custom-call | flops 1073741824 | bytes 3145728 | tf_op jit(solution)/shard_map/pallas_call | solution.py:342
  102.8 1.0 collective-permute-start.22
  103.8 1.1 collective-permute-start.21
  104.9 1.6 %collective-permute-start.28 = (bf16[256,512]{1,0:T(8,128)(2,1)S(1)}, bf16[256,512]{1,0:T(8,128)(2,1)S(1)}, u32[]{:S(2)}, u32[]{:S(2)}) collective-permute-start(bf16[256,512]{1,0:T(8,128)(2,1)S(1)} %add_convert_fusion.1), channel_id=1, source_target_pairs={{0,4},{1,5},{2,6},{3,7},{4,12},{5,13},{6,14},{7,15},{12,8},{13,9},... | collective-permute-start | bytes 786440 | tf_op jit(solution)/shard_map/ppermute | solution.py:221
  106.5 1.7 %collective-permute-done.25 = bf16[256,512]{1,0:T(8,128)(2,1)S(1)} collective-permute-done((bf16[256,512]{1,0:T(8,128)(2,1)S(1)}, bf16[256,512]{1,0:T(8,128)(2,1)S(1)}, u32[]{:S(2)}, u32[]{:S(2)}) %collective-permute-start.25) | collective-permute-done | bytes 262176 | tf_op jit(solution)/shard_map/ppermute | solution.py:21
  108.3 4.7 %collective-permute-start.26 = (bf16[256,512]{1,0:T(8,128)(2,1)S(1)}, bf16[256,512]{1,0:T(8,128)(2,1)S(1)}, u32[]{:S(2)}, u32[]{:S(2)}) collective-permute-start(bf16[256,512]{1,0:T(8,128)(2,1)S(1)} %add_convert_fusion.2), channel_id=1, source_target_pairs={{0,12},{1,13},{2,14},{3,15},{12,0},{13,1},{14,2},{15,3},{16,28},{1... | collective-permute-start | bytes 786440 | tf_op jit(solution)/shard_map/ppermute | solution.py:221
  113.1 0.8 collective-permute-done.22
  114.1 0.7 collective-permute-start.29
  115.2 2.4 %collective-permute-done.21 = bf16[256,512]{1,0:T(8,128)(2,1)S(1)} collective-permute-done((bf16[256,512]{1,0:T(8,128)(2,1)S(1)}, bf16[256,512]{1,0:T(8,128)(2,1)S(1)}, u32[]{:S(2)}, u32[]{:S(2)}) %collective-permute-start.21) | collective-permute-done | bytes 262176 | tf_op jit(solution)/shard_map/ppermute | solution.py:21
  117.7 3.1 %collective-permute-done.26.refs_2_ = bf16[256,512]{1,0:T(8,128)(2,1)S(1)} collective-permute-done((bf16[256,512]{1,0:T(8,128)(2,1)S(1)}, bf16[256,512]{1,0:T(8,128)(2,1)S(1)}, u32[]{:S(2)}, u32[]{:S(2)}) %collective-permute-start.26) | collective-permute-done | bytes 262176 | tf_op jit(solution)/shard_map/ppermute | solution.py:221
  120.8 2.7 %collective-permute-done.23.refs_1_ = bf16[256,512]{1,0:T(8,128)(2,1)S(1)} collective-permute-done((bf16[256,512]{1,0:T(8,128)(2,1)S(1)}, bf16[256,512]{1,0:T(8,128)(2,1)S(1)}, u32[]{:S(2)}, u32[]{:S(2)}) %collective-permute-start.23) | collective-permute-done | bytes 262176 | tf_op jit(solution)/shard_map/ppermute | solution.py:221
  123.5 1.0 finish.1
  (80 shorter events, 5.3 us)
Async XLA Ops:
  0.0 31.8 %copy-start = (bf16[12,64,1024]{2,1,0:T(8,128)(2,1)S(1)}, bf16[12,64,1024]{2,1,0:T(8,128)(2,1)}, u32[]{:S(2)}) copy-start(bf16[12,64,1024]{2,1,0:T(8,128)(2,1)} %refs_12_.1) | copy-start | bytes 4718596
  1.0 6.5 %collective-permute-start.1 = (bf16[128,512]{1,0:T(8,128)(2,1)S(1)}, bf16[128,512]{1,0:T(8,128)(2,1)S(1)}, u32[]{:S(2)}, u32[]{:S(2)}) collective-permute-start(bf16[128,512]{1,0:T(8,128)(2,1)S(1)} %constant_dynamic-slice_fusion), channel_id=1, source_target_pairs={{0,16},{16,0},{1,17},{17,1},{2,18},{18,2},{3,19},{19,3},{4,20},{20... | collective-permute-start | bytes 393224 | tf_op jit(solution)/shard_map/ppermute | solution.py:21
  7.6 1.0 copy-start.1
  8.5 72.9 %copy-start.2 = (bf16[256,512]{1,0:T(8,128)(2,1)S(1)}, bf16[256,512]{1,0:T(8,128)(2,1)}, u32[]{:S(2)}) copy-start(bf16[256,512]{1,0:T(8,128)(2,1)} %state.3) | copy-start | bytes 786436
  9.2 5.9 %collective-permute-start.2 = (bf16[144,256]{1,0:T(8,128)(2,1)S(1)}, bf16[144,256]{1,0:T(8,128)(2,1)S(1)}, u32[]{:S(2)}, u32[]{:S(2)}) collective-permute-start(bf16[144,256]{1,0:T(8,128)(2,1)S(1)} %get-tuple-element.48), channel_id=1, source_target_pairs={{0,4},{1,5},{2,6},{3,7},{4,0},{5,1},{6,2},{7,3},{8,12},{9,13},{10,... | collective-permute-start | bytes 221192 | tf_op jit(solution)/shard_map/ppermute | solution.py:221
  11.1 7.4 %collective-permute-start.3 = (bf16[144,256]{1,0:T(8,128)(2,1)S(1)}, bf16[144,256]{1,0:T(8,128)(2,1)S(1)}, u32[]{:S(2)}, u32[]{:S(2)}) collective-permute-start(bf16[144,256]{1,0:T(8,128)(2,1)S(1)} %get-tuple-element.49), channel_id=1, source_target_pairs={{0,8},{1,9},{2,10},{3,11},{4,12},{5,13},{6,14},{7,15},{8,0},{9,1},... | collective-permute-start | bytes 221192 | tf_op jit(solution)/shard_map/ppermute | solution.py:221
  13.7 6.3 %collective-permute-start.4 = (bf16[144,256]{1,0:T(8,128)(2,1)S(1)}, bf16[144,256]{1,0:T(8,128)(2,1)S(1)}, u32[]{:S(2)}, u32[]{:S(2)}) collective-permute-start(bf16[144,256]{1,0:T(8,128)(2,1)S(1)} %get-tuple-element.50), channel_id=1, source_target_pairs={{0,12},{1,13},{2,14},{3,15},{4,8},{5,9},{6,10},{7,11},{8,4},{9,5},... | collective-permute-start | bytes 221192 | tf_op jit(solution)/shard_map/ppermute | solution.py:221
  13.7 21.3 %collective-permute-start.14 = (bf16[16,128,128]{2,1,0:T(8,128)(2,1)}, bf16[16,128,128]{2,1,0:T(8,128)(2,1)}, u32[]{:S(2)}, u32[]{:S(2)}) collective-permute-start(bf16[16,128,128]{2,1,0:T(8,128)(2,1)} %bitcast.5.refs_8_), channel_id=1, source_target_pairs={{4,8},{5,9},{6,10},{7,11},{8,4},{9,5},{10,6},{11,7},{20,24},{21,25... | collective-permute-start | bytes 1572872 | tf_op jit(solution)/shard_map/ppermute | solution.py:221
  19.9 11.9 %copy-start.4 = (bf16[4,128,256]{2,1,0:T(8,128)(2,1)}, bf16[4,128,256]{2,1,0:T(8,128)(2,1)S(1)}, u32[]{:S(2)}) copy-start(bf16[4,128,256]{2,1,0:T(8,128)(2,1)S(1)} %get-tuple-element.52.refs_0_) | copy-start | bytes 786436
  19.9 6.4 %collective-permute-start.5 = (bf16[4,128,256]{2,1,0:T(8,128)(2,1)S(1)}, bf16[4,128,256]{2,1,0:T(8,128)(2,1)S(1)}, u32[]{:S(2)}, u32[]{:S(2)}) collective-permute-start(bf16[4,128,256]{2,1,0:T(8,128)(2,1)S(1)} %get-tuple-element.52.refs_0_), channel_id=1, source_target_pairs={{0,2},{1,3},{2,0},{3,1},{4,6},{5,7},{6,4},{7,5},{8,10},{9,11},{10,... | collective-permute-start | bytes 786440 | tf_op jit(solution)/shard_map/ppermute | solution.py:21
  21.5 10.3 %collective-permute-start.6 = (bf16[4,128,256]{2,1,0:T(8,128)(2,1)S(1)}, bf16[4,128,256]{2,1,0:T(8,128)(2,1)S(1)}, u32[]{:S(2)}, u32[]{:S(2)}) collective-permute-start(bf16[4,128,256]{2,1,0:T(8,128)(2,1)S(1)} %get-tuple-element.52.refs_0_), channel_id=1, source_target_pairs={{0,16},{16,0},{1,17},{17,1},{2,18},{18,2},{3,19},{19,3},{4,20},{20... | collective-permute-start | bytes 786440 | tf_op jit(solution)/shard_map/ppermute | solution.py:21
  23.0 9.7 %collective-permute-start.8 = (bf16[4,128,256]{2,1,0:T(8,128)(2,1)S(1)}, bf16[4,128,256]{2,1,0:T(8,128)(2,1)S(1)}, u32[]{:S(2)}, u32[]{:S(2)}) collective-permute-start(bf16[4,128,256]{2,1,0:T(8,128)(2,1)S(1)} %get-tuple-element.52.refs_0_), channel_id=1, source_target_pairs={{0,1},{1,0},{2,3},{3,2},{4,5},{5,4},{6,7},{7,6},{8,9},{9,8},{10,11... | collective-permute-start | bytes 786440 | tf_op jit(solution)/shard_map/ppermute | solution.py:21
  25.2 37.6 %collective-permute-start.17 = (bf16[7,64,1024]{2,1,0:T(8,128)(2,1)}, bf16[7,64,1024]{2,1,0:T(8,128)(2,1)}, u32[]{:S(2)}, u32[]{:S(2)}) collective-permute-start(bf16[7,64,1024]{2,1,0:T(8,128)(2,1)} %slice.65), channel_id=1, source_target_pairs={{0,2},{1,3},{2,0},{3,1},{4,6},{5,7},{6,4},{7,5},{8,10},{9,11},{10,... | collective-permute-start | bytes 2752520 | tf_op jit(solution)/shard_map/ppermute | solution.py:21
  26.4 6.4 %copy-start.6 = (bf16[4,128,256]{2,1,0:T(8,128)(2,1)}, bf16[4,128,256]{2,1,0:T(8,128)(2,1)S(1)}, u32[]{:S(2)}) copy-start(bf16[4,128,256]{2,1,0:T(8,128)(2,1)S(1)} %collective-permute-done.5.refs_1_) | copy-start | bytes 786436
  26.4 17.2 %collective-permute-start.13 = (bf16[16,128,128]{2,1,0:T(8,128)(2,1)}, bf16[16,128,128]{2,1,0:T(8,128)(2,1)}, u32[]{:S(2)}, u32[]{:S(2)}) collective-permute-start(bf16[16,128,128]{2,1,0:T(8,128)(2,1)} %bitcast.5.refs_8_), channel_id=1, source_target_pairs={{0,8},{1,9},{2,10},{3,11},{12,4},{13,5},{14,6},{15,7},{16,24},{17,... | collective-permute-start | bytes 1572872 | tf_op jit(solution)/shard_map/ppermute | solution.py:221
  31.8 3.2 %copy-start.8 = (bf16[4,128,256]{2,1,0:T(8,128)(2,1)}, bf16[4,128,256]{2,1,0:T(8,128)(2,1)S(1)}, u32[]{:S(2)}) copy-start(bf16[4,128,256]{2,1,0:T(8,128)(2,1)S(1)} %collective-permute-done.6.refs_2_) | copy-start | bytes 786436
  31.8 50.2 %collective-permute-start.16 = (bf16[12,64,1024]{2,1,0:T(8,128)(2,1)}, bf16[12,64,1024]{2,1,0:T(8,128)(2,1)S(1)}, u32[]{:S(2)}, u32[]{:S(2)}) collective-permute-start(bf16[12,64,1024]{2,1,0:T(8,128)(2,1)} %refs_12_.1), channel_id=1, source_target_pairs={{0,1},{1,0},{2,3},{3,2},{4,5},{5,4},{6,7},{7,6},{8,9},{9,8},{10,11... | collective-permute-start | bytes 4718600 | tf_op jit(solution)/shard_map/ppermute | solution.py:21
  32.8 0.7 copy-start.10
  33.5 28.9 %collective-permute-start.18 = (bf16[5,64,1024]{2,1,0:T(8,128)(2,1)}, bf16[5,64,1024]{2,1,0:T(8,128)(2,1)}, u32[]{:S(2)}, u32[]{:S(2)}) collective-permute-start(bf16[5,64,1024]{2,1,0:T(8,128)(2,1)} %slice.66), channel_id=1, source_target_pairs={{0,2},{1,3},{2,0},{3,1},{4,6},{5,7},{6,4},{7,5},{8,10},{9,11},{10,... | collective-permute-start | bytes 1966088 | tf_op jit(solution)/shard_map/ppermute | solution.py:21
  35.0 18.4 %collective-permute-start.12 = (bf16[16,128,128]{2,1,0:T(8,128)(2,1)}, bf16[16,128,128]{2,1,0:T(8,128)(2,1)}, u32[]{:S(2)}, u32[]{:S(2)}) collective-permute-start(bf16[16,128,128]{2,1,0:T(8,128)(2,1)} %bitcast.5.refs_8_), channel_id=1, source_target_pairs={{0,4},{1,5},{2,6},{3,7},{4,0},{5,1},{6,2},{7,3},{8,12},{9,13},{10,... | collective-permute-start | bytes 1572872 | tf_op jit(solution)/shard_map/ppermute | solution.py:221
  43.6 18.7 %collective-permute-start.7 = (bf16[4,128,256]{2,1,0:T(8,128)(2,1)}, bf16[4,128,256]{2,1,0:T(8,128)(2,1)}, u32[]{:S(2)}, u32[]{:S(2)}) collective-permute-start(bf16[4,128,256]{2,1,0:T(8,128)(2,1)} %copy-done.6), channel_id=1, source_target_pairs={{0,16},{16,0},{1,17},{17,1},{2,18},{18,2},{3,19},{19,3},{4,20},{20... | collective-permute-start | bytes 786440 | tf_op jit(solution)/shard_map/ppermute | solution.py:21
  53.4 9.6 %collective-permute-start.10 = (bf16[4,128,256]{2,1,0:T(8,128)(2,1)}, bf16[4,128,256]{2,1,0:T(8,128)(2,1)S(1)}, u32[]{:S(2)}, u32[]{:S(2)}) collective-permute-start(bf16[4,128,256]{2,1,0:T(8,128)(2,1)} %copy-done.8), channel_id=1, source_target_pairs={{0,1},{1,0},{2,3},{3,2},{4,5},{5,4},{6,7},{7,6},{8,9},{9,8},{10,11... | collective-permute-start | bytes 786440 | tf_op jit(solution)/shard_map/ppermute | solution.py:21
  62.3 2.2 %collective-permute-start.9 = (bf16[4,128,256]{2,1,0:T(8,128)(2,1)}, bf16[4,128,256]{2,1,0:T(8,128)(2,1)}, u32[]{:S(2)}, u32[]{:S(2)}) collective-permute-start(bf16[4,128,256]{2,1,0:T(8,128)(2,1)} %copy-done.6), channel_id=1, source_target_pairs={{0,1},{1,0},{2,3},{3,2},{4,5},{5,4},{6,7},{7,6},{8,9},{9,8},{10,11... | collective-permute-start | bytes 786440 | tf_op jit(solution)/shard_map/ppermute | solution.py:21
  62.3 3.5 %collective-permute-start.11 = (bf16[4,128,256]{2,1,0:T(8,128)(2,1)}, bf16[4,128,256]{2,1,0:T(8,128)(2,1)}, u32[]{:S(2)}, u32[]{:S(2)}) collective-permute-start(bf16[4,128,256]{2,1,0:T(8,128)(2,1)} %collective-permute-done.7.refs_3_), channel_id=1, source_target_pairs={{0,1},{1,0},{2,3},{3,2},{4,5},{5,4},{6,7},{7,6},{8,9},{9,8},{10,11... | collective-permute-start | bytes 786440 | tf_op jit(solution)/shard_map/ppermute | solution.py:21
  62.8 27.4 %collective-permute-start.19 = (bf16[7,64,1024]{2,1,0:T(8,128)(2,1)}, bf16[7,64,1024]{2,1,0:T(8,128)(2,1)}, u32[]{:S(2)}, u32[]{:S(2)}) collective-permute-start(bf16[7,64,1024]{2,1,0:T(8,128)(2,1)} %collective-permute-done.17.refs_0_), channel_id=1, source_target_pairs={{0,1},{1,0},{2,3},{3,2},{4,5},{5,4},{6,7},{7,6},{8,9},{9,8},{10,11... | collective-permute-start | bytes 2752520 | tf_op jit(solution)/shard_map/ppermute | solution.py:21
  63.0 0.7 copy-start.12
  63.7 26.6 %collective-permute-start.20 = (bf16[5,64,1024]{2,1,0:T(8,128)(2,1)}, bf16[5,64,1024]{2,1,0:T(8,128)(2,1)}, u32[]{:S(2)}, u32[]{:S(2)}) collective-permute-start(bf16[5,64,1024]{2,1,0:T(8,128)(2,1)} %collective-permute-done.18.refs_1_), channel_id=1, source_target_pairs={{0,1},{1,0},{2,3},{3,2},{4,5},{5,4},{6,7},{7,6},{8,9},{9,8},{10,11... | collective-permute-start | bytes 1966088 | tf_op jit(solution)/shard_map/ppermute | solution.py:21
  64.5 16.9 %collective-permute-start.15 = (bf16[16,128,128]{2,1,0:T(8,128)(2,1)}, bf16[16,128,128]{2,1,0:T(8,128)(2,1)S(1)}, u32[]{:S(2)}, u32[]{:S(2)}) collective-permute-start(bf16[16,128,128]{2,1,0:T(8,128)(2,1)} %collective-permute-done.14.refs_0_), channel_id=1, source_target_pairs={{8,12},{9,13},{10,14},{11,15},{4,0},{5,1},{6,2},{7,3},{24,28},{25,... | collective-permute-start | bytes 1572872 | tf_op jit(solution)/shard_map/ppermute | solution.py:221
  65.8 29.5 %collective-permute-start.24 = (bf16[16,128,128]{2,1,0:T(8,128)(2,1)}, bf16[16,128,128]{2,1,0:T(8,128)(2,1)S(1)}, u32[]{:S(2)}, u32[]{:S(2)}) collective-permute-start(bf16[16,128,128]{2,1,0:T(8,128)(2,1)} %collective-permute-done.13.refs_10_), channel_id=1, source_target_pairs={{8,12},{9,13},{10,14},{11,15},{4,0},{5,1},{6,2},{7,3},{24,28},{25,... | collective-permute-start | bytes 1572872 | tf_op jit(solution)/shard_map/ppermute | solution.py:221
  81.4 33.3 %collective-permute-start = (bf16[256,512]{1,0:T(8,128)(2,1)S(1)}, bf16[256,512]{1,0:T(8,128)(2,1)S(1)}, u32[]{:S(2)}, u32[]{:S(2)}) collective-permute-start(bf16[256,512]{1,0:T(8,128)(2,1)S(1)} %copy-done.2), channel_id=1, source_target_pairs={{0,16},{16,0},{1,17},{17,1},{2,18},{18,2},{3,19},{19,3},{4,20},{20... | collective-permute-start | bytes 786440 | tf_op jit(solution)/shard_map/ppermute | solution.py:21
  82.0 1.0 copy-start.5
  82.9 0.9 copy-start.7
  83.9 0.9 copy-start.9
  84.8 0.9 copy-start.11
  85.8 0.9 copy-start.13
  93.4 11.5 %collective-permute-start.27 = (bf16[256,512]{1,0:T(8,128)(2,1)S(1)}, bf16[256,512]{1,0:T(8,128)(2,1)S(1)}, u32[]{:S(2)}, u32[]{:S(2)}) collective-permute-start(bf16[256,512]{1,0:T(8,128)(2,1)S(1)} %get-tuple-element.64), channel_id=1, source_target_pairs={{0,16},{16,0},{1,17},{17,1},{2,18},{18,2},{3,19},{19,3},{4,20},{20... | collective-permute-start | bytes 786440 | tf_op jit(solution)/shard_map/ppermute | solution.py:21
  96.8 11.4 %collective-permute-start.25 = (bf16[256,512]{1,0:T(8,128)(2,1)S(1)}, bf16[256,512]{1,0:T(8,128)(2,1)S(1)}, u32[]{:S(2)}, u32[]{:S(2)}) collective-permute-start(bf16[256,512]{1,0:T(8,128)(2,1)S(1)} %get-tuple-element.62), channel_id=1, source_target_pairs={{0,16},{16,0},{1,17},{17,1},{2,18},{18,2},{3,19},{19,3},{4,20},{20... | collective-permute-start | bytes 786440 | tf_op jit(solution)/shard_map/ppermute | solution.py:21
  102.7 12.0 %copy-start.3 = (bf16[1024,512]{1,0:T(8,128)(2,1)S(1)}, bf16[1024,512]{1,0:T(8,128)(2,1)}, u32[]{:S(2)}) copy-start(bf16[1024,512]{1,0:T(8,128)(2,1)} %weight.1) | copy-start | bytes 3145732
  102.8 12.0 %copy-start.15 = (f32[512]{0:T(512)S(1)}, f32[512]{0:T(512)}, u32[]{:S(2)}) copy-start(f32[512]{0:T(512)} %param.15) | copy-start | bytes 6148
  102.8 11.1 %collective-permute-start.22 = (bf16[256,512]{1,0:T(8,128)(2,1)S(1)}, bf16[256,512]{1,0:T(8,128)(2,1)S(1)}, u32[]{:S(2)}, u32[]{:S(2)}) collective-permute-start(bf16[256,512]{1,0:T(8,128)(2,1)S(1)} %get-tuple-element.59), channel_id=1, source_target_pairs={{0,16},{16,0},{1,17},{17,1},{2,18},{18,2},{3,19},{19,3},{4,20},{20... | collective-permute-start | bytes 786440 | tf_op jit(solution)/shard_map/ppermute | solution.py:21
  103.8 13.9 %collective-permute-start.21 = (bf16[256,512]{1,0:T(8,128)(2,1)S(1)}, bf16[256,512]{1,0:T(8,128)(2,1)S(1)}, u32[]{:S(2)}, u32[]{:S(2)}) collective-permute-start(bf16[256,512]{1,0:T(8,128)(2,1)S(1)} %get-tuple-element.57), channel_id=1, source_target_pairs={{0,16},{16,0},{1,17},{17,1},{2,18},{18,2},{3,19},{19,3},{4,20},{20... | collective-permute-start | bytes 786440 | tf_op jit(solution)/shard_map/ppermute | solution.py:21
  104.9 9.1 %collective-permute-start.28 = (bf16[256,512]{1,0:T(8,128)(2,1)S(1)}, bf16[256,512]{1,0:T(8,128)(2,1)S(1)}, u32[]{:S(2)}, u32[]{:S(2)}) collective-permute-start(bf16[256,512]{1,0:T(8,128)(2,1)S(1)} %add_convert_fusion.1), channel_id=1, source_target_pairs={{0,4},{1,5},{2,6},{3,7},{4,12},{5,13},{6,14},{7,15},{12,8},{13,9},... | collective-permute-start | bytes 786440 | tf_op jit(solution)/shard_map/ppermute | solution.py:221
  108.2 15.3 %copy-start.14 = (f32[512]{0:T(512)S(1)}, f32[512]{0:T(512)}, u32[]{:S(2)}) copy-start(f32[512]{0:T(512)} %param.16) | copy-start | bytes 6148
  108.3 12.5 %collective-permute-start.26 = (bf16[256,512]{1,0:T(8,128)(2,1)S(1)}, bf16[256,512]{1,0:T(8,128)(2,1)S(1)}, u32[]{:S(2)}, u32[]{:S(2)}) collective-permute-start(bf16[256,512]{1,0:T(8,128)(2,1)S(1)} %add_convert_fusion.2), channel_id=1, source_target_pairs={{0,12},{1,13},{2,14},{3,15},{12,0},{13,1},{14,2},{15,3},{16,28},{1... | collective-permute-start | bytes 786440 | tf_op jit(solution)/shard_map/ppermute | solution.py:221
  113.9 9.6 %collective-permute-start.23 = (bf16[256,512]{1,0:T(8,128)(2,1)S(1)}, bf16[256,512]{1,0:T(8,128)(2,1)S(1)}, u32[]{:S(2)}, u32[]{:S(2)}) collective-permute-start(bf16[256,512]{1,0:T(8,128)(2,1)S(1)} %add_convert_fusion.3), channel_id=1, source_target_pairs={{0,4},{1,5},{2,6},{3,7},{4,0},{5,1},{6,2},{7,3},{8,12},{9,13},{10,... | collective-permute-start | bytes 786440 | tf_op jit(solution)/shard_map/ppermute | solution.py:221
  114.1 9.4 %collective-permute-start.29 = (bf16[256,512]{1,0:T(8,128)(2,1)S(1)}, bf16[256,512]{1,0:T(8,128)(2,1)S(1)}, u32[]{:S(2)}, u32[]{:S(2)}) collective-permute-start(bf16[256,512]{1,0:T(8,128)(2,1)S(1)} %add_convert_fusion), channel_id=1, source_target_pairs={{4,8},{5,9},{6,10},{7,11},{8,4},{9,5},{10,6},{11,7},{20,24},{21,25... | collective-permute-start | bytes 786440 | tf_op jit(solution)/shard_map/ppermute | solution.py:221

commit v4 on v3

--- a/solution.py
+++ b/solution.py
@@ -13,16 +13,19 @@
 ANY = pl.BlockSpec(memory_space=pl.ANY)
 SMEM = pl.BlockSpec(memory_space=pltpu.SMEM)
 VMEM = pl.BlockSpec(memory_space=pltpu.VMEM)
+HBM = pl.BlockSpec(memory_space=pltpu.HBM)
 GROUP = 4
 NOTE_ROWS = 16
 
+HOME = 16
+
 
 def swap(value, axis, size, bit):
     return lax.ppermute(value, axis, [(i, i ^ bit) for i in range(size)])
 
 
-def pack_kernel(n_rel, where, note, state, *refs):
-    others, outs = refs[:n_rel - 1], refs[n_rel - 1:]
+def pack_kernel(n_rel, where, note, *refs):
+    halves, outs = refs[:n_rel], refs[n_rel:]
     rows, width = outs[0].shape[0] - NOTE_ROWS, outs[0].shape[1]
     first = pl.multiple_of(where[2, 0], rows)
     for j, out in enumerate(outs):
@@ -31,10 +34,7 @@
 
             @pl.when(where[0, j] == r)
             def _(r=r, out=out, start=start):
-                if r:
-                    out[:rows] = others[r - 1][:, pl.ds(start, width)]
-                else:
-                    out[:rows] = state[pl.ds(first, rows), pl.ds(start, width)]
+                out[:rows] = halves[r][pl.ds(first, rows), pl.ds(start, width)]
 
         out[rows:] = note[...]
 
@@ -136,59 +136,59 @@
             outs[r][t * tile_rows:(t + 1) * tile_rows] = acc[t, :, pl.ds(start, own)].astype(outs[r].dtype)
 
 
-def early_kernel(members, places, way_counts, n_weights, table, turns, home, *refs):
+def early_kernel(members, places, way_counts, n_weights, table, *refs):
     states, tiles, weights, rest = take(refs, len(places), sum(way_counts), n_weights)
     made, held, rows_held, lists, state_sem, tile_sem, weight_sem = rest
     slots = lists.shape[1]
     chunks, rows = states[0].shape[0], states[0].shape[1]
     loads = []
     for n, ((i, r), ref) in enumerate(zip(places, states)):
-        first = pl.multiple_of(lax.bitwise_xor(home[1], r) * rows, rows)
+        first = pl.multiple_of(lax.bitwise_xor(table[4, HOME + 1], r) * rows, rows)
         to = rows_held.at[pl.ds(i * chunks, chunks), pl.ds(first, rows), :]
         loads.append(pltpu.make_async_copy(ref, to, state_sem.at[n]))
         loads[-1].start()
-    tile_loads = start_tiles(way_counts, home[2], tiles, lists, tile_sem)
-    weight_loads = start_weights(members, home[0], weights, held, weight_sem)
+    tile_loads = start_tiles(way_counts, table[4, HOME + 2], tiles, lists, tile_sem)
+    weight_loads = start_weights(members, table[4, HOME], weights, held, weight_sem)
     for load in loads:
         load.wait()
-    swapped = home[0] >= members // 2
+    swapped = table[4, HOME] >= members // 2
     for j, load in enumerate(tile_loads):
         load.wait()
-        multiply_tiles(turns[j], table, j * slots, swapped, lists.at[j], rows_held, made.at[j])
+        multiply_tiles(table[4, j], table, j * slots, swapped, lists.at[j], rows_held, made.at[j])
     for load in weight_loads:
         load.wait()
 
 
-def first_kernel(members, j, n_rel, n_weights, table, turns, home, made, own, *refs):
+def first_kernel(members, j, n_rel, n_weights, table, made, own, *refs):
     weights, outs, rest = take(refs, n_weights, n_rel)
     other, acc, weight_sem = rest
     slots = made.shape[1]
-    for load in start_weights(members, home[0], weights, other, weight_sem):
+    for load in start_weights(members, table[4, HOME], weights, other, weight_sem):
         load.wait()
-    add_messages(turns[j], table, j * slots, made.at[j], own, other, acc)
-    put_messages(n_rel, home[1], acc, outs)
-
-
-def late_kernel(members, way_counts, js, n_rel, table, turns, home, rows_held, own, other, *refs):
+    add_messages(table[4, j], table, j * slots, made.at[j], own, other, acc)
+    put_messages(n_rel, table[4, HOME + 1], acc, outs)
+
+
+def late_kernel(members, way_counts, js, n_rel, table, rows_held, own, other, *refs):
     tiles, outs, rest = take(refs, sum(way_counts), len(js) * n_rel)
     lists, made, acc, tile_sem = rest
     slots = lists.shape[1]
-    loads = start_tiles(way_counts, home[2], tiles, lists, tile_sem)
+    loads = start_tiles(way_counts, table[4, HOME + 2], tiles, lists, tile_sem)
     for g, j in enumerate(js):
         loads[g].wait()
         multiply_tiles(
-            turns[j], table, j * slots, home[0] >= members // 2, lists.at[g], rows_held, made.at[g]
+            table[4, j], table, j * slots, table[4, HOME] >= members // 2, lists.at[g], rows_held, made.at[g]
         )
-        add_messages(turns[j], table, j * slots, made.at[g], own, other, acc)
-        put_messages(n_rel, home[1], acc, outs[g * n_rel:(g + 1) * n_rel])
-
-
-def near_kernel(js, n_rel, table, turns, home, made, own, other, *refs):
+        add_messages(table[4, j], table, j * slots, made.at[g], own, other, acc)
+        put_messages(n_rel, table[4, HOME + 1], acc, outs[g * n_rel:(g + 1) * n_rel])
+
+
+def near_kernel(js, n_rel, table, made, own, other, *refs):
     outs, acc = refs[:-1], refs[-1]
     slots = made.shape[1]
     for g, j in enumerate(js):
-        add_messages(turns[j], table, j * slots, made.at[j], own, other, acc)
-        put_messages(n_rel, home[1], acc, outs[g * n_rel:(g + 1) * n_rel])
+        add_messages(table[4, j], table, j * slots, made.at[j], own, other, acc)
+        put_messages(n_rel, table[4, HOME + 1], acc, outs[g * n_rel:(g + 1) * n_rel])
 
 
 def finish_kernel(used, state, gate_open, bias, *refs):
@@ -224,10 +224,6 @@
         return along(value, [(q, q ^ j) for q in range(chunks)])
 
     rows = ent_dev // n_rel
-    others = []
-    for r in range(1, n_rel):
-        asked_rows = lax.dynamic_slice_in_dim(state, lax.bitwise_xor(rel, r) * rows, rows, 0)
-        others.append(swap(asked_rows, "rel", n_rel, r))
     halves = [state] + [swap(state, "rel", n_rel, r) for r in range(1, n_rel)]
 
     values = tile_values[0]
@@ -258,7 +254,7 @@
         out_specs=[VMEM] * chunks,
         compiler_params=pltpu.CompilerParams(vmem_limit_bytes=8 << 20),
         name="pack",
-    )(where, note, state, *others)
+    )(where, note, *halves)
     moved = [partner(pieces[j], j) for j in range(1, chunks)]
     own, notes = pl.pallas_call(
         functools.partial(stack_kernel, chunks),
@@ -278,15 +274,19 @@
     owner = source // per_tile
     place = lax.bitwise_xor(owner % members, member) * chunks
     place = place + lax.bitwise_xor(part, owner // members)
+    edge = jnp.logical_or(part == 0, part == chunks - 1).astype(jnp.int32)
+    turns = (counts + GROUP - 1) // GROUP
+    last = jnp.zeros((chunks * slots,), jnp.int32).at[:chunks].set(turns)
+    last = last.at[HOME:HOME + 3].set(jnp.stack([member, rel, edge]))
     table = jnp.stack([
         jnp.where(live, place, 0).reshape(-1),
         jnp.where(live, target, per_tile).reshape(-1),
         jnp.where(live, relation, 0).reshape(-1),
         (source % per_tile * tile_rows).reshape(-1),
+        last,
     ])
-    turns = (counts + GROUP - 1) // GROUP
-
-    cut = max(1, rel_dev * 7 // 12)
+
+    cut = max(1, rel_dev * 2 // 3)
     parts = (rel_weight[:cut], rel_weight[cut:])
     bits = [1 << b for b in reversed(range(members.bit_length() - 1))]
     rel_bits = [1 << b for b in reversed(range(n_rel.bit_length() - 1))]
@@ -319,8 +319,6 @@
     weights = [weights[order.index(i)] for i in range(members)]
     own_weights = [v for held in weights[:members // 2] for v in held]
     other_weights = [v for held in weights[members // 2:] for v in held]
-    edge = jnp.logical_or(part == 0, part == chunks - 1).astype(jnp.int32)
-    home = jnp.stack([member, rel, edge])
 
     gate_open = pl.pallas_call(
         functools.partial(gate_kernel, n_rel),
@@ -342,14 +340,14 @@
         return pl.pallas_call(
             body,
             out_shape=out_shape,
-            in_specs=[SMEM] * 3 + in_specs,
+            in_specs=[SMEM] + in_specs,
             out_specs=[VMEM] * len(out_shape),
             scratch_shapes=scratch,
             cost_estimate=pl.CostEstimate(
                 flops=flops, bytes_accessed=rel_dev * width * features, transcendentals=0
             ),
             compiler_params=pltpu.CompilerParams(vmem_limit_bytes=16 << 20),
-        )(table, turns, home, *operands)
+        )(table, *operands)
 
     def message_shapes(count):
         shape = (ent_dev, own_features)
@@ -361,7 +359,7 @@
     made, own_half, rows_held = call(
         functools.partial(early_kernel, members, tuple(places), early_ways, len(own_weights)),
         [*states, *flat, *own_weights],
-        [ANY] * (len(states) + len(flat) + len(own_weights)),
+        [HBM if v is values or v is rel_weight else ANY for v in [*states, *flat, *own_weights]],
         [
             products,
             jax.ShapeDtypeStruct(half_shape, BF16),

time: 125 us -> 126 us (level)
  waiting for transfers between devices: 57.8 us -> 51 us
  local copies, waits for them, and re-layouts: 12 us -> 15.5 us
  starting transfers between devices: 38.5 us -> 41.3 us
  Pallas kernels: 13.9 us -> 15.6 us
    ppermute x12, waiting for transfers between devices: 41.6 us -> 28.5 us  [along(): return lax.ppermute(value, 'ent', perm)]
    ppermute x18 -> x17, waiting for transfers between devices: 16.2 us -> 22.5 us  [swap(): return lax.ppermute(value, axis, [(i, i ^ bit) for i in range(size)])]
    ppermute x12, starting transfers between devices: 21 us -> 25.8 us  [along(): return lax.ppermute(value, 'ent', perm)]
    unnamed x33 -> x35, local copies, waits for them, and re-layouts: 7.16 us -> 10.5 us
    ppermute x18 -> x17, starting transfers between devices: 17.5 us -> 15.5 us  [swap(): return lax.ppermute(value, axis, [(i, i ^ bit) for i in range(size)])]
  transfers between devices with their start and end apart: 30 -> 29, of which waited for: 13 -> 14; matrix products, arithmetic and copies ran while one was open for 4% -> 5% of each run, Pallas kernels for 10% -> 12%
where the time goes in v4:
time: 126 us
  waiting for transfers between devices  51 us (40%)
  starting transfers between devices  41.3 us (33%)
  Pallas kernels  15.6 us (12%)
  local copies, waits for them, and re-layouts  15.5 us (12%)
  other arithmetic  1.33 us (1%)
    ppermute x12, waiting for transfers between devices, along(): return lax.ppermute(value, 'ent', perm)  28.5 us
    ppermute x12, starting transfers between devices, along(): return lax.ppermute(value, 'ent', perm)  25.8 us
    ppermute x17, waiting for transfers between devices, swap(): return lax.ppermute(value, axis, [(i, i ^ bit) for i in range(size)])  22.5 us
    ppermute x17, starting transfers between devices, swap(): return lax.ppermute(value, axis, [(i, i ^ bit) for i in range(size)])  15.5 us
    pallas_call x5, Pallas kernels, call(): pl.pallas_call(body, out_shape=out_shape, in_specs=[SMEM] + in_specs, out...  12.8 us
    unnamed x35, local copies, waits for them, and re-layouts  10.5 us
    slice x2, local copies, waits for them, and re-layouts, shards(): parts = (rel_weight[:cut], rel_weight[cut:])  4.15 us
  transfers between devices with their start and end apart: 29, of which 14 were waited for; matrix products, arithmetic and copies ran while one was open for 5% of the time, Pallas kernels for 12%

profile of v4, /device:TPU:0, one launch (start us, length us, event | category | flops | bytes accessed | tf_op | source)
XLA Modules:
  0.0 125.8 jit_solution(13112843432034018901)
XLA Ops:
  0.0 1.6 %collective-permute-start.13 = (bf16[16,128,128]{2,1,0:T(8,128)(2,1)}, bf16[16,128,128]{2,1,0:T(8,128)(2,1)}, u32[]{:S(2)}, u32[]{:S(2)}) collective-permute-start(bf16[16,128,128]{2,1,0:T(8,128)(2,1)} %bitcast.14), channel_id=1, source_target_pairs={{4,8},{5,9},{6,10},{7,11},{8,4},{9,5},{10,6},{11,7},{20,24},{21,25... | collective-permute-start | bytes 1572872 | tf_op jit(solution)/shard_map/ppermute | solution.py:221
  1.6 7.7 %collective-permute-start.12 = (bf16[16,128,128]{2,1,0:T(8,128)(2,1)}, bf16[16,128,128]{2,1,0:T(8,128)(2,1)}, u32[]{:S(2)}, u32[]{:S(2)}) collective-permute-start(bf16[16,128,128]{2,1,0:T(8,128)(2,1)} %bitcast.15), channel_id=1, source_target_pairs={{0,8},{1,9},{2,10},{3,11},{12,4},{13,5},{14,6},{15,7},{16,24},{17,... | collective-permute-start | bytes 1572872 | tf_op jit(solution)/shard_map/ppermute | solution.py:221
  9.3 1.5 %collective-permute-start = (bf16[256,512]{1,0:T(8,128)(2,1)}, bf16[256,512]{1,0:T(8,128)(2,1)S(1)}, u32[]{:S(2)}, u32[]{:S(2)}) collective-permute-start(bf16[256,512]{1,0:T(8,128)(2,1)} %state.1), channel_id=1, source_target_pairs={{0,16},{16,0},{1,17},{17,1},{2,18},{18,2},{3,19},{19,3},{4,20},{20... | collective-permute-start | bytes 786440 | tf_op jit(solution)/shard_map/ppermute | solution.py:24
  10.8 2.3 %slice.88 = bf16[8,64,1024]{2,1,0:T(8,128)(2,1)} slice(bf16[12,64,1024]{2,1,0:T(8,128)(2,1)} %refs_12_.1), slice={[0:8], [0:64], [0:1024]} | slice | bytes 2097152 | tf_op jit(solution)/shard_map/slice | solution.py:290
  13.1 1.5 %collective-permute-start.16 = (bf16[8,64,1024]{2,1,0:T(8,128)(2,1)}, bf16[8,64,1024]{2,1,0:T(8,128)(2,1)}, u32[]{:S(2)}, u32[]{:S(2)}) collective-permute-start(bf16[8,64,1024]{2,1,0:T(8,128)(2,1)} %slice.88), channel_id=1, source_target_pairs={{0,2},{1,3},{2,0},{3,1},{4,6},{5,7},{6,4},{7,5},{8,10},{9,11},{10,... | collective-permute-start | bytes 3145736 | tf_op jit(solution)/shard_map/ppermute | solution.py:24
  16.2 0.8 collective-permute-done.refs_1_
  17.0 0.9 copy-done.1
  18.7 3.0 %collective-permute-start.2 = (bf16[144,256]{1,0:T(8,128)(2,1)S(1)}, bf16[144,256]{1,0:T(8,128)(2,1)S(1)}, u32[]{:S(2)}, u32[]{:S(2)}) collective-permute-start(bf16[144,256]{1,0:T(8,128)(2,1)S(1)} %get-tuple-element.73), channel_id=1, source_target_pairs={{0,8},{1,9},{2,10},{3,11},{4,12},{5,13},{6,14},{7,15},{8,0},{9,1},... | collective-permute-start | bytes 221192 | tf_op jit(solution)/shard_map/ppermute | solution.py:221
  21.7 1.3 %collective-permute-done.1.refs_1_ = bf16[144,256]{1,0:T(8,128)(2,1)S(1)} collective-permute-done((bf16[144,256]{1,0:T(8,128)(2,1)S(1)}, bf16[144,256]{1,0:T(8,128)(2,1)S(1)}, u32[]{:S(2)}, u32[]{:S(2)}) %collective-permute-start.1) | collective-permute-done | bytes 73760 | tf_op jit(solution)/shard_map/ppermute | solution.py:221
  23.0 1.5 %collective-permute-start.11 = (bf16[16,128,128]{2,1,0:T(8,128)(2,1)}, bf16[16,128,128]{2,1,0:T(8,128)(2,1)}, u32[]{:S(2)}, u32[]{:S(2)}) collective-permute-start(bf16[16,128,128]{2,1,0:T(8,128)(2,1)} %bitcast.16), channel_id=1, source_target_pairs={{0,4},{1,5},{2,6},{3,7},{4,0},{5,1},{6,2},{7,3},{8,12},{9,13},{10,... | collective-permute-start | bytes 1572872 | tf_op jit(solution)/shard_map/ppermute | solution.py:221
  24.5 8.4 %collective-permute-done.2.refs_2_ = bf16[144,256]{1,0:T(8,128)(2,1)S(1)} collective-permute-done((bf16[144,256]{1,0:T(8,128)(2,1)S(1)}, bf16[144,256]{1,0:T(8,128)(2,1)S(1)}, u32[]{:S(2)}, u32[]{:S(2)}) %collective-permute-start.2) | collective-permute-done | bytes 73760 | tf_op jit(solution)/shard_map/ppermute | solution.py:221
  32.9 2.8 %collective-permute-start.3 = (bf16[144,256]{1,0:T(8,128)(2,1)S(1)}, bf16[144,256]{1,0:T(8,128)(2,1)S(1)}, u32[]{:S(2)}, u32[]{:S(2)}) collective-permute-start(bf16[144,256]{1,0:T(8,128)(2,1)S(1)} %get-tuple-element.74), channel_id=1, source_target_pairs={{0,12},{1,13},{2,14},{3,15},{4,8},{5,9},{6,10},{7,11},{8,4},{9,5},... | collective-permute-start | bytes 221192 | tf_op jit(solution)/shard_map/ppermute | solution.py:221
  35.7 1.9 %slice.89 = bf16[4,64,1024]{2,1,0:T(8,128)(2,1)} slice(bf16[12,64,1024]{2,1,0:T(8,128)(2,1)} %refs_12_.1), slice={[8:12], [0:64], [0:1024]} | slice | bytes 1048576 | tf_op jit(solution)/shard_map/slice | solution.py:290
  37.6 1.4 %collective-permute-done.3.refs_3_ = bf16[144,256]{1,0:T(8,128)(2,1)S(1)} collective-permute-done((bf16[144,256]{1,0:T(8,128)(2,1)S(1)}, bf16[144,256]{1,0:T(8,128)(2,1)S(1)}, u32[]{:S(2)}, u32[]{:S(2)}) %collective-permute-start.3) | collective-permute-done | bytes 73760 | tf_op jit(solution)/shard_map/ppermute | solution.py:221
  39.0 1.5 %collective-permute-start.17 = (bf16[4,64,1024]{2,1,0:T(8,128)(2,1)}, bf16[4,64,1024]{2,1,0:T(8,128)(2,1)}, u32[]{:S(2)}, u32[]{:S(2)}) collective-permute-start(bf16[4,64,1024]{2,1,0:T(8,128)(2,1)} %slice.89), channel_id=1, source_target_pairs={{0,2},{1,3},{2,0},{3,1},{4,6},{5,7},{6,4},{7,5},{8,10},{9,11},{10,... | collective-permute-start | bytes 1572872 | tf_op jit(solution)/shard_map/ppermute | solution.py:24
  40.6 0.7 stk.1
  41.8 1.5 %collective-permute-start.5 = (bf16[4,128,256]{2,1,0:T(8,128)(2,1)}, bf16[4,128,256]{2,1,0:T(8,128)(2,1)S(1)}, u32[]{:S(2)}, u32[]{:S(2)}) collective-permute-start(bf16[4,128,256]{2,1,0:T(8,128)(2,1)} %get-tuple-element.76.refs_0_), channel_id=1, source_target_pairs={{0,16},{16,0},{1,17},{17,1},{2,18},{18,2},{3,19},{19,3},{4,20},{20... | collective-permute-start | bytes 786440 | tf_op jit(solution)/shard_map/ppermute | solution.py:24
  43.4 10.8 %collective-permute-done.17.refs_1_ = bf16[4,64,1024]{2,1,0:T(8,128)(2,1)} collective-permute-done((bf16[4,64,1024]{2,1,0:T(8,128)(2,1)}, bf16[4,64,1024]{2,1,0:T(8,128)(2,1)}, u32[]{:S(2)}, u32[]{:S(2)}) %collective-permute-start.17) | collective-permute-done | bytes 524320 | tf_op jit(solution)/shard_map/ppermute | solution.py:24
  54.1 2.9 %collective-permute-done.4.refs_1_ = bf16[4,128,256]{2,1,0:T(8,128)(2,1)} collective-permute-done((bf16[4,128,256]{2,1,0:T(8,128)(2,1)}, bf16[4,128,256]{2,1,0:T(8,128)(2,1)}, u32[]{:S(2)}, u32[]{:S(2)}) %collective-permute-start.4) | collective-permute-done | bytes 262176 | tf_op jit(solution)/shard_map/ppermute | solution.py:24
  57.0 1.5 %collective-permute-start.6 = (bf16[4,128,256]{2,1,0:T(8,128)(2,1)}, bf16[4,128,256]{2,1,0:T(8,128)(2,1)}, u32[]{:S(2)}, u32[]{:S(2)}) collective-permute-start(bf16[4,128,256]{2,1,0:T(8,128)(2,1)} %collective-permute-done.4.refs_1_), channel_id=1, source_target_pairs={{0,16},{16,0},{1,17},{17,1},{2,18},{18,2},{3,19},{19,3},{4,20},{20... | collective-permute-start | bytes 786440 | tf_op jit(solution)/shard_map/ppermute | solution.py:24
  60.0 1.3 %collective-permute-start.14 = (bf16[16,128,128]{2,1,0:T(8,128)(2,1)}, bf16[16,128,128]{2,1,0:T(8,128)(2,1)S(1)}, u32[]{:S(2)}, u32[]{:S(2)}) collective-permute-start(bf16[16,128,128]{2,1,0:T(8,128)(2,1)} %collective-permute-done.13.refs_0_), channel_id=1, source_target_pairs={{8,12},{9,13},{10,14},{11,15},{4,0},{5,1},{6,2},{7,3},{24,28},{25,... | collective-permute-start | bytes 1572872 | tf_op jit(solution)/shard_map/ppermute | solution.py:221
  61.3 2.4 %collective-permute-done.6.refs_3_ = bf16[4,128,256]{2,1,0:T(8,128)(2,1)} collective-permute-done((bf16[4,128,256]{2,1,0:T(8,128)(2,1)}, bf16[4,128,256]{2,1,0:T(8,128)(2,1)}, u32[]{:S(2)}, u32[]{:S(2)}) %collective-permute-start.6) | collective-permute-done | bytes 262176 | tf_op jit(solution)/shard_map/ppermute | solution.py:24
  66.5 1.3 %collective-permute-start.23 = (bf16[16,128,128]{2,1,0:T(8,128)(2,1)}, bf16[16,128,128]{2,1,0:T(8,128)(2,1)}, u32[]{:S(2)}, u32[]{:S(2)}) collective-permute-start(bf16[16,128,128]{2,1,0:T(8,128)(2,1)} %collective-permute-done.12.refs_10_), channel_id=1, source_target_pairs={{8,12},{9,13},{10,14},{11,15},{4,0},{5,1},{6,2},{7,3},{24,28},{25,... | collective-permute-start | bytes 1572872 | tf_op jit(solution)/shard_map/ppermute | solution.py:221
  67.8 9.1 %collective-permute-done.14.refs_11_ = bf16[16,128,128]{2,1,0:T(8,128)(2,1)S(1)} collective-permute-done((bf16[16,128,128]{2,1,0:T(8,128)(2,1)}, bf16[16,128,128]{2,1,0:T(8,128)(2,1)S(1)}, u32[]{:S(2)}, u32[]{:S(2)}) %collective-permute-start.14) | collective-permute-done | bytes 524320 | tf_op jit(solution)/shard_map/ppermute | solution.py:221
  76.9 0.8 copy-done.5
  78.3 1.3 %collective-permute-done.10.refs_7_ = bf16[4,128,256]{2,1,0:T(8,128)(2,1)} collective-permute-done((bf16[4,128,256]{2,1,0:T(8,128)(2,1)}, bf16[4,128,256]{2,1,0:T(8,128)(2,1)}, u32[]{:S(2)}, u32[]{:S(2)}) %collective-permute-start.10) | collective-permute-done | bytes 262176 | tf_op jit(solution)/shard_map/ppermute | solution.py:24
  79.6 1.0 copy-done.4
  80.6 1.0 copy-done.6
  81.6 0.9 copy-done.8
  82.6 0.9 copy-done.10
  83.5 0.9 copy-done.12
  84.5 0.9 copy-done.14
  85.4 3.3 %shard_map.82 = (bf16[3,16,128,256]{3,2,1,0:T(8,128)(2,1)S(1)}, bf16[12,128,1024]{2,1,0:T(8,128)(2,1)S(1)}, bf16[16,256,256]{2,1,0:T(8,128)(2,1)S(1)}) custom-call(s32[5,64]{1,0:T(8,128)S(1)} %stack.26.table, bf16[4,128,256]{2,1,0:T(8,128)(2,1)} %get-tuple-element.76.refs_0_, bf16[4,128,256]{2,1,0:T(8,128)(2,1)} %collective-permute-done.4.refs_1_, ...), custom_call_target="tpu_custom_call" | custom-call | flops 402653184 | bytes 3145728 | tf_op jit(solution)/shard_map/pallas_call | solution.py:340
  88.8 3.1 %shard_map.83 = (f32[256,512]{1,0:T(8,128)S(1)}, bf16[256,512]{1,0:T(8,128)(2,1)S(1)}, bf16[12,128,1024]{2,1,0:T(8,128)(2,1)S(1)}) custom-call(s32[5,64]{1,0:T(8,128)S(1)} %stack.26.table, bf16[3,16,128,256]{3,2,1,0:T(8,128)(2,1)S(1)} %get-tuple-element.77.made, bf16[12,128,1024]{2,1,0:T(8,128)(2,1)S(1)} %get-tuple-element.78.own, ...), custom_call_target="tpu_custom_call" | custom-call | flops 1073741824 | bytes 3145728 | tf_op jit(solution)/shard_map/pallas_call | solution.py:340
  91.9 1.0 collective-permute-start.26
  92.9 2.5 %shard_map.86 = (f32[256,512]{1,0:T(8,128)S(1)}, bf16[256,512]{1,0:T(8,128)(2,1)S(1)}) custom-call(s32[5,64]{1,0:T(8,128)S(1)} %stack.26.table, bf16[16,256,256]{2,1,0:T(8,128)(2,1)S(1)} %get-tuple-element.84.rows_held, bf16[12,128,1024]{2,1,0:T(8,128)(2,1)S(1)} %get-tuple-element.78.own, bf16[12,128,1024]{2,1,0:T(8,128)(2,1)S(1)} %get-tuple-element.79.other, ...), custom_call_target="tpu_custom_call" | custom-call | flops 1207959552 | bytes 3145728 | tf_op jit(solution)/shard_map/pallas_call | solution.py:340
  95.4 3.3 %collective-permute-start.24 = (bf16[256,512]{1,0:T(8,128)(2,1)S(1)}, bf16[256,512]{1,0:T(8,128)(2,1)S(1)}, u32[]{:S(2)}, u32[]{:S(2)}) collective-permute-start(bf16[256,512]{1,0:T(8,128)(2,1)S(1)} %get-tuple-element.86), channel_id=1, source_target_pairs={{0,16},{16,0},{1,17},{17,1},{2,18},{18,2},{3,19},{19,3},{4,20},{20... | collective-permute-start | bytes 786440 | tf_op jit(solution)/shard_map/ppermute | solution.py:24
  98.7 1.2 shard_map.85
  99.9 2.7 %shard_map.84 = (f32[256,512]{1,0:T(8,128)S(1)}, bf16[256,512]{1,0:T(8,128)(2,1)S(1)}) custom-call(s32[5,64]{1,0:T(8,128)S(1)} %stack.26.table, bf16[3,16,128,256]{3,2,1,0:T(8,128)(2,1)S(1)} %get-tuple-element.77.made, bf16[12,128,1024]{2,1,0:T(8,128)(2,1)S(1)} %get-tuple-element.78.own, bf16[12,128,1024]{2,1,0:T(8,128)(2,1)S(1)} %get-tuple-element.79.other), custom_call_target="tpu_custom_call" | custom-call | flops 1073741824 | bytes 3145728 | tf_op jit(solution)/shard_map/pallas_call | solution.py:340
  102.7 1.0 collective-permute-start.21
  103.7 1.0 collective-permute-start.20
  104.9 1.5 %collective-permute-done.24 = bf16[256,512]{1,0:T(8,128)(2,1)S(1)} collective-permute-done((bf16[256,512]{1,0:T(8,128)(2,1)S(1)}, bf16[256,512]{1,0:T(8,128)(2,1)S(1)}, u32[]{:S(2)}, u32[]{:S(2)}) %collective-permute-start.24) | collective-permute-done | bytes 262176 | tf_op jit(solution)/shard_map/ppermute | solution.py:24
  106.4 5.8 %collective-permute-start.25 = (bf16[256,512]{1,0:T(8,128)(2,1)S(1)}, bf16[256,512]{1,0:T(8,128)(2,1)S(1)}, u32[]{:S(2)}, u32[]{:S(2)}) collective-permute-start(bf16[256,512]{1,0:T(8,128)(2,1)S(1)} %add_convert_fusion.2), channel_id=1, source_target_pairs={{0,12},{1,13},{2,14},{3,15},{12,0},{13,1},{14,2},{15,3},{16,28},{1... | collective-permute-start | bytes 786440 | tf_op jit(solution)/shard_map/ppermute | solution.py:221
  112.4 1.1 collective-permute-done.27.refs_4_
  114.8 2.8 %collective-permute-done.20 = bf16[256,512]{1,0:T(8,128)(2,1)S(1)} collective-permute-done((bf16[256,512]{1,0:T(8,128)(2,1)S(1)}, bf16[256,512]{1,0:T(8,128)(2,1)S(1)}, u32[]{:S(2)}, u32[]{:S(2)}) %collective-permute-start.20) | collective-permute-done | bytes 262176 | tf_op jit(solution)/shard_map/ppermute | solution.py:24
  117.7 1.7 %collective-permute-done.25.refs_2_ = bf16[256,512]{1,0:T(8,128)(2,1)S(1)} collective-permute-done((bf16[256,512]{1,0:T(8,128)(2,1)S(1)}, bf16[256,512]{1,0:T(8,128)(2,1)S(1)}, u32[]{:S(2)}, u32[]{:S(2)}) %collective-permute-start.25) | collective-permute-done | bytes 262176 | tf_op jit(solution)/shard_map/ppermute | solution.py:221
  119.4 5.4 %collective-permute-done.22.refs_1_ = bf16[256,512]{1,0:T(8,128)(2,1)S(1)} collective-permute-done((bf16[256,512]{1,0:T(8,128)(2,1)S(1)}, bf16[256,512]{1,0:T(8,128)(2,1)S(1)}, u32[]{:S(2)}, u32[]{:S(2)}) %collective-permute-start.22) | collective-permute-done | bytes 262176 | tf_op jit(solution)/shard_map/ppermute | solution.py:221
  124.8 1.0 finish.1
  (81 shorter events, 8.7 us)
Async XLA Ops:
  0.0 40.6 %copy-start = (bf16[12,64,1024]{2,1,0:T(8,128)(2,1)S(1)}, bf16[12,64,1024]{2,1,0:T(8,128)(2,1)}, u32[]{:S(2)}) copy-start(bf16[12,64,1024]{2,1,0:T(8,128)(2,1)} %refs_12_.1) | copy-start | bytes 4718596
  0.0 40.5 %collective-permute-start.13 = (bf16[16,128,128]{2,1,0:T(8,128)(2,1)}, bf16[16,128,128]{2,1,0:T(8,128)(2,1)}, u32[]{:S(2)}, u32[]{:S(2)}) collective-permute-start(bf16[16,128,128]{2,1,0:T(8,128)(2,1)} %bitcast.14), channel_id=1, source_target_pairs={{4,8},{5,9},{6,10},{7,11},{8,4},{9,5},{10,6},{11,7},{20,24},{21,25... | collective-permute-start | bytes 1572872 | tf_op jit(solution)/shard_map/ppermute | solution.py:221
  1.6 39.7 %collective-permute-start.12 = (bf16[16,128,128]{2,1,0:T(8,128)(2,1)}, bf16[16,128,128]{2,1,0:T(8,128)(2,1)}, u32[]{:S(2)}, u32[]{:S(2)}) collective-permute-start(bf16[16,128,128]{2,1,0:T(8,128)(2,1)} %bitcast.15), channel_id=1, source_target_pairs={{0,8},{1,9},{2,10},{3,11},{12,4},{13,5},{14,6},{15,7},{16,24},{17,... | collective-permute-start | bytes 1572872 | tf_op jit(solution)/shard_map/ppermute | solution.py:221
  9.3 7.7 %collective-permute-start = (bf16[256,512]{1,0:T(8,128)(2,1)}, bf16[256,512]{1,0:T(8,128)(2,1)S(1)}, u32[]{:S(2)}, u32[]{:S(2)}) collective-permute-start(bf16[256,512]{1,0:T(8,128)(2,1)} %state.1), channel_id=1, source_target_pairs={{0,16},{16,0},{1,17},{17,1},{2,18},{18,2},{3,19},{19,3},{4,20},{20... | collective-permute-start | bytes 786440 | tf_op jit(solution)/shard_map/ppermute | solution.py:24
  13.1 45.5 %collective-permute-start.16 = (bf16[8,64,1024]{2,1,0:T(8,128)(2,1)}, bf16[8,64,1024]{2,1,0:T(8,128)(2,1)}, u32[]{:S(2)}, u32[]{:S(2)}) collective-permute-start(bf16[8,64,1024]{2,1,0:T(8,128)(2,1)} %slice.88), channel_id=1, source_target_pairs={{0,2},{1,3},{2,0},{3,1},{4,6},{5,7},{6,4},{7,5},{8,10},{9,11},{10,... | collective-permute-start | bytes 3145736 | tf_op jit(solution)/shard_map/ppermute | solution.py:24
  17.0 1.0 copy-start.1
  18.6 4.4 %collective-permute-start.1 = (bf16[144,256]{1,0:T(8,128)(2,1)S(1)}, bf16[144,256]{1,0:T(8,128)(2,1)S(1)}, u32[]{:S(2)}, u32[]{:S(2)}) collective-permute-start(bf16[144,256]{1,0:T(8,128)(2,1)S(1)} %get-tuple-element.72), channel_id=1, source_target_pairs={{0,4},{1,5},{2,6},{3,7},{4,0},{5,1},{6,2},{7,3},{8,12},{9,13},{10,... | collective-permute-start | bytes 221192 | tf_op jit(solution)/shard_map/ppermute | solution.py:221
  18.7 14.2 %collective-permute-start.2 = (bf16[144,256]{1,0:T(8,128)(2,1)S(1)}, bf16[144,256]{1,0:T(8,128)(2,1)S(1)}, u32[]{:S(2)}, u32[]{:S(2)}) collective-permute-start(bf16[144,256]{1,0:T(8,128)(2,1)S(1)} %get-tuple-element.73), channel_id=1, source_target_pairs={{0,8},{1,9},{2,10},{3,11},{4,12},{5,13},{6,14},{7,15},{8,0},{9,1},... | collective-permute-start | bytes 221192 | tf_op jit(solution)/shard_map/ppermute | solution.py:221
  23.0 18.8 %collective-permute-start.11 = (bf16[16,128,128]{2,1,0:T(8,128)(2,1)}, bf16[16,128,128]{2,1,0:T(8,128)(2,1)}, u32[]{:S(2)}, u32[]{:S(2)}) collective-permute-start(bf16[16,128,128]{2,1,0:T(8,128)(2,1)} %bitcast.16), channel_id=1, source_target_pairs={{0,4},{1,5},{2,6},{3,7},{4,0},{5,1},{6,2},{7,3},{8,12},{9,13},{10,... | collective-permute-start | bytes 1572872 | tf_op jit(solution)/shard_map/ppermute | solution.py:221
  32.9 6.2 %collective-permute-start.3 = (bf16[144,256]{1,0:T(8,128)(2,1)S(1)}, bf16[144,256]{1,0:T(8,128)(2,1)S(1)}, u32[]{:S(2)}, u32[]{:S(2)}) collective-permute-start(bf16[144,256]{1,0:T(8,128)(2,1)S(1)} %get-tuple-element.74), channel_id=1, source_target_pairs={{0,12},{1,13},{2,14},{3,15},{4,8},{5,9},{6,10},{7,11},{8,4},{9,5},... | collective-permute-start | bytes 221192 | tf_op jit(solution)/shard_map/ppermute | solution.py:221
  39.0 15.1 %collective-permute-start.17 = (bf16[4,64,1024]{2,1,0:T(8,128)(2,1)}, bf16[4,64,1024]{2,1,0:T(8,128)(2,1)}, u32[]{:S(2)}, u32[]{:S(2)}) collective-permute-start(bf16[4,64,1024]{2,1,0:T(8,128)(2,1)} %slice.89), channel_id=1, source_target_pairs={{0,2},{1,3},{2,0},{3,1},{4,6},{5,7},{6,4},{7,5},{8,10},{9,11},{10,... | collective-permute-start | bytes 1572872 | tf_op jit(solution)/shard_map/ppermute | solution.py:24
  40.6 39.0 %collective-permute-start.15 = (bf16[12,64,1024]{2,1,0:T(8,128)(2,1)S(1)}, bf16[12,64,1024]{2,1,0:T(8,128)(2,1)S(1)}, u32[]{:S(2)}, u32[]{:S(2)}) collective-permute-start(bf16[12,64,1024]{2,1,0:T(8,128)(2,1)S(1)} %copy-done), channel_id=1, source_target_pairs={{0,1},{1,0},{2,3},{3,2},{4,5},{5,4},{6,7},{7,6},{8,9},{9,8},{10,11... | collective-permute-start | bytes 4718600 | tf_op jit(solution)/shard_map/ppermute | solution.py:24
  41.3 15.7 %collective-permute-start.4 = (bf16[4,128,256]{2,1,0:T(8,128)(2,1)}, bf16[4,128,256]{2,1,0:T(8,128)(2,1)}, u32[]{:S(2)}, u32[]{:S(2)}) collective-permute-start(bf16[4,128,256]{2,1,0:T(8,128)(2,1)} %get-tuple-element.76.refs_0_), channel_id=1, source_target_pairs={{0,2},{1,3},{2,0},{3,1},{4,6},{5,7},{6,4},{7,5},{8,10},{9,11},{10,... | collective-permute-start | bytes 786440 | tf_op jit(solution)/shard_map/ppermute | solution.py:24
  41.8 16.7 %collective-permute-start.5 = (bf16[4,128,256]{2,1,0:T(8,128)(2,1)}, bf16[4,128,256]{2,1,0:T(8,128)(2,1)S(1)}, u32[]{:S(2)}, u32[]{:S(2)}) collective-permute-start(bf16[4,128,256]{2,1,0:T(8,128)(2,1)} %get-tuple-element.76.refs_0_), channel_id=1, source_target_pairs={{0,16},{16,0},{1,17},{17,1},{2,18},{18,2},{3,19},{19,3},{4,20},{20... | collective-permute-start | bytes 786440 | tf_op jit(solution)/shard_map/ppermute | solution.py:24
  54.1 5.1 %collective-permute-start.7 = (bf16[4,128,256]{2,1,0:T(8,128)(2,1)}, bf16[4,128,256]{2,1,0:T(8,128)(2,1)S(1)}, u32[]{:S(2)}, u32[]{:S(2)}) collective-permute-start(bf16[4,128,256]{2,1,0:T(8,128)(2,1)} %get-tuple-element.76.refs_0_), channel_id=1, source_target_pairs={{0,1},{1,0},{2,3},{3,2},{4,5},{5,4},{6,7},{7,6},{8,9},{9,8},{10,11... | collective-permute-start | bytes 786440 | tf_op jit(solution)/shard_map/ppermute | solution.py:24
  57.0 6.7 %collective-permute-start.6 = (bf16[4,128,256]{2,1,0:T(8,128)(2,1)}, bf16[4,128,256]{2,1,0:T(8,128)(2,1)}, u32[]{:S(2)}, u32[]{:S(2)}) collective-permute-start(bf16[4,128,256]{2,1,0:T(8,128)(2,1)} %collective-permute-done.4.refs_1_), channel_id=1, source_target_pairs={{0,16},{16,0},{1,17},{17,1},{2,18},{18,2},{3,19},{19,3},{4,20},{20... | collective-permute-start | bytes 786440 | tf_op jit(solution)/shard_map/ppermute | solution.py:24
  58.5 5.9 %collective-permute-start.8 = (bf16[4,128,256]{2,1,0:T(8,128)(2,1)}, bf16[4,128,256]{2,1,0:T(8,128)(2,1)S(1)}, u32[]{:S(2)}, u32[]{:S(2)}) collective-permute-start(bf16[4,128,256]{2,1,0:T(8,128)(2,1)} %collective-permute-done.4.refs_1_), channel_id=1, source_target_pairs={{0,1},{1,0},{2,3},{3,2},{4,5},{5,4},{6,7},{7,6},{8,9},{9,8},{10,11... | collective-permute-start | bytes 786440 | tf_op jit(solution)/shard_map/ppermute | solution.py:24
  58.6 30.2 %collective-permute-start.18 = (bf16[8,64,1024]{2,1,0:T(8,128)(2,1)}, bf16[8,64,1024]{2,1,0:T(8,128)(2,1)}, u32[]{:S(2)}, u32[]{:S(2)}) collective-permute-start(bf16[8,64,1024]{2,1,0:T(8,128)(2,1)} %collective-permute-done.16.refs_0_), channel_id=1, source_target_pairs={{0,1},{1,0},{2,3},{3,2},{4,5},{5,4},{6,7},{7,6},{8,9},{9,8},{10,11... | collective-permute-start | bytes 3145736 | tf_op jit(solution)/shard_map/ppermute | solution.py:24
  59.3 0.7 copy-start.9
  60.0 16.9 %collective-permute-start.14 = (bf16[16,128,128]{2,1,0:T(8,128)(2,1)}, bf16[16,128,128]{2,1,0:T(8,128)(2,1)S(1)}, u32[]{:S(2)}, u32[]{:S(2)}) collective-permute-start(bf16[16,128,128]{2,1,0:T(8,128)(2,1)} %collective-permute-done.13.refs_0_), channel_id=1, source_target_pairs={{8,12},{9,13},{10,14},{11,15},{4,0},{5,1},{6,2},{7,3},{24,28},{25,... | collective-permute-start | bytes 1572872 | tf_op jit(solution)/shard_map/ppermute | solution.py:221
  63.7 2.0 %collective-permute-start.9 = (bf16[4,128,256]{2,1,0:T(8,128)(2,1)S(1)}, bf16[4,128,256]{2,1,0:T(8,128)(2,1)S(1)}, u32[]{:S(2)}, u32[]{:S(2)}) collective-permute-start(bf16[4,128,256]{2,1,0:T(8,128)(2,1)S(1)} %collective-permute-done.5.refs_2_), channel_id=1, source_target_pairs={{0,1},{1,0},{2,3},{3,2},{4,5},{5,4},{6,7},{7,6},{8,9},{9,8},{10,11... | collective-permute-start | bytes 786440 | tf_op jit(solution)/shard_map/ppermute | solution.py:24
  63.7 0.7 copy-start.7
  64.4 0.7 copy-start.11
  65.1 23.6 %collective-permute-start.19 = (bf16[4,64,1024]{2,1,0:T(8,128)(2,1)}, bf16[4,64,1024]{2,1,0:T(8,128)(2,1)}, u32[]{:S(2)}, u32[]{:S(2)}) collective-permute-start(bf16[4,64,1024]{2,1,0:T(8,128)(2,1)} %collective-permute-done.17.refs_1_), channel_id=1, source_target_pairs={{0,1},{1,0},{2,3},{3,2},{4,5},{5,4},{6,7},{7,6},{8,9},{9,8},{10,11... | collective-permute-start | bytes 1572872 | tf_op jit(solution)/shard_map/ppermute | solution.py:24
  65.7 0.7 copy-start.13
  66.5 26.5 %collective-permute-start.23 = (bf16[16,128,128]{2,1,0:T(8,128)(2,1)}, bf16[16,128,128]{2,1,0:T(8,128)(2,1)}, u32[]{:S(2)}, u32[]{:S(2)}) collective-permute-start(bf16[16,128,128]{2,1,0:T(8,128)(2,1)} %collective-permute-done.12.refs_10_), channel_id=1, source_target_pairs={{8,12},{9,13},{10,14},{11,15},{4,0},{5,1},{6,2},{7,3},{24,28},{25,... | collective-permute-start | bytes 1572872 | tf_op jit(solution)/shard_map/ppermute | solution.py:221
  76.9 0.8 copy-start.5
  77.7 1.9 %collective-permute-start.10 = (bf16[4,128,256]{2,1,0:T(8,128)(2,1)}, bf16[4,128,256]{2,1,0:T(8,128)(2,1)}, u32[]{:S(2)}, u32[]{:S(2)}) collective-permute-start(bf16[4,128,256]{2,1,0:T(8,128)(2,1)} %collective-permute-done.6.refs_3_), channel_id=1, source_target_pairs={{0,1},{1,0},{2,3},{3,2},{4,5},{5,4},{6,7},{7,6},{8,9},{9,8},{10,11... | collective-permute-start | bytes 786440 | tf_op jit(solution)/shard_map/ppermute | solution.py:24
  79.6 1.0 copy-start.4
  80.6 1.0 copy-start.6
  81.6 0.9 copy-start.8
  82.6 0.9 copy-start.10
  83.5 0.9 copy-start.12
  84.5 0.9 copy-start.14
  91.9 12.9 %collective-permute-start.26 = (bf16[256,512]{1,0:T(8,128)(2,1)S(1)}, bf16[256,512]{1,0:T(8,128)(2,1)S(1)}, u32[]{:S(2)}, u32[]{:S(2)}) collective-permute-start(bf16[256,512]{1,0:T(8,128)(2,1)S(1)} %get-tuple-element.88), channel_id=1, source_target_pairs={{0,16},{16,0},{1,17},{17,1},{2,18},{18,2},{3,19},{19,3},{4,20},{20... | collective-permute-start | bytes 786440 | tf_op jit(solution)/shard_map/ppermute | solution.py:24
  95.4 10.9 %collective-permute-start.24 = (bf16[256,512]{1,0:T(8,128)(2,1)S(1)}, bf16[256,512]{1,0:T(8,128)(2,1)S(1)}, u32[]{:S(2)}, u32[]{:S(2)}) collective-permute-start(bf16[256,512]{1,0:T(8,128)(2,1)S(1)} %get-tuple-element.86), channel_id=1, source_target_pairs={{0,16},{16,0},{1,17},{17,1},{2,18},{18,2},{3,19},{19,3},{4,20},{20... | collective-permute-start | bytes 786440 | tf_op jit(solution)/shard_map/ppermute | solution.py:24
  102.6 11.7 %copy-start.2 = (bf16[256,512]{1,0:T(8,128)(2,1)S(1)}, bf16[256,512]{1,0:T(8,128)(2,1)}, u32[]{:S(2)}) copy-start(bf16[256,512]{1,0:T(8,128)(2,1)} %state.1) | copy-start | bytes 786436
  102.6 11.7 %copy-start.3 = (bf16[1024,512]{1,0:T(8,128)(2,1)S(1)}, bf16[1024,512]{1,0:T(8,128)(2,1)}, u32[]{:S(2)}) copy-start(bf16[1024,512]{1,0:T(8,128)(2,1)} %weight.1) | copy-start | bytes 3145732
  102.6 11.7 %copy-start.16 = (f32[512]{0:T(512)S(1)}, f32[512]{0:T(512)}, u32[]{:S(2)}) copy-start(f32[512]{0:T(512)} %param.19) | copy-start | bytes 6148
  102.7 9.6 %collective-permute-start.21 = (bf16[256,512]{1,0:T(8,128)(2,1)S(1)}, bf16[256,512]{1,0:T(8,128)(2,1)S(1)}, u32[]{:S(2)}, u32[]{:S(2)}) collective-permute-start(bf16[256,512]{1,0:T(8,128)(2,1)S(1)} %get-tuple-element.83), channel_id=1, source_target_pairs={{0,16},{16,0},{1,17},{17,1},{2,18},{18,2},{3,19},{19,3},{4,20},{20... | collective-permute-start | bytes 786440 | tf_op jit(solution)/shard_map/ppermute | solution.py:24
  103.7 13.9 %collective-permute-start.20 = (bf16[256,512]{1,0:T(8,128)(2,1)S(1)}, bf16[256,512]{1,0:T(8,128)(2,1)S(1)}, u32[]{:S(2)}, u32[]{:S(2)}) collective-permute-start(bf16[256,512]{1,0:T(8,128)(2,1)S(1)} %get-tuple-element.81), channel_id=1, source_target_pairs={{0,16},{16,0},{1,17},{17,1},{2,18},{18,2},{3,19},{19,3},{4,20},{20... | collective-permute-start | bytes 786440 | tf_op jit(solution)/shard_map/ppermute | solution.py:24
  104.8 8.7 %collective-permute-start.27 = (bf16[256,512]{1,0:T(8,128)(2,1)S(1)}, bf16[256,512]{1,0:T(8,128)(2,1)S(1)}, u32[]{:S(2)}, u32[]{:S(2)}) collective-permute-start(bf16[256,512]{1,0:T(8,128)(2,1)S(1)} %add_convert_fusion.1), channel_id=1, source_target_pairs={{0,4},{1,5},{2,6},{3,7},{4,12},{5,13},{6,14},{7,15},{12,8},{13,9},... | collective-permute-start | bytes 786440 | tf_op jit(solution)/shard_map/ppermute | solution.py:221
  106.4 18.4 %copy-start.15 = (f32[512]{0:T(512)S(1)}, f32[512]{0:T(512)}, u32[]{:S(2)}) copy-start(f32[512]{0:T(512)} %param.20) | copy-start | bytes 6148
  106.4 12.9 %collective-permute-start.25 = (bf16[256,512]{1,0:T(8,128)(2,1)S(1)}, bf16[256,512]{1,0:T(8,128)(2,1)S(1)}, u32[]{:S(2)}, u32[]{:S(2)}) collective-permute-start(bf16[256,512]{1,0:T(8,128)(2,1)S(1)} %add_convert_fusion.2), channel_id=1, source_target_pairs={{0,12},{1,13},{2,14},{3,15},{12,0},{13,1},{14,2},{15,3},{16,28},{1... | collective-permute-start | bytes 786440 | tf_op jit(solution)/shard_map/ppermute | solution.py:221
  112.3 12.4 %collective-permute-start.22 = (bf16[256,512]{1,0:T(8,128)(2,1)S(1)}, bf16[256,512]{1,0:T(8,128)(2,1)S(1)}, u32[]{:S(2)}, u32[]{:S(2)}) collective-permute-start(bf16[256,512]{1,0:T(8,128)(2,1)S(1)} %add_convert_fusion.3), channel_id=1, source_target_pairs={{0,4},{1,5},{2,6},{3,7},{4,0},{5,1},{6,2},{7,3},{8,12},{9,13},{10,... | collective-permute-start | bytes 786440 | tf_op jit(solution)/shard_map/ppermute | solution.py:221
  113.6 11.2 %collective-permute-start.28 = (bf16[256,512]{1,0:T(8,128)(2,1)S(1)}, bf16[256,512]{1,0:T(8,128)(2,1)S(1)}, u32[]{:S(2)}, u32[]{:S(2)}) collective-permute-start(bf16[256,512]{1,0:T(8,128)(2,1)S(1)} %add_convert_fusion), channel_id=1, source_target_pairs={{4,8},{5,9},{6,10},{7,11},{8,4},{9,5},{10,6},{11,7},{20,24},{21,25... | collective-permute-start | bytes 786440 | tf_op jit(solution)/shard_map/ppermute | solution.py:221

commit v5 on v4

--- a/solution.py
+++ b/solution.py
@@ -214,6 +214,7 @@
     rel = lax.axis_index("rel")
     ent = lax.axis_index("ent")
     part, member = ent // members, ent % members
+    edge = jnp.logical_or(part == 0, part == chunks - 1).astype(jnp.int32)
     line = chunks == 4 and members == 4 and n_rel == 2
 
     def along(value, pairs):
@@ -230,10 +231,10 @@
     if line:
         near = along(values, [(0, 1), (1, 0), (2, 3), (3, 2)])
         middle = along(values, [(1, 2), (2, 1)])
-        inward = along(values, [(0, 2), (3, 1)])
-        edge_two = along(middle, [(2, 3), (1, 0)])
-        edge_three = along(inward, [(2, 3), (1, 0)])
-        tiles = [[values], [near], [inward, edge_two], [middle, edge_three]]
+        onward = jnp.where(edge == 1, values, middle)
+        two = along(onward, [(0, 2), (2, 3), (3, 1), (1, 0)])
+        edge_three = along(two, [(2, 3), (1, 0)])
+        tiles = [[values], [near], [two], [middle, edge_three]]
     else:
         tiles = [[values]] + [[partner(values, j)] for j in range(1, chunks)]
 
@@ -274,7 +275,6 @@
     owner = source // per_tile
     place = lax.bitwise_xor(owner % members, member) * chunks
     place = place + lax.bitwise_xor(part, owner // members)
-    edge = jnp.logical_or(part == 0, part == chunks - 1).astype(jnp.int32)
     turns = (counts + GROUP - 1) // GROUP
     last = jnp.zeros((chunks * slots,), jnp.int32).at[:chunks].set(turns)
     last = last.at[HOME:HOME + 3].set(jnp.stack([member, rel, edge]))
@@ -286,7 +286,7 @@
         last,
     ])
 
-    cut = max(1, rel_dev * 2 // 3)
+    cut = max(1, rel_dev * 7 // 12)
     parts = (rel_weight[:cut], rel_weight[cut:])
     bits = [1 << b for b in reversed(range(members.bit_length() - 1))]
     rel_bits = [1 << b for b in reversed(range(n_rel.bit_length() - 1))]
@@ -381,6 +381,16 @@
         [acc_scratch, pltpu.SemaphoreType.DMA((len(other_weights),))],
         slot_flops * features,
     )
+    results = {2: two}
+    for j in (1, 0):
+        results[j] = call(
+            functools.partial(near_kernel, (j,), n_rel),
+            [made, own_half, other_half],
+            [VMEM] * 3,
+            message_shapes(1),
+            [acc_scratch],
+            slot_flops * features,
+        )
     flat = [t for j in late for t in tiles[j]]
     rest = call(
         functools.partial(late_kernel, members, late_ways, late, n_rel),
@@ -395,16 +405,6 @@
         ],
         len(late) * slot_flops * (features + tile_rows),
     )
-    results = {2: two}
-    for j in (1, 0):
-        results[j] = call(
-            functools.partial(near_kernel, (j,), n_rel),
-            [made, own_half, other_half],
-            [VMEM] * 3,
-            message_shapes(1),
-            [acc_scratch],
-            slot_flops * features,
-        )
     for g, j in enumerate(late):
         results[j] = rest[g * n_rel:(g + 1) * n_rel]
 

time: 126 us -> 119 us (0.944)
  waiting for transfers between devices: 51 us -> 35.8 us
  local copies, waits for them, and re-layouts: 15.5 us -> 20.6 us
  other arithmetic: 1.33 us -> 4.75 us
  starting transfers between devices: 41.3 us -> 39.2 us
    ppermute x12 -> x11, waiting for transfers between devices: 28.5 us -> 12.7 us  [along(): return lax.ppermute(value, 'ent', perm)]
    unnamed x35 -> x45, local copies, waits for them, and re-layouts: 10.5 us -> 12.7 us
    ppermute x12 -> x11, starting transfers between devices: 25.8 us -> 23.7 us  [along(): return lax.ppermute(value, 'ent', perm)]
  transfers between devices with their start and end apart: 29 -> 28, of which waited for: 14 -> 10; matrix products, arithmetic and copies ran while one was open for 5% -> 11% of each run, Pallas kernels for 12% -> 13%
where the time goes in v5:
time: 119 us; the launch traced here: 118 us
  starting transfers between devices  39.2 us (33%)
  waiting for transfers between devices  35.8 us (30%)
  local copies, waits for them, and re-layouts  20.6 us (17%)
  Pallas kernels  16.7 us (14%)
  other arithmetic  4.75 us (4%)
    ppermute x11, starting transfers between devices, along(): return lax.ppermute(value, 'ent', perm)  23.7 us
    ppermute x17, waiting for transfers between devices, swap(): return lax.ppermute(value, axis, [(i, i ^ bit) for i in range(size)])  23.1 us
    ppermute x17, starting transfers between devices, swap(): return lax.ppermute(value, axis, [(i, i ^ bit) for i in range(size)])  15.5 us
    unnamed x45, local copies, waits for them, and re-layouts  12.7 us
    ppermute x11, waiting for transfers between devices, along(): return lax.ppermute(value, 'ent', perm)  12.7 us
    pallas_call x5, Pallas kernels, call(): pl.pallas_call(body, out_shape=out_shape, in_specs=[SMEM] + in_specs, out...  12.4 us
    slice x2, local copies, waits for them, and re-layouts, shards(): parts = (rel_weight[:cut], rel_weight[cut:])  4.21 us
  transfers between devices with their start and end apart: 28, of which 10 were waited for; matrix products, arithmetic and copies ran while one was open for 11% of the time, Pallas kernels for 13%

profile of v5, /device:TPU:0, one launch (start us, length us, event | category | flops | bytes accessed | tf_op | source)
XLA Modules:
  0.0 118.0 jit_solution(6601197204003660676)
XLA Ops:
  0.0 0.8 collective-permute-start.12
  0.8 5.9 %collective-permute-start.11 = (bf16[16,128,128]{2,1,0:T(8,128)(2,1)}, bf16[16,128,128]{2,1,0:T(8,128)(2,1)}, u32[]{:S(2)}, u32[]{:S(2)}) collective-permute-start(bf16[16,128,128]{2,1,0:T(8,128)(2,1)} %bitcast.16), channel_id=1, source_target_pairs={{0,4},{1,5},{2,6},{3,7},{4,0},{5,1},{6,2},{7,3},{8,12},{9,13},{10,... | collective-permute-start | bytes 1572872 | tf_op jit(solution)/shard_map/ppermute | solution.py:222
  6.7 1.5 %collective-permute-start = (bf16[256,512]{1,0:T(8,128)(2,1)}, bf16[256,512]{1,0:T(8,128)(2,1)S(1)}, u32[]{:S(2)}, u32[]{:S(2)}) collective-permute-start(bf16[256,512]{1,0:T(8,128)(2,1)} %state.1), channel_id=1, source_target_pairs={{0,16},{16,0},{1,17},{17,1},{2,18},{18,2},{3,19},{19,3},{4,20},{20... | collective-permute-start | bytes 786440 | tf_op jit(solution)/shard_map/ppermute | solution.py:24
  8.2 2.2 %slice.88 = bf16[7,64,1024]{2,1,0:T(8,128)(2,1)} slice(bf16[12,64,1024]{2,1,0:T(8,128)(2,1)} %refs_11_.1), slice={[0:7], [0:64], [0:1024]} | slice | bytes 1835008 | tf_op jit(solution)/shard_map/slice | solution.py:290
  10.4 1.5 %collective-permute-start.15 = (bf16[7,64,1024]{2,1,0:T(8,128)(2,1)}, bf16[7,64,1024]{2,1,0:T(8,128)(2,1)}, u32[]{:S(2)}, u32[]{:S(2)}) collective-permute-start(bf16[7,64,1024]{2,1,0:T(8,128)(2,1)} %slice.88), channel_id=1, source_target_pairs={{0,2},{1,3},{2,0},{3,1},{4,6},{5,7},{6,4},{7,5},{8,10},{9,11},{10,... | collective-permute-start | bytes 2752520 | tf_op jit(solution)/shard_map/ppermute | solution.py:24
  13.5 0.9 collective-permute-done.refs_1_
  14.4 0.9 copy-done.1
  15.4 1.3 %pack.1 = (bf16[144,256]{1,0:T(8,128)(2,1)S(1)}, bf16[144,256]{1,0:T(8,128)(2,1)S(1)}, bf16[144,256]{1,0:T(8,128)(2,1)S(1)}, bf16[144,256]{1,0:T(8,128)(2,1)}) custom-call(s32[3,4]{1,0:T(4,128)S(1)} %add_add_fusion.where, bf16[16,256]{1,0:T(8,128)(2,1)S(1)} %scatter.15.note, bf16[256,512]{1,0:T(8,128)(2,1)S(1)} %copy-done.1, ...), custom_call_target="tpu_custom_call" | custom-call | tf_op jit(solution)/shard_map/pack/pallas_call | solution.py:251
  17.6 1.6 %collective-permute-start.2 = (bf16[144,256]{1,0:T(8,128)(2,1)S(1)}, bf16[144,256]{1,0:T(8,128)(2,1)S(1)}, u32[]{:S(2)}, u32[]{:S(2)}) collective-permute-start(bf16[144,256]{1,0:T(8,128)(2,1)S(1)} %get-tuple-element.73), channel_id=1, source_target_pairs={{0,8},{1,9},{2,10},{3,11},{4,12},{5,13},{6,14},{7,15},{8,0},{9,1},... | collective-permute-start | bytes 221192 | tf_op jit(solution)/shard_map/ppermute | solution.py:222
  19.2 2.4 %collective-permute-done.1.refs_1_ = bf16[144,256]{1,0:T(8,128)(2,1)S(1)} collective-permute-done((bf16[144,256]{1,0:T(8,128)(2,1)S(1)}, bf16[144,256]{1,0:T(8,128)(2,1)S(1)}, u32[]{:S(2)}, u32[]{:S(2)}) %collective-permute-start.1) | collective-permute-done | bytes 73760 | tf_op jit(solution)/shard_map/ppermute | solution.py:222
  22.3 1.3 %collective-permute-start.3 = (bf16[144,256]{1,0:T(8,128)(2,1)}, bf16[144,256]{1,0:T(8,128)(2,1)}, u32[]{:S(2)}, u32[]{:S(2)}) collective-permute-start(bf16[144,256]{1,0:T(8,128)(2,1)} %get-tuple-element.74), channel_id=1, source_target_pairs={{0,12},{1,13},{2,14},{3,15},{4,8},{5,9},{6,10},{7,11},{8,4},{9,5},... | collective-permute-start | bytes 221192 | tf_op jit(solution)/shard_map/ppermute | solution.py:222
  23.6 2.0 %slice.89 = bf16[5,64,1024]{2,1,0:T(8,128)(2,1)} slice(bf16[12,64,1024]{2,1,0:T(8,128)(2,1)} %refs_11_.1), slice={[7:12], [0:64], [0:1024]} | slice | bytes 1310720 | tf_op jit(solution)/shard_map/slice | solution.py:290
  26.3 1.5 %collective-permute-start.16 = (bf16[5,64,1024]{2,1,0:T(8,128)(2,1)}, bf16[5,64,1024]{2,1,0:T(8,128)(2,1)S(1)}, u32[]{:S(2)}, u32[]{:S(2)}) collective-permute-start(bf16[5,64,1024]{2,1,0:T(8,128)(2,1)} %slice.89), channel_id=1, source_target_pairs={{0,2},{1,3},{2,0},{3,1},{4,6},{5,7},{6,4},{7,5},{8,10},{9,11},{10,... | collective-permute-start | bytes 1966088 | tf_op jit(solution)/shard_map/ppermute | solution.py:24
  27.8 1.0 collective-permute-done.3.refs_3_
  28.8 0.9 copy-done.14
  29.7 0.9 copy-done.16
  30.5 0.9 copy-done.18
  31.4 1.6 %stk.1 = (bf16[4,128,256]{2,1,0:T(8,128)(2,1)}, bf16[4,16,256]{2,1,0:T(8,128)(2,1)S(1)}) custom-call(bf16[144,256]{1,0:T(8,128)(2,1)S(1)} %copy-done.14, bf16[144,256]{1,0:T(8,128)(2,1)S(1)} %copy-done.16, bf16[144,256]{1,0:T(8,128)(2,1)S(1)} %copy-done.18, bf16[144,256]{1,0:T(8,128)(2,1)} %collective-permute-done.3.refs_3_), custom_call_target="tpu_custom_call" | custom-call | tf_op jit(solution)/shard_map/stk/pallas_call | solution.py:260
  33.6 1.5 %collective-permute-start.4 = (bf16[4,128,256]{2,1,0:T(8,128)(2,1)}, bf16[4,128,256]{2,1,0:T(8,128)(2,1)}, u32[]{:S(2)}, u32[]{:S(2)}) collective-permute-start(bf16[4,128,256]{2,1,0:T(8,128)(2,1)} %get-tuple-element.76.refs_0_), channel_id=1, source_target_pairs={{0,2},{1,3},{2,0},{3,1},{4,6},{5,7},{6,4},{7,5},{8,10},{9,11},{10,... | collective-permute-start | bytes 786440 | tf_op jit(solution)/shard_map/ppermute | solution.py:24
  36.5 1.5 %collective-permute-start.5 = (bf16[4,128,256]{2,1,0:T(8,128)(2,1)}, bf16[4,128,256]{2,1,0:T(8,128)(2,1)S(1)}, u32[]{:S(2)}, u32[]{:S(2)}) collective-permute-start(bf16[4,128,256]{2,1,0:T(8,128)(2,1)} %get-tuple-element.76.refs_0_), channel_id=1, source_target_pairs={{0,16},{16,0},{1,17},{17,1},{2,18},{18,2},{3,19},{19,3},{4,20},{20... | collective-permute-start | bytes 786440 | tf_op jit(solution)/shard_map/ppermute | solution.py:24
  38.0 13.7 %collective-permute-done.4.refs_1_ = bf16[4,128,256]{2,1,0:T(8,128)(2,1)} collective-permute-done((bf16[4,128,256]{2,1,0:T(8,128)(2,1)}, bf16[4,128,256]{2,1,0:T(8,128)(2,1)}, u32[]{:S(2)}, u32[]{:S(2)}) %collective-permute-start.4) | collective-permute-done | bytes 262176 | tf_op jit(solution)/shard_map/ppermute | solution.py:24
  51.7 1.1 broadcast_select_fusion
  53.4 0.7 copy-done.7
  55.4 7.4 %collective-permute-done.6.refs_3_ = bf16[4,128,256]{2,1,0:T(8,128)(2,1)} collective-permute-done((bf16[4,128,256]{2,1,0:T(8,128)(2,1)}, bf16[4,128,256]{2,1,0:T(8,128)(2,1)}, u32[]{:S(2)}, u32[]{:S(2)}) %collective-permute-start.6) | collective-permute-done | bytes 262176 | tf_op jit(solution)/shard_map/ppermute | solution.py:24
  65.3 2.0 %collective-permute-done.13.refs_10_ = bf16[16,128,128]{2,1,0:T(8,128)(2,1)} collective-permute-done((bf16[16,128,128]{2,1,0:T(8,128)(2,1)S(1)}, bf16[16,128,128]{2,1,0:T(8,128)(2,1)}, u32[]{:S(2)}, u32[]{:S(2)}) %collective-permute-start.13) | collective-permute-done | bytes 524320 | tf_op jit(solution)/shard_map/ppermute | solution.py:222
  67.3 1.3 %collective-permute-start.22 = (bf16[16,128,128]{2,1,0:T(8,128)(2,1)}, bf16[16,128,128]{2,1,0:T(8,128)(2,1)}, u32[]{:S(2)}, u32[]{:S(2)}) collective-permute-start(bf16[16,128,128]{2,1,0:T(8,128)(2,1)} %collective-permute-done.13.refs_10_), channel_id=1, source_target_pairs={{8,12},{9,13},{10,14},{11,15},{4,0},{5,1},{6,2},{7,3},{24,28},{25,... | collective-permute-start | bytes 1572872 | tf_op jit(solution)/shard_map/ppermute | solution.py:222
  70.0 0.7 lt.60
  70.8 1.2 %scatter.19 = s32[1,64]{1,0:T(1,128)} dynamic-update-slice(s32[1,64]{1,0:T(1,128)} %pad_bitcast_fusion, s32[1,3]{1,0:T(1,128)} %add_bitcast_fusion, s32[]{:T(128)} %constant.199.clone.1, s32[]{:T(128)} %constant.209.clone.1) | dynamic-update-slice | bytes 28 | tf_op jit(solution)/shard_map/scatter | solution.py:280
  73.3 0.9 copy-done.6
  74.2 0.9 copy-done.8
  75.2 0.9 copy-done.10
  76.1 0.9 copy-done.12
  77.1 3.3 %shard_map.82 = (bf16[3,16,128,256]{3,2,1,0:T(8,128)(2,1)S(1)}, bf16[12,128,1024]{2,1,0:T(8,128)(2,1)S(1)}, bf16[16,256,256]{2,1,0:T(8,128)(2,1)S(1)}) custom-call(s32[5,64]{1,0:T(8,128)S(1)} %stack.26.table, bf16[4,128,256]{2,1,0:T(8,128)(2,1)} %get-tuple-element.76.refs_0_, bf16[4,128,256]{2,1,0:T(8,128)(2,1)} %collective-permute-done.4.refs_1_, ...), custom_call_target="tpu_custom_call" | custom-call | flops 402653184 | bytes 3145728 | tf_op jit(solution)/shard_map/pallas_call | solution.py:340
  80.4 2.9 %shard_map.83 = (f32[256,512]{1,0:T(8,128)S(1)}, bf16[256,512]{1,0:T(8,128)(2,1)S(1)}, bf16[12,128,1024]{2,1,0:T(8,128)(2,1)S(1)}) custom-call(s32[5,64]{1,0:T(8,128)S(1)} %stack.26.table, bf16[3,16,128,256]{3,2,1,0:T(8,128)(2,1)S(1)} %get-tuple-element.77.made, bf16[12,128,1024]{2,1,0:T(8,128)(2,1)S(1)} %get-tuple-element.78.own, ...), custom_call_target="tpu_custom_call" | custom-call | flops 1073741824 | bytes 3145728 | tf_op jit(solution)/shard_map/pallas_call | solution.py:340
  83.3 1.1 collective-permute-start.25
  84.3 2.5 %shard_map.86 = (f32[256,512]{1,0:T(8,128)S(1)}, bf16[256,512]{1,0:T(8,128)(2,1)S(1)}) custom-call(s32[5,64]{1,0:T(8,128)S(1)} %stack.26.table, bf16[16,256,256]{2,1,0:T(8,128)(2,1)S(1)} %get-tuple-element.84.rows_held, bf16[12,128,1024]{2,1,0:T(8,128)(2,1)S(1)} %get-tuple-element.78.own, bf16[12,128,1024]{2,1,0:T(8,128)(2,1)S(1)} %get-tuple-element.79.other, ...), custom_call_target="tpu_custom_call" | custom-call | flops 1207959552 | bytes 3145728 | tf_op jit(solution)/shard_map/pallas_call | solution.py:340
  86.8 3.2 %collective-permute-start.23 = (bf16[256,512]{1,0:T(8,128)(2,1)S(1)}, bf16[256,512]{1,0:T(8,128)(2,1)S(1)}, u32[]{:S(2)}, u32[]{:S(2)}) collective-permute-start(bf16[256,512]{1,0:T(8,128)(2,1)S(1)} %get-tuple-element.86), channel_id=1, source_target_pairs={{0,16},{16,0},{1,17},{17,1},{2,18},{18,2},{3,19},{19,3},{4,20},{20... | collective-permute-start | bytes 786440 | tf_op jit(solution)/shard_map/ppermute | solution.py:24
  90.0 1.2 %shard_map.85 = (f32[256,512]{1,0:T(8,128)S(1)}, bf16[256,512]{1,0:T(8,128)(2,1)S(1)}) custom-call(s32[5,64]{1,0:T(8,128)S(1)} %stack.26.table, bf16[3,16,128,256]{3,2,1,0:T(8,128)(2,1)S(1)} %get-tuple-element.77.made, bf16[12,128,1024]{2,1,0:T(8,128)(2,1)S(1)} %get-tuple-element.78.own, bf16[12,128,1024]{2,1,0:T(8,128)(2,1)S(1)} %get-tuple-element.79.other), custom_call_target="tpu_custom_call" | custom-call | flops 1073741824 | bytes 3145728 | tf_op jit(solution)/shard_map/pallas_call | solution.py:340
  91.2 2.6 %shard_map.84 = (f32[256,512]{1,0:T(8,128)S(1)}, bf16[256,512]{1,0:T(8,128)(2,1)S(1)}) custom-call(s32[5,64]{1,0:T(8,128)S(1)} %stack.26.table, bf16[3,16,128,256]{3,2,1,0:T(8,128)(2,1)S(1)} %get-tuple-element.77.made, bf16[12,128,1024]{2,1,0:T(8,128)(2,1)S(1)} %get-tuple-element.78.own, bf16[12,128,1024]{2,1,0:T(8,128)(2,1)S(1)} %get-tuple-element.79.other), custom_call_target="tpu_custom_call" | custom-call | flops 1073741824 | bytes 3145728 | tf_op jit(solution)/shard_map/pallas_call | solution.py:340
  93.8 1.0 collective-permute-start.20
  94.8 1.1 collective-permute-start.19
  96.0 2.4 %collective-permute-start.26 = (bf16[256,512]{1,0:T(8,128)(2,1)S(1)}, bf16[256,512]{1,0:T(8,128)(2,1)S(1)}, u32[]{:S(2)}, u32[]{:S(2)}) collective-permute-start(bf16[256,512]{1,0:T(8,128)(2,1)S(1)} %add_convert_fusion.1), channel_id=1, source_target_pairs={{0,4},{1,5},{2,6},{3,7},{4,12},{5,13},{6,14},{7,15},{12,8},{13,9},... | collective-permute-start | bytes 786440 | tf_op jit(solution)/shard_map/ppermute | solution.py:222
  98.5 3.9 %collective-permute-start.24 = (bf16[256,512]{1,0:T(8,128)(2,1)S(1)}, bf16[256,512]{1,0:T(8,128)(2,1)S(1)}, u32[]{:S(2)}, u32[]{:S(2)}) collective-permute-start(bf16[256,512]{1,0:T(8,128)(2,1)S(1)} %add_convert_fusion.2), channel_id=1, source_target_pairs={{0,12},{1,13},{2,14},{3,15},{12,0},{13,1},{14,2},{15,3},{16,28},{1... | collective-permute-start | bytes 786440 | tf_op jit(solution)/shard_map/ppermute | solution.py:222
  102.4 0.7 collective-permute-done.20
  103.2 5.2 %collective-permute-start.21 = (bf16[256,512]{1,0:T(8,128)(2,1)S(1)}, bf16[256,512]{1,0:T(8,128)(2,1)S(1)}, u32[]{:S(2)}, u32[]{:S(2)}) collective-permute-start(bf16[256,512]{1,0:T(8,128)(2,1)S(1)} %add_convert_fusion.3), channel_id=1, source_target_pairs={{0,4},{1,5},{2,6},{3,7},{4,0},{5,1},{6,2},{7,3},{8,12},{9,13},{10,... | collective-permute-start | bytes 786440 | tf_op jit(solution)/shard_map/ppermute | solution.py:222
  109.7 1.9 %collective-permute-done.24.refs_2_ = bf16[256,512]{1,0:T(8,128)(2,1)S(1)} collective-permute-done((bf16[256,512]{1,0:T(8,128)(2,1)S(1)}, bf16[256,512]{1,0:T(8,128)(2,1)S(1)}, u32[]{:S(2)}, u32[]{:S(2)}) %collective-permute-start.24) | collective-permute-done | bytes 262176 | tf_op jit(solution)/shard_map/ppermute | solution.py:222
  111.6 5.4 %collective-permute-done.21.refs_1_ = bf16[256,512]{1,0:T(8,128)(2,1)S(1)} collective-permute-done((bf16[256,512]{1,0:T(8,128)(2,1)S(1)}, bf16[256,512]{1,0:T(8,128)(2,1)S(1)}, u32[]{:S(2)}, u32[]{:S(2)}) %collective-permute-start.21) | collective-permute-done | bytes 262176 | tf_op jit(solution)/shard_map/ppermute | solution.py:222
  117.0 1.0 finish.1
  (90 shorter events, 13.9 us)
Async XLA Ops:
  0.0 28.8 %copy-start = (bf16[12,64,1024]{2,1,0:T(8,128)(2,1)S(1)}, bf16[12,64,1024]{2,1,0:T(8,128)(2,1)}, u32[]{:S(2)}) copy-start(bf16[12,64,1024]{2,1,0:T(8,128)(2,1)} %refs_11_.1) | copy-start | bytes 4718596
  0.0 33.6 %collective-permute-start.12 = (bf16[16,128,128]{2,1,0:T(8,128)(2,1)}, bf16[16,128,128]{2,1,0:T(8,128)(2,1)S(1)}, u32[]{:S(2)}, u32[]{:S(2)}) collective-permute-start(bf16[16,128,128]{2,1,0:T(8,128)(2,1)} %bitcast.15), channel_id=1, source_target_pairs={{4,8},{5,9},{6,10},{7,11},{8,4},{9,5},{10,6},{11,7},{20,24},{21,25... | collective-permute-start | bytes 1572872 | tf_op jit(solution)/shard_map/ppermute | solution.py:222
  0.8 35.6 %collective-permute-start.11 = (bf16[16,128,128]{2,1,0:T(8,128)(2,1)}, bf16[16,128,128]{2,1,0:T(8,128)(2,1)}, u32[]{:S(2)}, u32[]{:S(2)}) collective-permute-start(bf16[16,128,128]{2,1,0:T(8,128)(2,1)} %bitcast.16), channel_id=1, source_target_pairs={{0,4},{1,5},{2,6},{3,7},{4,0},{5,1},{6,2},{7,3},{8,12},{9,13},{10,... | collective-permute-start | bytes 1572872 | tf_op jit(solution)/shard_map/ppermute | solution.py:222
  6.7 7.7 %collective-permute-start = (bf16[256,512]{1,0:T(8,128)(2,1)}, bf16[256,512]{1,0:T(8,128)(2,1)S(1)}, u32[]{:S(2)}, u32[]{:S(2)}) collective-permute-start(bf16[256,512]{1,0:T(8,128)(2,1)} %state.1), channel_id=1, source_target_pairs={{0,16},{16,0},{1,17},{17,1},{2,18},{18,2},{3,19},{19,3},{4,20},{20... | collective-permute-start | bytes 786440 | tf_op jit(solution)/shard_map/ppermute | solution.py:24
  10.4 44.4 %collective-permute-start.15 = (bf16[7,64,1024]{2,1,0:T(8,128)(2,1)}, bf16[7,64,1024]{2,1,0:T(8,128)(2,1)}, u32[]{:S(2)}, u32[]{:S(2)}) collective-permute-start(bf16[7,64,1024]{2,1,0:T(8,128)(2,1)} %slice.88), channel_id=1, source_target_pairs={{0,2},{1,3},{2,0},{3,1},{4,6},{5,7},{6,4},{7,5},{8,10},{9,11},{10,... | collective-permute-start | bytes 2752520 | tf_op jit(solution)/shard_map/ppermute | solution.py:24
  14.4 1.0 copy-start.1
  15.4 57.9 %copy-start.3 = (bf16[1,16,128,128]{3,2,1,0:T(8,128)(2,1)S(1)}, bf16[1,16,128,128]{3,2,1,0:T(8,128)(2,1)}, u32[]{:S(2)}) copy-start(bf16[1,16,128,128]{3,2,1,0:T(8,128)(2,1)} %param.21) | copy-start | bytes 1572868
  17.3 4.4 %collective-permute-start.1 = (bf16[144,256]{1,0:T(8,128)(2,1)S(1)}, bf16[144,256]{1,0:T(8,128)(2,1)S(1)}, u32[]{:S(2)}, u32[]{:S(2)}) collective-permute-start(bf16[144,256]{1,0:T(8,128)(2,1)S(1)} %get-tuple-element.72), channel_id=1, source_target_pairs={{0,4},{1,5},{2,6},{3,7},{4,0},{5,1},{6,2},{7,3},{8,12},{9,13},{10,... | collective-permute-start | bytes 221192 | tf_op jit(solution)/shard_map/ppermute | solution.py:222
  17.6 8.0 %collective-permute-start.2 = (bf16[144,256]{1,0:T(8,128)(2,1)S(1)}, bf16[144,256]{1,0:T(8,128)(2,1)S(1)}, u32[]{:S(2)}, u32[]{:S(2)}) collective-permute-start(bf16[144,256]{1,0:T(8,128)(2,1)S(1)} %get-tuple-element.73), channel_id=1, source_target_pairs={{0,8},{1,9},{2,10},{3,11},{4,12},{5,13},{6,14},{7,15},{8,0},{9,1},... | collective-permute-start | bytes 221192 | tf_op jit(solution)/shard_map/ppermute | solution.py:222
  21.6 0.7 copy-start.15
  22.3 6.5 %collective-permute-start.3 = (bf16[144,256]{1,0:T(8,128)(2,1)}, bf16[144,256]{1,0:T(8,128)(2,1)}, u32[]{:S(2)}, u32[]{:S(2)}) collective-permute-start(bf16[144,256]{1,0:T(8,128)(2,1)} %get-tuple-element.74), channel_id=1, source_target_pairs={{0,12},{1,13},{2,14},{3,15},{4,8},{5,9},{6,10},{7,11},{8,4},{9,5},... | collective-permute-start | bytes 221192 | tf_op jit(solution)/shard_map/ppermute | solution.py:222
  25.6 0.6 copy-start.17
  26.3 28.4 %collective-permute-start.16 = (bf16[5,64,1024]{2,1,0:T(8,128)(2,1)}, bf16[5,64,1024]{2,1,0:T(8,128)(2,1)S(1)}, u32[]{:S(2)}, u32[]{:S(2)}) collective-permute-start(bf16[5,64,1024]{2,1,0:T(8,128)(2,1)} %slice.89), channel_id=1, source_target_pairs={{0,2},{1,3},{2,0},{3,1},{4,6},{5,7},{6,4},{7,5},{8,10},{9,11},{10,... | collective-permute-start | bytes 1966088 | tf_op jit(solution)/shard_map/ppermute | solution.py:24
  28.8 44.5 %collective-permute-start.14 = (bf16[12,64,1024]{2,1,0:T(8,128)(2,1)S(1)}, bf16[12,64,1024]{2,1,0:T(8,128)(2,1)}, u32[]{:S(2)}, u32[]{:S(2)}) collective-permute-start(bf16[12,64,1024]{2,1,0:T(8,128)(2,1)S(1)} %copy-done), channel_id=1, source_target_pairs={{0,1},{1,0},{2,3},{3,2},{4,5},{5,4},{6,7},{7,6},{8,9},{9,8},{10,11... | collective-permute-start | bytes 4718600 | tf_op jit(solution)/shard_map/ppermute | solution.py:24
  28.8 0.9 copy-start.14
  29.7 0.9 copy-start.16
  30.5 0.9 copy-start.18
  33.6 18.0 %collective-permute-start.4 = (bf16[4,128,256]{2,1,0:T(8,128)(2,1)}, bf16[4,128,256]{2,1,0:T(8,128)(2,1)}, u32[]{:S(2)}, u32[]{:S(2)}) collective-permute-start(bf16[4,128,256]{2,1,0:T(8,128)(2,1)} %get-tuple-element.76.refs_0_), channel_id=1, source_target_pairs={{0,2},{1,3},{2,0},{3,1},{4,6},{5,7},{6,4},{7,5},{8,10},{9,11},{10,... | collective-permute-start | bytes 786440 | tf_op jit(solution)/shard_map/ppermute | solution.py:24
  36.5 16.3 %collective-permute-start.5 = (bf16[4,128,256]{2,1,0:T(8,128)(2,1)}, bf16[4,128,256]{2,1,0:T(8,128)(2,1)S(1)}, u32[]{:S(2)}, u32[]{:S(2)}) collective-permute-start(bf16[4,128,256]{2,1,0:T(8,128)(2,1)} %get-tuple-element.76.refs_0_), channel_id=1, source_target_pairs={{0,16},{16,0},{1,17},{17,1},{2,18},{18,2},{3,19},{19,3},{4,20},{20... | collective-permute-start | bytes 786440 | tf_op jit(solution)/shard_map/ppermute | solution.py:24
  51.7 1.7 %collective-permute-start.7 = (bf16[4,128,256]{2,1,0:T(8,128)(2,1)}, bf16[4,128,256]{2,1,0:T(8,128)(2,1)S(1)}, u32[]{:S(2)}, u32[]{:S(2)}) collective-permute-start(bf16[4,128,256]{2,1,0:T(8,128)(2,1)} %get-tuple-element.76.refs_0_), channel_id=1, source_target_pairs={{0,1},{1,0},{2,3},{3,2},{4,5},{5,4},{6,7},{7,6},{8,9},{9,8},{10,11... | collective-permute-start | bytes 786440 | tf_op jit(solution)/shard_map/ppermute | solution.py:24
  52.8 14.5 %collective-permute-start.13 = (bf16[16,128,128]{2,1,0:T(8,128)(2,1)S(1)}, bf16[16,128,128]{2,1,0:T(8,128)(2,1)}, u32[]{:S(2)}, u32[]{:S(2)}) collective-permute-start(bf16[16,128,128]{2,1,0:T(8,128)(2,1)S(1)} %broadcast_select_fusion), channel_id=1, source_target_pairs={{0,8},{1,9},{2,10},{3,11},{8,12},{9,13},{10,14},{11,15},{12,4},{13... | collective-permute-start | bytes 1572872 | tf_op jit(solution)/shard_map/ppermute | solution.py:222
  53.4 0.7 copy-start.7
  54.1 8.7 %collective-permute-start.6 = (bf16[4,128,256]{2,1,0:T(8,128)(2,1)}, bf16[4,128,256]{2,1,0:T(8,128)(2,1)}, u32[]{:S(2)}, u32[]{:S(2)}) collective-permute-start(bf16[4,128,256]{2,1,0:T(8,128)(2,1)} %collective-permute-done.4.refs_1_), channel_id=1, source_target_pairs={{0,16},{16,0},{1,17},{17,1},{2,18},{18,2},{3,19},{19,3},{4,20},{20... | collective-permute-start | bytes 786440 | tf_op jit(solution)/shard_map/ppermute | solution.py:24
  54.7 8.8 %collective-permute-start.8 = (bf16[4,128,256]{2,1,0:T(8,128)(2,1)}, bf16[4,128,256]{2,1,0:T(8,128)(2,1)S(1)}, u32[]{:S(2)}, u32[]{:S(2)}) collective-permute-start(bf16[4,128,256]{2,1,0:T(8,128)(2,1)} %collective-permute-done.4.refs_1_), channel_id=1, source_target_pairs={{0,1},{1,0},{2,3},{3,2},{4,5},{5,4},{6,7},{7,6},{8,9},{9,8},{10,11... | collective-permute-start | bytes 786440 | tf_op jit(solution)/shard_map/ppermute | solution.py:24
  54.8 25.6 %collective-permute-start.17 = (bf16[7,64,1024]{2,1,0:T(8,128)(2,1)}, bf16[7,64,1024]{2,1,0:T(8,128)(2,1)}, u32[]{:S(2)}, u32[]{:S(2)}) collective-permute-start(bf16[7,64,1024]{2,1,0:T(8,128)(2,1)} %collective-permute-done.15.refs_0_), channel_id=1, source_target_pairs={{0,1},{1,0},{2,3},{3,2},{4,5},{5,4},{6,7},{7,6},{8,9},{9,8},{10,11... | collective-permute-start | bytes 2752520 | tf_op jit(solution)/shard_map/ppermute | solution.py:24
  62.8 5.8 %collective-permute-start.9 = (bf16[4,128,256]{2,1,0:T(8,128)(2,1)S(1)}, bf16[4,128,256]{2,1,0:T(8,128)(2,1)S(1)}, u32[]{:S(2)}, u32[]{:S(2)}) collective-permute-start(bf16[4,128,256]{2,1,0:T(8,128)(2,1)S(1)} %collective-permute-done.5.refs_2_), channel_id=1, source_target_pairs={{0,1},{1,0},{2,3},{3,2},{4,5},{5,4},{6,7},{7,6},{8,9},{9,8},{10,11... | collective-permute-start | bytes 786440 | tf_op jit(solution)/shard_map/ppermute | solution.py:24
  62.8 0.7 copy-start.5
  63.5 0.7 copy-start.9
  64.2 16.2 %collective-permute-start.18 = (bf16[5,64,1024]{2,1,0:T(8,128)(2,1)S(1)}, bf16[5,64,1024]{2,1,0:T(8,128)(2,1)}, u32[]{:S(2)}, u32[]{:S(2)}) collective-permute-start(bf16[5,64,1024]{2,1,0:T(8,128)(2,1)S(1)} %collective-permute-done.16.refs_1_), channel_id=1, source_target_pairs={{0,1},{1,0},{2,3},{3,2},{4,5},{5,4},{6,7},{7,6},{8,9},{9,8},{10,11... | collective-permute-start | bytes 1966088 | tf_op jit(solution)/shard_map/ppermute | solution.py:24
  67.3 17.1 %collective-permute-start.22 = (bf16[16,128,128]{2,1,0:T(8,128)(2,1)}, bf16[16,128,128]{2,1,0:T(8,128)(2,1)}, u32[]{:S(2)}, u32[]{:S(2)}) collective-permute-start(bf16[16,128,128]{2,1,0:T(8,128)(2,1)} %collective-permute-done.13.refs_10_), channel_id=1, source_target_pairs={{8,12},{9,13},{10,14},{11,15},{4,0},{5,1},{6,2},{7,3},{24,28},{25,... | collective-permute-start | bytes 1572872 | tf_op jit(solution)/shard_map/ppermute | solution.py:222
  68.6 0.7 copy-start.11
  69.3 4.0 %collective-permute-start.10 = (bf16[4,128,256]{2,1,0:T(8,128)(2,1)}, bf16[4,128,256]{2,1,0:T(8,128)(2,1)}, u32[]{:S(2)}, u32[]{:S(2)}) collective-permute-start(bf16[4,128,256]{2,1,0:T(8,128)(2,1)} %collective-permute-done.6.refs_3_), channel_id=1, source_target_pairs={{0,1},{1,0},{2,3},{3,2},{4,5},{5,4},{6,7},{7,6},{8,9},{9,8},{10,11... | collective-permute-start | bytes 786440 | tf_op jit(solution)/shard_map/ppermute | solution.py:24
  73.3 1.0 copy-start.6
  74.2 0.9 copy-start.8
  75.2 0.9 copy-start.10
  76.1 0.9 copy-start.12
  83.3 12.6 %collective-permute-start.25 = (bf16[256,512]{1,0:T(8,128)(2,1)S(1)}, bf16[256,512]{1,0:T(8,128)(2,1)S(1)}, u32[]{:S(2)}, u32[]{:S(2)}) collective-permute-start(bf16[256,512]{1,0:T(8,128)(2,1)S(1)} %get-tuple-element.88), channel_id=1, source_target_pairs={{0,16},{16,0},{1,17},{17,1},{2,18},{18,2},{3,19},{19,3},{4,20},{20... | collective-permute-start | bytes 786440 | tf_op jit(solution)/shard_map/ppermute | solution.py:24
  86.8 11.6 %collective-permute-start.23 = (bf16[256,512]{1,0:T(8,128)(2,1)S(1)}, bf16[256,512]{1,0:T(8,128)(2,1)S(1)}, u32[]{:S(2)}, u32[]{:S(2)}) collective-permute-start(bf16[256,512]{1,0:T(8,128)(2,1)S(1)} %get-tuple-element.86), channel_id=1, source_target_pairs={{0,16},{16,0},{1,17},{17,1},{2,18},{18,2},{3,19},{19,3},{4,20},{20... | collective-permute-start | bytes 786440 | tf_op jit(solution)/shard_map/ppermute | solution.py:24
  93.7 15.4 %copy-start.2 = (bf16[256,512]{1,0:T(8,128)(2,1)S(1)}, bf16[256,512]{1,0:T(8,128)(2,1)}, u32[]{:S(2)}) copy-start(bf16[256,512]{1,0:T(8,128)(2,1)} %state.1) | copy-start | bytes 786436
  93.8 15.4 %copy-start.4 = (bf16[1024,512]{1,0:T(8,128)(2,1)S(1)}, bf16[1024,512]{1,0:T(8,128)(2,1)}, u32[]{:S(2)}) copy-start(bf16[1024,512]{1,0:T(8,128)(2,1)} %weight.1) | copy-start | bytes 3145732
  93.8 15.4 %copy-start.20 = (f32[512]{0:T(512)S(1)}, f32[512]{0:T(512)}, u32[]{:S(2)}) copy-start(f32[512]{0:T(512)} %param.19) | copy-start | bytes 6148
  93.8 9.3 %collective-permute-start.20 = (bf16[256,512]{1,0:T(8,128)(2,1)S(1)}, bf16[256,512]{1,0:T(8,128)(2,1)S(1)}, u32[]{:S(2)}, u32[]{:S(2)}) collective-permute-start(bf16[256,512]{1,0:T(8,128)(2,1)S(1)} %get-tuple-element.83), channel_id=1, source_target_pairs={{0,16},{16,0},{1,17},{17,1},{2,18},{18,2},{3,19},{19,3},{4,20},{20... | collective-permute-start | bytes 786440 | tf_op jit(solution)/shard_map/ppermute | solution.py:24
  94.8 14.8 %collective-permute-start.19 = (bf16[256,512]{1,0:T(8,128)(2,1)S(1)}, bf16[256,512]{1,0:T(8,128)(2,1)S(1)}, u32[]{:S(2)}, u32[]{:S(2)}) collective-permute-start(bf16[256,512]{1,0:T(8,128)(2,1)S(1)} %get-tuple-element.81), channel_id=1, source_target_pairs={{0,16},{16,0},{1,17},{17,1},{2,18},{18,2},{3,19},{19,3},{4,20},{20... | collective-permute-start | bytes 786440 | tf_op jit(solution)/shard_map/ppermute | solution.py:24
  96.0 12.4 %collective-permute-start.26 = (bf16[256,512]{1,0:T(8,128)(2,1)S(1)}, bf16[256,512]{1,0:T(8,128)(2,1)S(1)}, u32[]{:S(2)}, u32[]{:S(2)}) collective-permute-start(bf16[256,512]{1,0:T(8,128)(2,1)S(1)} %add_convert_fusion.1), channel_id=1, source_target_pairs={{0,4},{1,5},{2,6},{3,7},{4,12},{5,13},{6,14},{7,15},{12,8},{13,9},... | collective-permute-start | bytes 786440 | tf_op jit(solution)/shard_map/ppermute | solution.py:222
  98.4 18.6 %copy-start.19 = (f32[512]{0:T(512)S(1)}, f32[512]{0:T(512)}, u32[]{:S(2)}) copy-start(f32[512]{0:T(512)} %param.20) | copy-start | bytes 6148
  98.5 13.1 %collective-permute-start.24 = (bf16[256,512]{1,0:T(8,128)(2,1)S(1)}, bf16[256,512]{1,0:T(8,128)(2,1)S(1)}, u32[]{:S(2)}, u32[]{:S(2)}) collective-permute-start(bf16[256,512]{1,0:T(8,128)(2,1)S(1)} %add_convert_fusion.2), channel_id=1, source_target_pairs={{0,12},{1,13},{2,14},{3,15},{12,0},{13,1},{14,2},{15,3},{16,28},{1... | collective-permute-start | bytes 786440 | tf_op jit(solution)/shard_map/ppermute | solution.py:222
  103.2 13.8 %collective-permute-start.21 = (bf16[256,512]{1,0:T(8,128)(2,1)S(1)}, bf16[256,512]{1,0:T(8,128)(2,1)S(1)}, u32[]{:S(2)}, u32[]{:S(2)}) collective-permute-start(bf16[256,512]{1,0:T(8,128)(2,1)S(1)} %add_convert_fusion.3), channel_id=1, source_target_pairs={{0,4},{1,5},{2,6},{3,7},{4,0},{5,1},{6,2},{7,3},{8,12},{9,13},{10,... | collective-permute-start | bytes 786440 | tf_op jit(solution)/shard_map/ppermute | solution.py:222
  108.4 8.6 %collective-permute-start.27 = (bf16[256,512]{1,0:T(8,128)(2,1)S(1)}, bf16[256,512]{1,0:T(8,128)(2,1)S(1)}, u32[]{:S(2)}, u32[]{:S(2)}) collective-permute-start(bf16[256,512]{1,0:T(8,128)(2,1)S(1)} %add_convert_fusion), channel_id=1, source_target_pairs={{4,8},{5,9},{6,10},{7,11},{8,4},{9,5},{10,6},{11,7},{20,24},{21,25... | collective-permute-start | bytes 786440 | tf_op jit(solution)/shard_map/ppermute | solution.py:222
  (2 other events, 1.2 us)

commit v6 on v5

--- a/solution.py
+++ b/solution.py
@@ -79,18 +79,15 @@
     return loads
 
 
-def start_weights(members, member, weights, held, sems):
+def start_weights(members, member, weights, low, held, sems):
     half = members // 2
-    per_block = len(weights) // half
     loads = []
-    for n, ref in enumerate(weights):
-        i, p = n // per_block, n % per_block
+    for i, ref in enumerate(weights):
         block = ref.shape[1]
-        low = sum(weights[i * per_block + q].shape[0] for q in range(p))
         start = pl.multiple_of(lax.bitwise_xor(i, member % half) * block, block)
         loads.append(
             pltpu.make_async_copy(
-                ref, held.at[pl.ds(low, ref.shape[0]), pl.ds(start, block), :], sems.at[n]
+                ref, held.at[pl.ds(low, ref.shape[0]), pl.ds(start, block), :], sems.at[i]
             )
         )
         loads[-1].start()
@@ -136,9 +133,10 @@
             outs[r][t * tile_rows:(t + 1) * tile_rows] = acc[t, :, pl.ds(start, own)].astype(outs[r].dtype)
 
 
-def early_kernel(members, places, way_counts, n_weights, table, *refs):
-    states, tiles, weights, rest = take(refs, len(places), sum(way_counts), n_weights)
-    made, held, rows_held, lists, state_sem, tile_sem, weight_sem = rest
+def early_kernel(members, places, way_counts, table, *refs):
+    half = members // 2
+    states, tiles, weights, others, rest = take(refs, len(places), sum(way_counts), half, half)
+    made, held, other, rows_held, lists, state_sem, tile_sem, weight_sem, other_sem = rest
     slots = lists.shape[1]
     chunks, rows = states[0].shape[0], states[0].shape[1]
     loads = []
@@ -148,7 +146,8 @@
         loads.append(pltpu.make_async_copy(ref, to, state_sem.at[n]))
         loads[-1].start()
     tile_loads = start_tiles(way_counts, table[4, HOME + 2], tiles, lists, tile_sem)
-    weight_loads = start_weights(members, table[4, HOME], weights, held, weight_sem)
+    weight_loads = start_weights(members, table[4, HOME], weights, 0, held, weight_sem)
+    weight_loads += start_weights(members, table[4, HOME], others, 0, other, other_sem)
     for load in loads:
         load.wait()
     swapped = table[4, HOME] >= members // 2
@@ -159,11 +158,13 @@
         load.wait()
 
 
-def first_kernel(members, j, n_rel, n_weights, table, made, own, *refs):
-    weights, outs, rest = take(refs, n_weights, n_rel)
+def first_kernel(members, j, n_rel, table, made, own, begun, *refs):
+    weights, outs, rest = take(refs, members // 2, n_rel)
     other, acc, weight_sem = rest
+    del begun
     slots = made.shape[1]
-    for load in start_weights(members, table[4, HOME], weights, other, weight_sem):
+    low = other.shape[0] - weights[0].shape[0]
+    for load in start_weights(members, table[4, HOME], weights, low, other, weight_sem):
         load.wait()
     add_messages(table[4, j], table, j * slots, made.at[j], own, other, acc)
     put_messages(n_rel, table[4, HOME + 1], acc, outs)
@@ -286,7 +287,7 @@
         last,
     ])
 
-    cut = max(1, rel_dev * 7 // 12)
+    cut = max(1, rel_dev * 2 // 3)
     parts = (rel_weight[:cut], rel_weight[cut:])
     bits = [1 << b for b in reversed(range(members.bit_length() - 1))]
     rel_bits = [1 << b for b in reversed(range(n_rel.bit_length() - 1))]
@@ -317,8 +318,8 @@
         weights = weights + more
         order = order + [o | bit for o in order]
     weights = [weights[order.index(i)] for i in range(members)]
-    own_weights = [v for held in weights[:members // 2] for v in held]
-    other_weights = [v for held in weights[members // 2:] for v in held]
+    own_weights = [held[0] for held in weights[:members // 2]]
+    other_weights = [[held[n] for held in weights[members // 2:]] for n in range(2)]
 
     gate_open = pl.pallas_call(
         functools.partial(gate_kernel, n_rel),
@@ -336,17 +337,18 @@
     products = jax.ShapeDtypeStruct((len(early), slots, tile_rows, width), BF16)
     acc_scratch = pltpu.VMEM((per_tile + 1, tile_rows, features), F32)
 
-    def call(body, operands, in_specs, out_shape, scratch, flops):
+    def call(body, operands, in_specs, out_shape, scratch, flops, aliases=None):
         return pl.pallas_call(
             body,
             out_shape=out_shape,
             in_specs=[SMEM] + in_specs,
             out_specs=[VMEM] * len(out_shape),
             scratch_shapes=scratch,
+            input_output_aliases=aliases or {},
             cost_estimate=pl.CostEstimate(
                 flops=flops, bytes_accessed=rel_dev * width * features, transcendentals=0
             ),
-            compiler_params=pltpu.CompilerParams(vmem_limit_bytes=16 << 20),
+            compiler_params=pltpu.CompilerParams(vmem_limit_bytes=20 << 20),
         )(table, *operands)
 
     def message_shapes(count):
@@ -356,12 +358,14 @@
 
     slot_flops = 2 * slots * tile_rows * width
     flat = [t for j in early for t in tiles[j]]
-    made, own_half, rows_held = call(
-        functools.partial(early_kernel, members, tuple(places), early_ways, len(own_weights)),
-        [*states, *flat, *own_weights],
-        [HBM if v is values or v is rel_weight else ANY for v in [*states, *flat, *own_weights]],
+    operands = [*states, *flat, *own_weights, *other_weights[0]]
+    made, own_half, begun, rows_held = call(
+        functools.partial(early_kernel, members, tuple(places), early_ways),
+        operands,
+        [HBM if v is values or v is rel_weight else ANY for v in operands],
         [
             products,
+            jax.ShapeDtypeStruct(half_shape, BF16),
             jax.ShapeDtypeStruct(half_shape, BF16),
             jax.ShapeDtypeStruct((members * chunks, ent_dev, width), BF16),
         ],
@@ -369,17 +373,19 @@
             pltpu.VMEM((len(early), slots, tile_rows, tile_rows), BF16),
             pltpu.SemaphoreType.DMA((len(states),)),
             pltpu.SemaphoreType.DMA((len(early),)),
-            pltpu.SemaphoreType.DMA((len(own_weights),)),
+            pltpu.SemaphoreType.DMA((members // 2,)),
+            pltpu.SemaphoreType.DMA((members // 2,)),
         ],
         len(early) * slot_flops * tile_rows,
     )
     *two, other_half = call(
-        functools.partial(first_kernel, members, 2, n_rel, len(other_weights)),
-        [made, own_half, *other_weights],
-        [VMEM] * 2 + [ANY] * len(other_weights),
+        functools.partial(first_kernel, members, 2, n_rel),
+        [made, own_half, begun, *other_weights[1]],
+        [VMEM] * 3 + [ANY] * (members // 2),
         message_shapes(1) + [jax.ShapeDtypeStruct(half_shape, BF16)],
-        [acc_scratch, pltpu.SemaphoreType.DMA((len(other_weights),))],
+        [acc_scratch, pltpu.SemaphoreType.DMA((members // 2,))],
         slot_flops * features,
+        {3: n_rel},
     )
     results = {2: two}
     for j in (1, 0):

time: 119 us -> 120 us (level)
  waiting for transfers between devices: 35.8 us -> 43.2 us
  local copies, waits for them, and re-layouts: 20.6 us -> 17.5 us
  other arithmetic: 4.75 us -> 1.91 us
    ppermute x11, waiting for transfers between devices: 12.7 us -> 26.6 us  [along(): return lax.ppermute(value, 'ent', perm)]
    ppermute x17, waiting for transfers between devices: 23.1 us -> 16.6 us  [swap(): return lax.ppermute(value, axis, [(i, i ^ bit) for i in range(size)])]
    unnamed x45 -> x43, local copies, waits for them, and re-layouts: 12.7 us -> 11.7 us
  transfers between devices with their start and end apart: 28 -> 28, of which waited for: 10 -> 10; matrix products, arithmetic and copies ran while one was open for 11% -> 4% of each run, Pallas kernels for 13% -> 12%
where the time goes in v6:
time: 120 us; the launch traced here: 119 us
  waiting for transfers between devices  43.2 us (36%)
  starting transfers between devices  40.2 us (34%)
  local copies, waits for them, and re-layouts  17.5 us (15%)
  Pallas kernels  15.5 us (13%)
  other arithmetic  1.91 us (2%)
    ppermute x11, waiting for transfers between devices, along(): return lax.ppermute(value, 'ent', perm)  26.6 us
    ppermute x11, starting transfers between devices, along(): return lax.ppermute(value, 'ent', perm)  24.3 us
    ppermute x17, waiting for transfers between devices, swap(): return lax.ppermute(value, axis, [(i, i ^ bit) for i in range(size)])  16.6 us
    ppermute x17, starting transfers between devices, swap(): return lax.ppermute(value, axis, [(i, i ^ bit) for i in range(size)])  15.9 us
    pallas_call x5, Pallas kernels, call(): pl.pallas_call(body, out_shape=out_shape, in_specs=[SMEM] + in_specs, out...  11.9 us
    unnamed x43, local copies, waits for them, and re-layouts  11.7 us
    slice x2, local copies, waits for them, and re-layouts, shards(): parts = (rel_weight[:cut], rel_weight[cut:])  4.32 us
  transfers between devices with their start and end apart: 28, of which 10 were waited for; matrix products, arithmetic and copies ran while one was open for 4% of the time, Pallas kernels for 12%

profile of v6, /device:TPU:0, one launch (start us, length us, event | category | flops | bytes accessed | tf_op | source)
XLA Modules:
  0.0 119.3 jit_solution(13813497278789287429)
XLA Ops:
  0.0 2.4 %slice.88 = bf16[8,64,1024]{2,1,0:T(8,128)(2,1)} slice(bf16[12,64,1024]{2,1,0:T(8,128)(2,1)} %refs_11_.1), slice={[0:8], [0:64], [0:1024]} | slice | bytes 2097152 | tf_op jit(solution)/shard_map/slice | solution.py:291
  2.4 3.0 %collective-permute-start.15 = (bf16[8,64,1024]{2,1,0:T(8,128)(2,1)}, bf16[8,64,1024]{2,1,0:T(8,128)(2,1)}, u32[]{:S(2)}, u32[]{:S(2)}) collective-permute-start(bf16[8,64,1024]{2,1,0:T(8,128)(2,1)} %slice.88), channel_id=1, source_target_pairs={{0,2},{1,3},{2,0},{3,1},{4,6},{5,7},{6,4},{7,5},{8,10},{9,11},{10,... | collective-permute-start | bytes 3145736 | tf_op jit(solution)/shard_map/ppermute | solution.py:24
  5.4 1.5 %collective-permute-start = (bf16[256,512]{1,0:T(8,128)(2,1)}, bf16[256,512]{1,0:T(8,128)(2,1)S(1)}, u32[]{:S(2)}, u32[]{:S(2)}) collective-permute-start(bf16[256,512]{1,0:T(8,128)(2,1)} %state.1), channel_id=1, source_target_pairs={{0,16},{16,0},{1,17},{17,1},{2,18},{18,2},{3,19},{19,3},{4,20},{20... | collective-permute-start | bytes 786440 | tf_op jit(solution)/shard_map/ppermute | solution.py:24
  7.0 0.7 convert_element_type.47
  8.5 4.9 %collective-permute-done.refs_1_ = bf16[256,512]{1,0:T(8,128)(2,1)S(1)} collective-permute-done((bf16[256,512]{1,0:T(8,128)(2,1)}, bf16[256,512]{1,0:T(8,128)(2,1)S(1)}, u32[]{:S(2)}, u32[]{:S(2)}) %collective-permute-start) | collective-permute-done | bytes 262176 | tf_op jit(solution)/shard_map/ppermute | solution.py:24
  13.4 0.9 copy-done.1
  14.4 1.3 %pack.1 = (bf16[144,256]{1,0:T(8,128)(2,1)S(1)}, bf16[144,256]{1,0:T(8,128)(2,1)S(1)}, bf16[144,256]{1,0:T(8,128)(2,1)S(1)}, bf16[144,256]{1,0:T(8,128)(2,1)}) custom-call(s32[3,4]{1,0:T(4,128)S(1)} %add_add_fusion.where, bf16[16,256]{1,0:T(8,128)(2,1)S(1)} %scatter.15.note, bf16[256,512]{1,0:T(8,128)(2,1)S(1)} %copy-done.1, ...), custom_call_target="tpu_custom_call" | custom-call | tf_op jit(solution)/shard_map/pack/pallas_call | solution.py:252
  15.7 1.6 %collective-permute-start.1 = (bf16[144,256]{1,0:T(8,128)(2,1)S(1)}, bf16[144,256]{1,0:T(8,128)(2,1)S(1)}, u32[]{:S(2)}, u32[]{:S(2)}) collective-permute-start(bf16[144,256]{1,0:T(8,128)(2,1)S(1)} %get-tuple-element.73), channel_id=1, source_target_pairs={{0,4},{1,5},{2,6},{3,7},{4,0},{5,1},{6,2},{7,3},{8,12},{9,13},{10,... | collective-permute-start | bytes 221192 | tf_op jit(solution)/shard_map/ppermute | solution.py:223
  17.9 4.4 %collective-permute-start.11 = (bf16[16,128,128]{2,1,0:T(8,128)(2,1)}, bf16[16,128,128]{2,1,0:T(8,128)(2,1)}, u32[]{:S(2)}, u32[]{:S(2)}) collective-permute-start(bf16[16,128,128]{2,1,0:T(8,128)(2,1)} %bitcast.16), channel_id=1, source_target_pairs={{0,4},{1,5},{2,6},{3,7},{4,0},{5,1},{6,2},{7,3},{8,12},{9,13},{10,... | collective-permute-start | bytes 1572872 | tf_op jit(solution)/shard_map/ppermute | solution.py:223
  22.4 1.9 %slice.89 = bf16[4,64,1024]{2,1,0:T(8,128)(2,1)} slice(bf16[12,64,1024]{2,1,0:T(8,128)(2,1)} %refs_11_.1), slice={[8:12], [0:64], [0:1024]} | slice | bytes 1048576 | tf_op jit(solution)/shard_map/slice | solution.py:291
  24.7 10.9 %collective-permute-done.2.refs_2_ = bf16[144,256]{1,0:T(8,128)(2,1)S(1)} collective-permute-done((bf16[144,256]{1,0:T(8,128)(2,1)S(1)}, bf16[144,256]{1,0:T(8,128)(2,1)S(1)}, u32[]{:S(2)}, u32[]{:S(2)}) %collective-permute-start.2) | collective-permute-done | bytes 73760 | tf_op jit(solution)/shard_map/ppermute | solution.py:223
  36.3 2.6 %collective-permute-start.3 = (bf16[144,256]{1,0:T(8,128)(2,1)}, bf16[144,256]{1,0:T(8,128)(2,1)}, u32[]{:S(2)}, u32[]{:S(2)}) collective-permute-start(bf16[144,256]{1,0:T(8,128)(2,1)} %get-tuple-element.75), channel_id=1, source_target_pairs={{0,12},{1,13},{2,14},{3,15},{4,8},{5,9},{6,10},{7,11},{8,4},{9,5},... | collective-permute-start | bytes 221192 | tf_op jit(solution)/shard_map/ppermute | solution.py:223
  39.0 3.8 %collective-permute-done.3.refs_3_ = bf16[144,256]{1,0:T(8,128)(2,1)} collective-permute-done((bf16[144,256]{1,0:T(8,128)(2,1)}, bf16[144,256]{1,0:T(8,128)(2,1)}, u32[]{:S(2)}, u32[]{:S(2)}) %collective-permute-start.3) | collective-permute-done | bytes 73760 | tf_op jit(solution)/shard_map/ppermute | solution.py:223
  43.4 0.9 copy-done.18
  44.3 0.9 stk.1
  45.8 1.5 %collective-permute-start.5 = (bf16[4,128,256]{2,1,0:T(8,128)(2,1)S(1)}, bf16[4,128,256]{2,1,0:T(8,128)(2,1)S(1)}, u32[]{:S(2)}, u32[]{:S(2)}) collective-permute-start(bf16[4,128,256]{2,1,0:T(8,128)(2,1)S(1)} %get-tuple-element.77.refs_0_), channel_id=1, source_target_pairs={{0,16},{16,0},{1,17},{17,1},{2,18},{18,2},{3,19},{19,3},{4,20},{20... | collective-permute-start | bytes 786440 | tf_op jit(solution)/shard_map/ppermute | solution.py:24
  47.9 6.1 %collective-permute-done.4.refs_1_ = bf16[4,128,256]{2,1,0:T(8,128)(2,1)S(1)} collective-permute-done((bf16[4,128,256]{2,1,0:T(8,128)(2,1)S(1)}, bf16[4,128,256]{2,1,0:T(8,128)(2,1)S(1)}, u32[]{:S(2)}, u32[]{:S(2)}) %collective-permute-start.4) | collective-permute-done | bytes 262176 | tf_op jit(solution)/shard_map/ppermute | solution.py:24
  54.2 1.5 %collective-permute-start.6 = (bf16[4,128,256]{2,1,0:T(8,128)(2,1)S(1)}, bf16[4,128,256]{2,1,0:T(8,128)(2,1)}, u32[]{:S(2)}, u32[]{:S(2)}) collective-permute-start(bf16[4,128,256]{2,1,0:T(8,128)(2,1)S(1)} %collective-permute-done.4.refs_1_), channel_id=1, source_target_pairs={{0,16},{16,0},{1,17},{17,1},{2,18},{18,2},{3,19},{19,3},{4,20},{20... | collective-permute-start | bytes 786440 | tf_op jit(solution)/shard_map/ppermute | solution.py:24
  55.7 0.7 copy-done.11
  56.5 0.7 copy-done.7
  57.3 4.7 %collective-permute-done.6.refs_3_ = bf16[4,128,256]{2,1,0:T(8,128)(2,1)} collective-permute-done((bf16[4,128,256]{2,1,0:T(8,128)(2,1)S(1)}, bf16[4,128,256]{2,1,0:T(8,128)(2,1)}, u32[]{:S(2)}, u32[]{:S(2)}) %collective-permute-start.6) | collective-permute-done | bytes 262176 | tf_op jit(solution)/shard_map/ppermute | solution.py:24
  62.0 0.7 copy-done.13
  63.2 0.7 copy-done.9
  64.0 3.6 %collective-permute-done.13.refs_10_ = bf16[16,128,128]{2,1,0:T(8,128)(2,1)} collective-permute-done((bf16[16,128,128]{2,1,0:T(8,128)(2,1)S(1)}, bf16[16,128,128]{2,1,0:T(8,128)(2,1)}, u32[]{:S(2)}, u32[]{:S(2)}) %collective-permute-start.13) | collective-permute-done | bytes 524320 | tf_op jit(solution)/shard_map/ppermute | solution.py:223
  67.6 1.3 %collective-permute-start.22 = (bf16[16,128,128]{2,1,0:T(8,128)(2,1)}, bf16[16,128,128]{2,1,0:T(8,128)(2,1)}, u32[]{:S(2)}, u32[]{:S(2)}) collective-permute-start(bf16[16,128,128]{2,1,0:T(8,128)(2,1)} %collective-permute-done.13.refs_10_), channel_id=1, source_target_pairs={{8,12},{9,13},{10,14},{11,15},{4,0},{5,1},{6,2},{7,3},{24,28},{25,... | collective-permute-start | bytes 1572872 | tf_op jit(solution)/shard_map/ppermute | solution.py:223
  68.9 0.7 copy-done.15
  70.0 0.8 scatter.19
  71.5 0.9 copy-done.6
  72.5 0.9 copy-done.8
  73.4 0.9 copy-done.10
  74.4 0.9 copy-done.12
  75.3 0.9 copy-done.14
  76.3 0.9 copy-done.16
  77.2 3.3 %shard_map.82 = (bf16[3,16,128,256]{3,2,1,0:T(8,128)(2,1)S(1)}, bf16[12,128,1024]{2,1,0:T(8,128)(2,1)S(1)}, bf16[12,128,1024]{2,1,0:T(8,128)(2,1)S(1)}, bf16[16,256,256]{2,1,0:T(8,128)(2,1)S(1)}) custom-call(s32[5,64]{1,0:T(8,128)S(1)} %stack.26.table, bf16[4,128,256]{2,1,0:T(8,128)(2,1)S(1)} %copy-done.6, bf16[4,128,256]{2,1,0:T(8,128)(2,1)S(1)} %copy-done.8, ...), custom_call_target="tpu_custom_call" | custom-call | flops 402653184 | bytes 3145728 | tf_op jit(solution)/shard_map/pallas_call | solution.py:341
  80.6 2.3 %shard_map.83 = (f32[256,512]{1,0:T(8,128)S(1)}, bf16[256,512]{1,0:T(8,128)(2,1)S(1)}, bf16[12,128,1024]{2,1,0:T(8,128)(2,1)S(1)}) custom-call(s32[5,64]{1,0:T(8,128)S(1)} %stack.26.table, bf16[3,16,128,256]{3,2,1,0:T(8,128)(2,1)S(1)} %get-tuple-element.78.made, bf16[12,128,1024]{2,1,0:T(8,128)(2,1)S(1)} %get-tuple-element.79.own, ...), custom_call_target="tpu_custom_call", output_to_operand_aliasing={{2}: (3, {})} | custom-call | flops 1073741824 | bytes 3145728 | tf_op jit(solution)/shard_map/pallas_call | solution.py:341
  82.9 1.9 %collective-permute-start.25 = (bf16[256,512]{1,0:T(8,128)(2,1)S(1)}, bf16[256,512]{1,0:T(8,128)(2,1)S(1)}, u32[]{:S(2)}, u32[]{:S(2)}) collective-permute-start(bf16[256,512]{1,0:T(8,128)(2,1)S(1)} %get-tuple-element.90), channel_id=1, source_target_pairs={{0,16},{16,0},{1,17},{17,1},{2,18},{18,2},{3,19},{19,3},{4,20},{20... | collective-permute-start | bytes 786440 | tf_op jit(solution)/shard_map/ppermute | solution.py:24
  84.7 2.5 %shard_map.86 = (f32[256,512]{1,0:T(8,128)S(1)}, bf16[256,512]{1,0:T(8,128)(2,1)S(1)}) custom-call(s32[5,64]{1,0:T(8,128)S(1)} %stack.26.table, bf16[16,256,256]{2,1,0:T(8,128)(2,1)S(1)} %get-tuple-element.86.rows_held, bf16[12,128,1024]{2,1,0:T(8,128)(2,1)S(1)} %get-tuple-element.79.own, bf16[12,128,1024]{2,1,0:T(8,128)(2,1)S(1)} %get-tuple-element.81.other, ...), custom_call_target="tpu_custom_call" | custom-call | flops 1207959552 | bytes 3145728 | tf_op jit(solution)/shard_map/pallas_call | solution.py:341
  87.2 2.3 %collective-permute-start.23 = (bf16[256,512]{1,0:T(8,128)(2,1)S(1)}, bf16[256,512]{1,0:T(8,128)(2,1)S(1)}, u32[]{:S(2)}, u32[]{:S(2)}) collective-permute-start(bf16[256,512]{1,0:T(8,128)(2,1)S(1)} %get-tuple-element.88), channel_id=1, source_target_pairs={{0,16},{16,0},{1,17},{17,1},{2,18},{18,2},{3,19},{19,3},{4,20},{20... | collective-permute-start | bytes 786440 | tf_op jit(solution)/shard_map/ppermute | solution.py:24
  89.6 1.2 shard_map.85
  90.8 2.6 %shard_map.84 = (f32[256,512]{1,0:T(8,128)S(1)}, bf16[256,512]{1,0:T(8,128)(2,1)S(1)}) custom-call(s32[5,64]{1,0:T(8,128)S(1)} %stack.26.table, bf16[3,16,128,256]{3,2,1,0:T(8,128)(2,1)S(1)} %get-tuple-element.78.made, bf16[12,128,1024]{2,1,0:T(8,128)(2,1)S(1)} %get-tuple-element.79.own, bf16[12,128,1024]{2,1,0:T(8,128)(2,1)S(1)} %get-tuple-element.81.other), custom_call_target="tpu_custom_call" | custom-call | flops 1073741824 | bytes 3145728 | tf_op jit(solution)/shard_map/pallas_call | solution.py:341
  93.4 1.0 collective-permute-start.20
  94.4 1.1 collective-permute-start.19
  95.5 3.3 %collective-permute-start.26 = (bf16[256,512]{1,0:T(8,128)(2,1)S(1)}, bf16[256,512]{1,0:T(8,128)(2,1)S(1)}, u32[]{:S(2)}, u32[]{:S(2)}) collective-permute-start(bf16[256,512]{1,0:T(8,128)(2,1)S(1)} %add_convert_fusion.1), channel_id=1, source_target_pairs={{0,4},{1,5},{2,6},{3,7},{4,12},{5,13},{6,14},{7,15},{12,8},{13,9},... | collective-permute-start | bytes 786440 | tf_op jit(solution)/shard_map/ppermute | solution.py:223
  98.9 5.1 %collective-permute-start.24 = (bf16[256,512]{1,0:T(8,128)(2,1)S(1)}, bf16[256,512]{1,0:T(8,128)(2,1)S(1)}, u32[]{:S(2)}, u32[]{:S(2)}) collective-permute-start(bf16[256,512]{1,0:T(8,128)(2,1)S(1)} %add_convert_fusion.2), channel_id=1, source_target_pairs={{0,12},{1,13},{2,14},{3,15},{12,0},{13,1},{14,2},{15,3},{16,28},{1... | collective-permute-start | bytes 786440 | tf_op jit(solution)/shard_map/ppermute | solution.py:223
  104.1 4.6 %collective-permute-start.21 = (bf16[256,512]{1,0:T(8,128)(2,1)S(1)}, bf16[256,512]{1,0:T(8,128)(2,1)S(1)}, u32[]{:S(2)}, u32[]{:S(2)}) collective-permute-start(bf16[256,512]{1,0:T(8,128)(2,1)S(1)} %add_convert_fusion.3), channel_id=1, source_target_pairs={{0,4},{1,5},{2,6},{3,7},{4,0},{5,1},{6,2},{7,3},{8,12},{9,13},{10,... | collective-permute-start | bytes 786440 | tf_op jit(solution)/shard_map/ppermute | solution.py:223
  110.1 2.8 %collective-permute-done.24.refs_2_ = bf16[256,512]{1,0:T(8,128)(2,1)S(1)} collective-permute-done((bf16[256,512]{1,0:T(8,128)(2,1)S(1)}, bf16[256,512]{1,0:T(8,128)(2,1)S(1)}, u32[]{:S(2)}, u32[]{:S(2)}) %collective-permute-start.24) | collective-permute-done | bytes 262176 | tf_op jit(solution)/shard_map/ppermute | solution.py:223
  112.9 5.5 %collective-permute-done.21.refs_1_ = bf16[256,512]{1,0:T(8,128)(2,1)S(1)} collective-permute-done((bf16[256,512]{1,0:T(8,128)(2,1)S(1)}, bf16[256,512]{1,0:T(8,128)(2,1)S(1)}, u32[]{:S(2)}, u32[]{:S(2)}) %collective-permute-start.21) | collective-permute-done | bytes 262176 | tf_op jit(solution)/shard_map/ppermute | solution.py:223
  118.3 1.0 finish.1
  (88 shorter events, 7.5 us)
Async XLA Ops:
  0.0 42.8 %copy-start = (bf16[12,64,1024]{2,1,0:T(8,128)(2,1)S(1)}, bf16[12,64,1024]{2,1,0:T(8,128)(2,1)}, u32[]{:S(2)}) copy-start(bf16[12,64,1024]{2,1,0:T(8,128)(2,1)} %refs_11_.1) | copy-start | bytes 4718596
  0.0 47.8 %copy-start.3 = (bf16[1,16,128,128]{3,2,1,0:T(8,128)(2,1)S(1)}, bf16[1,16,128,128]{3,2,1,0:T(8,128)(2,1)}, u32[]{:S(2)}) copy-start(bf16[1,16,128,128]{3,2,1,0:T(8,128)(2,1)} %param.21) | copy-start | bytes 1572868
  2.4 44.9 %collective-permute-start.15 = (bf16[8,64,1024]{2,1,0:T(8,128)(2,1)}, bf16[8,64,1024]{2,1,0:T(8,128)(2,1)}, u32[]{:S(2)}, u32[]{:S(2)}) collective-permute-start(bf16[8,64,1024]{2,1,0:T(8,128)(2,1)} %slice.88), channel_id=1, source_target_pairs={{0,2},{1,3},{2,0},{3,1},{4,6},{5,7},{6,4},{7,5},{8,10},{9,11},{10,... | collective-permute-start | bytes 3145736 | tf_op jit(solution)/shard_map/ppermute | solution.py:24
  5.4 8.0 %collective-permute-start = (bf16[256,512]{1,0:T(8,128)(2,1)}, bf16[256,512]{1,0:T(8,128)(2,1)S(1)}, u32[]{:S(2)}, u32[]{:S(2)}) collective-permute-start(bf16[256,512]{1,0:T(8,128)(2,1)} %state.1), channel_id=1, source_target_pairs={{0,16},{16,0},{1,17},{17,1},{2,18},{18,2},{3,19},{19,3},{4,20},{20... | collective-permute-start | bytes 786440 | tf_op jit(solution)/shard_map/ppermute | solution.py:24
  13.4 1.0 copy-start.1
  15.7 9.1 %collective-permute-start.1 = (bf16[144,256]{1,0:T(8,128)(2,1)S(1)}, bf16[144,256]{1,0:T(8,128)(2,1)S(1)}, u32[]{:S(2)}, u32[]{:S(2)}) collective-permute-start(bf16[144,256]{1,0:T(8,128)(2,1)S(1)} %get-tuple-element.73), channel_id=1, source_target_pairs={{0,4},{1,5},{2,6},{3,7},{4,0},{5,1},{6,2},{7,3},{8,12},{9,13},{10,... | collective-permute-start | bytes 221192 | tf_op jit(solution)/shard_map/ppermute | solution.py:223
  17.2 28.0 %collective-permute-start.12 = (bf16[16,128,128]{2,1,0:T(8,128)(2,1)}, bf16[16,128,128]{2,1,0:T(8,128)(2,1)S(1)}, u32[]{:S(2)}, u32[]{:S(2)}) collective-permute-start(bf16[16,128,128]{2,1,0:T(8,128)(2,1)} %bitcast.15), channel_id=1, source_target_pairs={{4,8},{5,9},{6,10},{7,11},{8,4},{9,5},{10,6},{11,7},{20,24},{21,25... | collective-permute-start | bytes 1572872 | tf_op jit(solution)/shard_map/ppermute | solution.py:223
  17.9 27.9 %collective-permute-start.11 = (bf16[16,128,128]{2,1,0:T(8,128)(2,1)}, bf16[16,128,128]{2,1,0:T(8,128)(2,1)}, u32[]{:S(2)}, u32[]{:S(2)}) collective-permute-start(bf16[16,128,128]{2,1,0:T(8,128)(2,1)} %bitcast.16), channel_id=1, source_target_pairs={{0,4},{1,5},{2,6},{3,7},{4,0},{5,1},{6,2},{7,3},{8,12},{9,13},{10,... | collective-permute-start | bytes 1572872 | tf_op jit(solution)/shard_map/ppermute | solution.py:223
  24.2 23.1 %collective-permute-start.17 = (bf16[4,64,1024]{2,1,0:T(8,128)(2,1)}, bf16[4,64,1024]{2,1,0:T(8,128)(2,1)S(1)}, u32[]{:S(2)}, u32[]{:S(2)}) collective-permute-start(bf16[4,64,1024]{2,1,0:T(8,128)(2,1)} %slice.89), channel_id=1, source_target_pairs={{0,2},{1,3},{2,0},{3,1},{4,6},{5,7},{6,4},{7,5},{8,10},{9,11},{10,... | collective-permute-start | bytes 1572872 | tf_op jit(solution)/shard_map/ppermute | solution.py:24
  24.7 11.0 %collective-permute-start.2 = (bf16[144,256]{1,0:T(8,128)(2,1)S(1)}, bf16[144,256]{1,0:T(8,128)(2,1)S(1)}, u32[]{:S(2)}, u32[]{:S(2)}) collective-permute-start(bf16[144,256]{1,0:T(8,128)(2,1)S(1)} %get-tuple-element.74), channel_id=1, source_target_pairs={{0,8},{1,9},{2,10},{3,11},{4,12},{5,13},{6,14},{7,15},{8,0},{9,1},... | collective-permute-start | bytes 221192 | tf_op jit(solution)/shard_map/ppermute | solution.py:223
  36.3 6.5 %collective-permute-start.3 = (bf16[144,256]{1,0:T(8,128)(2,1)}, bf16[144,256]{1,0:T(8,128)(2,1)}, u32[]{:S(2)}, u32[]{:S(2)}) collective-permute-start(bf16[144,256]{1,0:T(8,128)(2,1)} %get-tuple-element.75), channel_id=1, source_target_pairs={{0,12},{1,13},{2,14},{3,15},{4,8},{5,9},{6,10},{7,11},{8,4},{9,5},... | collective-permute-start | bytes 221192 | tf_op jit(solution)/shard_map/ppermute | solution.py:223
  42.8 28.7 %collective-permute-start.14 = (bf16[12,64,1024]{2,1,0:T(8,128)(2,1)S(1)}, bf16[12,64,1024]{2,1,0:T(8,128)(2,1)}, u32[]{:S(2)}, u32[]{:S(2)}) collective-permute-start(bf16[12,64,1024]{2,1,0:T(8,128)(2,1)S(1)} %copy-done), channel_id=1, source_target_pairs={{0,1},{1,0},{2,3},{3,2},{4,5},{5,4},{6,7},{7,6},{8,9},{9,8},{10,11... | collective-permute-start | bytes 4718600 | tf_op jit(solution)/shard_map/ppermute | solution.py:24
  43.4 0.9 copy-start.18
  45.2 12.1 %copy-start.5 = (bf16[4,128,256]{2,1,0:T(8,128)(2,1)}, bf16[4,128,256]{2,1,0:T(8,128)(2,1)S(1)}, u32[]{:S(2)}) copy-start(bf16[4,128,256]{2,1,0:T(8,128)(2,1)S(1)} %get-tuple-element.77.refs_0_) | copy-start | bytes 786436
  45.2 8.8 %collective-permute-start.4 = (bf16[4,128,256]{2,1,0:T(8,128)(2,1)S(1)}, bf16[4,128,256]{2,1,0:T(8,128)(2,1)S(1)}, u32[]{:S(2)}, u32[]{:S(2)}) collective-permute-start(bf16[4,128,256]{2,1,0:T(8,128)(2,1)S(1)} %get-tuple-element.77.refs_0_), channel_id=1, source_target_pairs={{0,2},{1,3},{2,0},{3,1},{4,6},{5,7},{6,4},{7,5},{8,10},{9,11},{10,... | collective-permute-start | bytes 786440 | tf_op jit(solution)/shard_map/ppermute | solution.py:24
  45.8 8.4 %collective-permute-start.5 = (bf16[4,128,256]{2,1,0:T(8,128)(2,1)S(1)}, bf16[4,128,256]{2,1,0:T(8,128)(2,1)S(1)}, u32[]{:S(2)}, u32[]{:S(2)}) collective-permute-start(bf16[4,128,256]{2,1,0:T(8,128)(2,1)S(1)} %get-tuple-element.77.refs_0_), channel_id=1, source_target_pairs={{0,16},{16,0},{1,17},{17,1},{2,18},{18,2},{3,19},{19,3},{4,20},{20... | collective-permute-start | bytes 786440 | tf_op jit(solution)/shard_map/ppermute | solution.py:24
  47.3 8.4 %collective-permute-start.7 = (bf16[4,128,256]{2,1,0:T(8,128)(2,1)S(1)}, bf16[4,128,256]{2,1,0:T(8,128)(2,1)S(1)}, u32[]{:S(2)}, u32[]{:S(2)}) collective-permute-start(bf16[4,128,256]{2,1,0:T(8,128)(2,1)S(1)} %get-tuple-element.77.refs_0_), channel_id=1, source_target_pairs={{0,1},{1,0},{2,3},{3,2},{4,5},{5,4},{6,7},{7,6},{8,9},{9,8},{10,11... | collective-permute-start | bytes 786440 | tf_op jit(solution)/shard_map/ppermute | solution.py:24
  47.3 24.2 %collective-permute-start.16 = (bf16[8,64,1024]{2,1,0:T(8,128)(2,1)}, bf16[8,64,1024]{2,1,0:T(8,128)(2,1)}, u32[]{:S(2)}, u32[]{:S(2)}) collective-permute-start(bf16[8,64,1024]{2,1,0:T(8,128)(2,1)} %collective-permute-done.15.refs_13_), channel_id=1, source_target_pairs={{0,1},{1,0},{2,3},{3,2},{4,5},{5,4},{6,7},{7,6},{8,9},{9,8},{10,11... | collective-permute-start | bytes 3145736 | tf_op jit(solution)/shard_map/ppermute | solution.py:24
  54.0 13.6 %collective-permute-start.13 = (bf16[16,128,128]{2,1,0:T(8,128)(2,1)S(1)}, bf16[16,128,128]{2,1,0:T(8,128)(2,1)}, u32[]{:S(2)}, u32[]{:S(2)}) collective-permute-start(bf16[16,128,128]{2,1,0:T(8,128)(2,1)S(1)} %broadcast_select_fusion), channel_id=1, source_target_pairs={{0,8},{1,9},{2,10},{3,11},{8,12},{9,13},{10,14},{11,15},{12,4},{13... | collective-permute-start | bytes 1572872 | tf_op jit(solution)/shard_map/ppermute | solution.py:223
  54.2 7.7 %collective-permute-start.6 = (bf16[4,128,256]{2,1,0:T(8,128)(2,1)S(1)}, bf16[4,128,256]{2,1,0:T(8,128)(2,1)}, u32[]{:S(2)}, u32[]{:S(2)}) collective-permute-start(bf16[4,128,256]{2,1,0:T(8,128)(2,1)S(1)} %collective-permute-done.4.refs_1_), channel_id=1, source_target_pairs={{0,16},{16,0},{1,17},{17,1},{2,18},{18,2},{3,19},{19,3},{4,20},{20... | collective-permute-start | bytes 786440 | tf_op jit(solution)/shard_map/ppermute | solution.py:24
  55.7 0.7 copy-start.11
  56.4 5.5 %collective-permute-start.8 = (bf16[4,128,256]{2,1,0:T(8,128)(2,1)S(1)}, bf16[4,128,256]{2,1,0:T(8,128)(2,1)S(1)}, u32[]{:S(2)}, u32[]{:S(2)}) collective-permute-start(bf16[4,128,256]{2,1,0:T(8,128)(2,1)S(1)} %collective-permute-done.4.refs_1_), channel_id=1, source_target_pairs={{0,1},{1,0},{2,3},{3,2},{4,5},{5,4},{6,7},{7,6},{8,9},{9,8},{10,11... | collective-permute-start | bytes 786440 | tf_op jit(solution)/shard_map/ppermute | solution.py:24
  56.4 0.7 copy-start.7
  62.0 18.6 %collective-permute-start.18 = (bf16[4,64,1024]{2,1,0:T(8,128)(2,1)S(1)}, bf16[4,64,1024]{2,1,0:T(8,128)(2,1)}, u32[]{:S(2)}, u32[]{:S(2)}) collective-permute-start(bf16[4,64,1024]{2,1,0:T(8,128)(2,1)S(1)} %collective-permute-done.17.refs_0_), channel_id=1, source_target_pairs={{0,1},{1,0},{2,3},{3,2},{4,5},{5,4},{6,7},{7,6},{8,9},{9,8},{10,11... | collective-permute-start | bytes 1572872 | tf_op jit(solution)/shard_map/ppermute | solution.py:24
  62.0 0.7 copy-start.13
  62.7 6.2 %collective-permute-start.9 = (bf16[4,128,256]{2,1,0:T(8,128)(2,1)S(1)}, bf16[4,128,256]{2,1,0:T(8,128)(2,1)S(1)}, u32[]{:S(2)}, u32[]{:S(2)}) collective-permute-start(bf16[4,128,256]{2,1,0:T(8,128)(2,1)S(1)} %collective-permute-done.5.refs_2_), channel_id=1, source_target_pairs={{0,1},{1,0},{2,3},{3,2},{4,5},{5,4},{6,7},{7,6},{8,9},{9,8},{10,11... | collective-permute-start | bytes 786440 | tf_op jit(solution)/shard_map/ppermute | solution.py:24
  63.2 0.7 copy-start.9
  67.6 17.2 %collective-permute-start.22 = (bf16[16,128,128]{2,1,0:T(8,128)(2,1)}, bf16[16,128,128]{2,1,0:T(8,128)(2,1)}, u32[]{:S(2)}, u32[]{:S(2)}) collective-permute-start(bf16[16,128,128]{2,1,0:T(8,128)(2,1)} %collective-permute-done.13.refs_10_), channel_id=1, source_target_pairs={{8,12},{9,13},{10,14},{11,15},{4,0},{5,1},{6,2},{7,3},{24,28},{25,... | collective-permute-start | bytes 1572872 | tf_op jit(solution)/shard_map/ppermute | solution.py:223
  68.9 0.7 copy-start.15
  69.6 1.9 %collective-permute-start.10 = (bf16[4,128,256]{2,1,0:T(8,128)(2,1)}, bf16[4,128,256]{2,1,0:T(8,128)(2,1)}, u32[]{:S(2)}, u32[]{:S(2)}) collective-permute-start(bf16[4,128,256]{2,1,0:T(8,128)(2,1)} %collective-permute-done.6.refs_3_), channel_id=1, source_target_pairs={{0,1},{1,0},{2,3},{3,2},{4,5},{5,4},{6,7},{7,6},{8,9},{9,8},{10,11... | collective-permute-start | bytes 786440 | tf_op jit(solution)/shard_map/ppermute | solution.py:24
  71.5 1.0 copy-start.6
  72.5 0.9 copy-start.8
  73.4 0.9 copy-start.10
  74.4 0.9 copy-start.12
  75.3 0.9 copy-start.14
  76.3 0.9 copy-start.16
  82.9 12.6 %collective-permute-start.25 = (bf16[256,512]{1,0:T(8,128)(2,1)S(1)}, bf16[256,512]{1,0:T(8,128)(2,1)S(1)}, u32[]{:S(2)}, u32[]{:S(2)}) collective-permute-start(bf16[256,512]{1,0:T(8,128)(2,1)S(1)} %get-tuple-element.90), channel_id=1, source_target_pairs={{0,16},{16,0},{1,17},{17,1},{2,18},{18,2},{3,19},{19,3},{4,20},{20... | collective-permute-start | bytes 786440 | tf_op jit(solution)/shard_map/ppermute | solution.py:24
  87.2 11.6 %collective-permute-start.23 = (bf16[256,512]{1,0:T(8,128)(2,1)S(1)}, bf16[256,512]{1,0:T(8,128)(2,1)S(1)}, u32[]{:S(2)}, u32[]{:S(2)}) collective-permute-start(bf16[256,512]{1,0:T(8,128)(2,1)S(1)} %get-tuple-element.88), channel_id=1, source_target_pairs={{0,16},{16,0},{1,17},{17,1},{2,18},{18,2},{3,19},{19,3},{4,20},{20... | collective-permute-start | bytes 786440 | tf_op jit(solution)/shard_map/ppermute | solution.py:24
  93.3 16.2 %copy-start.2 = (bf16[256,512]{1,0:T(8,128)(2,1)S(1)}, bf16[256,512]{1,0:T(8,128)(2,1)}, u32[]{:S(2)}) copy-start(bf16[256,512]{1,0:T(8,128)(2,1)} %state.1) | copy-start | bytes 786436
  93.3 16.2 %copy-start.4 = (bf16[1024,512]{1,0:T(8,128)(2,1)S(1)}, bf16[1024,512]{1,0:T(8,128)(2,1)}, u32[]{:S(2)}) copy-start(bf16[1024,512]{1,0:T(8,128)(2,1)} %weight.1) | copy-start | bytes 3145732
  93.4 16.2 %copy-start.20 = (f32[512]{0:T(512)S(1)}, f32[512]{0:T(512)}, u32[]{:S(2)}) copy-start(f32[512]{0:T(512)} %param.19) | copy-start | bytes 6148
  93.4 10.7 %collective-permute-start.20 = (bf16[256,512]{1,0:T(8,128)(2,1)S(1)}, bf16[256,512]{1,0:T(8,128)(2,1)S(1)}, u32[]{:S(2)}, u32[]{:S(2)}) collective-permute-start(bf16[256,512]{1,0:T(8,128)(2,1)S(1)} %get-tuple-element.85), channel_id=1, source_target_pairs={{0,16},{16,0},{1,17},{17,1},{2,18},{18,2},{3,19},{19,3},{4,20},{20... | collective-permute-start | bytes 786440 | tf_op jit(solution)/shard_map/ppermute | solution.py:24
  94.4 15.7 %collective-permute-start.19 = (bf16[256,512]{1,0:T(8,128)(2,1)S(1)}, bf16[256,512]{1,0:T(8,128)(2,1)S(1)}, u32[]{:S(2)}, u32[]{:S(2)}) collective-permute-start(bf16[256,512]{1,0:T(8,128)(2,1)S(1)} %get-tuple-element.83), channel_id=1, source_target_pairs={{0,16},{16,0},{1,17},{17,1},{2,18},{18,2},{3,19},{19,3},{4,20},{20... | collective-permute-start | bytes 786440 | tf_op jit(solution)/shard_map/ppermute | solution.py:24
  95.5 13.2 %collective-permute-start.26 = (bf16[256,512]{1,0:T(8,128)(2,1)S(1)}, bf16[256,512]{1,0:T(8,128)(2,1)S(1)}, u32[]{:S(2)}, u32[]{:S(2)}) collective-permute-start(bf16[256,512]{1,0:T(8,128)(2,1)S(1)} %add_convert_fusion.1), channel_id=1, source_target_pairs={{0,4},{1,5},{2,6},{3,7},{4,12},{5,13},{6,14},{7,15},{12,8},{13,9},... | collective-permute-start | bytes 786440 | tf_op jit(solution)/shard_map/ppermute | solution.py:223
  98.8 19.5 %copy-start.19 = (f32[512]{0:T(512)S(1)}, f32[512]{0:T(512)}, u32[]{:S(2)}) copy-start(f32[512]{0:T(512)} %param.20) | copy-start | bytes 6148
  98.9 14.0 %collective-permute-start.24 = (bf16[256,512]{1,0:T(8,128)(2,1)S(1)}, bf16[256,512]{1,0:T(8,128)(2,1)S(1)}, u32[]{:S(2)}, u32[]{:S(2)}) collective-permute-start(bf16[256,512]{1,0:T(8,128)(2,1)S(1)} %add_convert_fusion.2), channel_id=1, source_target_pairs={{0,12},{1,13},{2,14},{3,15},{12,0},{13,1},{14,2},{15,3},{16,28},{1... | collective-permute-start | bytes 786440 | tf_op jit(solution)/shard_map/ppermute | solution.py:223
  104.1 14.2 %collective-permute-start.21 = (bf16[256,512]{1,0:T(8,128)(2,1)S(1)}, bf16[256,512]{1,0:T(8,128)(2,1)S(1)}, u32[]{:S(2)}, u32[]{:S(2)}) collective-permute-start(bf16[256,512]{1,0:T(8,128)(2,1)S(1)} %add_convert_fusion.3), channel_id=1, source_target_pairs={{0,4},{1,5},{2,6},{3,7},{4,0},{5,1},{6,2},{7,3},{8,12},{9,13},{10,... | collective-permute-start | bytes 786440 | tf_op jit(solution)/shard_map/ppermute | solution.py:223
  108.8 9.5 %collective-permute-start.27 = (bf16[256,512]{1,0:T(8,128)(2,1)S(1)}, bf16[256,512]{1,0:T(8,128)(2,1)S(1)}, u32[]{:S(2)}, u32[]{:S(2)}) collective-permute-start(bf16[256,512]{1,0:T(8,128)(2,1)S(1)} %add_convert_fusion), channel_id=1, source_target_pairs={{4,8},{5,9},{6,10},{7,11},{8,4},{9,5},{10,6},{11,7},{20,24},{21,25... | collective-permute-start | bytes 786440 | tf_op jit(solution)/shard_map/ppermute | solution.py:223
  (1 other events, 0.6 us)

commit v7 on v6

--- a/solution.py
+++ b/solution.py
@@ -287,8 +287,9 @@
         last,
     ])
 
-    cut = max(1, rel_dev * 2 // 3)
-    parts = (rel_weight[:cut], rel_weight[cut:])
+    cut = max(1, rel_dev * 7 // 12)
+    parts = [rel_weight[:cut]]
+    parts.append(rel_weight[cut:])
     bits = [1 << b for b in reversed(range(members.bit_length() - 1))]
     rel_bits = [1 << b for b in reversed(range(n_rel.bit_length() - 1))]
     states, places = [own], [(0, 0)]

time: 120 us -> 118 us (0.983)
  waiting for transfers between devices: 43.2 us -> 36 us
  local copies, waits for them, and re-layouts: 17.5 us -> 20.6 us
  other arithmetic: 1.91 us -> 4.76 us
  starting transfers between devices: 40.2 us -> 39 us
    ppermute x11, waiting for transfers between devices: 26.6 us -> 12.7 us  [along(): return lax.ppermute(value, 'ent', perm)]
    ppermute x17, waiting for transfers between devices: 16.6 us -> 23.2 us  [swap(): return lax.ppermute(value, axis, [(i, i ^ bit) for i in range(size)])]
    unnamed x43 -> x45, local copies, waits for them, and re-layouts: 11.7 us -> 12.7 us
  transfers between devices with their start and end apart: 28 -> 28, of which waited for: 10 -> 10; matrix products, arithmetic and copies ran while one was open for 4% -> 11% of each run, Pallas kernels for 12% -> 13%
where the time goes in v7:
time: 118 us
  starting transfers between devices  39 us (33%)
  waiting for transfers between devices  36 us (31%)
  local copies, waits for them, and re-layouts  20.6 us (17%)
  Pallas kernels  16.3 us (14%)
  other arithmetic  4.76 us (4%)
    ppermute x11, starting transfers between devices, along(): return lax.ppermute(value, 'ent', perm)  23.6 us
    ppermute x17, waiting for transfers between devices, swap(): return lax.ppermute(value, axis, [(i, i ^ bit) for i in range(size)])  23.2 us
    ppermute x17, starting transfers between devices, swap(): return lax.ppermute(value, axis, [(i, i ^ bit) for i in range(size)])  15.4 us
    unnamed x45, local copies, waits for them, and re-layouts  12.7 us
    ppermute x11, waiting for transfers between devices, along(): return lax.ppermute(value, 'ent', perm)  12.7 us
    pallas_call x5, Pallas kernels, call(): pl.pallas_call(body, out_shape=out_shape, in_specs=[SMEM] + in_specs, out...  11.9 us
  transfers between devices with their start and end apart: 28, of which 10 were waited for; matrix products, arithmetic and copies ran while one was open for 11% of the time, Pallas kernels for 13%

profile of v7, /device:TPU:0, one launch (start us, length us, event | category | flops | bytes accessed | tf_op | source)
XLA Modules:
  0.0 117.5 jit_solution(9806279673113421892)
XLA Ops:
  0.0 0.8 collective-permute-start.12
  0.8 5.9 %collective-permute-start.11 = (bf16[16,128,128]{2,1,0:T(8,128)(2,1)}, bf16[16,128,128]{2,1,0:T(8,128)(2,1)}, u32[]{:S(2)}, u32[]{:S(2)}) collective-permute-start(bf16[16,128,128]{2,1,0:T(8,128)(2,1)} %bitcast.16), channel_id=1, source_target_pairs={{0,4},{1,5},{2,6},{3,7},{4,0},{5,1},{6,2},{7,3},{8,12},{9,13},{10,... | collective-permute-start | bytes 1572872 | tf_op jit(solution)/shard_map/ppermute | solution.py:223
  6.7 1.5 %collective-permute-start = (bf16[256,512]{1,0:T(8,128)(2,1)}, bf16[256,512]{1,0:T(8,128)(2,1)S(1)}, u32[]{:S(2)}, u32[]{:S(2)}) collective-permute-start(bf16[256,512]{1,0:T(8,128)(2,1)} %state.1), channel_id=1, source_target_pairs={{0,16},{16,0},{1,17},{17,1},{2,18},{18,2},{3,19},{19,3},{4,20},{20... | collective-permute-start | bytes 786440 | tf_op jit(solution)/shard_map/ppermute | solution.py:24
  8.2 2.2 %slice.88 = bf16[7,64,1024]{2,1,0:T(8,128)(2,1)} slice(bf16[12,64,1024]{2,1,0:T(8,128)(2,1)} %refs_11_.1), slice={[0:7], [0:64], [0:1024]} | slice | bytes 1835008 | tf_op jit(solution)/shard_map/slice | solution.py:291
  10.4 1.5 %collective-permute-start.15 = (bf16[7,64,1024]{2,1,0:T(8,128)(2,1)}, bf16[7,64,1024]{2,1,0:T(8,128)(2,1)}, u32[]{:S(2)}, u32[]{:S(2)}) collective-permute-start(bf16[7,64,1024]{2,1,0:T(8,128)(2,1)} %slice.88), channel_id=1, source_target_pairs={{0,2},{1,3},{2,0},{3,1},{4,6},{5,7},{6,4},{7,5},{8,10},{9,11},{10,... | collective-permute-start | bytes 2752520 | tf_op jit(solution)/shard_map/ppermute | solution.py:24
  13.5 0.9 collective-permute-done.refs_1_
  14.4 0.9 copy-done.1
  15.4 1.3 %pack.1 = (bf16[144,256]{1,0:T(8,128)(2,1)S(1)}, bf16[144,256]{1,0:T(8,128)(2,1)S(1)}, bf16[144,256]{1,0:T(8,128)(2,1)S(1)}, bf16[144,256]{1,0:T(8,128)(2,1)}) custom-call(s32[3,4]{1,0:T(4,128)S(1)} %add_add_fusion.where, bf16[16,256]{1,0:T(8,128)(2,1)S(1)} %scatter.15.note, bf16[256,512]{1,0:T(8,128)(2,1)S(1)} %copy-done.1, ...), custom_call_target="tpu_custom_call" | custom-call | tf_op jit(solution)/shard_map/pack/pallas_call | solution.py:252
  17.6 1.6 %collective-permute-start.2 = (bf16[144,256]{1,0:T(8,128)(2,1)S(1)}, bf16[144,256]{1,0:T(8,128)(2,1)S(1)}, u32[]{:S(2)}, u32[]{:S(2)}) collective-permute-start(bf16[144,256]{1,0:T(8,128)(2,1)S(1)} %get-tuple-element.74), channel_id=1, source_target_pairs={{0,8},{1,9},{2,10},{3,11},{4,12},{5,13},{6,14},{7,15},{8,0},{9,1},... | collective-permute-start | bytes 221192 | tf_op jit(solution)/shard_map/ppermute | solution.py:223
  19.2 2.4 %collective-permute-done.1.refs_1_ = bf16[144,256]{1,0:T(8,128)(2,1)S(1)} collective-permute-done((bf16[144,256]{1,0:T(8,128)(2,1)S(1)}, bf16[144,256]{1,0:T(8,128)(2,1)S(1)}, u32[]{:S(2)}, u32[]{:S(2)}) %collective-permute-start.1) | collective-permute-done | bytes 73760 | tf_op jit(solution)/shard_map/ppermute | solution.py:223
  22.3 1.3 %collective-permute-start.3 = (bf16[144,256]{1,0:T(8,128)(2,1)}, bf16[144,256]{1,0:T(8,128)(2,1)}, u32[]{:S(2)}, u32[]{:S(2)}) collective-permute-start(bf16[144,256]{1,0:T(8,128)(2,1)} %get-tuple-element.75), channel_id=1, source_target_pairs={{0,12},{1,13},{2,14},{3,15},{4,8},{5,9},{6,10},{7,11},{8,4},{9,5},... | collective-permute-start | bytes 221192 | tf_op jit(solution)/shard_map/ppermute | solution.py:223
  23.6 2.0 %slice.89 = bf16[5,64,1024]{2,1,0:T(8,128)(2,1)} slice(bf16[12,64,1024]{2,1,0:T(8,128)(2,1)} %refs_11_.1), slice={[7:12], [0:64], [0:1024]} | slice | bytes 1310720 | tf_op jit(solution)/shard_map/slice | solution.py:292
  26.3 1.5 %collective-permute-start.17 = (bf16[5,64,1024]{2,1,0:T(8,128)(2,1)}, bf16[5,64,1024]{2,1,0:T(8,128)(2,1)S(1)}, u32[]{:S(2)}, u32[]{:S(2)}) collective-permute-start(bf16[5,64,1024]{2,1,0:T(8,128)(2,1)} %slice.89), channel_id=1, source_target_pairs={{0,2},{1,3},{2,0},{3,1},{4,6},{5,7},{6,4},{7,5},{8,10},{9,11},{10,... | collective-permute-start | bytes 1966088 | tf_op jit(solution)/shard_map/ppermute | solution.py:24
  27.8 1.0 collective-permute-done.3.refs_3_
  28.8 0.9 copy-done.14
  29.7 0.9 copy-done.16
  30.5 0.9 copy-done.18
  31.4 1.6 %stk.1 = (bf16[4,128,256]{2,1,0:T(8,128)(2,1)}, bf16[4,16,256]{2,1,0:T(8,128)(2,1)S(1)}) custom-call(bf16[144,256]{1,0:T(8,128)(2,1)S(1)} %copy-done.14, bf16[144,256]{1,0:T(8,128)(2,1)S(1)} %copy-done.16, bf16[144,256]{1,0:T(8,128)(2,1)S(1)} %copy-done.18, bf16[144,256]{1,0:T(8,128)(2,1)} %collective-permute-done.3.refs_3_), custom_call_target="tpu_custom_call" | custom-call | tf_op jit(solution)/shard_map/stk/pallas_call | solution.py:261
  33.6 1.5 %collective-permute-start.4 = (bf16[4,128,256]{2,1,0:T(8,128)(2,1)}, bf16[4,128,256]{2,1,0:T(8,128)(2,1)}, u32[]{:S(2)}, u32[]{:S(2)}) collective-permute-start(bf16[4,128,256]{2,1,0:T(8,128)(2,1)} %get-tuple-element.77.refs_0_), channel_id=1, source_target_pairs={{0,2},{1,3},{2,0},{3,1},{4,6},{5,7},{6,4},{7,5},{8,10},{9,11},{10,... | collective-permute-start | bytes 786440 | tf_op jit(solution)/shard_map/ppermute | solution.py:24
  36.5 1.5 %collective-permute-start.5 = (bf16[4,128,256]{2,1,0:T(8,128)(2,1)}, bf16[4,128,256]{2,1,0:T(8,128)(2,1)S(1)}, u32[]{:S(2)}, u32[]{:S(2)}) collective-permute-start(bf16[4,128,256]{2,1,0:T(8,128)(2,1)} %get-tuple-element.77.refs_0_), channel_id=1, source_target_pairs={{0,16},{16,0},{1,17},{17,1},{2,18},{18,2},{3,19},{19,3},{4,20},{20... | collective-permute-start | bytes 786440 | tf_op jit(solution)/shard_map/ppermute | solution.py:24
  38.0 13.7 %collective-permute-done.4.refs_1_ = bf16[4,128,256]{2,1,0:T(8,128)(2,1)} collective-permute-done((bf16[4,128,256]{2,1,0:T(8,128)(2,1)}, bf16[4,128,256]{2,1,0:T(8,128)(2,1)}, u32[]{:S(2)}, u32[]{:S(2)}) %collective-permute-start.4) | collective-permute-done | bytes 262176 | tf_op jit(solution)/shard_map/ppermute | solution.py:24
  51.7 1.1 broadcast_select_fusion
  53.4 0.7 copy-done.7
  55.3 7.4 %collective-permute-done.6.refs_3_ = bf16[4,128,256]{2,1,0:T(8,128)(2,1)} collective-permute-done((bf16[4,128,256]{2,1,0:T(8,128)(2,1)}, bf16[4,128,256]{2,1,0:T(8,128)(2,1)}, u32[]{:S(2)}, u32[]{:S(2)}) %collective-permute-start.6) | collective-permute-done | bytes 262176 | tf_op jit(solution)/shard_map/ppermute | solution.py:24
  65.3 2.0 %collective-permute-done.13.refs_10_ = bf16[16,128,128]{2,1,0:T(8,128)(2,1)} collective-permute-done((bf16[16,128,128]{2,1,0:T(8,128)(2,1)S(1)}, bf16[16,128,128]{2,1,0:T(8,128)(2,1)}, u32[]{:S(2)}, u32[]{:S(2)}) %collective-permute-start.13) | collective-permute-done | bytes 524320 | tf_op jit(solution)/shard_map/ppermute | solution.py:223
  67.3 1.3 %collective-permute-start.22 = (bf16[16,128,128]{2,1,0:T(8,128)(2,1)}, bf16[16,128,128]{2,1,0:T(8,128)(2,1)}, u32[]{:S(2)}, u32[]{:S(2)}) collective-permute-start(bf16[16,128,128]{2,1,0:T(8,128)(2,1)} %collective-permute-done.13.refs_10_), channel_id=1, source_target_pairs={{8,12},{9,13},{10,14},{11,15},{4,0},{5,1},{6,2},{7,3},{24,28},{25,... | collective-permute-start | bytes 1572872 | tf_op jit(solution)/shard_map/ppermute | solution.py:223
  70.0 0.7 lt.60
  70.8 1.2 %scatter.19 = s32[1,64]{1,0:T(1,128)} dynamic-update-slice(s32[1,64]{1,0:T(1,128)} %pad_bitcast_fusion, s32[1,3]{1,0:T(1,128)} %add_bitcast_fusion, s32[]{:T(128)} %constant.199.clone.1, s32[]{:T(128)} %constant.209.clone.1) | dynamic-update-slice | bytes 28 | tf_op jit(solution)/shard_map/scatter | solution.py:281
  73.3 0.9 copy-done.6
  74.2 0.9 copy-done.8
  75.2 0.9 copy-done.10
  76.1 0.9 copy-done.12
  77.1 3.4 %shard_map.82 = (bf16[3,16,128,256]{3,2,1,0:T(8,128)(2,1)S(1)}, bf16[12,128,1024]{2,1,0:T(8,128)(2,1)S(1)}, bf16[12,128,1024]{2,1,0:T(8,128)(2,1)S(1)}, bf16[16,256,256]{2,1,0:T(8,128)(2,1)S(1)}) custom-call(s32[5,64]{1,0:T(8,128)S(1)} %stack.26.table, bf16[4,128,256]{2,1,0:T(8,128)(2,1)} %get-tuple-element.77.refs_0_, ...), custom_call_target="tpu_custom_call" | custom-call | flops 402653184 | bytes 3145728 | tf_op jit(solution)/shard_map/pallas_call | solution.py:342
  80.5 2.3 %shard_map.83 = (f32[256,512]{1,0:T(8,128)S(1)}, bf16[256,512]{1,0:T(8,128)(2,1)S(1)}, bf16[12,128,1024]{2,1,0:T(8,128)(2,1)S(1)}) custom-call(s32[5,64]{1,0:T(8,128)S(1)} %stack.26.table, bf16[3,16,128,256]{3,2,1,0:T(8,128)(2,1)S(1)} %get-tuple-element.78.made, bf16[12,128,1024]{2,1,0:T(8,128)(2,1)S(1)} %get-tuple-element.79.own, ...), custom_call_target="tpu_custom_call", output_to_operand_aliasing={{2}: (3, {})} | custom-call | flops 1073741824 | bytes 3145728 | tf_op jit(solution)/shard_map/pallas_call | solution.py:342
  82.8 1.0 collective-permute-start.25
  83.8 2.5 %shard_map.86 = (f32[256,512]{1,0:T(8,128)S(1)}, bf16[256,512]{1,0:T(8,128)(2,1)S(1)}) custom-call(s32[5,64]{1,0:T(8,128)S(1)} %stack.26.table, bf16[16,256,256]{2,1,0:T(8,128)(2,1)S(1)} %get-tuple-element.86.rows_held, bf16[12,128,1024]{2,1,0:T(8,128)(2,1)S(1)} %get-tuple-element.79.own, bf16[12,128,1024]{2,1,0:T(8,128)(2,1)S(1)} %get-tuple-element.81.other, ...), custom_call_target="tpu_custom_call" | custom-call | flops 1207959552 | bytes 3145728 | tf_op jit(solution)/shard_map/pallas_call | solution.py:342
  86.3 3.2 %collective-permute-start.23 = (bf16[256,512]{1,0:T(8,128)(2,1)S(1)}, bf16[256,512]{1,0:T(8,128)(2,1)S(1)}, u32[]{:S(2)}, u32[]{:S(2)}) collective-permute-start(bf16[256,512]{1,0:T(8,128)(2,1)S(1)} %get-tuple-element.88), channel_id=1, source_target_pairs={{0,16},{16,0},{1,17},{17,1},{2,18},{18,2},{3,19},{19,3},{4,20},{20... | collective-permute-start | bytes 786440 | tf_op jit(solution)/shard_map/ppermute | solution.py:24
  89.5 1.2 %shard_map.85 = (f32[256,512]{1,0:T(8,128)S(1)}, bf16[256,512]{1,0:T(8,128)(2,1)S(1)}) custom-call(s32[5,64]{1,0:T(8,128)S(1)} %stack.26.table, bf16[3,16,128,256]{3,2,1,0:T(8,128)(2,1)S(1)} %get-tuple-element.78.made, bf16[12,128,1024]{2,1,0:T(8,128)(2,1)S(1)} %get-tuple-element.79.own, bf16[12,128,1024]{2,1,0:T(8,128)(2,1)S(1)} %get-tuple-element.81.other), custom_call_target="tpu_custom_call" | custom-call | flops 1073741824 | bytes 3145728 | tf_op jit(solution)/shard_map/pallas_call | solution.py:342
  90.7 2.6 %shard_map.84 = (f32[256,512]{1,0:T(8,128)S(1)}, bf16[256,512]{1,0:T(8,128)(2,1)S(1)}) custom-call(s32[5,64]{1,0:T(8,128)S(1)} %stack.26.table, bf16[3,16,128,256]{3,2,1,0:T(8,128)(2,1)S(1)} %get-tuple-element.78.made, bf16[12,128,1024]{2,1,0:T(8,128)(2,1)S(1)} %get-tuple-element.79.own, bf16[12,128,1024]{2,1,0:T(8,128)(2,1)S(1)} %get-tuple-element.81.other), custom_call_target="tpu_custom_call" | custom-call | flops 1073741824 | bytes 3145728 | tf_op jit(solution)/shard_map/pallas_call | solution.py:342
  93.3 1.0 collective-permute-start.20
  94.3 1.1 collective-permute-start.19
  95.5 2.4 %collective-permute-start.26 = (bf16[256,512]{1,0:T(8,128)(2,1)S(1)}, bf16[256,512]{1,0:T(8,128)(2,1)S(1)}, u32[]{:S(2)}, u32[]{:S(2)}) collective-permute-start(bf16[256,512]{1,0:T(8,128)(2,1)S(1)} %add_convert_fusion.1), channel_id=1, source_target_pairs={{0,4},{1,5},{2,6},{3,7},{4,12},{5,13},{6,14},{7,15},{12,8},{13,9},... | collective-permute-start | bytes 786440 | tf_op jit(solution)/shard_map/ppermute | solution.py:223
  98.0 3.9 %collective-permute-start.24 = (bf16[256,512]{1,0:T(8,128)(2,1)S(1)}, bf16[256,512]{1,0:T(8,128)(2,1)S(1)}, u32[]{:S(2)}, u32[]{:S(2)}) collective-permute-start(bf16[256,512]{1,0:T(8,128)(2,1)S(1)} %add_convert_fusion.2), channel_id=1, source_target_pairs={{0,12},{1,13},{2,14},{3,15},{12,0},{13,1},{14,2},{15,3},{16,28},{1... | collective-permute-start | bytes 786440 | tf_op jit(solution)/shard_map/ppermute | solution.py:223
  101.8 0.8 collective-permute-done.20
  102.8 5.1 %collective-permute-start.21 = (bf16[256,512]{1,0:T(8,128)(2,1)S(1)}, bf16[256,512]{1,0:T(8,128)(2,1)S(1)}, u32[]{:S(2)}, u32[]{:S(2)}) collective-permute-start(bf16[256,512]{1,0:T(8,128)(2,1)S(1)} %add_convert_fusion.3), channel_id=1, source_target_pairs={{0,4},{1,5},{2,6},{3,7},{4,0},{5,1},{6,2},{7,3},{8,12},{9,13},{10,... | collective-permute-start | bytes 786440 | tf_op jit(solution)/shard_map/ppermute | solution.py:223
  109.2 2.0 %collective-permute-done.24.refs_2_ = bf16[256,512]{1,0:T(8,128)(2,1)S(1)} collective-permute-done((bf16[256,512]{1,0:T(8,128)(2,1)S(1)}, bf16[256,512]{1,0:T(8,128)(2,1)S(1)}, u32[]{:S(2)}, u32[]{:S(2)}) %collective-permute-start.24) | collective-permute-done | bytes 262176 | tf_op jit(solution)/shard_map/ppermute | solution.py:223
  111.1 5.4 %collective-permute-done.21.refs_1_ = bf16[256,512]{1,0:T(8,128)(2,1)S(1)} collective-permute-done((bf16[256,512]{1,0:T(8,128)(2,1)S(1)}, bf16[256,512]{1,0:T(8,128)(2,1)S(1)}, u32[]{:S(2)}, u32[]{:S(2)}) %collective-permute-start.21) | collective-permute-done | bytes 262176 | tf_op jit(solution)/shard_map/ppermute | solution.py:223
  116.5 1.0 finish.1
  (90 shorter events, 13.8 us)
Async XLA Ops:
  0.0 28.8 %copy-start = (bf16[12,64,1024]{2,1,0:T(8,128)(2,1)S(1)}, bf16[12,64,1024]{2,1,0:T(8,128)(2,1)}, u32[]{:S(2)}) copy-start(bf16[12,64,1024]{2,1,0:T(8,128)(2,1)} %refs_11_.1) | copy-start | bytes 4718596
  0.0 33.6 %collective-permute-start.12 = (bf16[16,128,128]{2,1,0:T(8,128)(2,1)}, bf16[16,128,128]{2,1,0:T(8,128)(2,1)S(1)}, u32[]{:S(2)}, u32[]{:S(2)}) collective-permute-start(bf16[16,128,128]{2,1,0:T(8,128)(2,1)} %bitcast.15), channel_id=1, source_target_pairs={{4,8},{5,9},{6,10},{7,11},{8,4},{9,5},{10,6},{11,7},{20,24},{21,25... | collective-permute-start | bytes 1572872 | tf_op jit(solution)/shard_map/ppermute | solution.py:223
  0.8 35.6 %collective-permute-start.11 = (bf16[16,128,128]{2,1,0:T(8,128)(2,1)}, bf16[16,128,128]{2,1,0:T(8,128)(2,1)}, u32[]{:S(2)}, u32[]{:S(2)}) collective-permute-start(bf16[16,128,128]{2,1,0:T(8,128)(2,1)} %bitcast.16), channel_id=1, source_target_pairs={{0,4},{1,5},{2,6},{3,7},{4,0},{5,1},{6,2},{7,3},{8,12},{9,13},{10,... | collective-permute-start | bytes 1572872 | tf_op jit(solution)/shard_map/ppermute | solution.py:223
  6.7 7.7 %collective-permute-start = (bf16[256,512]{1,0:T(8,128)(2,1)}, bf16[256,512]{1,0:T(8,128)(2,1)S(1)}, u32[]{:S(2)}, u32[]{:S(2)}) collective-permute-start(bf16[256,512]{1,0:T(8,128)(2,1)} %state.1), channel_id=1, source_target_pairs={{0,16},{16,0},{1,17},{17,1},{2,18},{18,2},{3,19},{19,3},{4,20},{20... | collective-permute-start | bytes 786440 | tf_op jit(solution)/shard_map/ppermute | solution.py:24
  10.4 44.2 %collective-permute-start.15 = (bf16[7,64,1024]{2,1,0:T(8,128)(2,1)}, bf16[7,64,1024]{2,1,0:T(8,128)(2,1)}, u32[]{:S(2)}, u32[]{:S(2)}) collective-permute-start(bf16[7,64,1024]{2,1,0:T(8,128)(2,1)} %slice.88), channel_id=1, source_target_pairs={{0,2},{1,3},{2,0},{3,1},{4,6},{5,7},{6,4},{7,5},{8,10},{9,11},{10,... | collective-permute-start | bytes 2752520 | tf_op jit(solution)/shard_map/ppermute | solution.py:24
  14.4 1.0 copy-start.1
  15.4 57.9 %copy-start.3 = (bf16[1,16,128,128]{3,2,1,0:T(8,128)(2,1)S(1)}, bf16[1,16,128,128]{3,2,1,0:T(8,128)(2,1)}, u32[]{:S(2)}) copy-start(bf16[1,16,128,128]{3,2,1,0:T(8,128)(2,1)} %param.21) | copy-start | bytes 1572868
  17.3 4.4 %collective-permute-start.1 = (bf16[144,256]{1,0:T(8,128)(2,1)S(1)}, bf16[144,256]{1,0:T(8,128)(2,1)S(1)}, u32[]{:S(2)}, u32[]{:S(2)}) collective-permute-start(bf16[144,256]{1,0:T(8,128)(2,1)S(1)} %get-tuple-element.73), channel_id=1, source_target_pairs={{0,4},{1,5},{2,6},{3,7},{4,0},{5,1},{6,2},{7,3},{8,12},{9,13},{10,... | collective-permute-start | bytes 221192 | tf_op jit(solution)/shard_map/ppermute | solution.py:223
  17.6 8.0 %collective-permute-start.2 = (bf16[144,256]{1,0:T(8,128)(2,1)S(1)}, bf16[144,256]{1,0:T(8,128)(2,1)S(1)}, u32[]{:S(2)}, u32[]{:S(2)}) collective-permute-start(bf16[144,256]{1,0:T(8,128)(2,1)S(1)} %get-tuple-element.74), channel_id=1, source_target_pairs={{0,8},{1,9},{2,10},{3,11},{4,12},{5,13},{6,14},{7,15},{8,0},{9,1},... | collective-permute-start | bytes 221192 | tf_op jit(solution)/shard_map/ppermute | solution.py:223
  21.6 0.7 copy-start.15
  22.3 6.5 %collective-permute-start.3 = (bf16[144,256]{1,0:T(8,128)(2,1)}, bf16[144,256]{1,0:T(8,128)(2,1)}, u32[]{:S(2)}, u32[]{:S(2)}) collective-permute-start(bf16[144,256]{1,0:T(8,128)(2,1)} %get-tuple-element.75), channel_id=1, source_target_pairs={{0,12},{1,13},{2,14},{3,15},{4,8},{5,9},{6,10},{7,11},{8,4},{9,5},... | collective-permute-start | bytes 221192 | tf_op jit(solution)/shard_map/ppermute | solution.py:223
  25.6 0.6 copy-start.17
  26.3 28.4 %collective-permute-start.17 = (bf16[5,64,1024]{2,1,0:T(8,128)(2,1)}, bf16[5,64,1024]{2,1,0:T(8,128)(2,1)S(1)}, u32[]{:S(2)}, u32[]{:S(2)}) collective-permute-start(bf16[5,64,1024]{2,1,0:T(8,128)(2,1)} %slice.89), channel_id=1, source_target_pairs={{0,2},{1,3},{2,0},{3,1},{4,6},{5,7},{6,4},{7,5},{8,10},{9,11},{10,... | collective-permute-start | bytes 1966088 | tf_op jit(solution)/shard_map/ppermute | solution.py:24
  28.8 44.5 %collective-permute-start.14 = (bf16[12,64,1024]{2,1,0:T(8,128)(2,1)S(1)}, bf16[12,64,1024]{2,1,0:T(8,128)(2,1)}, u32[]{:S(2)}, u32[]{:S(2)}) collective-permute-start(bf16[12,64,1024]{2,1,0:T(8,128)(2,1)S(1)} %copy-done), channel_id=1, source_target_pairs={{0,1},{1,0},{2,3},{3,2},{4,5},{5,4},{6,7},{7,6},{8,9},{9,8},{10,11... | collective-permute-start | bytes 4718600 | tf_op jit(solution)/shard_map/ppermute | solution.py:24
  28.8 0.9 copy-start.14
  29.7 0.9 copy-start.16
  30.5 0.9 copy-start.18
  33.6 18.0 %collective-permute-start.4 = (bf16[4,128,256]{2,1,0:T(8,128)(2,1)}, bf16[4,128,256]{2,1,0:T(8,128)(2,1)}, u32[]{:S(2)}, u32[]{:S(2)}) collective-permute-start(bf16[4,128,256]{2,1,0:T(8,128)(2,1)} %get-tuple-element.77.refs_0_), channel_id=1, source_target_pairs={{0,2},{1,3},{2,0},{3,1},{4,6},{5,7},{6,4},{7,5},{8,10},{9,11},{10,... | collective-permute-start | bytes 786440 | tf_op jit(solution)/shard_map/ppermute | solution.py:24
  36.5 16.3 %collective-permute-start.5 = (bf16[4,128,256]{2,1,0:T(8,128)(2,1)}, bf16[4,128,256]{2,1,0:T(8,128)(2,1)S(1)}, u32[]{:S(2)}, u32[]{:S(2)}) collective-permute-start(bf16[4,128,256]{2,1,0:T(8,128)(2,1)} %get-tuple-element.77.refs_0_), channel_id=1, source_target_pairs={{0,16},{16,0},{1,17},{17,1},{2,18},{18,2},{3,19},{19,3},{4,20},{20... | collective-permute-start | bytes 786440 | tf_op jit(solution)/shard_map/ppermute | solution.py:24
  51.7 1.7 %collective-permute-start.7 = (bf16[4,128,256]{2,1,0:T(8,128)(2,1)}, bf16[4,128,256]{2,1,0:T(8,128)(2,1)S(1)}, u32[]{:S(2)}, u32[]{:S(2)}) collective-permute-start(bf16[4,128,256]{2,1,0:T(8,128)(2,1)} %get-tuple-element.77.refs_0_), channel_id=1, source_target_pairs={{0,1},{1,0},{2,3},{3,2},{4,5},{5,4},{6,7},{7,6},{8,9},{9,8},{10,11... | collective-permute-start | bytes 786440 | tf_op jit(solution)/shard_map/ppermute | solution.py:24
  52.8 14.5 %collective-permute-start.13 = (bf16[16,128,128]{2,1,0:T(8,128)(2,1)S(1)}, bf16[16,128,128]{2,1,0:T(8,128)(2,1)}, u32[]{:S(2)}, u32[]{:S(2)}) collective-permute-start(bf16[16,128,128]{2,1,0:T(8,128)(2,1)S(1)} %broadcast_select_fusion), channel_id=1, source_target_pairs={{0,8},{1,9},{2,10},{3,11},{8,12},{9,13},{10,14},{11,15},{12,4},{13... | collective-permute-start | bytes 1572872 | tf_op jit(solution)/shard_map/ppermute | solution.py:223
  53.4 0.7 copy-start.7
  54.1 8.7 %collective-permute-start.6 = (bf16[4,128,256]{2,1,0:T(8,128)(2,1)}, bf16[4,128,256]{2,1,0:T(8,128)(2,1)}, u32[]{:S(2)}, u32[]{:S(2)}) collective-permute-start(bf16[4,128,256]{2,1,0:T(8,128)(2,1)} %collective-permute-done.4.refs_1_), channel_id=1, source_target_pairs={{0,16},{16,0},{1,17},{17,1},{2,18},{18,2},{3,19},{19,3},{4,20},{20... | collective-permute-start | bytes 786440 | tf_op jit(solution)/shard_map/ppermute | solution.py:24
  54.7 8.8 %collective-permute-start.8 = (bf16[4,128,256]{2,1,0:T(8,128)(2,1)}, bf16[4,128,256]{2,1,0:T(8,128)(2,1)S(1)}, u32[]{:S(2)}, u32[]{:S(2)}) collective-permute-start(bf16[4,128,256]{2,1,0:T(8,128)(2,1)} %collective-permute-done.4.refs_1_), channel_id=1, source_target_pairs={{0,1},{1,0},{2,3},{3,2},{4,5},{5,4},{6,7},{7,6},{8,9},{9,8},{10,11... | collective-permute-start | bytes 786440 | tf_op jit(solution)/shard_map/ppermute | solution.py:24
  54.7 18.6 %collective-permute-start.16 = (bf16[7,64,1024]{2,1,0:T(8,128)(2,1)}, bf16[7,64,1024]{2,1,0:T(8,128)(2,1)}, u32[]{:S(2)}, u32[]{:S(2)}) collective-permute-start(bf16[7,64,1024]{2,1,0:T(8,128)(2,1)} %collective-permute-done.15.refs_13_), channel_id=1, source_target_pairs={{0,1},{1,0},{2,3},{3,2},{4,5},{5,4},{6,7},{7,6},{8,9},{9,8},{10,11... | collective-permute-start | bytes 2752520 | tf_op jit(solution)/shard_map/ppermute | solution.py:24
  62.8 5.8 %collective-permute-start.9 = (bf16[4,128,256]{2,1,0:T(8,128)(2,1)S(1)}, bf16[4,128,256]{2,1,0:T(8,128)(2,1)S(1)}, u32[]{:S(2)}, u32[]{:S(2)}) collective-permute-start(bf16[4,128,256]{2,1,0:T(8,128)(2,1)S(1)} %collective-permute-done.5.refs_2_), channel_id=1, source_target_pairs={{0,1},{1,0},{2,3},{3,2},{4,5},{5,4},{6,7},{7,6},{8,9},{9,8},{10,11... | collective-permute-start | bytes 786440 | tf_op jit(solution)/shard_map/ppermute | solution.py:24
  62.8 0.7 copy-start.5
  63.5 0.7 copy-start.9
  64.2 16.3 %collective-permute-start.18 = (bf16[5,64,1024]{2,1,0:T(8,128)(2,1)S(1)}, bf16[5,64,1024]{2,1,0:T(8,128)(2,1)}, u32[]{:S(2)}, u32[]{:S(2)}) collective-permute-start(bf16[5,64,1024]{2,1,0:T(8,128)(2,1)S(1)} %collective-permute-done.17.refs_0_), channel_id=1, source_target_pairs={{0,1},{1,0},{2,3},{3,2},{4,5},{5,4},{6,7},{7,6},{8,9},{9,8},{10,11... | collective-permute-start | bytes 1966088 | tf_op jit(solution)/shard_map/ppermute | solution.py:24
  67.3 16.6 %collective-permute-start.22 = (bf16[16,128,128]{2,1,0:T(8,128)(2,1)}, bf16[16,128,128]{2,1,0:T(8,128)(2,1)}, u32[]{:S(2)}, u32[]{:S(2)}) collective-permute-start(bf16[16,128,128]{2,1,0:T(8,128)(2,1)} %collective-permute-done.13.refs_10_), channel_id=1, source_target_pairs={{8,12},{9,13},{10,14},{11,15},{4,0},{5,1},{6,2},{7,3},{24,28},{25,... | collective-permute-start | bytes 1572872 | tf_op jit(solution)/shard_map/ppermute | solution.py:223
  68.6 0.7 copy-start.11
  69.3 4.0 %collective-permute-start.10 = (bf16[4,128,256]{2,1,0:T(8,128)(2,1)}, bf16[4,128,256]{2,1,0:T(8,128)(2,1)}, u32[]{:S(2)}, u32[]{:S(2)}) collective-permute-start(bf16[4,128,256]{2,1,0:T(8,128)(2,1)} %collective-permute-done.6.refs_3_), channel_id=1, source_target_pairs={{0,1},{1,0},{2,3},{3,2},{4,5},{5,4},{6,7},{7,6},{8,9},{9,8},{10,11... | collective-permute-start | bytes 786440 | tf_op jit(solution)/shard_map/ppermute | solution.py:24
  73.3 1.0 copy-start.6
  74.2 0.9 copy-start.8
  75.2 0.9 copy-start.10
  76.1 0.9 copy-start.12
  82.8 12.6 %collective-permute-start.25 = (bf16[256,512]{1,0:T(8,128)(2,1)S(1)}, bf16[256,512]{1,0:T(8,128)(2,1)S(1)}, u32[]{:S(2)}, u32[]{:S(2)}) collective-permute-start(bf16[256,512]{1,0:T(8,128)(2,1)S(1)} %get-tuple-element.90), channel_id=1, source_target_pairs={{0,16},{16,0},{1,17},{17,1},{2,18},{18,2},{3,19},{19,3},{4,20},{20... | collective-permute-start | bytes 786440 | tf_op jit(solution)/shard_map/ppermute | solution.py:24
  86.3 11.6 %collective-permute-start.23 = (bf16[256,512]{1,0:T(8,128)(2,1)S(1)}, bf16[256,512]{1,0:T(8,128)(2,1)S(1)}, u32[]{:S(2)}, u32[]{:S(2)}) collective-permute-start(bf16[256,512]{1,0:T(8,128)(2,1)S(1)} %get-tuple-element.88), channel_id=1, source_target_pairs={{0,16},{16,0},{1,17},{17,1},{2,18},{18,2},{3,19},{19,3},{4,20},{20... | collective-permute-start | bytes 786440 | tf_op jit(solution)/shard_map/ppermute | solution.py:24
  93.3 15.3 %copy-start.2 = (bf16[256,512]{1,0:T(8,128)(2,1)S(1)}, bf16[256,512]{1,0:T(8,128)(2,1)}, u32[]{:S(2)}) copy-start(bf16[256,512]{1,0:T(8,128)(2,1)} %state.1) | copy-start | bytes 786436
  93.3 15.3 %copy-start.4 = (bf16[1024,512]{1,0:T(8,128)(2,1)S(1)}, bf16[1024,512]{1,0:T(8,128)(2,1)}, u32[]{:S(2)}) copy-start(bf16[1024,512]{1,0:T(8,128)(2,1)} %weight.1) | copy-start | bytes 3145732
  93.3 15.3 %copy-start.20 = (f32[512]{0:T(512)S(1)}, f32[512]{0:T(512)}, u32[]{:S(2)}) copy-start(f32[512]{0:T(512)} %param.19) | copy-start | bytes 6148
  93.3 9.4 %collective-permute-start.20 = (bf16[256,512]{1,0:T(8,128)(2,1)S(1)}, bf16[256,512]{1,0:T(8,128)(2,1)S(1)}, u32[]{:S(2)}, u32[]{:S(2)}) collective-permute-start(bf16[256,512]{1,0:T(8,128)(2,1)S(1)} %get-tuple-element.85), channel_id=1, source_target_pairs={{0,16},{16,0},{1,17},{17,1},{2,18},{18,2},{3,19},{19,3},{4,20},{20... | collective-permute-start | bytes 786440 | tf_op jit(solution)/shard_map/ppermute | solution.py:24
  94.3 14.8 %collective-permute-start.19 = (bf16[256,512]{1,0:T(8,128)(2,1)S(1)}, bf16[256,512]{1,0:T(8,128)(2,1)S(1)}, u32[]{:S(2)}, u32[]{:S(2)}) collective-permute-start(bf16[256,512]{1,0:T(8,128)(2,1)S(1)} %get-tuple-element.83), channel_id=1, source_target_pairs={{0,16},{16,0},{1,17},{17,1},{2,18},{18,2},{3,19},{19,3},{4,20},{20... | collective-permute-start | bytes 786440 | tf_op jit(solution)/shard_map/ppermute | solution.py:24
  95.5 12.3 %collective-permute-start.26 = (bf16[256,512]{1,0:T(8,128)(2,1)S(1)}, bf16[256,512]{1,0:T(8,128)(2,1)S(1)}, u32[]{:S(2)}, u32[]{:S(2)}) collective-permute-start(bf16[256,512]{1,0:T(8,128)(2,1)S(1)} %add_convert_fusion.1), channel_id=1, source_target_pairs={{0,4},{1,5},{2,6},{3,7},{4,12},{5,13},{6,14},{7,15},{12,8},{13,9},... | collective-permute-start | bytes 786440 | tf_op jit(solution)/shard_map/ppermute | solution.py:223
  97.9 18.6 %copy-start.19 = (f32[512]{0:T(512)S(1)}, f32[512]{0:T(512)}, u32[]{:S(2)}) copy-start(f32[512]{0:T(512)} %param.20) | copy-start | bytes 6148
  98.0 13.2 %collective-permute-start.24 = (bf16[256,512]{1,0:T(8,128)(2,1)S(1)}, bf16[256,512]{1,0:T(8,128)(2,1)S(1)}, u32[]{:S(2)}, u32[]{:S(2)}) collective-permute-start(bf16[256,512]{1,0:T(8,128)(2,1)S(1)} %add_convert_fusion.2), channel_id=1, source_target_pairs={{0,12},{1,13},{2,14},{3,15},{12,0},{13,1},{14,2},{15,3},{16,28},{1... | collective-permute-start | bytes 786440 | tf_op jit(solution)/shard_map/ppermute | solution.py:223
  102.8 13.7 %collective-permute-start.21 = (bf16[256,512]{1,0:T(8,128)(2,1)S(1)}, bf16[256,512]{1,0:T(8,128)(2,1)S(1)}, u32[]{:S(2)}, u32[]{:S(2)}) collective-permute-start(bf16[256,512]{1,0:T(8,128)(2,1)S(1)} %add_convert_fusion.3), channel_id=1, source_target_pairs={{0,4},{1,5},{2,6},{3,7},{4,0},{5,1},{6,2},{7,3},{8,12},{9,13},{10,... | collective-permute-start | bytes 786440 | tf_op jit(solution)/shard_map/ppermute | solution.py:223
  107.9 8.6 %collective-permute-start.27 = (bf16[256,512]{1,0:T(8,128)(2,1)S(1)}, bf16[256,512]{1,0:T(8,128)(2,1)S(1)}, u32[]{:S(2)}, u32[]{:S(2)}) collective-permute-start(bf16[256,512]{1,0:T(8,128)(2,1)S(1)} %add_convert_fusion), channel_id=1, source_target_pairs={{4,8},{5,9},{6,10},{7,11},{8,4},{9,5},{10,6},{11,7},{20,24},{21,25... | collective-permute-start | bytes 786440 | tf_op jit(solution)/shard_map/ppermute | solution.py:223
  (2 other events, 1.2 us)

commit v8 on v7

--- a/solution.py
+++ b/solution.py
@@ -17,7 +17,8 @@
 GROUP = 4
 NOTE_ROWS = 16
 
-HOME = 16
+PLACE, TARGET, RELATION, FIRST, TURNS, MEMBER, REL, EDGE = range(8)
+LANES = 128
 
 
 def swap(value, axis, size, bit):
@@ -25,18 +26,25 @@
 
 
 def pack_kernel(n_rel, where, note, *refs):
-    halves, outs = refs[:n_rel], refs[n_rel:]
+    halves, outs, sems = refs[:n_rel], refs[n_rel:-1], refs[-1]
     rows, width = outs[0].shape[0] - NOTE_ROWS, outs[0].shape[1]
     first = pl.multiple_of(where[2, 0], rows)
+    copies = []
     for j, out in enumerate(outs):
         start = pl.multiple_of(where[1, j], width)
-        for r in range(n_rel):
-
-            @pl.when(where[0, j] == r)
-            def _(r=r, out=out, start=start):
-                out[:rows] = halves[r][pl.ds(first, rows), pl.ds(start, width)]
-
+        options = [
+            pltpu.make_async_copy(
+                half.at[pl.ds(first, rows), pl.ds(start, width)], out.at[pl.ds(0, rows), :], sems.at[j]
+            )
+            for half in halves
+        ]
+        for r, option in enumerate(options):
+            pl.when(where[0, j] == r)(option.start)
+        copies.append(options[0])
+    for out in outs:
         out[rows:] = note[...]
+    for copy in copies:
+        copy.wait()
 
 
 def gate_kernel(n_rel, rel, weight, bias, *refs):
@@ -49,12 +57,33 @@
     out[...] = jax.nn.sigmoid(total)
 
 
-def stack_kernel(count, *refs):
-    pieces, (out, notes) = refs[:count], refs[count:]
+def stack_kernel(count, sizes, here, *refs):
+    pieces, (out, table) = refs[:count], refs[count:]
+    members, per_tile, tile_rows, slots = sizes
+    part, member = here[0], here[1]
     rows = out.shape[1]
+    tile_bits, member_bits = per_tile.bit_length() - 1, members.bit_length() - 1
+    lane = lax.broadcasted_iota(jnp.int32, (1, LANES), 1)
     for j, piece in enumerate(pieces):
         out[j] = piece[:rows]
-        notes[j] = piece[rows:]
+        note = piece[rows:, :LANES].astype(F32).astype(jnp.int32)
+        source, live_total = note[0:1], note[3:4]
+        live = jnp.logical_and(lane < live_total, lane < slots)
+        owner = lax.shift_right_logical(source, tile_bits)
+        place = lax.bitwise_xor(owner & (members - 1), member) * count
+        place = place + lax.bitwise_xor(lax.shift_right_logical(owner, member_bits), part)
+        values = {
+            PLACE: jnp.where(live, place, 0),
+            TARGET: jnp.where(live, note[1:2], per_tile),
+            RELATION: jnp.where(live, note[2:3], 0),
+            FIRST: jnp.where(live, (source & (per_tile - 1)) * tile_rows, 0),
+            TURNS: lax.shift_right_logical(live_total + (GROUP - 1), GROUP.bit_length() - 1),
+            MEMBER: jnp.full((1, LANES), member, jnp.int32),
+            REL: jnp.full((1, LANES), here[2], jnp.int32),
+            EDGE: jnp.full((1, LANES), here[3], jnp.int32),
+        }
+        for row, value in values.items():
+            table[8 * j + row:8 * j + row + 1, :] = value
 
 
 def take(refs, *counts):
@@ -94,34 +123,34 @@
     return loads
 
 
-def multiply_tiles(turns, table, base, swapped, lists, rows_held, made):
+def multiply_tiles(table, j, swapped, lists, rows_held, made):
     tile_rows = lists.shape[1]
 
     def step(n, _):
         for u in range(GROUP):
             s = n * GROUP + u
-            first = pl.multiple_of(table[3, base + s], tile_rows)
-            rows = rows_held[table[0, base + s], pl.ds(first, tile_rows), :]
+            first = pl.multiple_of(table[8 * j + FIRST, s], tile_rows)
+            rows = rows_held[table[8 * j + PLACE, s], pl.ds(first, tile_rows), :]
             product = jnp.dot(lists[s], rows, preferred_element_type=F32)
             turned = pltpu.roll(product, product.shape[1] // 2, 1)
             made[s] = jnp.where(swapped, turned, product).astype(BF16)
         return 0
 
-    lax.fori_loop(0, turns, step, 0)
-
-
-def add_messages(turns, table, base, made, own, other, acc):
+    lax.fori_loop(0, table[8 * j + TURNS, 0], step, 0)
+
+
+def add_messages(table, j, made, own, other, acc):
     acc[:-1] = jnp.zeros((acc.shape[0] - 1,) + acc.shape[1:], F32)
 
     def step(n, _):
         for u in range(GROUP):
             s = n * GROUP + u
-            relation = table[2, base + s]
+            relation = table[8 * j + RELATION, s]
             weight = jnp.concatenate([own[relation], other[relation]], axis=0)
-            acc[table[1, base + s]] += jnp.dot(made[s], weight, preferred_element_type=F32)
+            acc[table[8 * j + TARGET, s]] += jnp.dot(made[s], weight, preferred_element_type=F32)
         return 0
 
-    lax.fori_loop(0, turns, step, 0)
+    lax.fori_loop(0, table[8 * j + TURNS, 0], step, 0)
 
 
 def put_messages(n_rel, rel, acc, outs):
@@ -137,23 +166,22 @@
     half = members // 2
     states, tiles, weights, others, rest = take(refs, len(places), sum(way_counts), half, half)
     made, held, other, rows_held, lists, state_sem, tile_sem, weight_sem, other_sem = rest
-    slots = lists.shape[1]
     chunks, rows = states[0].shape[0], states[0].shape[1]
     loads = []
     for n, ((i, r), ref) in enumerate(zip(places, states)):
-        first = pl.multiple_of(lax.bitwise_xor(table[4, HOME + 1], r) * rows, rows)
+        first = pl.multiple_of(lax.bitwise_xor(table[REL, 0], r) * rows, rows)
         to = rows_held.at[pl.ds(i * chunks, chunks), pl.ds(first, rows), :]
         loads.append(pltpu.make_async_copy(ref, to, state_sem.at[n]))
         loads[-1].start()
-    tile_loads = start_tiles(way_counts, table[4, HOME + 2], tiles, lists, tile_sem)
-    weight_loads = start_weights(members, table[4, HOME], weights, 0, held, weight_sem)
-    weight_loads += start_weights(members, table[4, HOME], others, 0, other, other_sem)
+    tile_loads = start_tiles(way_counts, table[EDGE, 0], tiles, lists, tile_sem)
+    weight_loads = start_weights(members, table[MEMBER, 0], weights, 0, held, weight_sem)
+    weight_loads += start_weights(members, table[MEMBER, 0], others, 0, other, other_sem)
     for load in loads:
         load.wait()
-    swapped = table[4, HOME] >= members // 2
+    swapped = table[MEMBER, 0] >= members // 2
     for j, load in enumerate(tile_loads):
         load.wait()
-        multiply_tiles(table[4, j], table, j * slots, swapped, lists.at[j], rows_held, made.at[j])
+        multiply_tiles(table, j, swapped, lists.at[j], rows_held, made.at[j])
     for load in weight_loads:
         load.wait()
 
@@ -162,34 +190,29 @@
     weights, outs, rest = take(refs, members // 2, n_rel)
     other, acc, weight_sem = rest
     del begun
-    slots = made.shape[1]
     low = other.shape[0] - weights[0].shape[0]
-    for load in start_weights(members, table[4, HOME], weights, low, other, weight_sem):
+    for load in start_weights(members, table[MEMBER, 0], weights, low, other, weight_sem):
         load.wait()
-    add_messages(table[4, j], table, j * slots, made.at[j], own, other, acc)
-    put_messages(n_rel, table[4, HOME + 1], acc, outs)
+    add_messages(table, j, made.at[j], own, other, acc)
+    put_messages(n_rel, table[REL, 0], acc, outs)
 
 
 def late_kernel(members, way_counts, js, n_rel, table, rows_held, own, other, *refs):
     tiles, outs, rest = take(refs, sum(way_counts), len(js) * n_rel)
     lists, made, acc, tile_sem = rest
-    slots = lists.shape[1]
-    loads = start_tiles(way_counts, table[4, HOME + 2], tiles, lists, tile_sem)
+    loads = start_tiles(way_counts, table[EDGE, 0], tiles, lists, tile_sem)
     for g, j in enumerate(js):
         loads[g].wait()
-        multiply_tiles(
-            table[4, j], table, j * slots, table[4, HOME] >= members // 2, lists.at[g], rows_held, made.at[g]
-        )
-        add_messages(table[4, j], table, j * slots, made.at[g], own, other, acc)
-        put_messages(n_rel, table[4, HOME + 1], acc, outs[g * n_rel:(g + 1) * n_rel])
+        multiply_tiles(table, j, table[MEMBER, 0] >= members // 2, lists.at[g], rows_held, made.at[g])
+        add_messages(table, j, made.at[g], own, other, acc)
+        put_messages(n_rel, table[REL, 0], acc, outs[g * n_rel:(g + 1) * n_rel])
 
 
 def near_kernel(js, n_rel, table, made, own, other, *refs):
     outs, acc = refs[:-1], refs[-1]
-    slots = made.shape[1]
     for g, j in enumerate(js):
-        add_messages(table[4, j], table, j * slots, made.at[j], own, other, acc)
-        put_messages(n_rel, table[4, HOME + 1], acc, outs[g * n_rel:(g + 1) * n_rel])
+        add_messages(table, j, made.at[j], own, other, acc)
+        put_messages(n_rel, table[REL, 0], acc, outs[g * n_rel:(g + 1) * n_rel])
 
 
 def finish_kernel(used, state, gate_open, bias, *refs):
@@ -241,7 +264,7 @@
 
     note = jnp.zeros((NOTE_ROWS, width), BF16)
     note = note.at[:3, :slots].set(tile_index[0].astype(BF16))
-    note = note.at[3, :1].set(tile_count[0].astype(BF16))
+    note = note.at[3].set(tile_count[0, 0].astype(BF16))
     asked = lax.bitwise_xor(part, jnp.arange(chunks, dtype=jnp.int32))
     per_half = chunks // n_rel
     where = jnp.stack([
@@ -252,42 +275,28 @@
     pieces = pl.pallas_call(
         functools.partial(pack_kernel, n_rel),
         out_shape=[jax.ShapeDtypeStruct((rows + NOTE_ROWS, width), BF16) for _ in range(chunks)],
-        in_specs=[SMEM] + [VMEM] * (n_rel + 1),
+        in_specs=[SMEM, VMEM] + [HBM] * n_rel,
         out_specs=[VMEM] * chunks,
+        scratch_shapes=[pltpu.SemaphoreType.DMA((chunks,))],
         compiler_params=pltpu.CompilerParams(vmem_limit_bytes=8 << 20),
         name="pack",
     )(where, note, *halves)
     moved = [partner(pieces[j], j) for j in range(1, chunks)]
-    own, notes = pl.pallas_call(
-        functools.partial(stack_kernel, chunks),
+    assert per_tile & (per_tile - 1) == 0 and members & (members - 1) == 0 and slots <= LANES <= width
+    here = jnp.stack([part, member, rel, edge])
+    own, table = pl.pallas_call(
+        functools.partial(stack_kernel, chunks, (members, per_tile, tile_rows, slots)),
         out_shape=[
             jax.ShapeDtypeStruct((chunks, rows, width), BF16),
-            jax.ShapeDtypeStruct((chunks, NOTE_ROWS, width), BF16),
+            jax.ShapeDtypeStruct((8 * chunks, LANES), jnp.int32),
         ],
-        in_specs=[VMEM] * chunks,
+        in_specs=[SMEM] + [VMEM] * chunks,
         out_specs=[VMEM] * 2,
         compiler_params=pltpu.CompilerParams(vmem_limit_bytes=8 << 20),
         name="stk",
-    )(pieces[0], *moved)
-    notes = notes[:, :4, :slots].astype(jnp.int32)
-    counts = notes[:, 3, 0]
-    source, target, relation = notes[:, 0], notes[:, 1], notes[:, 2]
-    live = jnp.arange(slots, dtype=jnp.int32)[None] < counts[:, None]
-    owner = source // per_tile
-    place = lax.bitwise_xor(owner % members, member) * chunks
-    place = place + lax.bitwise_xor(part, owner // members)
-    turns = (counts + GROUP - 1) // GROUP
-    last = jnp.zeros((chunks * slots,), jnp.int32).at[:chunks].set(turns)
-    last = last.at[HOME:HOME + 3].set(jnp.stack([member, rel, edge]))
-    table = jnp.stack([
-        jnp.where(live, place, 0).reshape(-1),
-        jnp.where(live, target, per_tile).reshape(-1),
-        jnp.where(live, relation, 0).reshape(-1),
-        (source % per_tile * tile_rows).reshape(-1),
-        last,
-    ])
-
-    cut = max(1, rel_dev * 7 // 12)
+    )(here, pieces[0], *moved)
+
+    cut = max(1, rel_dev * 2 // 3)
     parts = [rel_weight[:cut]]
     parts.append(rel_weight[cut:])
     bits = [1 << b for b in reversed(range(members.bit_length() - 1))]

time: 118 us -> 108 us (0.915)
  waiting for transfers between devices: 36 us -> 48.8 us
  local copies, waits for them, and re-layouts: 20.6 us -> 8.41 us
  starting transfers between devices: 39 us -> 34.4 us
  other arithmetic: 4.76 us -> 1.26 us
  Pallas kernels: 16.3 us -> 13.1 us
    ppermute x11, waiting for transfers between devices: 12.7 us -> 27.2 us  [along(): return lax.ppermute(value, 'ent', perm)]
    unnamed x45 -> x23, local copies, waits for them, and re-layouts: 12.7 us -> 4.01 us
    ppermute x11, starting transfers between devices: 23.6 us -> 17.3 us  [along(): return lax.ppermute(value, 'ent', perm)]
    ppermute x17, starting transfers between devices: 15.4 us -> 17.1 us  [swap(): return lax.ppermute(value, axis, [(i, i ^ bit) for i in range(size)])]
    ppermute x17, waiting for transfers between devices: 23.2 us -> 21.7 us  [swap(): return lax.ppermute(value, axis, [(i, i ^ bit) for i in range(size)])]
    pallas_call x5, Pallas kernels: 11.9 us -> 10.4 us  [call(): pl.pallas_call(body, out_shape=out_shape, in_specs=[SMEM] + in_specs, out...]
    scatter x2 -> x1, local copies, waits for them, and re-layouts: 1.23 us -> 0.04 us  [shards(): note = note.at[3].set(tile_count[0, 0].astype(BF16))]
    another operation x2 -> x1, local copies, waits for them, and re-layouts: 1.19 us -> 0.01 us  [shards(): jnp.stack([jnp.where(live, place, 0).reshape(-1), jnp.where(live, target,...]
  transfers between devices with their start and end apart: 28 -> 28, of which waited for: 10 -> 10; matrix products, arithmetic and copies ran while one was open for 11% -> 3% of each run, Pallas kernels for 13% -> 11%
where the time goes in v8:
time: 108 us; the launch traced here: 107 us
  waiting for transfers between devices  48.8 us (45%)
  starting transfers between devices  34.4 us (32%)
  Pallas kernels  13.1 us (12%)
  local copies, waits for them, and re-layouts  8.41 us (8%)
  other arithmetic  1.26 us (1%)
    ppermute x11, waiting for transfers between devices, along(): return lax.ppermute(value, 'ent', perm)  27.2 us
    ppermute x17, waiting for transfers between devices, swap(): return lax.ppermute(value, axis, [(i, i ^ bit) for i in range(size)])  21.7 us
    ppermute x11, starting transfers between devices, along(): return lax.ppermute(value, 'ent', perm)  17.3 us
    ppermute x17, starting transfers between devices, swap(): return lax.ppermute(value, axis, [(i, i ^ bit) for i in range(size)])  17.1 us
    pallas_call x5, Pallas kernels, call(): pl.pallas_call(body, out_shape=out_shape, in_specs=[SMEM] + in_specs, out...  10.4 us
    unnamed x23, local copies, waits for them, and re-layouts  4.01 us
    slice x1, local copies, waits for them, and re-layouts, shards(): parts = [rel_weight[:cut]]  2.41 us
  transfers between devices with their start and end apart: 28, of which 10 were waited for; matrix products, arithmetic and copies ran while one was open for 3% of the time, Pallas kernels for 11%

profile of v8, /device:TPU:0, one launch (start us, length us, event | category | flops | bytes accessed | tf_op | source)
XLA Modules:
  0.0 106.9 jit_solution(16004488892296650419)
XLA Ops:
  0.0 2.4 %slice.41 = bf16[8,64,1024]{2,1,0:T(8,128)(2,1)} slice(bf16[12,64,1024]{2,1,0:T(8,128)(2,1)} %refs_11_.1), slice={[0:8], [0:64], [0:1024]} | slice | bytes 2097152 | tf_op jit(solution)/shard_map/slice | solution.py:300
  2.4 3.0 %collective-permute-start.15 = (bf16[8,64,1024]{2,1,0:T(8,128)(2,1)}, bf16[8,64,1024]{2,1,0:T(8,128)(2,1)}, u32[]{:S(2)}, u32[]{:S(2)}) collective-permute-start(bf16[8,64,1024]{2,1,0:T(8,128)(2,1)} %slice.41), channel_id=1, source_target_pairs={{0,2},{1,3},{2,0},{3,1},{4,6},{5,7},{6,4},{7,5},{8,10},{9,11},{10,... | collective-permute-start | bytes 3145736 | tf_op jit(solution)/shard_map/ppermute | solution.py:25
  5.4 1.5 %collective-permute-start = (bf16[256,512]{1,0:T(8,128)(2,1)}, bf16[256,512]{1,0:T(8,128)(2,1)S(1)}, u32[]{:S(2)}, u32[]{:S(2)}) collective-permute-start(bf16[256,512]{1,0:T(8,128)(2,1)} %state.1), channel_id=1, source_target_pairs={{0,16},{16,0},{1,17},{17,1},{2,18},{18,2},{3,19},{19,3},{4,20},{20... | collective-permute-start | bytes 786440 | tf_op jit(solution)/shard_map/ppermute | solution.py:25
  7.0 0.7 convert_element_type.46
  8.5 4.9 %collective-permute-done.refs_1_ = bf16[256,512]{1,0:T(8,128)(2,1)S(1)} collective-permute-done((bf16[256,512]{1,0:T(8,128)(2,1)}, bf16[256,512]{1,0:T(8,128)(2,1)S(1)}, u32[]{:S(2)}, u32[]{:S(2)}) %collective-permute-start) | collective-permute-done | bytes 262176 | tf_op jit(solution)/shard_map/ppermute | solution.py:25
  13.4 0.9 copy-done.1
  14.3 0.7 pack.1
  15.0 1.6 %collective-permute-start.1 = (bf16[144,256]{1,0:T(8,128)(2,1)S(1)}, bf16[144,256]{1,0:T(8,128)(2,1)S(1)}, u32[]{:S(2)}, u32[]{:S(2)}) collective-permute-start(bf16[144,256]{1,0:T(8,128)(2,1)S(1)} %get-tuple-element.49), channel_id=1, source_target_pairs={{0,4},{1,5},{2,6},{3,7},{4,0},{5,1},{6,2},{7,3},{8,12},{9,13},{10,... | collective-permute-start | bytes 221192 | tf_op jit(solution)/shard_map/ppermute | solution.py:246
  16.7 2.6 %collective-permute-start.2 = (bf16[144,256]{1,0:T(8,128)(2,1)S(1)}, bf16[144,256]{1,0:T(8,128)(2,1)S(1)}, u32[]{:S(2)}, u32[]{:S(2)}) collective-permute-start(bf16[144,256]{1,0:T(8,128)(2,1)S(1)} %get-tuple-element.50), channel_id=1, source_target_pairs={{0,8},{1,9},{2,10},{3,11},{4,12},{5,13},{6,14},{7,15},{8,0},{9,1},... | collective-permute-start | bytes 221192 | tf_op jit(solution)/shard_map/ppermute | solution.py:246
  19.3 0.7 collective-permute-start.12
  20.0 2.2 %collective-permute-start.11 = (bf16[16,128,128]{2,1,0:T(8,128)(2,1)}, bf16[16,128,128]{2,1,0:T(8,128)(2,1)}, u32[]{:S(2)}, u32[]{:S(2)}) collective-permute-start(bf16[16,128,128]{2,1,0:T(8,128)(2,1)} %bitcast.14), channel_id=1, source_target_pairs={{0,4},{1,5},{2,6},{3,7},{4,0},{5,1},{6,2},{7,3},{8,12},{9,13},{10,... | collective-permute-start | bytes 1572872 | tf_op jit(solution)/shard_map/ppermute | solution.py:246
  22.1 1.9 %slice.42 = bf16[4,64,1024]{2,1,0:T(8,128)(2,1)} slice(bf16[12,64,1024]{2,1,0:T(8,128)(2,1)} %refs_11_.1), slice={[8:12], [0:64], [0:1024]} | slice | bytes 1048576 | tf_op jit(solution)/shard_map/slice | solution.py:301
  24.0 0.5 collective-permute-start.17
  24.5 0.6 copy-done.5
  25.2 2.5 %collective-permute-start.3 = (bf16[144,256]{1,0:T(8,128)(2,1)S(1)}, bf16[144,256]{1,0:T(8,128)(2,1)S(1)}, u32[]{:S(2)}, u32[]{:S(2)}) collective-permute-start(bf16[144,256]{1,0:T(8,128)(2,1)S(1)} %get-tuple-element.51), channel_id=1, source_target_pairs={{0,12},{1,13},{2,14},{3,15},{4,8},{5,9},{6,10},{7,11},{8,4},{9,5},... | collective-permute-start | bytes 221192 | tf_op jit(solution)/shard_map/ppermute | solution.py:246
  27.6 8.6 %collective-permute-done.3.refs_3_ = bf16[144,256]{1,0:T(8,128)(2,1)S(1)} collective-permute-done((bf16[144,256]{1,0:T(8,128)(2,1)S(1)}, bf16[144,256]{1,0:T(8,128)(2,1)S(1)}, u32[]{:S(2)}, u32[]{:S(2)}) %collective-permute-start.3) | collective-permute-done | bytes 73760 | tf_op jit(solution)/shard_map/ppermute | solution.py:246
  36.3 0.6 copy-done.7
  37.0 0.9 copy-done.6
  37.9 0.9 copy-done.8
  38.8 0.6 stk.1
  39.3 0.6 collective-permute-start.4
  39.9 1.5 %collective-permute-start.5 = (bf16[4,128,256]{2,1,0:T(8,128)(2,1)S(1)}, bf16[4,128,256]{2,1,0:T(8,128)(2,1)S(1)}, u32[]{:S(2)}, u32[]{:S(2)}) collective-permute-start(bf16[4,128,256]{2,1,0:T(8,128)(2,1)S(1)} %get-tuple-element.53.refs_0_), channel_id=1, source_target_pairs={{0,16},{16,0},{1,17},{17,1},{2,18},{18,2},{3,19},{19,3},{4,20},{20... | collective-permute-start | bytes 786440 | tf_op jit(solution)/shard_map/ppermute | solution.py:25
  41.4 0.5 collective-permute-start.16
  42.0 6.1 %collective-permute-done.4.refs_1_ = bf16[4,128,256]{2,1,0:T(8,128)(2,1)S(1)} collective-permute-done((bf16[4,128,256]{2,1,0:T(8,128)(2,1)S(1)}, bf16[4,128,256]{2,1,0:T(8,128)(2,1)S(1)}, u32[]{:S(2)}, u32[]{:S(2)}) %collective-permute-start.4) | collective-permute-done | bytes 262176 | tf_op jit(solution)/shard_map/ppermute | solution.py:25
  48.1 2.4 %collective-permute-start.13 = (bf16[16,128,128]{2,1,0:T(8,128)(2,1)S(1)}, bf16[16,128,128]{2,1,0:T(8,128)(2,1)S(1)}, u32[]{:S(2)}, u32[]{:S(2)}) collective-permute-start(bf16[16,128,128]{2,1,0:T(8,128)(2,1)S(1)} %broadcast_select_fusion), channel_id=1, source_target_pairs={{0,8},{1,9},{2,10},{3,11},{8,12},{9,13},{10,14},{11,15},{12,4},{13... | collective-permute-start | bytes 1572872 | tf_op jit(solution)/shard_map/ppermute | solution.py:246
  50.5 1.5 %collective-permute-start.6 = (bf16[4,128,256]{2,1,0:T(8,128)(2,1)S(1)}, bf16[4,128,256]{2,1,0:T(8,128)(2,1)S(1)}, u32[]{:S(2)}, u32[]{:S(2)}) collective-permute-start(bf16[4,128,256]{2,1,0:T(8,128)(2,1)S(1)} %collective-permute-done.4.refs_1_), channel_id=1, source_target_pairs={{0,16},{16,0},{1,17},{17,1},{2,18},{18,2},{3,19},{19,3},{4,20},{20... | collective-permute-start | bytes 786440 | tf_op jit(solution)/shard_map/ppermute | solution.py:25
  52.0 6.1 %collective-permute-done.6.refs_3_ = bf16[4,128,256]{2,1,0:T(8,128)(2,1)S(1)} collective-permute-done((bf16[4,128,256]{2,1,0:T(8,128)(2,1)S(1)}, bf16[4,128,256]{2,1,0:T(8,128)(2,1)S(1)}, u32[]{:S(2)}, u32[]{:S(2)}) %collective-permute-start.6) | collective-permute-done | bytes 262176 | tf_op jit(solution)/shard_map/ppermute | solution.py:25
  58.1 0.5 collective-permute-start.18
  58.6 3.0 %collective-permute-done.13.refs_10_ = bf16[16,128,128]{2,1,0:T(8,128)(2,1)S(1)} collective-permute-done((bf16[16,128,128]{2,1,0:T(8,128)(2,1)S(1)}, bf16[16,128,128]{2,1,0:T(8,128)(2,1)S(1)}, u32[]{:S(2)}, u32[]{:S(2)}) %collective-permute-start.13) | collective-permute-done | bytes 524320 | tf_op jit(solution)/shard_map/ppermute | solution.py:246
  61.6 1.3 %collective-permute-start.22 = (bf16[16,128,128]{2,1,0:T(8,128)(2,1)S(1)}, bf16[16,128,128]{2,1,0:T(8,128)(2,1)S(1)}, u32[]{:S(2)}, u32[]{:S(2)}) collective-permute-start(bf16[16,128,128]{2,1,0:T(8,128)(2,1)S(1)} %collective-permute-done.13.refs_10_), channel_id=1, source_target_pairs={{8,12},{9,13},{10,14},{11,15},{4,0},{5,1},{6,2},{7,3},{24,28},{25,... | collective-permute-start | bytes 1572872 | tf_op jit(solution)/shard_map/ppermute | solution.py:246
  63.0 1.5 %collective-permute-done.10.refs_7_ = bf16[4,128,256]{2,1,0:T(8,128)(2,1)S(1)} collective-permute-done((bf16[4,128,256]{2,1,0:T(8,128)(2,1)S(1)}, bf16[4,128,256]{2,1,0:T(8,128)(2,1)S(1)}, u32[]{:S(2)}, u32[]{:S(2)}) %collective-permute-start.10) | collective-permute-done | bytes 262176 | tf_op jit(solution)/shard_map/ppermute | solution.py:25
  64.5 3.0 %shard_map.82 = (bf16[3,16,128,256]{3,2,1,0:T(8,128)(2,1)S(1)}, bf16[12,128,1024]{2,1,0:T(8,128)(2,1)S(1)}, bf16[12,128,1024]{2,1,0:T(8,128)(2,1)S(1)}, bf16[16,256,256]{2,1,0:T(8,128)(2,1)S(1)}) custom-call(s32[32,128]{1,0:T(8,128)S(1)} %get-tuple-element.52.table, bf16[4,128,256]{2,1,0:T(8,128)(2,1)S(1)} %get-tuple-element.53.refs_0_, ...), custom_call_target="tpu_custom_call" | custom-call | flops 402653184 | bytes 3145728 | tf_op jit(solution)/shard_map/pallas_call | solution.py:351
  67.6 1.5 %shard_map.83 = (f32[256,512]{1,0:T(8,128)S(1)}, bf16[256,512]{1,0:T(8,128)(2,1)S(1)}, bf16[12,128,1024]{2,1,0:T(8,128)(2,1)S(1)}) custom-call(s32[32,128]{1,0:T(8,128)S(1)} %get-tuple-element.52.table, bf16[3,16,128,256]{3,2,1,0:T(8,128)(2,1)S(1)} %get-tuple-element.54.made, ...), custom_call_target="tpu_custom_call", output_to_operand_aliasing={{2}: (3, {})} | custom-call | flops 1073741824 | bytes 3145728 | tf_op jit(solution)/shard_map/pallas_call | solution.py:351
  69.1 1.7 %collective-permute-start.25 = (bf16[256,512]{1,0:T(8,128)(2,1)S(1)}, bf16[256,512]{1,0:T(8,128)(2,1)S(1)}, u32[]{:S(2)}, u32[]{:S(2)}) collective-permute-start(bf16[256,512]{1,0:T(8,128)(2,1)S(1)} %get-tuple-element.66), channel_id=1, source_target_pairs={{0,16},{16,0},{1,17},{17,1},{2,18},{18,2},{3,19},{19,3},{4,20},{20... | collective-permute-start | bytes 786440 | tf_op jit(solution)/shard_map/ppermute | solution.py:25
  70.8 5.3 %collective-permute-done.22.refs_1_ = bf16[16,128,128]{2,1,0:T(8,128)(2,1)S(1)} collective-permute-done((bf16[16,128,128]{2,1,0:T(8,128)(2,1)S(1)}, bf16[16,128,128]{2,1,0:T(8,128)(2,1)S(1)}, u32[]{:S(2)}, u32[]{:S(2)}) %collective-permute-start.22) | collective-permute-done | bytes 524320 | tf_op jit(solution)/shard_map/ppermute | solution.py:246
  76.1 1.7 %shard_map.86 = (f32[256,512]{1,0:T(8,128)S(1)}, bf16[256,512]{1,0:T(8,128)(2,1)S(1)}) custom-call(s32[32,128]{1,0:T(8,128)S(1)} %get-tuple-element.52.table, bf16[16,256,256]{2,1,0:T(8,128)(2,1)S(1)} %get-tuple-element.62.rows_held, bf16[12,128,1024]{2,1,0:T(8,128)(2,1)S(1)} %get-tuple-element.55.own, bf16[12,128,1024]{2,1,0:T(8,128)(2,1)S(1)} %get-tuple-element.57.other, ...), custom_call_target="tpu_custom_call" | custom-call | flops 1207959552 | bytes 3145728 | tf_op jit(solution)/shard_map/pallas_call | solution.py:351
  77.8 3.6 %collective-permute-start.23 = (bf16[256,512]{1,0:T(8,128)(2,1)S(1)}, bf16[256,512]{1,0:T(8,128)(2,1)S(1)}, u32[]{:S(2)}, u32[]{:S(2)}) collective-permute-start(bf16[256,512]{1,0:T(8,128)(2,1)S(1)} %get-tuple-element.64), channel_id=1, source_target_pairs={{0,16},{16,0},{1,17},{17,1},{2,18},{18,2},{3,19},{19,3},{4,20},{20... | collective-permute-start | bytes 786440 | tf_op jit(solution)/shard_map/ppermute | solution.py:25
  81.4 1.4 %shard_map.85 = (f32[256,512]{1,0:T(8,128)S(1)}, bf16[256,512]{1,0:T(8,128)(2,1)S(1)}) custom-call(s32[32,128]{1,0:T(8,128)S(1)} %get-tuple-element.52.table, bf16[3,16,128,256]{3,2,1,0:T(8,128)(2,1)S(1)} %get-tuple-element.54.made, bf16[12,128,1024]{2,1,0:T(8,128)(2,1)S(1)} %get-tuple-element.55.own, bf16[12,128,1024]{2,1,0:T(8,128)(2,1)S(1)} %get-tuple-element.57.other), custom_call_target="tpu_custom_call" | custom-call | flops 1073741824 | bytes 3145728 | tf_op jit(solution)/shard_map/pallas_call | solution.py:351
  82.8 2.8 %shard_map.84 = (f32[256,512]{1,0:T(8,128)S(1)}, bf16[256,512]{1,0:T(8,128)(2,1)S(1)}) custom-call(s32[32,128]{1,0:T(8,128)S(1)} %get-tuple-element.52.table, bf16[3,16,128,256]{3,2,1,0:T(8,128)(2,1)S(1)} %get-tuple-element.54.made, bf16[12,128,1024]{2,1,0:T(8,128)(2,1)S(1)} %get-tuple-element.55.own, bf16[12,128,1024]{2,1,0:T(8,128)(2,1)S(1)} %get-tuple-element.57.other), custom_call_target="tpu_custom_call" | custom-call | flops 1073741824 | bytes 3145728 | tf_op jit(solution)/shard_map/pallas_call | solution.py:351
  85.6 1.0 collective-permute-start.20
  86.6 1.1 %collective-permute-start.19 = (bf16[256,512]{1,0:T(8,128)(2,1)S(1)}, bf16[256,512]{1,0:T(8,128)(2,1)S(1)}, u32[]{:S(2)}, u32[]{:S(2)}) collective-permute-start(bf16[256,512]{1,0:T(8,128)(2,1)S(1)} %get-tuple-element.59), channel_id=1, source_target_pairs={{0,16},{16,0},{1,17},{17,1},{2,18},{18,2},{3,19},{19,3},{4,20},{20... | collective-permute-start | bytes 786440 | tf_op jit(solution)/shard_map/ppermute | solution.py:25
  88.0 3.2 %collective-permute-start.24 = (bf16[256,512]{1,0:T(8,128)(2,1)S(1)}, bf16[256,512]{1,0:T(8,128)(2,1)S(1)}, u32[]{:S(2)}, u32[]{:S(2)}) collective-permute-start(bf16[256,512]{1,0:T(8,128)(2,1)S(1)} %add_convert_fusion.2), channel_id=1, source_target_pairs={{0,12},{1,13},{2,14},{3,15},{12,0},{13,1},{14,2},{15,3},{16,28},{1... | collective-permute-start | bytes 786440 | tf_op jit(solution)/shard_map/ppermute | solution.py:246
  91.2 3.0 %collective-permute-done.20 = bf16[256,512]{1,0:T(8,128)(2,1)S(1)} collective-permute-done((bf16[256,512]{1,0:T(8,128)(2,1)S(1)}, bf16[256,512]{1,0:T(8,128)(2,1)S(1)}, u32[]{:S(2)}, u32[]{:S(2)}) %collective-permute-start.20) | collective-permute-done | bytes 262176 | tf_op jit(solution)/shard_map/ppermute | solution.py:25
  94.3 7.1 %collective-permute-done.26.refs_4_ = bf16[256,512]{1,0:T(8,128)(2,1)S(1)} collective-permute-done((bf16[256,512]{1,0:T(8,128)(2,1)S(1)}, bf16[256,512]{1,0:T(8,128)(2,1)S(1)}, u32[]{:S(2)}, u32[]{:S(2)}) %collective-permute-start.26) | collective-permute-done | bytes 262176 | tf_op jit(solution)/shard_map/ppermute | solution.py:246
  101.5 0.7 collective-permute-start.27
  102.3 0.5 gate.1.gate_open
  102.8 3.1 %collective-permute-done.21.refs_1_ = bf16[256,512]{1,0:T(8,128)(2,1)S(1)} collective-permute-done((bf16[256,512]{1,0:T(8,128)(2,1)S(1)}, bf16[256,512]{1,0:T(8,128)(2,1)S(1)}, u32[]{:S(2)}, u32[]{:S(2)}) %collective-permute-start.21) | collective-permute-done | bytes 262176 | tf_op jit(solution)/shard_map/ppermute | solution.py:246
  105.9 1.0 finish.1
  (56 shorter events, 1.0 us)
Async XLA Ops:
  0.0 36.9 %copy-start = (bf16[12,64,1024]{2,1,0:T(8,128)(2,1)S(1)}, bf16[12,64,1024]{2,1,0:T(8,128)(2,1)}, u32[]{:S(2)}) copy-start(bf16[12,64,1024]{2,1,0:T(8,128)(2,1)} %refs_11_.1) | copy-start | bytes 4718596
  0.0 41.9 %copy-start.3 = (bf16[1,16,128,128]{3,2,1,0:T(8,128)(2,1)S(1)}, bf16[1,16,128,128]{3,2,1,0:T(8,128)(2,1)}, u32[]{:S(2)}) copy-start(bf16[1,16,128,128]{3,2,1,0:T(8,128)(2,1)} %param.17) | copy-start | bytes 1572868
  2.4 39.0 %collective-permute-start.15 = (bf16[8,64,1024]{2,1,0:T(8,128)(2,1)}, bf16[8,64,1024]{2,1,0:T(8,128)(2,1)}, u32[]{:S(2)}, u32[]{:S(2)}) collective-permute-start(bf16[8,64,1024]{2,1,0:T(8,128)(2,1)} %slice.41), channel_id=1, source_target_pairs={{0,2},{1,3},{2,0},{3,1},{4,6},{5,7},{6,4},{7,5},{8,10},{9,11},{10,... | collective-permute-start | bytes 3145736 | tf_op jit(solution)/shard_map/ppermute | solution.py:25
  5.4 8.0 %collective-permute-start = (bf16[256,512]{1,0:T(8,128)(2,1)}, bf16[256,512]{1,0:T(8,128)(2,1)S(1)}, u32[]{:S(2)}, u32[]{:S(2)}) collective-permute-start(bf16[256,512]{1,0:T(8,128)(2,1)} %state.1), channel_id=1, source_target_pairs={{0,16},{16,0},{1,17},{17,1},{2,18},{18,2},{3,19},{19,3},{4,20},{20... | collective-permute-start | bytes 786440 | tf_op jit(solution)/shard_map/ppermute | solution.py:25
  13.4 1.0 copy-start.1
  15.0 9.0 %collective-permute-start.1 = (bf16[144,256]{1,0:T(8,128)(2,1)S(1)}, bf16[144,256]{1,0:T(8,128)(2,1)S(1)}, u32[]{:S(2)}, u32[]{:S(2)}) collective-permute-start(bf16[144,256]{1,0:T(8,128)(2,1)S(1)} %get-tuple-element.49), channel_id=1, source_target_pairs={{0,4},{1,5},{2,6},{3,7},{4,0},{5,1},{6,2},{7,3},{8,12},{9,13},{10,... | collective-permute-start | bytes 221192 | tf_op jit(solution)/shard_map/ppermute | solution.py:246
  16.7 7.8 %collective-permute-start.2 = (bf16[144,256]{1,0:T(8,128)(2,1)S(1)}, bf16[144,256]{1,0:T(8,128)(2,1)S(1)}, u32[]{:S(2)}, u32[]{:S(2)}) collective-permute-start(bf16[144,256]{1,0:T(8,128)(2,1)S(1)} %get-tuple-element.50), channel_id=1, source_target_pairs={{0,8},{1,9},{2,10},{3,11},{4,12},{5,13},{6,14},{7,15},{8,0},{9,1},... | collective-permute-start | bytes 221192 | tf_op jit(solution)/shard_map/ppermute | solution.py:246
  19.3 20.1 %collective-permute-start.12 = (bf16[16,128,128]{2,1,0:T(8,128)(2,1)}, bf16[16,128,128]{2,1,0:T(8,128)(2,1)S(1)}, u32[]{:S(2)}, u32[]{:S(2)}) collective-permute-start(bf16[16,128,128]{2,1,0:T(8,128)(2,1)} %bitcast.13), channel_id=1, source_target_pairs={{4,8},{5,9},{6,10},{7,11},{8,4},{9,5},{10,6},{11,7},{20,24},{21,25... | collective-permute-start | bytes 1572872 | tf_op jit(solution)/shard_map/ppermute | solution.py:246
  20.0 20.0 %collective-permute-start.11 = (bf16[16,128,128]{2,1,0:T(8,128)(2,1)}, bf16[16,128,128]{2,1,0:T(8,128)(2,1)}, u32[]{:S(2)}, u32[]{:S(2)}) collective-permute-start(bf16[16,128,128]{2,1,0:T(8,128)(2,1)} %bitcast.14), channel_id=1, source_target_pairs={{0,4},{1,5},{2,6},{3,7},{4,0},{5,1},{6,2},{7,3},{8,12},{9,13},{10,... | collective-permute-start | bytes 1572872 | tf_op jit(solution)/shard_map/ppermute | solution.py:246
  24.0 17.4 %collective-permute-start.17 = (bf16[4,64,1024]{2,1,0:T(8,128)(2,1)}, bf16[4,64,1024]{2,1,0:T(8,128)(2,1)S(1)}, u32[]{:S(2)}, u32[]{:S(2)}) collective-permute-start(bf16[4,64,1024]{2,1,0:T(8,128)(2,1)} %slice.42), channel_id=1, source_target_pairs={{0,2},{1,3},{2,0},{3,1},{4,6},{5,7},{6,4},{7,5},{8,10},{9,11},{10,... | collective-permute-start | bytes 1572872 | tf_op jit(solution)/shard_map/ppermute | solution.py:25
  24.5 0.6 copy-start.5
  25.2 11.1 %collective-permute-start.3 = (bf16[144,256]{1,0:T(8,128)(2,1)S(1)}, bf16[144,256]{1,0:T(8,128)(2,1)S(1)}, u32[]{:S(2)}, u32[]{:S(2)}) collective-permute-start(bf16[144,256]{1,0:T(8,128)(2,1)S(1)} %get-tuple-element.51), channel_id=1, source_target_pairs={{0,12},{1,13},{2,14},{3,15},{4,8},{5,9},{6,10},{7,11},{8,4},{9,5},... | collective-permute-start | bytes 221192 | tf_op jit(solution)/shard_map/ppermute | solution.py:246
  36.3 0.6 copy-start.7
  36.9 27.6 %collective-permute-start.14 = (bf16[12,64,1024]{2,1,0:T(8,128)(2,1)S(1)}, bf16[12,64,1024]{2,1,0:T(8,128)(2,1)}, u32[]{:S(2)}, u32[]{:S(2)}) collective-permute-start(bf16[12,64,1024]{2,1,0:T(8,128)(2,1)S(1)} %copy-done), channel_id=1, source_target_pairs={{0,1},{1,0},{2,3},{3,2},{4,5},{5,4},{6,7},{7,6},{8,9},{9,8},{10,11... | collective-permute-start | bytes 4718600 | tf_op jit(solution)/shard_map/ppermute | solution.py:25
  37.0 0.9 copy-start.6
  37.9 0.9 copy-start.8
  39.3 8.8 %collective-permute-start.4 = (bf16[4,128,256]{2,1,0:T(8,128)(2,1)S(1)}, bf16[4,128,256]{2,1,0:T(8,128)(2,1)S(1)}, u32[]{:S(2)}, u32[]{:S(2)}) collective-permute-start(bf16[4,128,256]{2,1,0:T(8,128)(2,1)S(1)} %get-tuple-element.53.refs_0_), channel_id=1, source_target_pairs={{0,2},{1,3},{2,0},{3,1},{4,6},{5,7},{6,4},{7,5},{8,10},{9,11},{10,... | collective-permute-start | bytes 786440 | tf_op jit(solution)/shard_map/ppermute | solution.py:25
  39.9 10.6 %collective-permute-start.5 = (bf16[4,128,256]{2,1,0:T(8,128)(2,1)S(1)}, bf16[4,128,256]{2,1,0:T(8,128)(2,1)S(1)}, u32[]{:S(2)}, u32[]{:S(2)}) collective-permute-start(bf16[4,128,256]{2,1,0:T(8,128)(2,1)S(1)} %get-tuple-element.53.refs_0_), channel_id=1, source_target_pairs={{0,16},{16,0},{1,17},{17,1},{2,18},{18,2},{3,19},{19,3},{4,20},{20... | collective-permute-start | bytes 786440 | tf_op jit(solution)/shard_map/ppermute | solution.py:25
  41.4 10.6 %collective-permute-start.7 = (bf16[4,128,256]{2,1,0:T(8,128)(2,1)S(1)}, bf16[4,128,256]{2,1,0:T(8,128)(2,1)S(1)}, u32[]{:S(2)}, u32[]{:S(2)}) collective-permute-start(bf16[4,128,256]{2,1,0:T(8,128)(2,1)S(1)} %get-tuple-element.53.refs_0_), channel_id=1, source_target_pairs={{0,1},{1,0},{2,3},{3,2},{4,5},{5,4},{6,7},{7,6},{8,9},{9,8},{10,11... | collective-permute-start | bytes 786440 | tf_op jit(solution)/shard_map/ppermute | solution.py:25
  41.4 23.1 %collective-permute-start.16 = (bf16[8,64,1024]{2,1,0:T(8,128)(2,1)}, bf16[8,64,1024]{2,1,0:T(8,128)(2,1)S(1)}, u32[]{:S(2)}, u32[]{:S(2)}) collective-permute-start(bf16[8,64,1024]{2,1,0:T(8,128)(2,1)} %collective-permute-done.15.refs_13_), channel_id=1, source_target_pairs={{0,1},{1,0},{2,3},{3,2},{4,5},{5,4},{6,7},{7,6},{8,9},{9,8},{10,11... | collective-permute-start | bytes 3145736 | tf_op jit(solution)/shard_map/ppermute | solution.py:25
  48.1 13.5 %collective-permute-start.13 = (bf16[16,128,128]{2,1,0:T(8,128)(2,1)S(1)}, bf16[16,128,128]{2,1,0:T(8,128)(2,1)S(1)}, u32[]{:S(2)}, u32[]{:S(2)}) collective-permute-start(bf16[16,128,128]{2,1,0:T(8,128)(2,1)S(1)} %broadcast_select_fusion), channel_id=1, source_target_pairs={{0,8},{1,9},{2,10},{3,11},{8,12},{9,13},{10,14},{11,15},{12,4},{13... | collective-permute-start | bytes 1572872 | tf_op jit(solution)/shard_map/ppermute | solution.py:246
  50.5 7.6 %collective-permute-start.6 = (bf16[4,128,256]{2,1,0:T(8,128)(2,1)S(1)}, bf16[4,128,256]{2,1,0:T(8,128)(2,1)S(1)}, u32[]{:S(2)}, u32[]{:S(2)}) collective-permute-start(bf16[4,128,256]{2,1,0:T(8,128)(2,1)S(1)} %collective-permute-done.4.refs_1_), channel_id=1, source_target_pairs={{0,16},{16,0},{1,17},{17,1},{2,18},{18,2},{3,19},{19,3},{4,20},{20... | collective-permute-start | bytes 786440 | tf_op jit(solution)/shard_map/ppermute | solution.py:25
  52.0 6.1 %collective-permute-start.8 = (bf16[4,128,256]{2,1,0:T(8,128)(2,1)S(1)}, bf16[4,128,256]{2,1,0:T(8,128)(2,1)S(1)}, u32[]{:S(2)}, u32[]{:S(2)}) collective-permute-start(bf16[4,128,256]{2,1,0:T(8,128)(2,1)S(1)} %collective-permute-done.4.refs_1_), channel_id=1, source_target_pairs={{0,1},{1,0},{2,3},{3,2},{4,5},{5,4},{6,7},{7,6},{8,9},{9,8},{10,11... | collective-permute-start | bytes 786440 | tf_op jit(solution)/shard_map/ppermute | solution.py:25
  58.1 4.8 %collective-permute-start.9 = (bf16[4,128,256]{2,1,0:T(8,128)(2,1)S(1)}, bf16[4,128,256]{2,1,0:T(8,128)(2,1)S(1)}, u32[]{:S(2)}, u32[]{:S(2)}) collective-permute-start(bf16[4,128,256]{2,1,0:T(8,128)(2,1)S(1)} %collective-permute-done.5.refs_2_), channel_id=1, source_target_pairs={{0,1},{1,0},{2,3},{3,2},{4,5},{5,4},{6,7},{7,6},{8,9},{9,8},{10,11... | collective-permute-start | bytes 786440 | tf_op jit(solution)/shard_map/ppermute | solution.py:25
  58.1 9.4 %collective-permute-start.18 = (bf16[4,64,1024]{2,1,0:T(8,128)(2,1)S(1)}, bf16[4,64,1024]{2,1,0:T(8,128)(2,1)S(1)}, u32[]{:S(2)}, u32[]{:S(2)}) collective-permute-start(bf16[4,64,1024]{2,1,0:T(8,128)(2,1)S(1)} %collective-permute-done.17.refs_0_), channel_id=1, source_target_pairs={{0,1},{1,0},{2,3},{3,2},{4,5},{5,4},{6,7},{7,6},{8,9},{9,8},{10,11... | collective-permute-start | bytes 1572872 | tf_op jit(solution)/shard_map/ppermute | solution.py:25
  61.6 14.5 %collective-permute-start.22 = (bf16[16,128,128]{2,1,0:T(8,128)(2,1)S(1)}, bf16[16,128,128]{2,1,0:T(8,128)(2,1)S(1)}, u32[]{:S(2)}, u32[]{:S(2)}) collective-permute-start(bf16[16,128,128]{2,1,0:T(8,128)(2,1)S(1)} %collective-permute-done.13.refs_10_), channel_id=1, source_target_pairs={{8,12},{9,13},{10,14},{11,15},{4,0},{5,1},{6,2},{7,3},{24,28},{25,... | collective-permute-start | bytes 1572872 | tf_op jit(solution)/shard_map/ppermute | solution.py:246
  62.9 1.6 %collective-permute-start.10 = (bf16[4,128,256]{2,1,0:T(8,128)(2,1)S(1)}, bf16[4,128,256]{2,1,0:T(8,128)(2,1)S(1)}, u32[]{:S(2)}, u32[]{:S(2)}) collective-permute-start(bf16[4,128,256]{2,1,0:T(8,128)(2,1)S(1)} %collective-permute-done.6.refs_3_), channel_id=1, source_target_pairs={{0,1},{1,0},{2,3},{3,2},{4,5},{5,4},{6,7},{7,6},{8,9},{9,8},{10,11... | collective-permute-start | bytes 786440 | tf_op jit(solution)/shard_map/ppermute | solution.py:25
  69.1 18.6 %collective-permute-start.25 = (bf16[256,512]{1,0:T(8,128)(2,1)S(1)}, bf16[256,512]{1,0:T(8,128)(2,1)S(1)}, u32[]{:S(2)}, u32[]{:S(2)}) collective-permute-start(bf16[256,512]{1,0:T(8,128)(2,1)S(1)} %get-tuple-element.66), channel_id=1, source_target_pairs={{0,16},{16,0},{1,17},{17,1},{2,18},{18,2},{3,19},{19,3},{4,20},{20... | collective-permute-start | bytes 786440 | tf_op jit(solution)/shard_map/ppermute | solution.py:25
  77.8 10.1 %collective-permute-start.23 = (bf16[256,512]{1,0:T(8,128)(2,1)S(1)}, bf16[256,512]{1,0:T(8,128)(2,1)S(1)}, u32[]{:S(2)}, u32[]{:S(2)}) collective-permute-start(bf16[256,512]{1,0:T(8,128)(2,1)S(1)} %get-tuple-element.64), channel_id=1, source_target_pairs={{0,16},{16,0},{1,17},{17,1},{2,18},{18,2},{3,19},{19,3},{4,20},{20... | collective-permute-start | bytes 786440 | tf_op jit(solution)/shard_map/ppermute | solution.py:25
  85.6 16.6 %copy-start.2 = (bf16[256,512]{1,0:T(8,128)(2,1)S(1)}, bf16[256,512]{1,0:T(8,128)(2,1)}, u32[]{:S(2)}) copy-start(bf16[256,512]{1,0:T(8,128)(2,1)} %state.1) | copy-start | bytes 786436
  85.6 16.6 %copy-start.4 = (bf16[1024,512]{1,0:T(8,128)(2,1)S(1)}, bf16[1024,512]{1,0:T(8,128)(2,1)}, u32[]{:S(2)}) copy-start(bf16[1024,512]{1,0:T(8,128)(2,1)} %weight.1) | copy-start | bytes 3145732
  85.6 16.6 %copy-start.10 = (f32[512]{0:T(512)S(1)}, f32[512]{0:T(512)}, u32[]{:S(2)}) copy-start(f32[512]{0:T(512)} %param.15) | copy-start | bytes 6148
  85.6 8.6 %collective-permute-start.20 = (bf16[256,512]{1,0:T(8,128)(2,1)S(1)}, bf16[256,512]{1,0:T(8,128)(2,1)S(1)}, u32[]{:S(2)}, u32[]{:S(2)}) collective-permute-start(bf16[256,512]{1,0:T(8,128)(2,1)S(1)} %get-tuple-element.61), channel_id=1, source_target_pairs={{0,16},{16,0},{1,17},{17,1},{2,18},{18,2},{3,19},{19,3},{4,20},{20... | collective-permute-start | bytes 786440 | tf_op jit(solution)/shard_map/ppermute | solution.py:25
  86.6 16.1 %collective-permute-start.19 = (bf16[256,512]{1,0:T(8,128)(2,1)S(1)}, bf16[256,512]{1,0:T(8,128)(2,1)S(1)}, u32[]{:S(2)}, u32[]{:S(2)}) collective-permute-start(bf16[256,512]{1,0:T(8,128)(2,1)S(1)} %get-tuple-element.59), channel_id=1, source_target_pairs={{0,16},{16,0},{1,17},{17,1},{2,18},{18,2},{3,19},{19,3},{4,20},{20... | collective-permute-start | bytes 786440 | tf_op jit(solution)/shard_map/ppermute | solution.py:25
  87.8 13.7 %collective-permute-start.26 = (bf16[256,512]{1,0:T(8,128)(2,1)S(1)}, bf16[256,512]{1,0:T(8,128)(2,1)S(1)}, u32[]{:S(2)}, u32[]{:S(2)}) collective-permute-start(bf16[256,512]{1,0:T(8,128)(2,1)S(1)} %add_convert_fusion.1), channel_id=1, source_target_pairs={{0,4},{1,5},{2,6},{3,7},{4,12},{5,13},{6,14},{7,15},{12,8},{13,9},... | collective-permute-start | bytes 786440 | tf_op jit(solution)/shard_map/ppermute | solution.py:246
  87.9 18.1 %copy-start.9 = (f32[512]{0:T(512)S(1)}, f32[512]{0:T(512)}, u32[]{:S(2)}) copy-start(f32[512]{0:T(512)} %param.16) | copy-start | bytes 6148
  88.0 14.8 %collective-permute-start.24 = (bf16[256,512]{1,0:T(8,128)(2,1)S(1)}, bf16[256,512]{1,0:T(8,128)(2,1)S(1)}, u32[]{:S(2)}, u32[]{:S(2)}) collective-permute-start(bf16[256,512]{1,0:T(8,128)(2,1)S(1)} %add_convert_fusion.2), channel_id=1, source_target_pairs={{0,12},{1,13},{2,14},{3,15},{12,0},{13,1},{14,2},{15,3},{16,28},{1... | collective-permute-start | bytes 786440 | tf_op jit(solution)/shard_map/ppermute | solution.py:246
  94.3 11.7 %collective-permute-start.21 = (bf16[256,512]{1,0:T(8,128)(2,1)S(1)}, bf16[256,512]{1,0:T(8,128)(2,1)S(1)}, u32[]{:S(2)}, u32[]{:S(2)}) collective-permute-start(bf16[256,512]{1,0:T(8,128)(2,1)S(1)} %add_convert_fusion.3), channel_id=1, source_target_pairs={{0,4},{1,5},{2,6},{3,7},{4,0},{5,1},{6,2},{7,3},{8,12},{9,13},{10,... | collective-permute-start | bytes 786440 | tf_op jit(solution)/shard_map/ppermute | solution.py:246
  101.5 4.4 %collective-permute-start.27 = (bf16[256,512]{1,0:T(8,128)(2,1)S(1)}, bf16[256,512]{1,0:T(8,128)(2,1)S(1)}, u32[]{:S(2)}, u32[]{:S(2)}) collective-permute-start(bf16[256,512]{1,0:T(8,128)(2,1)S(1)} %add_convert_fusion), channel_id=1, source_target_pairs={{4,8},{5,9},{6,10},{7,11},{8,4},{9,5},{10,6},{11,7},{20,24},{21,25... | collective-permute-start | bytes 786440 | tf_op jit(solution)/shard_map/ppermute | solution.py:246
